TPU v7x, 32 devices: a whole 2x2x4 slice. The times are simulated.
32 devices in a mesh: parts: 2 (over y), row: 4 (over x, core), dp: 4 (over z).
Axes of the slice: x: 2, y: 2, z: 4, core: 2. Of those that a mesh axis runs over, the one named last changes fastest.
Arguments:
- activations: bfloat16 [1024, 13312], P(('parts', 'dp'), 'row'), parts along dimension 0, may hold values from -6 to 6
- cotangent: bfloat16 [1024, 8192], P(('parts', 'dp'), 'row'), parts along dimension 0, may hold values from -0.19921875 to 0.19921875
- forget_labels: int32 [1024], P(('parts', 'dp')), parts along dimension 0, may hold values 0 or 1
- kept_blocks: bfloat16 [4, 256, 128, 128], P('row', 'dp'), may hold values from -0.09375 to 0.09375
- block_ids: int32 [4, 256], P('row', 'dp'), may hold values from -1 to 1663, as said below
- adapter_a: bfloat16 [13312, 64], P('row'), may hold values from -0.0546875 to 0.0546875
- output_adapter: bfloat16 [64, 8192], P(None, 'row'), may hold values from -0.75 to 0.75
Outputs:
- projected: bfloat16 [1024, 8192], P(('parts', 'dp'), 'row'), parts along dimension 0
- input_adapter_gradient: float32 [26624, 64], P(('parts', 'row')), parts along dimension 0
- output_adapter_gradient: float32 [128, 8192], P('parts', 'row'), parts along dimension 0
There are 2 independent parts, one for each index of `parts`. A program takes and returns all parts, laid end to end along the dimension named above; an argument that names none is the same for every part. Nothing has to cross between parts.
Inputs may be any that keep to these rules, and one draw needn't show every extreme that they name: Each row of block_ids names distinct blocks of its row shard, live slots first and -1 after them; one row shard fills all 256 slots and the emptiest fills half of them; every row shard holds its last block.
All inputs are finite; a program needn't handle non-finite values. No bound on the sum of `forget_labels` on one device may be relied on, other than what follows from the above.
Results may differ from a plain program's by a relative error of at most 0.0048.
Values may be sent and summed in bfloat16 or wider, within the bound.
No kernel may reach another device: no remote copies, remote signals or barrier semaphores. Data moves between devices by JAX's collectives and lax.ppermute only.
A program may use at most 192 MiB of HBM per device.

v0:
```python
import jax
import jax.numpy as jnp
from jax import lax
from jax.sharding import PartitionSpec as P

D = 8192


adapter_scale = 2.0


def body(activations, cotangent, forget_labels, kept_blocks, block_ids, adapter_a, output_adapter):
    tokens_here = activations.shape[0]
    shard_rows = activations.shape[1]
    tile = kept_blocks.shape[-1]
    row_blocks = shard_rows // tile
    col_blocks = D // tile
    low_part = jnp.dot(activations, adapter_a, preferred_element_type=jnp.float32)
    signs = (1 - 2 * forget_labels).astype(cotangent.dtype)
    signed_cotangent = cotangent * signs[:, None]
    tiled_rows = activations.reshape(tokens_here, row_blocks, tile)
    empty = jnp.zeros((col_blocks, tokens_here, tile), jnp.float32)
    weights = lax.all_gather(kept_blocks, "dp", axis=1, tiled=True)[0]
    idents = lax.all_gather(block_ids, "dp", axis=1, tiled=True)[0]
    block_row = jnp.maximum(idents, 0) // col_blocks
    block_col = jnp.where(idents >= 0, idents % col_blocks, col_blocks).astype(jnp.int32)
    picked = jnp.take(tiled_rows, block_row, axis=1)
    products = jnp.einsum("tkb,kbn->ktn", picked, weights, preferred_element_type=jnp.float32)
    partial_value = empty.at[block_col].add(products, mode="drop")
    partial_value = partial_value.transpose(1, 0, 2).reshape(tokens_here, D)
    frozen_product = lax.psum_scatter(partial_value, "row", scatter_dimension=1, tiled=True)
    low = lax.psum(low_part, "row")
    signed_all, adapter_all = (
        lax.all_gather(signed_cotangent, "row", axis=1, tiled=True),
        lax.all_gather(output_adapter, "row", axis=1, tiled=True),
    )
    back = lax.dot_general(
        signed_all, adapter_all, (((1,), (1,)), ((), ())), preferred_element_type=jnp.float32
    )
    low_rank_output = low.astype(jnp.bfloat16)
    projected = (
        frozen_product
        + adapter_scale
        * jnp.dot(low_rank_output, output_adapter, preferred_element_type=jnp.float32)
    ).astype(jnp.bfloat16)
    output_gradient_piece = adapter_scale * lax.dot_general(
        low_rank_output,
        signed_cotangent,
        (((0,), (0,)), ((), ())),
        preferred_element_type=jnp.float32,
    )
    backward_output_adapter = back.astype(jnp.bfloat16)
    input_gradient_piece = adapter_scale * lax.dot_general(
        activations,
        backward_output_adapter,
        (((0,), (0,)), ((), ())),
        preferred_element_type=jnp.float32,
    )
    input_adapter_gradient, output_adapter_gradient = lax.psum(
        (input_gradient_piece, output_gradient_piece), "dp"
    )
    return (projected, input_adapter_gradient, output_adapter_gradient)


def solution(mesh):
    placed = (
        P(("parts", "dp"), "row"),
        P(("parts", "dp"), "row"),
        P(("parts", "dp")),
        P("row", "dp", None, None),
        P("row", "dp"),
        P("row", None),
        P(None, "row"),
    )
    return jax.shard_map(
        body,
        mesh=mesh,
        in_specs=placed,
        out_specs=(P(("parts", "dp"), "row"), P(("parts", "row"), None), P("parts", "row")),
        check_vma=False,
    )
```

profile of v0, /device:TPU:0, one launch (start us, length us, event | category | flops | bytes accessed | tf_op | source)
XLA Modules:
  0.0 352.6 jit_solution(9419142973890749879)
XLA Ops:
  7.2 0.0 all-gather.4.cloned.1.call-start
  7.2 0.7 all-gather.4.cloned.1.call-update
  7.9 0.0 all-gather.8.cloned.1.call-start
  8.0 0.7 all-gather.8.cloned.1.call-update
  8.7 0.0 all-gather.6.cloned.1.call-start
  8.7 0.7 subtract_convert_fusion
  9.4 1.9 broadcast_multiply_fusion
  11.3 0.0 all-gather.6.cloned.1.call-update
  11.3 0.0 reduce-scatter.2.cloned.1.call-start
  11.4 1.2 dynamic-slice
  13.3 0.8 bitcast_dynamic-update-slice_fusion
  14.0 9.9 %all-reduce = s32[256]{0:T(256)S(1)} all-reduce(s32[256]{0:T(256)S(1)} %bitcast_dynamic-update-slice_fusion), channel_id=1, replica_groups=mesh['parts'=2,'row'=4,'dp'=4] {'dp'}, use_global_device_ids=true, to_apply=%add | all-reduce | flops 256 | bytes 2048
  24.0 1.6 copy.13
  25.6 0.6 copy.14
  26.2 8.6 %gather_fusion = bf16[256,128,128]{2,1,0:T(8,128)(2,1)} fusion(bf16[128,26,128]{2,0,1:T(8,128)(2,1)S(1)} %copy.14, s32[1024]{0:T(1024)S(1)} %pad_clamp_fusion), kind=kCustom, calls=%fused_computation | custom fusion | bytes 16778240 | tf_op jit(solution)/shard_map/jit(_take)/gather | solution.py:27
  34.9 127.1 %all-gather.4.cloned.1.call-done = bf16[1,256,128,128]{3,2,0,1:T(8,128)(2,1)} async-done(((bf16[1,64,128,128]{3,2,0,1:T(8,128)(2,1)}), bf16[1,256,128,128]{3,2,0,1:T(8,128)(2,1)}) %all-gather.4.cloned.1.call-update) | async-done | bytes 8388624 | tf_op jit(solution)/shard_map/all_gather | solution.py:23
  162.0 13.9 %fusion = f32[256,128,128]{2,1,0:T(8,128)} fusion(bf16[1,256,128,128]{3,2,0,1:T(8,128)(2,1)} %all-gather.4.cloned.1.call-done, bf16[256,128,128]{2,1,0:T(8,128)(2,1)} %gather_fusion, pred[256]{0:T(512)(128)(4,1)S(1)} %compare_and_fusion), kind=kOutput, calls=%fused_computation.2 | convolution fusion | flops 1077936128 | bytes 33554688 | tf_op jit(solution)/shard_map/tkb,kbn->ktn/dot_general | solution.py:28
  175.9 2.4 broadcast_in_dim.17
  178.3 51.6 %scatter_fusion = f32[64,128,128]{2,1,0:T(8,128)} fusion(f32[64,128,128]{2,1,0:T(8,128)} %broadcast_in_dim.17, s32[256]{0:T(256)S(1)} %bitcast.34, f32[256,128,128]{2,1,0:T(8,128)} %fusion), kind=kCustom, calls=%fused_computation.1 | custom fusion | flops 4194304 | bytes 50332672 | tf_op jit(solution)/shard_map/scatter-add | solution.py:29
  229.9 4.6 %copy_bitcast_fusion = f32[128,8192]{1,0:T(8,128)} fusion(f32[64,128,128]{2,1,0:T(8,128)} %scatter_fusion), kind=kLoop, calls=%fused_computation.9 | loop fusion | bytes 8388608 | tf_op jit(solution)/shard_map/reshape | solution.py:30
  234.6 0.0 reduce-scatter.2.cloned.1.call-update
  234.6 0.0 all-reduce.4.cloned.1.call-start
  234.7 0.4 fusion.14
  235.1 10.8 %psum.21 = bf16[128,64]{0,1:T(8,128)(2,1)S(1)} all-reduce(f32[128,64]{0,1:T(8,128)S(1)} %fusion.14), channel_id=1, replica_groups=mesh['parts'=2,'row'=4,'dp'=4] {'row'}, use_global_device_ids=true, to_apply=%region_2.3 | all-reduce | flops 8192 | bytes 49152 | tf_op jit(solution)/shard_map/psum | solution.py:32
  245.9 1.0 convolution_multiply_fusion.2
  246.9 4.0 %fusion.5 = f32[3328,64]{0,1:T(8,128)} fusion(bf16[128,3328]{1,0:T(8,128)(2,1)S(1)} %copy-done.1, bf16[128,8192]{1,0:T(8,128)(2,1)} %all-gather.6.cloned.1.call-done, bf16[64,8192]{1,0:T(8,128)(2,1)} %all-gather.8.cloned.1.call-done), kind=kOutput, calls=%fused_computation.8 | convolution fusion | flops 188964864 | bytes 4849664 | tf_op jit(solution)/shard_map/dot_general | solution.py:53
  250.9 0.0 all-reduce.4.cloned.1.call-update
  251.0 25.7 %reduce-scatter.2.cloned.1.call-done = f32[128,2048]{1,0:T(8,128)} async-done(((f32[128,8192]{1,0:T(8,128)}), f32[128,2048]{1,0:T(8,128)}) %reduce-scatter.2.cloned.1.call-update) | async-done | bytes 1048592 | tf_op jit(solution)/shard_map/reduce_scatter | solution.py:31
  276.7 2.3 fusion.8
  279.0 63.1 %all-reduce.4.cloned.1.call-done = (f32[3328,64]{0,1:T(8,128)}, f32[64,2048]{1,0:T(8,128)}) async-done(((f32[3328,64]{0,1:T(8,128)}, f32[64,2048]{1,0:T(8,128)}), (f32[3328,64]{0,1:T(8,128)}, f32[64,2048]{1,0:T(8,128)})) %all-reduce.4.cloned.1.call-update) | async-done | bytes 1376272 | tf_op jit(solution)/shard_map/psum | solution.py:59
  342.1 2.1 copy.23
  344.2 1.9 copy.24
  (16 shorter events, 0.1 us)
Async XLA Ops:
  7.2 227.5 %copy-start = (bf16[3328,64]{0,1:T(8,128)(2,1)S(1)}, bf16[3328,64]{0,1:T(8,128)(2,1)}, u32[]{:S(2)}) copy-start(bf16[3328,64]{0,1:T(8,128)(2,1)} %param.12) | copy-start | bytes 1277956
  7.2 154.8 %all-gather.4.cloned.1.call-start = ((), (), s32[]{:S(2)}) async-start(), calls=%async_computation.1 | async-start | bytes 10485760 | tf_op jit(solution)/shard_map/all_gather | solution.py:23
  7.9 239.0 %all-gather.8.cloned.1.call-start = ((), (), s32[]{:S(2)}) async-start(), calls=%async_computation.4 | async-start | bytes 1310720 | tf_op jit(solution)/shard_map/all_gather | solution.py:35
  8.7 238.3 %all-gather.6.cloned.1.call-start = ((), (), s32[]{:S(2)}) async-start(), calls=%async_computation.3 | async-start | bytes 2621440 | tf_op jit(solution)/shard_map/all_gather | solution.py:34
  11.3 265.3 %reduce-scatter.2.cloned.1.call-start = ((), (), s32[]{:S(2)}) async-start(), calls=%async_computation.2 | async-start | bytes 5242880 | tf_op jit(solution)/shard_map/reduce_scatter | solution.py:31
  229.9 4.7 %copy-start.1 = (bf16[128,3328]{1,0:T(8,128)(2,1)S(1)}, bf16[128,3328]{1,0:T(8,128)(2,1)}, u32[]{:S(2)}) copy-start(bf16[128,3328]{1,0:T(8,128)(2,1)} %param.7) | copy-start | bytes 2555908
  229.9 16.0 %copy-start.2 = (bf16[128,2048]{1,0:T(8,128)(2,1)S(1)}, bf16[128,2048]{1,0:T(8,128)(2,1)}, u32[]{:S(2)}) copy-start(bf16[128,2048]{1,0:T(8,128)(2,1)} %broadcast_multiply_fusion) | copy-start | bytes 1572868
  234.6 42.1 %copy-start.3 = (bf16[64,2048]{1,0:T(8,128)(2,1)S(1)}, bf16[64,2048]{1,0:T(8,128)(2,1)}, u32[]{:S(2)}) copy-start(bf16[64,2048]{1,0:T(8,128)(2,1)} %param.13) | copy-start | bytes 786436
  234.6 107.5 %all-reduce.4.cloned.1.call-start = ((), (), s32[]{:S(2)}) async-start(), calls=%async_computation.5 | async-start | bytes 2752512 | tf_op jit(solution)/shard_map/psum | solution.py:59
Sparse Core Ops, SparseCore 0:
  9.6 152.3 all-gather.3
  163.5 14.9 all-gather.7
  180.6 22.5 all-gather.5
  234.7 41.8 reduce-scatter.1
  279.7 62.3 all-reduce.3
where the time goes:
time: 353 us
  waiting for transfers between devices  217 us (61%)
  other arithmetic  54.3 us (15%)
  local copies, waits for them, and re-layouts  23.9 us (7%)
  matrix products  21.7 us (6%)
  blocking collectives  20.7 us (6%)
  between operations  14.5 us (4%)
    all_gather x1, waiting for transfers between devices, body(): weights = lax.all_gather(kept_blocks, 'dp', axis=1, tiled=True)[0]  127 us
    psum x1, waiting for transfers between devices, body(): lax.psum((input_gradient_piece, output_gradient_piece), 'dp')  63.1 us
    scatter-add x1, other arithmetic, body(): partial_value = empty.at[block_col].add(products, mode='drop')  51.6 us
    reduce_scatter x1, waiting for transfers between devices, body(): lax.psum_scatter(partial_value, 'row', scatter_dimension=1, tiled=True)  25.7 us
    dot_general x1, matrix products, body(): jnp.einsum('tkb,kbn->ktn', picked, weights, preferred_element_type=jnp.fl...  13.9 us
    psum x1, blocking collectives, body(): low = lax.psum(low_part, 'row')  10.8 us
    unnamed x1, blocking collectives  9.89 us
    gather x1, local copies, waits for them, and re-layouts, body(): picked = jnp.take(tiled_rows, block_row, axis=1)  8.62 us
  transfers between devices with their start and end apart: 5, of which 3 were waited for; matrix products, arithmetic and copies ran while one was open for 27% of the time, Pallas kernels for 0%

commit v1 on v0

v1 whole, which is shorter than its diff:
```python
import functools

import jax
import jax.numpy as jnp
from jax import lax
from jax.experimental import pallas as pl
from jax.experimental.pallas import tpu as pltpu
from jax.sharding import PartitionSpec as P

D = 8192

adapter_scale = 2.0

F32 = jnp.float32
BF16 = jnp.bfloat16


def fill_tiles(tiles_ref, own_ref, mate_ref):
    row_blocks, _, tile = tiles_ref.shape
    tokens = own_ref.shape[0]
    for i in range(row_blocks):
        tiles_ref[i, :tokens, :] = own_ref[:, i * tile:(i + 1) * tile]
        tiles_ref[i, tokens:, :] = mate_ref[:, i * tile:(i + 1) * tile]


def add_blocks(sum_ref, tiles_ref, blocks_ref, ids_ref, base, col_blocks, unroll):
    count = blocks_ref.shape[0]

    def one(step, carry):
        for u in range(unroll):
            k = step * unroll + u
            ident = ids_ref[base + k]
            live = ident >= 0
            row = jnp.where(live, ident, 0) // col_blocks
            col = jnp.where(live, ident % col_blocks, col_blocks)
            sum_ref[col] += jnp.dot(tiles_ref[row], blocks_ref[k], preferred_element_type=F32)
        return carry

    lax.fori_loop(0, count // unroll, one, 0)


def first_kernel(ids_ref, own_ref, mate_ref, blocks_ref, total_ref, tiles_ref, sum_ref, *, col_blocks):
    sum_ref[...] = jnp.zeros_like(sum_ref)
    fill_tiles(tiles_ref, own_ref, mate_ref)
    add_blocks(sum_ref, tiles_ref, blocks_ref, ids_ref, 0, col_blocks, 8)
    total_ref[...] = sum_ref[:col_blocks]


def more_kernel(base_ref, ids_ref, own_ref, mate_ref, total_in_ref, *rest, col_blocks, count):
    blocks, (total_ref, tiles_ref, sum_ref) = rest[:count], rest[count:]
    fill_tiles(tiles_ref, own_ref, mate_ref)
    sum_ref[:col_blocks] = total_in_ref[...]
    for j, blocks_ref in enumerate(blocks):
        add_blocks(sum_ref, tiles_ref, blocks_ref, ids_ref, base_ref[j], col_blocks, blocks_ref.shape[0])
    total_ref[...] = sum_ref[:col_blocks]


def last_kernel(base_ref, ids_ref, own_ref, mate_ref, total_in_ref, *rest, col_blocks, count):
    blocks, (send_mate, keep_mate, send_own, keep_own, tiles_ref, sum_ref) = rest[:count], rest[count:]
    tokens = own_ref.shape[0]
    chips, share = keep_own.shape[0], keep_own.shape[1]
    fill_tiles(tiles_ref, own_ref, mate_ref)
    sum_ref[:col_blocks] = total_in_ref[...]
    for j, blocks_ref in enumerate(blocks):
        add_blocks(sum_ref, tiles_ref, blocks_ref, ids_ref, base_ref[j], col_blocks, blocks_ref.shape[0])
    core = base_ref[count]
    for chip in range(chips):
        mine = (2 * chip + core) * share
        other = (2 * chip + 1 - core) * share
        for q in range(share):
            send_mate[chip, q] = sum_ref[other + q, tokens:, :].astype(BF16)
            keep_mate[chip, q] = sum_ref[mine + q, tokens:, :]
            send_own[chip, q] = sum_ref[other + q, :tokens, :].astype(BF16)
            keep_own[chip, q] = sum_ref[mine + q, :tokens, :]


def final_kernel(low_ref, adapter_ref, keep_ref, core_ref, *rest):
    pieces, out_ref = rest[:-1], rest[-1]
    share, _, tile = keep_ref.shape
    for q in range(share):
        total = keep_ref[q] + core_ref[q].astype(F32)
        for piece in pieces:
            total += piece[q].astype(F32)
        cols = slice(q * tile, (q + 1) * tile)
        extra = jnp.dot(low_ref[...], adapter_ref[:, cols], preferred_element_type=F32)
        out_ref[:, cols] = (total + adapter_scale * extra).astype(BF16)


VMEM_LIMIT = 48 * 1024 * 1024
smem = functools.partial(pl.BlockSpec, memory_space=pltpu.SMEM)
vmem = functools.partial(pl.BlockSpec, memory_space=pltpu.VMEM)


def call(kernel, outs, scratch, scalars, arrays):
    return pl.pallas_call(
        kernel,
        out_shape=outs,
        in_specs=[smem()] * len(scalars) + [vmem()] * len(arrays),
        out_specs=jax.tree.map(lambda _: vmem(), outs),
        scratch_shapes=scratch,
        compiler_params=pltpu.CompilerParams(vmem_limit_bytes=VMEM_LIMIT),
    )(*scalars, *arrays)


def make_body(n_parts, n_row, n_dp):
    chips = n_row // 2
    group = n_dp // 2

    def core_swap(value):
        return lax.ppermute(value, "row", [(i, i ^ 1) for i in range(n_row)])

    def chip_shift(value, d):
        pairs = [(2 * a + c, 2 * ((a + d) % chips) + c) for a in range(chips) for c in range(2)]
        return lax.ppermute(value, "row", pairs)

    def mate_swap(value):
        return lax.ppermute(value, "dp", [(i, i ^ 1) for i in range(n_dp)])

    def group_shift(value, d):
        pairs = [(2 * a + h, 2 * ((a + d) % group) + h) for a in range(group) for h in range(2)]
        return lax.ppermute(value, "dp", pairs)

    def part_shift(value, d):
        return lax.ppermute(value, "parts", [(i, (i + d) % n_parts) for i in range(n_parts)])

    def body(activations, cotangent, forget_labels, kept_blocks, block_ids, adapter_a, output_adapter):
        tokens, shard_rows = activations.shape
        rank = adapter_a.shape[1]
        feats = cotangent.shape[1]
        tile = kept_blocks.shape[-1]
        slots = kept_blocks.shape[1]
        row_blocks = shard_rows // tile
        col_blocks = D // tile
        share = col_blocks // n_row
        part = lax.axis_index("parts")
        row_index = lax.axis_index("row")
        dp_index = lax.axis_index("dp")
        core, chip = row_index % 2, row_index // 2
        half_bit = dp_index % 2
        blocks = kept_blocks[0]
        ids = block_ids[0]

        held = slots // n_parts
        chunks = 4
        size = held // chunks
        own_share = lax.dynamic_slice_in_dim(blocks, part * held, held, axis=0)
        mate_activations = mate_swap(activations)
        far_ids = [group_shift(ids, d) for d in range(1, group)]
        arrivals = []
        for d in range(1, group):
            for i in range(chunks):
                direct = group_shift(own_share[i * size:(i + 1) * size], d)
                arrivals.append((direct, d, 0, i))
        direct_last = arrivals[-1][0]
        for direct, d, _, i in list(arrivals):
            for e in range(1, n_parts):
                arrivals.append((part_shift(direct, e), d, e, i))

        signs = (1 - 2 * forget_labels).astype(F32)[:, None]
        low_part = jnp.dot(activations, adapter_a, preferred_element_type=F32)
        back_part = signs * lax.dot_general(
            cotangent, output_adapter, (((1,), (1,)), ((), ())), preferred_element_type=F32
        )
        both = jnp.concatenate([low_part, back_part], axis=1)
        both = both + core_swap(both)
        pieces = jnp.zeros((chips,) + both.shape, F32)
        pieces = lax.dynamic_update_index_in_dim(pieces, both, chip, 0)
        for d in range(1, chips):
            pieces = lax.dynamic_update_index_in_dim(pieces, chip_shift(both, d), (chip - d) % chips, 0)
        both = pieces.sum(axis=0).astype(BF16)
        low_b, back_b = both[:, :rank], both[:, rank:]
        mate_back_b = mate_swap(back_b)

        contract_tokens = (((0,), (0,)), ((), ()))
        in_grad = adapter_scale * (
            lax.dot_general(back_b, activations, contract_tokens, preferred_element_type=F32)
            + lax.dot_general(mate_back_b, mate_activations, contract_tokens, preferred_element_type=F32)
        )
        out_grad = adapter_scale * lax.dot_general(
            low_b * signs.astype(BF16), cotangent, contract_tokens, preferred_element_type=F32
        )
        in_half, out_half = shard_rows // 2, feats // 2
        in_mine = lax.dynamic_slice_in_dim(in_grad, half_bit * in_half, in_half, axis=1)
        out_mine = lax.dynamic_slice_in_dim(out_grad, half_bit * out_half, out_half, axis=1)
        out_other = lax.dynamic_slice_in_dim(out_grad, (1 - half_bit) * out_half, out_half, axis=1)
        out_mine = out_mine + mate_swap(out_other)
        grads = jnp.concatenate([in_mine, out_mine], axis=1).astype(BF16)
        grads, direct_last = lax.optimization_barrier((grads, direct_last))
        arrivals = [
            (direct_last,) + item[1:] if (item[1], item[2], item[3]) == (group - 1, 0, chunks - 1) else item
            for item in arrivals
        ]
        pieces = jnp.zeros((group,) + grads.shape, BF16)
        pieces = lax.dynamic_update_index_in_dim(pieces, grads, dp_index // 2, 0)
        for d in range(1, group):
            pieces = lax.dynamic_update_index_in_dim(
                pieces, group_shift(grads, d), (dp_index // 2 - d) % group, 0
            )
        grads = pieces.astype(F32).sum(axis=0)
        mate_grads = mate_swap(grads)
        low_side = jnp.where(half_bit == 0, grads, mate_grads)
        high_side = jnp.where(half_bit == 0, mate_grads, grads)
        input_adapter_gradient = jnp.concatenate([low_side[:, :in_half], high_side[:, :in_half]], axis=1).T
        output_adapter_gradient = jnp.concatenate([low_side[:, in_half:], high_side[:, in_half:]], axis=1)

        both_tokens = 2 * tokens
        scratch = [
            pltpu.VMEM((row_blocks, both_tokens, tile), BF16),
            pltpu.VMEM((col_blocks + 1, both_tokens, tile), F32),
        ]
        total_shape = jax.ShapeDtypeStruct((col_blocks, both_tokens, tile), F32)
        total = call(
            functools.partial(first_kernel, col_blocks=col_blocks),
            total_shape, scratch, (ids,), (activations, mate_activations, blocks),
        )
        all_ids = jnp.concatenate(far_ids)

        def bases(items, *more):
            starts = [(d - 1) * slots + ((part - e) % n_parts) * held + i * size for _, d, e, i in items]
            return jnp.stack(starts + list(more)).astype(jnp.int32)

        late = [item for item in arrivals if item[2] > 0 and item[1] == group - 1 and item[3] >= chunks - 2]
        late.insert(0, arrivals[(group - 1) * chunks - 1])
        late_keys = [item[1:] for item in late]
        early = [item for item in arrivals if item[1:] not in late_keys]
        total = call(
            functools.partial(more_kernel, col_blocks=col_blocks, count=len(early)),
            total_shape, scratch, (bases(early), all_ids),
            (activations, mate_activations, total) + tuple(item[0] for item in early),
        )
        piece = (chips, share, tokens, tile)
        send_mate, keep_mate, send_own, keep_own = call(
            functools.partial(last_kernel, col_blocks=col_blocks, count=len(late)),
            tuple(jax.ShapeDtypeStruct(piece, t) for t in (BF16, F32, BF16, F32)),
            scratch, (bases(late, core), all_ids),
            (activations, mate_activations, total) + tuple(item[0] for item in late),
        )

        def at(value, where):
            return lax.dynamic_index_in_dim(value, where % chips, 0, keepdims=False)

        core_mate = core_swap(send_mate)
        core_own = core_swap(send_own)

        def over_chips(keep, got):
            result = []
            for d in range(1, chips):
                sent = (at(keep, chip + d) + at(got, chip + d).astype(F32)).astype(BF16)
                result.append(chip_shift(sent, d))
            return result

        mate_total = at(keep_mate, chip) + at(core_mate, chip).astype(F32)
        for piece_got in over_chips(keep_mate, core_mate):
            mate_total += piece_got.astype(F32)
        own_pieces = over_chips(keep_own, core_own)
        from_mate = mate_swap(mate_total.astype(BF16))
        projected = call(
            final_kernel,
            jax.ShapeDtypeStruct((tokens, feats), BF16), [], (),
            (low_b, output_adapter, at(keep_own, chip), at(core_own, chip)) + tuple(own_pieces) + (from_mate,),
        )
        return projected, input_adapter_gradient, output_adapter_gradient

    return body


def solution(mesh):
    placed = (
        P(("parts", "dp"), "row"),
        P(("parts", "dp"), "row"),
        P(("parts", "dp")),
        P("row", "dp", None, None),
        P("row", "dp"),
        P("row", None),
        P(None, "row"),
    )
    return jax.shard_map(
        make_body(mesh.shape["parts"], mesh.shape["row"], mesh.shape["dp"]),
        mesh=mesh,
        in_specs=placed,
        out_specs=(P(("parts", "dp"), "row"), P(("parts", "row"), None), P("parts", "row")),
        check_vma=False,
    )
```

time: 353 us -> 153 us (0.43)
  waiting for transfers between devices: 217 us -> 86.1 us
  other arithmetic: 54.3 us -> 7 us
  Pallas kernels: 0 us -> 24.9 us
  starting transfers between devices: 0.2 us -> 24.3 us
  blocking collectives: 20.7 us -> 0 us
  local copies, waits for them, and re-layouts: 23.9 us -> 5.26 us
  matrix products: 21.7 us -> 3.9 us
  between operations: 14.5 us -> 0.99 us
    all_gather x3 -> x0, waiting for transfers between devices: 127 us -> none  [the longest x1 127 us: body(): weights = lax.all_gather(kept_blocks, 'dp', axis=1, tiled=True)[0]]
    ppermute x0 -> x21, waiting for transfers between devices: none -> 86.1 us  [the longest x5 43.3 us: mate_swap(): return lax.ppermute(value, 'dp', [(i, i ^ 1) for i in range(n_dp)])]
    psum x1 -> x0, waiting for transfers between devices: 63.1 us -> none  [body(): lax.psum((input_gradient_piece, output_gradient_piece), 'dp')]
    scatter-add x1 -> x0, other arithmetic: 51.6 us -> none  [body(): partial_value = empty.at[block_col].add(products, mode='drop')]
    reduce_scatter x1 -> x0, waiting for transfers between devices: 25.7 us -> none  [body(): lax.psum_scatter(partial_value, 'row', scatter_dimension=1, tiled=True)]
    pallas_call x0 -> x4, Pallas kernels: none -> 24.9 us  [call(): pl.pallas_call(kernel, out_shape=outs, in_specs=[smem()] * len(scalars) +...]
    ppermute x0 -> x21, starting transfers between devices: none -> 24.3 us  [the longest x6 8.69 us: group_shift(): return lax.ppermute(value, 'dp', pairs)]
    dot_general x5, matrix products: 21.7 us -> 3.9 us  [the longest x1 1.64 us: body(): low_part = jnp.dot(activations, adapter_a, preferred_element_type=F32)]
  transfers between devices with their start and end apart: 5 -> 21, of which waited for: 3 -> 7; matrix products, arithmetic and copies ran while one was open for 27% -> 7% of each run, Pallas kernels for 0% -> 11%
where the time goes in v1:
time: 153 us; the launch traced here: 152 us
  waiting for transfers between devices  86.1 us (56%)
  Pallas kernels  24.9 us (16%)
  starting transfers between devices  24.3 us (16%)
  other arithmetic  7 us (5%)
  local copies, waits for them, and re-layouts  5.26 us (3%)
  matrix products  3.9 us (3%)
    ppermute x5, waiting for transfers between devices, mate_swap(): return lax.ppermute(value, 'dp', [(i, i ^ 1) for i in range(n_dp)])  43.3 us
    ppermute x6, waiting for transfers between devices, group_shift(): return lax.ppermute(value, 'dp', pairs)  34.3 us
    pallas_call x4, Pallas kernels, call(): pl.pallas_call(kernel, out_shape=outs, in_specs=[smem()] * len(scalars) +...  24.9 us
    ppermute x6, starting transfers between devices, group_shift(): return lax.ppermute(value, 'dp', pairs)  8.69 us
    ppermute x3, waiting for transfers between devices, chip_shift(): return lax.ppermute(value, 'row', pairs)  8.53 us
    ppermute x4, starting transfers between devices, part_shift(): lax.ppermute(value, 'parts', [(i, (i + d) % n_parts) for i in range(n_par...  5.17 us
    ppermute x5, starting transfers between devices, mate_swap(): return lax.ppermute(value, 'dp', [(i, i ^ 1) for i in range(n_dp)])  5.11 us
    ppermute x3, starting transfers between devices, chip_shift(): return lax.ppermute(value, 'row', pairs)  4.76 us
  transfers between devices with their start and end apart: 21, of which 7 were waited for; matrix products, arithmetic and copies ran while one was open for 7% of the time, Pallas kernels for 11%

profile of v1, /device:TPU:0, one launch (start us, length us, event | category | flops | bytes accessed | tf_op | source)
XLA Modules:
  0.0 152.5 jit_solution(7626807307245469333)
XLA Ops:
  1.4 1.6 %fusion.14 = f32[128,64]{0,1:T(8,128)S(1)} fusion(bf16[128,3328]{1,0:T(8,128)(2,1)} %own_ref.5, bf16[3328,64]{0,1:T(8,128)(2,1)} %param.12), kind=kOutput, calls=%fused_computation.40 | convolution fusion | flops 54525952 | bytes 1310720 | tf_op jit(solution)/shard_map/dot_general | solution.py:160
  3.1 1.3 convolution_multiply_fusion.1
  4.9 2.7 %collective-permute-start.3 = (bf16[128,3328]{1,0:T(8,128)(2,1)S(1)}, bf16[128,3328]{1,0:T(8,128)(2,1)S(1)}, u32[]{:S(2)}, u32[]{:S(2)}) collective-permute-start(bf16[128,3328]{1,0:T(8,128)(2,1)S(1)} %copy-done.1), channel_id=1, source_target_pairs={{0,1},{1,0},{2,3},{3,2},{4,5},{5,4},{6,7},{7,6},{8,9},{9,8},{10,11... | collective-permute-start | bytes 2555912 | tf_op jit(solution)/shard_map/ppermute | solution.py:117
  7.6 1.6 %collective-permute-start.1 = (f32[128,128]{0,1:T(8,128)S(1)}, f32[128,128]{0,1:T(8,128)S(1)}, u32[]{:S(2)}, u32[]{:S(2)}) collective-permute-start(f32[128,128]{0,1:T(8,128)S(1)} %get-tuple-element.16), channel_id=1, source_target_pairs={{0,8},{4,12},{8,0},{12,4},{1,9},{5,13},{9,1},{13,5},{2,10},{6,14},... | collective-permute-start | bytes 196616 | tf_op jit(solution)/shard_map/ppermute | solution.py:114
  9.1 2.2 %dynamic-slice_bitcast_fusion.2 = (bf16[8,128,128]{2,1,0:T(8,128)(2,1)}, bf16[8,128,128]{2,1,0:T(8,128)(2,1)}, bf16[8,128,128]{2,1,0:T(8,128)(2,1)}, bf16[8,128,128]{2,1,0:T(8,128)(2,1)}) fusion(bf16[1,64,128,128]{3,2,1,0:T(8,128)(2,1)} %param.10, s32[]{:T(128)S(6)} %add.170, s32[]{:T(128)S(6)} %add.169, s32[]{:T(128)S(6)} %add.168, s32[]{:T(128)S(6)} %select_n.126), kind=kLoop, calls=%fused_computation.21 | loop fusion | bytes 2097168 | tf_op jit(solution)/shard_map/slice | solution.py:152
  11.3 2.6 %collective-permute-start.4 = (bf16[8,128,128]{2,1,0:T(8,128)(2,1)}, bf16[8,128,128]{2,1,0:T(8,128)(2,1)S(1)}, u32[]{:S(2)}, u32[]{:S(2)}) collective-permute-start(bf16[8,128,128]{2,1,0:T(8,128)(2,1)} %get-tuple-element.22), channel_id=1, source_target_pairs={{0,2},{1,3},{2,0},{3,1},{4,6},{5,7},{6,4},{7,5},{8,10},{9,11},{10,... | collective-permute-start | bytes 786440 | tf_op jit(solution)/shard_map/ppermute | solution.py:121
  15.5 1.2 collective-permute-start.10
  16.7 0.9 collective-permute-start.9
  17.7 26.9 %collective-permute-done.9 = bf16[128,64]{1,0:T(8,128)(2,1)S(1)} collective-permute-done((bf16[128,64]{1,0:T(8,128)(2,1)S(1)}, bf16[128,64]{1,0:T(8,128)(2,1)S(1)}, u32[]{:S(2)}, u32[]{:S(2)}) %collective-permute-start.9) | collective-permute-done | bytes 16416 | tf_op jit(solution)/shard_map/ppermute | solution.py:117
  44.6 2.8 %collective-permute-start.6 = (bf16[8,128,128]{2,1,0:T(8,128)(2,1)}, bf16[8,128,128]{2,1,0:T(8,128)(2,1)S(1)}, u32[]{:S(2)}, u32[]{:S(2)}) collective-permute-start(bf16[8,128,128]{2,1,0:T(8,128)(2,1)} %get-tuple-element.20), channel_id=1, source_target_pairs={{0,2},{1,3},{2,0},{3,1},{4,6},{5,7},{6,4},{7,5},{8,10},{9,11},{10,... | collective-permute-start | bytes 786440 | tf_op jit(solution)/shard_map/ppermute | solution.py:121
  48.0 1.1 add_convert_fusion.2
  49.1 2.8 %collective-permute-start.2 = (s32[64]{0:T(128)S(1)}, s32[64]{0:T(128)S(1)}, u32[]{:S(2)}, u32[]{:S(2)}) collective-permute-start(s32[64]{0:T(128)S(1)} %bitcast.50), channel_id=1, source_target_pairs={{0,2},{1,3},{2,0},{3,1},{4,6},{5,7},{6,4},{7,5},{8,10},{9,11},{10,... | collective-permute-start | bytes 776 | tf_op jit(solution)/shard_map/ppermute | solution.py:121
  52.0 1.5 %collective-permute-start.7 = (bf16[8,128,128]{2,1,0:T(8,128)(2,1)S(1)}, bf16[8,128,128]{2,1,0:T(8,128)(2,1)S(1)}, u32[]{:S(2)}, u32[]{:S(2)}) collective-permute-start(bf16[8,128,128]{2,1,0:T(8,128)(2,1)S(1)} %collective-permute-done.4.rest_0_), channel_id=1, source_target_pairs={{0,16},{16,0},{1,17},{17,1},{2,18},{18,2},{3,19},{19,3},{4,20},{20... | collective-permute-start | bytes 786440 | tf_op jit(solution)/shard_map/ppermute | solution.py:124
  53.5 12.7 %collective-permute-done.6.rest_2_ = bf16[8,128,128]{2,1,0:T(8,128)(2,1)S(1)} collective-permute-done((bf16[8,128,128]{2,1,0:T(8,128)(2,1)}, bf16[8,128,128]{2,1,0:T(8,128)(2,1)S(1)}, u32[]{:S(2)}, u32[]{:S(2)}) %collective-permute-start.6) | collective-permute-done | bytes 262176 | tf_op jit(solution)/shard_map/ppermute | solution.py:121
  66.2 1.6 %collective-permute-start.8 = (bf16[8,128,128]{2,1,0:T(8,128)(2,1)S(1)}, bf16[8,128,128]{2,1,0:T(8,128)(2,1)S(1)}, u32[]{:S(2)}, u32[]{:S(2)}) collective-permute-start(bf16[8,128,128]{2,1,0:T(8,128)(2,1)S(1)} %collective-permute-done.5.rest_1_), channel_id=1, source_target_pairs={{0,16},{16,0},{1,17},{17,1},{2,18},{18,2},{3,19},{19,3},{4,20},{20... | collective-permute-start | bytes 786440 | tf_op jit(solution)/shard_map/ppermute | solution.py:124
  67.8 2.9 %collective-permute-done.11.rest_0_ = bf16[8,128,128]{2,1,0:T(8,128)(2,1)S(1)} collective-permute-done((bf16[8,128,128]{2,1,0:T(8,128)(2,1)}, bf16[8,128,128]{2,1,0:T(8,128)(2,1)S(1)}, u32[]{:S(2)}, u32[]{:S(2)}) %collective-permute-start.11) | collective-permute-done | bytes 262176 | tf_op jit(solution)/shard_map/ppermute | solution.py:121
  70.7 1.6 %collective-permute-start.12 = (bf16[8,128,128]{2,1,0:T(8,128)(2,1)S(1)}, bf16[8,128,128]{2,1,0:T(8,128)(2,1)S(1)}, u32[]{:S(2)}, u32[]{:S(2)}) collective-permute-start(bf16[8,128,128]{2,1,0:T(8,128)(2,1)S(1)} %collective-permute-done.6.rest_2_), channel_id=1, source_target_pairs={{0,16},{16,0},{1,17},{17,1},{2,18},{18,2},{3,19},{19,3},{4,20},{20... | collective-permute-start | bytes 786440 | tf_op jit(solution)/shard_map/ppermute | solution.py:124
  73.1 7.5 %shard_map.94.total_in_ref = f32[64,256,128]{2,1,0:T(8,128)} custom-call(s32[64]{0:T(128)S(1)} %bitcast.51, bf16[128,3328]{1,0:T(8,128)(2,1)S(1)} %copy-done.1, bf16[128,3328]{1,0:T(8,128)(2,1)S(1)} %collective-permute-done.3.mate_ref, bf16[64,128,128]{2,1,0:T(8,128)(2,1)S(1)} %bitcast.49), custom_call_target="tpu_custom_call" | custom-call | tf_op jit(solution)/shard_map/pallas_call | solution.py:95
  80.7 8.9 %shard_map.95.total_in_ref = f32[64,256,128]{2,1,0:T(8,128)} custom-call(s32[5]{0:T(128)S(1)} %stack.43.base_ref, s32[64]{0:T(128)S(1)} %collective-permute-done.2.ids_ref, bf16[128,3328]{1,0:T(8,128)(2,1)S(1)} %copy-done.1, bf16[128,3328]{1,0:T(8,128)(2,1)S(1)} %collective-permute-done.3.mate_ref, f32[64,256,128]{2,1,0:T(8,128)} %shard_map.94.total_in_ref, ...), custom_call_target="tpu_custom_call" | custom-call | tf_op jit(solution)/shard_map/pallas_call | solution.py:95
  89.6 7.3 %shard_map.96 = (bf16[2,16,128,128]{3,2,1,0:T(8,128)(2,1)}, f32[2,16,128,128]{3,2,1,0:T(8,128)}, bf16[2,16,128,128]{3,2,1,0:T(8,128)(2,1)S(1)}, f32[2,16,128,128]{3,2,1,0:T(8,128)}) custom-call(s32[4]{0:T(128)S(1)} %pad_add_fusion.base_ref, s32[64]{0:T(128)S(1)} %collective-permute-done.2.ids_ref, bf16[128,3328]{1,0:T(8,128)(2,1)S(1)} %copy-done.1, ...), custom_call_target="tpu_custom_call" | custom-call | tf_op jit(solution)/shard_map/pallas_call | solution.py:95
  96.9 1.0 copy-done.5
  97.9 18.6 %collective-permute-done.19 = bf16[64,2688]{1,0:T(8,128)(2,1)S(1)} collective-permute-done((bf16[64,2688]{1,0:T(8,128)(2,1)S(1)}, bf16[64,2688]{1,0:T(8,128)(2,1)S(1)}, u32[]{:S(2)}, u32[]{:S(2)}) %collective-permute-start.19) | collective-permute-done | bytes 344096 | tf_op jit(solution)/shard_map/ppermute | solution.py:121
  116.9 1.5 fusion.2
  118.4 1.6 %collective-permute-start.17 = (bf16[16,128,128]{2,1,0:T(8,128)(2,1)S(1)}, bf16[16,128,128]{2,1,0:T(8,128)(2,1)S(1)}, u32[]{:S(2)}, u32[]{:S(2)}) collective-permute-start(bf16[16,128,128]{2,1,0:T(8,128)(2,1)S(1)} %fusion.2), channel_id=1, source_target_pairs={{0,8},{4,12},{8,0},{12,4},{1,9},{5,13},{9,1},{13,5},{2,10},{6,14},... | collective-permute-start | bytes 1572872 | tf_op jit(solution)/shard_map/ppermute | solution.py:114
  120.0 13.8 %collective-permute-done.20 = f32[64,2688]{1,0:T(8,128)S(1)} collective-permute-done((f32[64,2688]{1,0:T(8,128)S(1)}, f32[64,2688]{1,0:T(8,128)S(1)}, u32[]{:S(2)}, u32[]{:S(2)}) %collective-permute-start.20) | collective-permute-done | bytes 688160 | tf_op jit(solution)/shard_map/ppermute | solution.py:117
  134.1 0.8 pad_maximum_fusion
  135.9 1.6 %collective-permute-start.15 = (bf16[16,128,128]{2,1,0:T(8,128)(2,1)S(1)}, bf16[16,128,128]{2,1,0:T(8,128)(2,1)S(1)}, u32[]{:S(2)}, u32[]{:S(2)}) collective-permute-start(bf16[16,128,128]{2,1,0:T(8,128)(2,1)S(1)} %get-tuple-element.17), channel_id=1, source_target_pairs={{0,8},{4,12},{8,0},{12,4},{1,9},{5,13},{9,1},{13,5},{2,10},{6,14},... | collective-permute-start | bytes 1572872 | tf_op jit(solution)/shard_map/ppermute | solution.py:114
  137.5 1.2 fusion
  139.1 1.0 maximum_bitcast_fusion
  140.1 8.5 %collective-permute-done.15.rest_0_ = bf16[16,128,128]{2,1,0:T(8,128)(2,1)S(1)} collective-permute-done((bf16[16,128,128]{2,1,0:T(8,128)(2,1)S(1)}, bf16[16,128,128]{2,1,0:T(8,128)(2,1)S(1)}, u32[]{:S(2)}, u32[]{:S(2)}) %collective-permute-start.15) | collective-permute-done | bytes 524320 | tf_op jit(solution)/shard_map/ppermute | solution.py:114
  148.7 2.6 %collective-permute-done.18.rest_1_ = bf16[16,128,128]{2,1,0:T(8,128)(2,1)S(1)} collective-permute-done((bf16[16,128,128]{2,1,0:T(8,128)(2,1)S(1)}, bf16[16,128,128]{2,1,0:T(8,128)(2,1)S(1)}, u32[]{:S(2)}, u32[]{:S(2)}) %collective-permute-start.18) | collective-permute-done | bytes 524320 | tf_op jit(solution)/shard_map/ppermute | solution.py:117
  151.3 1.2 shard_map.97
  (67 shorter events, 6.5 us)
Async XLA Ops:
  0.6 2.4 %copy-start = (bf16[128,2048]{1,0:T(8,128)(2,1)S(1)}, bf16[128,2048]{1,0:T(8,128)(2,1)}, u32[]{:S(2)}) copy-start(bf16[128,2048]{1,0:T(8,128)(2,1)} %param.8) | copy-start | bytes 1572868
  0.6 4.2 %copy-start.1 = (bf16[128,3328]{1,0:T(8,128)(2,1)S(1)}, bf16[128,3328]{1,0:T(8,128)(2,1)}, u32[]{:S(2)}) copy-start(bf16[128,3328]{1,0:T(8,128)(2,1)} %own_ref.5) | copy-start | bytes 2555908
  4.4 3.2 %collective-permute-start = (f32[128,128]{0,1:T(8,128)S(1)}, f32[128,128]{0,1:T(8,128)S(1)}, u32[]{:S(2)}, u32[]{:S(2)}) collective-permute-start(f32[128,128]{0,1:T(8,128)S(1)} %pad_maximum_fusion.2), channel_id=1, source_target_pairs={{0,4},{4,0},{8,12},{12,8},{1,5},{5,1},{9,13},{13,9},{2,6},{6,2},{1... | collective-permute-start | bytes 196616 | tf_op jit(solution)/shard_map/ppermute | solution.py:110
  4.9 67.4 %collective-permute-start.3 = (bf16[128,3328]{1,0:T(8,128)(2,1)S(1)}, bf16[128,3328]{1,0:T(8,128)(2,1)S(1)}, u32[]{:S(2)}, u32[]{:S(2)}) collective-permute-start(bf16[128,3328]{1,0:T(8,128)(2,1)S(1)} %copy-done.1), channel_id=1, source_target_pairs={{0,1},{1,0},{2,3},{3,2},{4,5},{5,4},{6,7},{7,6},{8,9},{9,8},{10,11... | collective-permute-start | bytes 2555912 | tf_op jit(solution)/shard_map/ppermute | solution.py:117
  7.6 6.6 %collective-permute-start.1 = (f32[128,128]{0,1:T(8,128)S(1)}, f32[128,128]{0,1:T(8,128)S(1)}, u32[]{:S(2)}, u32[]{:S(2)}) collective-permute-start(f32[128,128]{0,1:T(8,128)S(1)} %get-tuple-element.16), channel_id=1, source_target_pairs={{0,8},{4,12},{8,0},{12,4},{1,9},{5,13},{9,1},{13,5},{2,10},{6,14},... | collective-permute-start | bytes 196616 | tf_op jit(solution)/shard_map/ppermute | solution.py:114
  11.3 37.8 %collective-permute-start.4 = (bf16[8,128,128]{2,1,0:T(8,128)(2,1)}, bf16[8,128,128]{2,1,0:T(8,128)(2,1)S(1)}, u32[]{:S(2)}, u32[]{:S(2)}) collective-permute-start(bf16[8,128,128]{2,1,0:T(8,128)(2,1)} %get-tuple-element.22), channel_id=1, source_target_pairs={{0,2},{1,3},{2,0},{3,1},{4,6},{5,7},{6,4},{7,5},{8,10},{9,11},{10,... | collective-permute-start | bytes 786440 | tf_op jit(solution)/shard_map/ppermute | solution.py:121
  13.9 38.0 %collective-permute-start.5 = (bf16[8,128,128]{2,1,0:T(8,128)(2,1)}, bf16[8,128,128]{2,1,0:T(8,128)(2,1)S(1)}, u32[]{:S(2)}, u32[]{:S(2)}) collective-permute-start(bf16[8,128,128]{2,1,0:T(8,128)(2,1)} %get-tuple-element.21), channel_id=1, source_target_pairs={{0,2},{1,3},{2,0},{3,1},{4,6},{5,7},{6,4},{7,5},{8,10},{9,11},{10,... | collective-permute-start | bytes 786440 | tf_op jit(solution)/shard_map/ppermute | solution.py:121
  14.4 34.7 %copy-start.4 = (s32[1,64]{1,0:T(1,128)S(1)}, s32[1,64]{1,0:T(1,128)}, u32[]{:S(2)}) copy-start(s32[1,64]{1,0:T(1,128)} %param.11) | copy-start | bytes 772
  15.5 31.9 %collective-permute-start.10 = (f32[64,1024]{1,0:T(8,128)}, f32[64,1024]{1,0:T(8,128)}, u32[]{:S(2)}, u32[]{:S(2)}) collective-permute-start(f32[64,1024]{1,0:T(8,128)} %constant_dynamic-slice_fusion), channel_id=1, source_target_pairs={{0,1},{1,0},{2,3},{3,2},{4,5},{5,4},{6,7},{7,6},{8,9},{9,8},{10,11... | collective-permute-start | bytes 786440 | tf_op jit(solution)/shard_map/ppermute | solution.py:117
  16.7 27.9 %collective-permute-start.9 = (bf16[128,64]{1,0:T(8,128)(2,1)S(1)}, bf16[128,64]{1,0:T(8,128)(2,1)S(1)}, u32[]{:S(2)}, u32[]{:S(2)}) collective-permute-start(bf16[128,64]{1,0:T(8,128)(2,1)S(1)} %get-tuple-element.25), channel_id=1, source_target_pairs={{0,1},{1,0},{2,3},{3,2},{4,5},{5,4},{6,7},{7,6},{8,9},{9,8},{10,11... | collective-permute-start | bytes 49160 | tf_op jit(solution)/shard_map/ppermute | solution.py:117
  44.6 21.5 %collective-permute-start.6 = (bf16[8,128,128]{2,1,0:T(8,128)(2,1)}, bf16[8,128,128]{2,1,0:T(8,128)(2,1)S(1)}, u32[]{:S(2)}, u32[]{:S(2)}) collective-permute-start(bf16[8,128,128]{2,1,0:T(8,128)(2,1)} %get-tuple-element.20), channel_id=1, source_target_pairs={{0,2},{1,3},{2,0},{3,1},{4,6},{5,7},{6,4},{7,5},{8,10},{9,11},{10,... | collective-permute-start | bytes 786440 | tf_op jit(solution)/shard_map/ppermute | solution.py:121
  47.4 23.3 %collective-permute-start.11 = (bf16[8,128,128]{2,1,0:T(8,128)(2,1)}, bf16[8,128,128]{2,1,0:T(8,128)(2,1)S(1)}, u32[]{:S(2)}, u32[]{:S(2)}) collective-permute-start(bf16[8,128,128]{2,1,0:T(8,128)(2,1)} %get-tuple-element.19), channel_id=1, source_target_pairs={{0,2},{1,3},{2,0},{3,1},{4,6},{5,7},{6,4},{7,5},{8,10},{9,11},{10,... | collective-permute-start | bytes 786440 | tf_op jit(solution)/shard_map/ppermute | solution.py:121
  47.9 25.2 %copy-start.2 = (bf16[1,64,128,128]{3,2,1,0:T(8,128)(2,1)S(1)}, bf16[1,64,128,128]{3,2,1,0:T(8,128)(2,1)}, u32[]{:S(2)}) copy-start(bf16[1,64,128,128]{3,2,1,0:T(8,128)(2,1)} %param.10) | copy-start | bytes 6291460
  49.1 31.5 %collective-permute-start.2 = (s32[64]{0:T(128)S(1)}, s32[64]{0:T(128)S(1)}, u32[]{:S(2)}, u32[]{:S(2)}) collective-permute-start(s32[64]{0:T(128)S(1)} %bitcast.50), channel_id=1, source_target_pairs={{0,2},{1,3},{2,0},{3,1},{4,6},{5,7},{6,4},{7,5},{8,10},{9,11},{10,... | collective-permute-start | bytes 776 | tf_op jit(solution)/shard_map/ppermute | solution.py:121
  52.0 28.7 %collective-permute-start.7 = (bf16[8,128,128]{2,1,0:T(8,128)(2,1)S(1)}, bf16[8,128,128]{2,1,0:T(8,128)(2,1)S(1)}, u32[]{:S(2)}, u32[]{:S(2)}) collective-permute-start(bf16[8,128,128]{2,1,0:T(8,128)(2,1)S(1)} %collective-permute-done.4.rest_0_), channel_id=1, source_target_pairs={{0,16},{16,0},{1,17},{17,1},{2,18},{18,2},{3,19},{19,3},{4,20},{20... | collective-permute-start | bytes 786440 | tf_op jit(solution)/shard_map/ppermute | solution.py:124
  66.2 14.5 %collective-permute-start.8 = (bf16[8,128,128]{2,1,0:T(8,128)(2,1)S(1)}, bf16[8,128,128]{2,1,0:T(8,128)(2,1)S(1)}, u32[]{:S(2)}, u32[]{:S(2)}) collective-permute-start(bf16[8,128,128]{2,1,0:T(8,128)(2,1)S(1)} %collective-permute-done.5.rest_1_), channel_id=1, source_target_pairs={{0,16},{16,0},{1,17},{17,1},{2,18},{18,2},{3,19},{19,3},{4,20},{20... | collective-permute-start | bytes 786440 | tf_op jit(solution)/shard_map/ppermute | solution.py:124
  70.7 18.8 %collective-permute-start.12 = (bf16[8,128,128]{2,1,0:T(8,128)(2,1)S(1)}, bf16[8,128,128]{2,1,0:T(8,128)(2,1)S(1)}, u32[]{:S(2)}, u32[]{:S(2)}) collective-permute-start(bf16[8,128,128]{2,1,0:T(8,128)(2,1)S(1)} %collective-permute-done.6.rest_2_), channel_id=1, source_target_pairs={{0,16},{16,0},{1,17},{17,1},{2,18},{18,2},{3,19},{19,3},{4,20},{20... | collective-permute-start | bytes 786440 | tf_op jit(solution)/shard_map/ppermute | solution.py:124
  72.3 17.3 %collective-permute-start.13 = (bf16[8,128,128]{2,1,0:T(8,128)(2,1)S(1)}, bf16[8,128,128]{2,1,0:T(8,128)(2,1)S(1)}, u32[]{:S(2)}, u32[]{:S(2)}) collective-permute-start(bf16[8,128,128]{2,1,0:T(8,128)(2,1)S(1)} %collective-permute-done.11.rest_0_), channel_id=1, source_target_pairs={{0,16},{16,0},{1,17},{17,1},{2,18},{18,2},{3,19},{19,3},{4,20},{20... | collective-permute-start | bytes 786440 | tf_op jit(solution)/shard_map/ppermute | solution.py:124
  96.9 1.0 copy-start.5
  97.8 19.0 %copy-start.6 = (bf16[2,16,128,128]{3,2,1,0:T(8,128)(2,1)S(1)}, bf16[2,16,128,128]{3,2,1,0:T(8,128)(2,1)}, u32[]{:S(2)}) copy-start(bf16[2,16,128,128]{3,2,1,0:T(8,128)(2,1)} %copy-done.5) | copy-start | bytes 3145732
  97.8 19.1 %collective-permute-start.16 = (bf16[2,16,128,128]{3,2,1,0:T(8,128)(2,1)}, bf16[2,16,128,128]{3,2,1,0:T(8,128)(2,1)}, u32[]{:S(2)}, u32[]{:S(2)}) collective-permute-start(bf16[2,16,128,128]{3,2,1,0:T(8,128)(2,1)} %get-tuple-element.13), channel_id=1, source_target_pairs={{0,4},{4,0},{8,12},{12,8},{1,5},{5,1},{9,13},{13,9},{2,6},{6,2},{1... | collective-permute-start | bytes 3145736 | tf_op jit(solution)/shard_map/ppermute | solution.py:110
  97.8 18.7 %collective-permute-start.19 = (bf16[64,2688]{1,0:T(8,128)(2,1)S(1)}, bf16[64,2688]{1,0:T(8,128)(2,1)S(1)}, u32[]{:S(2)}, u32[]{:S(2)}) collective-permute-start(bf16[64,2688]{1,0:T(8,128)(2,1)S(1)} %pad_maximum_fusion.1), channel_id=1, source_target_pairs={{0,2},{1,3},{2,0},{3,1},{4,6},{5,7},{6,4},{7,5},{8,10},{9,11},{10,... | collective-permute-start | bytes 1032200 | tf_op jit(solution)/shard_map/ppermute | solution.py:121
  116.7 17.1 %collective-permute-start.20 = (f32[64,2688]{1,0:T(8,128)S(1)}, f32[64,2688]{1,0:T(8,128)S(1)}, u32[]{:S(2)}, u32[]{:S(2)}) collective-permute-start(f32[64,2688]{1,0:T(8,128)S(1)} %convert_reduce_fusion), channel_id=1, source_target_pairs={{0,1},{1,0},{2,3},{3,2},{4,5},{5,4},{6,7},{7,6},{8,9},{9,8},{10,11... | collective-permute-start | bytes 2064392 | tf_op jit(solution)/shard_map/ppermute | solution.py:117
  116.8 18.1 %collective-permute-start.14 = (bf16[2,16,128,128]{3,2,1,0:T(8,128)(2,1)S(1)}, bf16[2,16,128,128]{3,2,1,0:T(8,128)(2,1)S(1)}, u32[]{:S(2)}, u32[]{:S(2)}) collective-permute-start(bf16[2,16,128,128]{3,2,1,0:T(8,128)(2,1)S(1)} %copy-done.6), channel_id=1, source_target_pairs={{0,4},{4,0},{8,12},{12,8},{1,5},{5,1},{9,13},{13,9},{2,6},{6,2},{1... | collective-permute-start | bytes 3145736 | tf_op jit(solution)/shard_map/ppermute | solution.py:110
  118.4 19.1 %collective-permute-start.17 = (bf16[16,128,128]{2,1,0:T(8,128)(2,1)S(1)}, bf16[16,128,128]{2,1,0:T(8,128)(2,1)S(1)}, u32[]{:S(2)}, u32[]{:S(2)}) collective-permute-start(bf16[16,128,128]{2,1,0:T(8,128)(2,1)S(1)} %fusion.2), channel_id=1, source_target_pairs={{0,8},{4,12},{8,0},{12,4},{1,9},{5,13},{9,1},{13,5},{2,10},{6,14},... | collective-permute-start | bytes 1572872 | tf_op jit(solution)/shard_map/ppermute | solution.py:114
  133.9 1.8 %copy-start.7 = (f32[2,16,128,128]{3,2,1,0:T(8,128)S(1)}, f32[2,16,128,128]{3,2,1,0:T(8,128)}, u32[]{:S(2)}) copy-start(f32[2,16,128,128]{3,2,1,0:T(8,128)} %get-tuple-element.10) | copy-start | bytes 6291460
  135.7 1.8 %copy-start.8 = (f32[2,16,128,128]{3,2,1,0:T(8,128)S(1)}, f32[2,16,128,128]{3,2,1,0:T(8,128)}, u32[]{:S(2)}) copy-start(f32[2,16,128,128]{3,2,1,0:T(8,128)} %get-tuple-element.12) | copy-start | bytes 6291460
  135.9 15.4 %copy-start.3 = (bf16[64,2048]{1,0:T(8,128)(2,1)S(1)}, bf16[64,2048]{1,0:T(8,128)(2,1)}, u32[]{:S(2)}) copy-start(bf16[64,2048]{1,0:T(8,128)(2,1)} %adapter_ref.1) | copy-start | bytes 786436
  135.9 12.7 %collective-permute-start.15 = (bf16[16,128,128]{2,1,0:T(8,128)(2,1)S(1)}, bf16[16,128,128]{2,1,0:T(8,128)(2,1)S(1)}, u32[]{:S(2)}, u32[]{:S(2)}) collective-permute-start(bf16[16,128,128]{2,1,0:T(8,128)(2,1)S(1)} %get-tuple-element.17), channel_id=1, source_target_pairs={{0,8},{4,12},{8,0},{12,4},{1,9},{5,13},{9,1},{13,5},{2,10},{6,14},... | collective-permute-start | bytes 1572872 | tf_op jit(solution)/shard_map/ppermute | solution.py:114
  138.8 12.5 %collective-permute-start.18 = (bf16[16,128,128]{2,1,0:T(8,128)(2,1)S(1)}, bf16[16,128,128]{2,1,0:T(8,128)(2,1)S(1)}, u32[]{:S(2)}, u32[]{:S(2)}) collective-permute-start(bf16[16,128,128]{2,1,0:T(8,128)(2,1)S(1)} %fusion), channel_id=1, source_target_pairs={{0,1},{1,0},{2,3},{3,2},{4,5},{5,4},{6,7},{7,6},{8,9},{9,8},{10,11... | collective-permute-start | bytes 1572872 | tf_op jit(solution)/shard_map/ppermute | solution.py:117

commit v2 on v0

v2 whole, which is shorter than its diff:
```python
import functools

import jax
import jax.numpy as jnp
from jax import lax
from jax.experimental import pallas as pl
from jax.experimental.pallas import tpu as pltpu
from jax.sharding import PartitionSpec as P

D = 8192

adapter_scale = 2.0

F32 = jnp.float32
BF16 = jnp.bfloat16


def add_blocks(total_ref, tiles_ref, blocks_ref, ids_ref, base, col_blocks, unroll):
    count = blocks_ref.shape[0]

    def one(step, carry):
        for u in range(unroll):
            k = step * unroll + u
            ident = ids_ref[base + k]
            known = jnp.maximum(ident, 0)
            row = lax.div(known, col_blocks)
            col = jnp.where(ident >= 0, lax.rem(known, col_blocks), col_blocks)
            total_ref[col] += jnp.dot(tiles_ref[row], blocks_ref[k], preferred_element_type=F32)
        return carry

    lax.fori_loop(0, count // unroll, one, 0)


def first_kernel(ids_ref, own_ref, mate_ref, blocks_ref, total_ref, tiles_ref, *, col_blocks):
    row_blocks, _, tile = tiles_ref.shape
    tokens = own_ref.shape[0]
    total_ref[...] = jnp.zeros_like(total_ref)
    for i in range(row_blocks):
        tiles_ref[i, :tokens, :] = own_ref[:, i * tile:(i + 1) * tile]
        tiles_ref[i, tokens:, :] = mate_ref[:, i * tile:(i + 1) * tile]
    add_blocks(total_ref, tiles_ref, blocks_ref, ids_ref, 0, col_blocks, 8)


def add_arrivals(where_ref, ids_ref, tiles_ref, blocks, total_ref, places, parts, held, col_blocks):
    for blocks_ref, (offset, shift, start) in zip(blocks, places):
        source = lax.rem(where_ref[0] + (parts - shift), parts)
        base = offset + source * held + start
        add_blocks(total_ref, tiles_ref, blocks_ref, ids_ref, base, col_blocks, 4)


def more_kernel(where_ref, ids_ref, tiles_ref, old_ref, *rest, **plan):
    add_arrivals(where_ref, ids_ref, tiles_ref, rest[:-1], rest[-1], **plan)


def last_kernel(where_ref, ids_ref, tiles_ref, old_ref, *rest, **plan):
    blocks, (total_ref, send_mate, send_own) = rest[:-3], rest[-3:]
    add_arrivals(where_ref, ids_ref, tiles_ref, blocks, total_ref, **plan)
    chips, share, tokens, _ = send_mate.shape
    for chip in range(chips):
        other = (2 * chip + 1 - where_ref[1]) * share
        for q in range(share):
            send_mate[chip, q] = total_ref[other + q, tokens:, :].astype(BF16)
            send_own[chip, q] = total_ref[other + q, :tokens, :].astype(BF16)


def chip_kernel(where_ref, total_ref, core_ref, leaving_ref, *, first):
    chips, share, tokens, _ = core_ref.shape
    for d in range(1, chips):
        to_chip = lax.rem(where_ref[2] + d, chips)
        mine = (2 * to_chip + where_ref[1]) * share
        for q in range(share):
            value = total_ref[mine + q, first:first + tokens, :] + core_ref[to_chip, q].astype(F32)
            leaving_ref[d - 1, q] = value.astype(BF16)


def mate_kernel(where_ref, total_ref, core_ref, *rest):
    pieces, out_ref = rest[:-1], rest[-1]
    _, share, tokens, _ = core_ref.shape
    chip = where_ref[2]
    mine = (2 * chip + where_ref[1]) * share
    for q in range(share):
        value = total_ref[mine + q, tokens:, :] + core_ref[chip, q].astype(F32)
        for piece in pieces:
            value += piece[q].astype(F32)
        out_ref[q] = value.astype(BF16)


def final_kernel(where_ref, low_ref, adapter_ref, total_ref, core_ref, *rest):
    pieces, out_ref = rest[:-1], rest[-1]
    _, share, tokens, tile = core_ref.shape
    chip = where_ref[2]
    mine = (2 * chip + where_ref[1]) * share
    for q in range(share):
        value = total_ref[mine + q, :tokens, :] + core_ref[chip, q].astype(F32)
        for piece in pieces:
            value += piece[q].astype(F32)
        cols = slice(q * tile, (q + 1) * tile)
        extra = jnp.dot(low_ref[...], adapter_ref[:, cols], preferred_element_type=F32)
        out_ref[:, cols] = (value + adapter_scale * extra).astype(BF16)


def call(kernel, outs, scalars, arrays, flops, aliases=None):
    smem = pl.BlockSpec(memory_space=pltpu.SMEM)
    vmem = pl.BlockSpec(memory_space=pltpu.VMEM)
    return pl.pallas_call(
        kernel,
        out_shape=outs,
        in_specs=[smem] * len(scalars) + [vmem] * len(arrays),
        out_specs=tuple(vmem for _ in outs),
        input_output_aliases=aliases or {},
        cost_estimate=pl.CostEstimate(flops=flops, transcendentals=0, bytes_accessed=1 << 20),
        compiler_params=pltpu.CompilerParams(vmem_limit_bytes=4 * 1024 * 1024),
    )(*scalars, *arrays)


def on_chip(value):
    return pltpu.with_memory_space_constraint(value, pltpu.VMEM)


def after(value, *needed):
    return lax.optimization_barrier((value,) + needed)[0]


def make_body(n_parts, n_row, n_dp):
    chips = n_row // 2
    group = n_dp // 2

    def core_swap(value):
        return lax.ppermute(value, "row", [(i, i ^ 1) for i in range(n_row)])

    def chip_shift(value, d):
        pairs = [(2 * a + c, 2 * ((a + d) % chips) + c) for a in range(chips) for c in range(2)]
        return lax.ppermute(value, "row", pairs)

    def mate_swap(value):
        return lax.ppermute(value, "dp", [(i, i ^ 1) for i in range(n_dp)])

    def group_shift(value, d):
        pairs = [(2 * a + h, 2 * ((a + d) % group) + h) for a in range(group) for h in range(2)]
        return lax.ppermute(value, "dp", pairs)

    def part_shift(value, d):
        return lax.ppermute(value, "parts", [(i, (i + d) % n_parts) for i in range(n_parts)])

    def in_order_sum(own, received, place, count):
        if count == 2:
            return own.astype(F32) + received[0].astype(F32)
        stack = jnp.zeros((count,) + own.shape, own.dtype)
        stack = lax.dynamic_update_index_in_dim(stack, own, place, 0)
        for d, value in enumerate(received, 1):
            stack = lax.dynamic_update_index_in_dim(stack, value, lax.rem(place + (count - d), count), 0)
        return stack.astype(F32).sum(axis=0)

    def body(activations, cotangent, forget_labels, kept_blocks, block_ids, adapter_a, output_adapter):
        tokens, shard_rows = activations.shape
        rank = adapter_a.shape[1]
        feats = cotangent.shape[1]
        slots, tile = kept_blocks.shape[1], kept_blocks.shape[-1]
        row_blocks = shard_rows // tile
        col_blocks = D // tile
        share = col_blocks // n_row
        part = lax.axis_index("parts")
        row_index = lax.axis_index("row")
        dp_index = lax.axis_index("dp")
        core, chip = lax.rem(row_index, 2), lax.div(row_index, 2)
        half_bit, place = lax.rem(dp_index, 2), lax.div(dp_index, 2)
        where = jnp.stack([part, core, chip]).astype(jnp.int32)
        blocks = kept_blocks[0]
        ids = block_ids[0]

        far_ids = [group_shift(ids, d) for d in range(1, group)]
        mate_activations = mate_swap(activations)
        held = slots // n_parts
        sizes = [held * k // 32 for k in (12, 12, 8)]
        starts = [sum(sizes[:k]) for k in range(len(sizes))]
        own_share = lax.dynamic_slice_in_dim(blocks, part * held, held, axis=0)
        all_ids = far_ids[0] if group == 2 else jnp.concatenate(far_ids)
        direct = []
        for d in range(1, group):
            for start, size in zip(starts, sizes):
                leaving = own_share[start:start + size]
                if start > 0:
                    leaving = after(leaving, all_ids)
                direct.append((group_shift(leaving, d), ((d - 1) * slots, 0, start)))

        adapter_early = after(adapter_a, all_ids)
        signs = (1 - 2 * forget_labels).astype(F32)[:, None]
        low_part = jnp.dot(activations, adapter_early, preferred_element_type=F32)
        back_part = signs * lax.dot_general(
            cotangent, after(output_adapter, all_ids), (((1,), (1,)), ((), ())), preferred_element_type=F32
        )
        both = jnp.concatenate([low_part, back_part], axis=1)
        both = both + core_swap(both)
        both = in_order_sum(both, [chip_shift(both, d) for d in range(1, chips)], chip, chips).astype(BF16)
        low_b, back_b = both[:, :rank], both[:, rank:]
        contract_tokens = (((0,), (0,)), ((), ()))
        out_grad = adapter_scale * lax.dot_general(
            low_b * signs.astype(BF16), cotangent, contract_tokens, preferred_element_type=F32
        )
        in_half, out_half = shard_rows // 2, feats // 2
        out_mine = lax.dynamic_slice_in_dim(out_grad, half_bit * out_half, out_half, axis=1)
        out_other = lax.dynamic_slice_in_dim(out_grad, (1 - half_bit) * out_half, out_half, axis=1)
        mate_pack = mate_swap(jnp.concatenate([out_other, back_b.astype(F32).T], axis=1))

        both_tokens = 2 * tokens
        per_block = 2 * both_tokens * tile * tile
        total_shape = pltpu.VMEM((col_blocks + 1, both_tokens, tile), F32)
        total, tiles = call(
            functools.partial(first_kernel, col_blocks=col_blocks),
            (total_shape, pltpu.VMEM((row_blocks, both_tokens, tile), BF16)),
            (ids,), (activations, mate_activations, blocks), slots * per_block,
        )
        swapped = []
        for k, (value, (offset, _, start)) in enumerate(direct):
            if k == len(direct) - 1:
                value = after(value, total)
            for e in range(1, n_parts):
                swapped.append((part_shift(value, e), (offset, e, start)))

        gate = direct[-2][0]
        mate_pack = after(mate_pack, gate)
        mate_out, mate_back_b = mate_pack[:, :out_half], mate_pack[:, out_half:].astype(BF16)
        in_grad = adapter_scale * (
            lax.dot_general(back_b, activations, contract_tokens, preferred_element_type=F32)
            + jnp.dot(mate_back_b, mate_activations, preferred_element_type=F32)
        )
        in_mine = lax.dynamic_slice_in_dim(in_grad, half_bit * in_half, in_half, axis=1)
        grads = jnp.concatenate([in_mine, out_mine + mate_out], axis=1).astype(BF16)
        grads = after(grads, direct[-1][0])
        far_grads = [group_shift(grads, d) for d in range(1, group)]

        late = [direct[-1]] + swapped[-2 * (n_parts - 1):]
        early = direct[:-1] + swapped[:-2 * (n_parts - 1)]

        def plan(items):
            return dict(places=[item[1] for item in items], parts=n_parts, held=held, col_blocks=col_blocks)

        def work(items):
            return sum(item[0].shape[0] for item in items) * per_block

        (total,) = call(
            functools.partial(more_kernel, **plan(early)), (total_shape,), (where, all_ids),
            (on_chip(tiles), on_chip(total)) + tuple(item[0] for item in early), work(early), {3: 0},
        )
        send = pltpu.VMEM((chips, share, tokens, tile), BF16)
        total, send_mate, send_own = call(
            functools.partial(last_kernel, **plan(late)), (total_shape, send, send), (where, all_ids),
            (on_chip(tiles), on_chip(total)) + tuple(item[0] for item in late), work(late), {3: 0},
        )

        def for_chips(first, core_got, *needed):
            (leaving,) = call(
                functools.partial(chip_kernel, first=first),
                (pltpu.VMEM((chips - 1, share, tokens, tile), BF16),), (where,), (on_chip(total), core_got), 0,
            )
            if needed:
                leaving = after(leaving, *needed)
            return leaving, [chip_shift(leaving[d - 1], d) for d in range(1, chips)]

        core_mate = core_swap(send_mate)
        core_own = core_swap(send_own)
        leaving, mate_pieces = for_chips(tokens, core_mate)
        far_grads = [after(value, leaving) for value in far_grads]
        grads = in_order_sum(grads, far_grads, place, group)
        mate_grads = mate_swap(grads)
        (mate_total,) = call(
            mate_kernel, (pltpu.VMEM((share, tokens, tile), BF16),), (where,),
            (on_chip(total), core_mate) + tuple(mate_pieces), 0,
        )
        from_mate = mate_swap(mate_total)
        _, own_pieces = for_chips(0, core_own, mate_total)
        mate_grads = after(mate_grads, mate_total)
        low_side = jnp.where(half_bit == 0, grads, mate_grads)
        high_side = jnp.where(half_bit == 0, mate_grads, grads)
        input_adapter_gradient = jnp.concatenate([low_side[:, :in_half], high_side[:, :in_half]], axis=1).T
        output_adapter_gradient = jnp.concatenate([low_side[:, in_half:], high_side[:, in_half:]], axis=1)
        (projected,) = call(
            final_kernel, (jax.ShapeDtypeStruct((tokens, feats), BF16),), (where,),
            (low_b, output_adapter, on_chip(total), core_own) + tuple(own_pieces) + (from_mate,),
            2 * tokens * rank * feats,
        )
        return projected, input_adapter_gradient, output_adapter_gradient

    return body


def solution(mesh):
    placed = (
        P(("parts", "dp"), "row"),
        P(("parts", "dp"), "row"),
        P(("parts", "dp")),
        P("row", "dp", None, None),
        P("row", "dp"),
        P("row", None),
        P(None, "row"),
    )
    return jax.shard_map(
        make_body(mesh.shape["parts"], mesh.shape["row"], mesh.shape["dp"]),
        mesh=mesh,
        in_specs=placed,
        out_specs=(P(("parts", "dp"), "row"), P(("parts", "row"), None), P("parts", "row")),
        check_vma=False,
    )
```

time: 353 us -> 129 us (0.37)
  waiting for transfers between devices: 217 us -> 66.9 us
  other arithmetic: 54.3 us -> 10 us
  starting transfers between devices: 0.2 us -> 21.4 us
  blocking collectives: 20.7 us -> 0 us
  matrix products: 21.7 us -> 5.72 us
  local copies, waits for them, and re-layouts: 23.9 us -> 8.19 us
  Pallas kernels: 0 us -> 15.4 us
  between operations: 14.5 us -> 0.95 us
    all_gather x3 -> x0, waiting for transfers between devices: 127 us -> none  [the longest x1 127 us: body(): weights = lax.all_gather(kept_blocks, 'dp', axis=1, tiled=True)[0]]
    ppermute x0 -> x18, waiting for transfers between devices: none -> 66.9 us  [the longest x5 45 us: group_shift(): return lax.ppermute(value, 'dp', pairs)]
    psum x1 -> x0, waiting for transfers between devices: 63.1 us -> none  [body(): lax.psum((input_gradient_piece, output_gradient_piece), 'dp')]
    scatter-add x1 -> x0, other arithmetic: 51.6 us -> none  [body(): partial_value = empty.at[block_col].add(products, mode='drop')]
    reduce_scatter x1 -> x0, waiting for transfers between devices: 25.7 us -> none  [body(): lax.psum_scatter(partial_value, 'row', scatter_dimension=1, tiled=True)]
    ppermute x0 -> x18, starting transfers between devices: none -> 21.4 us  [the longest x5 8.03 us: group_shift(): return lax.ppermute(value, 'dp', pairs)]
    dot_general x5, matrix products: 21.7 us -> 5.72 us  [the longest x1 2.1 us: body(): jnp.dot(mate_back_b, mate_activations, preferred_element_type=F32)]
    pallas_call x0 -> x7, Pallas kernels: none -> 15.4 us  [call(): pl.pallas_call(kernel, out_shape=outs, in_specs=[smem] * len(scalars) + [...]
  transfers between devices with their start and end apart: 5 -> 18, of which waited for: 3 -> 8; matrix products, arithmetic and copies ran while one was open for 27% -> 15% of each run, Pallas kernels for 0% -> 8%
where the time goes in v2:
time: 129 us
  waiting for transfers between devices  66.9 us (52%)
  starting transfers between devices  21.4 us (17%)
  Pallas kernels  15.4 us (12%)
  other arithmetic  10 us (8%)
  local copies, waits for them, and re-layouts  8.19 us (6%)
  matrix products  5.72 us (4%)
    ppermute x5, waiting for transfers between devices, group_shift(): return lax.ppermute(value, 'dp', pairs)  45 us
    ppermute x3, waiting for transfers between devices, chip_shift(): return lax.ppermute(value, 'row', pairs)  16.9 us
    pallas_call x7, Pallas kernels, call(): pl.pallas_call(kernel, out_shape=outs, in_specs=[smem] * len(scalars) + [...  15.4 us
    ppermute x5, starting transfers between devices, group_shift(): return lax.ppermute(value, 'dp', pairs)  8.03 us
    ppermute x3, waiting for transfers between devices, part_shift(): lax.ppermute(value, 'parts', [(i, (i + d) % n_parts) for i in range(n_par...  5.04 us
    ppermute x4, starting transfers between devices, mate_swap(): return lax.ppermute(value, 'dp', [(i, i ^ 1) for i in range(n_dp)])  4.96 us
    ppermute x3, starting transfers between devices, chip_shift(): return lax.ppermute(value, 'row', pairs)  4.53 us
    unnamed x36, local copies, waits for them, and re-layouts  4.12 us
  transfers between devices with their start and end apart: 18, of which 8 were waited for; matrix products, arithmetic and copies ran while one was open for 15% of the time, Pallas kernels for 8%

profile of v2, /device:TPU:0, one launch (start us, length us, event | category | flops | bytes accessed | tf_op | source)
XLA Modules:
  0.0 128.6 jit_solution(3202144935149662754)
XLA Ops:
  0.7 4.1 %collective-permute-start = (s32[64]{0:T(128)}, s32[64]{0:T(128)S(1)}, u32[]{:S(2)}, u32[]{:S(2)}) collective-permute-start(s32[64]{0:T(128)} %bitcast.33), channel_id=1, source_target_pairs={{0,2},{1,3},{2,0},{3,1},{4,6},{5,7},{6,4},{7,5},{8,10},{9,11},{10,... | collective-permute-start | bytes 776 | tf_op jit(solution)/shard_map/ppermute | solution.py:140
  4.8 1.6 %collective-permute-start.3 = (bf16[128,3328]{1,0:T(8,128)(2,1)}, bf16[128,3328]{1,0:T(8,128)(2,1)}, u32[]{:S(2)}, u32[]{:S(2)}) collective-permute-start(bf16[128,3328]{1,0:T(8,128)(2,1)} %own_ref.1), channel_id=1, source_target_pairs={{0,1},{1,0},{2,3},{3,2},{4,5},{5,4},{6,7},{7,6},{8,9},{9,8},{10,11... | collective-permute-start | bytes 2555912 | tf_op jit(solution)/shard_map/ppermute | solution.py:136
  7.0 1.7 %convolution_bitcast_fusion = f32[128,64]{1,0:T(8,128)S(1)} fusion(bf16[3328,64]{0,1:T(8,128)(2,1)} %param.12, bf16[128,3328]{1,0:T(8,128)(2,1)} %own_ref.1), kind=kOutput, calls=%fused_computation.3 | convolution fusion | flops 54525952 | bytes 1310720 | tf_op jit(solution)/shard_map/dot_general | solution.py:188
  8.7 1.3 fusion
  12.3 2.3 %collective-permute-start.4 = (bf16[12,128,128]{2,1,0:T(8,128)(2,1)}, bf16[12,128,128]{2,1,0:T(8,128)(2,1)}, u32[]{:S(2)}, u32[]{:S(2)}) collective-permute-start(bf16[12,128,128]{2,1,0:T(8,128)(2,1)} %get-tuple-element.34), channel_id=1, source_target_pairs={{0,2},{1,3},{2,0},{3,1},{4,6},{5,7},{6,4},{7,5},{8,10},{9,11},{10,... | collective-permute-start | bytes 1179656 | tf_op jit(solution)/shard_map/ppermute | solution.py:140
  14.6 1.0 fusion.17
  15.6 1.6 %collective-permute-start.2 = (f32[128,128]{1,0:T(8,128)S(1)}, f32[128,128]{1,0:T(8,128)S(1)}, u32[]{:S(2)}, u32[]{:S(2)}) collective-permute-start(f32[128,128]{1,0:T(8,128)S(1)} %fusion.17), channel_id=1, source_target_pairs={{0,8},{4,12},{8,0},{12,4},{1,9},{5,13},{9,1},{13,5},{2,10},{6,14},... | collective-permute-start | bytes 196616 | tf_op jit(solution)/shard_map/ppermute | solution.py:133
  18.5 1.4 %collective-permute-done.2 = f32[128,128]{1,0:T(8,128)S(1)} collective-permute-done((f32[128,128]{1,0:T(8,128)S(1)}, f32[128,128]{1,0:T(8,128)S(1)}, u32[]{:S(2)}, u32[]{:S(2)}) %collective-permute-start.2) | collective-permute-done | bytes 65568 | tf_op jit(solution)/shard_map/ppermute | solution.py:133
  21.8 1.5 %copy.18 = f32[64,128]{1,0:T(8,128)} copy(f32[64,128]{0,1:T(8,128)} %get-tuple-element.37) | data formatting | bytes 65536 | tf_op jit(solution)/shard_map/transpose | solution.py:203
  23.4 1.7 %pad_maximum_fusion.2 = f32[64,1152]{1,0:T(8,128)} fusion(f32[64,128]{1,0:T(8,128)} %copy.18, f32[64,1024]{1,0:T(8,128)} %constant_dynamic-slice_fusion), kind=kLoop, calls=%fused_computation.15 | loop fusion | flops 73728 | bytes 589824 | tf_op jit(solution)/shard_map/concatenate | solution.py:203
  25.1 1.6 %collective-permute-start.15 = (f32[64,1152]{1,0:T(8,128)}, f32[64,1152]{1,0:T(8,128)}, u32[]{:S(2)}, u32[]{:S(2)}) collective-permute-start(f32[64,1152]{1,0:T(8,128)} %pad_maximum_fusion.2), channel_id=1, source_target_pairs={{0,1},{1,0},{2,3},{3,2},{4,5},{5,4},{6,7},{7,6},{8,9},{9,8},{10,11... | collective-permute-start | bytes 884744 | tf_op jit(solution)/shard_map/ppermute | solution.py:136
  27.6 13.6 %collective-permute-done.4.rest_0_ = bf16[12,128,128]{2,1,0:T(8,128)(2,1)} collective-permute-done((bf16[12,128,128]{2,1,0:T(8,128)(2,1)}, bf16[12,128,128]{2,1,0:T(8,128)(2,1)}, u32[]{:S(2)}, u32[]{:S(2)}) %collective-permute-start.4) | collective-permute-done | bytes 393248 | tf_op jit(solution)/shard_map/ppermute | solution.py:140
  41.2 1.2 collective-permute-start.6
  42.5 13.9 %collective-permute-done.5.rest_1_ = bf16[12,128,128]{2,1,0:T(8,128)(2,1)} collective-permute-done((bf16[12,128,128]{2,1,0:T(8,128)(2,1)}, bf16[12,128,128]{2,1,0:T(8,128)(2,1)}, u32[]{:S(2)}, u32[]{:S(2)}) %collective-permute-start.5) | collective-permute-done | bytes 393248 | tf_op jit(solution)/shard_map/ppermute | solution.py:140
  56.3 1.5 %collective-permute-start.8 = (bf16[12,128,128]{2,1,0:T(8,128)(2,1)}, bf16[12,128,128]{2,1,0:T(8,128)(2,1)S(1)}, u32[]{:S(2)}, u32[]{:S(2)}) collective-permute-start(bf16[12,128,128]{2,1,0:T(8,128)(2,1)} %collective-permute-done.5.rest_1_), channel_id=1, source_target_pairs={{0,16},{16,0},{1,17},{17,1},{2,18},{18,2},{3,19},{19,3},{4,20},{20... | collective-permute-start | bytes 1179656 | tf_op jit(solution)/shard_map/ppermute | solution.py:143
  58.3 4.4 %shard_map.94 = (f32[65,256,128]{2,1,0:T(8,128)S(1)}, bf16[26,256,128]{2,1,0:T(8,128)(2,1)S(1)}) custom-call(s32[64]{0:T(128)S(1)} %bitcast.34, bf16[128,3328]{1,0:T(8,128)(2,1)S(1)} %copy-done.3, bf16[128,3328]{1,0:T(8,128)(2,1)} %collective-permute-done.3.mate_ref, bf16[64,128,128]{2,1,0:T(8,128)(2,1)S(1)} %bitcast.30), custom_call_target="tpu_custom_call" | custom-call | flops 536870912 | bytes 1048576 | tf_op jit(solution)/shard_map/pallas_call | solution.py:105
  63.3 1.0 add_convert_fusion
  64.3 3.2 %shard_map.95.old_ref = f32[65,256,128]{2,1,0:T(8,128)S(1)} custom-call(s32[3]{0:T(128)S(1)} %pad_add_fusion.where_ref, s32[64]{0:T(128)S(1)} %collective-permute-done.ids_ref, bf16[26,256,128]{2,1,0:T(8,128)(2,1)S(1)} %get-tuple-element.20.tiles_ref, f32[65,256,128]{2,1,0:T(8,128)S(1)} %get-tuple-element.21.old_ref, ...), custom_call_target="tpu_custom_call", output_to_operand_aliasing={{}: (3, {})} | custom-call | flops 301989888 | bytes 1048576 | tf_op jit(solution)/shard_map/pallas_call | solution.py:105
  67.5 1.1 collective-permute-done.8.rest_1_
  68.6 3.9 %collective-permute-done.9.rest_2_ = bf16[8,128,128]{2,1,0:T(8,128)(2,1)S(1)} collective-permute-done((bf16[8,128,128]{2,1,0:T(8,128)(2,1)S(1)}, bf16[8,128,128]{2,1,0:T(8,128)(2,1)S(1)}, u32[]{:S(2)}, u32[]{:S(2)}) %collective-permute-start.9) | collective-permute-done | bytes 262176 | tf_op jit(solution)/shard_map/ppermute | solution.py:143
  72.5 3.3 %shard_map.96 = (f32[65,256,128]{2,1,0:T(8,128)S(1)}, bf16[2,16,128,128]{3,2,1,0:T(8,128)(2,1)S(1)}, bf16[2,16,128,128]{3,2,1,0:T(8,128)(2,1)}) custom-call(s32[3]{0:T(128)S(1)} %pad_add_fusion.where_ref, s32[64]{0:T(128)S(1)} %collective-permute-done.ids_ref, ...), custom_call_target="tpu_custom_call", output_to_operand_aliasing={{0}: (3, {})} | custom-call | flops 234881024 | bytes 1048576 | tf_op jit(solution)/shard_map/pallas_call | solution.py:105
  75.8 2.1 %fusion.6 = f32[64,3328]{1,0:T(8,128)S(1)} fusion(bf16[128,3328]{1,0:T(8,128)(2,1)} %collective-permute-done.3.mate_ref, f32[64,1152]{1,0:T(8,128)} %collective-permute-done.15), kind=kOutput, calls=%fused_computation.25 | convolution fusion | flops 54525952 | bytes 1720320 | tf_op jit(solution)/shard_map/dot_general | solution.py:225
  79.4 17.5 %collective-permute-done.16 = bf16[64,2688]{1,0:T(8,128)(2,1)S(1)} collective-permute-done((bf16[64,2688]{1,0:T(8,128)(2,1)S(1)}, bf16[64,2688]{1,0:T(8,128)(2,1)S(1)}, u32[]{:S(2)}, u32[]{:S(2)}) %collective-permute-start.16) | collective-permute-done | bytes 344096 | tf_op jit(solution)/shard_map/ppermute | solution.py:140
  97.8 1.5 %collective-permute-start.12 = (bf16[16,128,128]{2,1,0:T(8,128)(2,1)S(1)}, bf16[16,128,128]{2,1,0:T(8,128)(2,1)}, u32[]{:S(2)}, u32[]{:S(2)}) collective-permute-start(bf16[16,128,128]{2,1,0:T(8,128)(2,1)S(1)} %bitcast.32), channel_id=1, source_target_pairs={{0,8},{4,12},{8,0},{12,4},{1,9},{5,13},{9,1},{13,5},{2,10},{6,14},... | collective-permute-start | bytes 1572872 | tf_op jit(solution)/shard_map/ppermute | solution.py:133
  99.3 3.4 %copy-done.2 = f32[65,256,128]{2,1,0:T(8,128)S(1)} copy-done((f32[65,256,128]{2,1,0:T(8,128)S(1)}, f32[65,256,128]{2,1,0:T(8,128)}, u32[]{:S(2)}) %copy-start.2) | copy-done | bytes 8519704
  103.4 8.1 %collective-permute-done.12.rest_0_ = bf16[16,128,128]{2,1,0:T(8,128)(2,1)} collective-permute-done((bf16[16,128,128]{2,1,0:T(8,128)(2,1)S(1)}, bf16[16,128,128]{2,1,0:T(8,128)(2,1)}, u32[]{:S(2)}, u32[]{:S(2)}) %collective-permute-start.12) | collective-permute-done | bytes 524320 | tf_op jit(solution)/shard_map/ppermute | solution.py:133
  111.5 1.4 %shard_map.99 = bf16[16,128,128]{2,1,0:T(8,128)(2,1)S(1)} custom-call(s32[3]{0:T(128)S(1)} %pad_add_fusion.where_ref, f32[65,256,128]{2,1,0:T(8,128)S(1)} %copy-done.2, bf16[2,16,128,128]{3,2,1,0:T(8,128)(2,1)S(1)} %collective-permute-done.11.core_ref, bf16[16,128,128]{2,1,0:T(8,128)(2,1)} %collective-permute-done.12.rest_0_), custom_call_target="tpu_custom_call" | custom-call | bytes 1048576 | tf_op jit(solution)/shard_map/pallas_call | solution.py:105
  112.9 1.8 %collective-permute-start.14 = (bf16[16,128,128]{2,1,0:T(8,128)(2,1)S(1)}, bf16[16,128,128]{2,1,0:T(8,128)(2,1)S(1)}, u32[]{:S(2)}, u32[]{:S(2)}) collective-permute-start(bf16[16,128,128]{2,1,0:T(8,128)(2,1)S(1)} %shard_map.99), channel_id=1, source_target_pairs={{0,1},{1,0},{2,3},{3,2},{4,5},{5,4},{6,7},{7,6},{8,9},{9,8},{10,11... | collective-permute-start | bytes 1572872 | tf_op jit(solution)/shard_map/ppermute | solution.py:136
  114.7 1.5 %collective-permute-start.13 = (bf16[16,128,128]{2,1,0:T(8,128)(2,1)S(1)}, bf16[16,128,128]{2,1,0:T(8,128)(2,1)S(1)}, u32[]{:S(2)}, u32[]{:S(2)}) collective-permute-start(bf16[16,128,128]{2,1,0:T(8,128)(2,1)S(1)} %bitcast.31), channel_id=1, source_target_pairs={{0,8},{4,12},{8,0},{12,4},{1,9},{5,13},{9,1},{13,5},{2,10},{6,14},... | collective-permute-start | bytes 1572872 | tf_op jit(solution)/shard_map/ppermute | solution.py:133
  116.2 1.2 broadcast_select_fusion.1
  119.4 7.4 %collective-permute-done.13.rest_0_ = bf16[16,128,128]{2,1,0:T(8,128)(2,1)S(1)} collective-permute-done((bf16[16,128,128]{2,1,0:T(8,128)(2,1)S(1)}, bf16[16,128,128]{2,1,0:T(8,128)(2,1)S(1)}, u32[]{:S(2)}, u32[]{:S(2)}) %collective-permute-start.13) | collective-permute-done | bytes 524320 | tf_op jit(solution)/shard_map/ppermute | solution.py:133
  126.9 1.8 %shard_map.100 = bf16[128,2048]{1,0:T(8,128)(2,1)} custom-call(s32[3]{0:T(128)S(1)} %pad_add_fusion.where_ref, bf16[128,64]{1,0:T(8,128)(2,1)S(1)} %get-tuple-element.38.low_ref, bf16[64,2048]{1,0:T(8,128)(2,1)S(1)} %copy-done.5, f32[65,256,128]{2,1,0:T(8,128)S(1)} %bitcast.29, bf16[2,16,128,128]{3,2,1,0:T(8,128)(2,1)S(1)} %collective-permute-done.10.core_ref, ...), custom_call_target="tpu_custom_call" | custom-call | flops 33554432 | bytes 1048576 | tf_op jit(solution)/shard_map/pallas_call | solution.py:105
  (75 shorter events, 13.2 us)
Async XLA Ops:
  0.6 8.0 %copy-start = (bf16[128,2048]{1,0:T(8,128)(2,1)S(1)}, bf16[128,2048]{1,0:T(8,128)(2,1)}, u32[]{:S(2)}) copy-start(bf16[128,2048]{1,0:T(8,128)(2,1)} %param.8) | copy-start | bytes 1572868
  0.6 10.7 %copy-start.4 = (bf16[1,64,128,128]{3,2,1,0:T(8,128)(2,1)S(1)}, bf16[1,64,128,128]{3,2,1,0:T(8,128)(2,1)}, u32[]{:S(2)}) copy-start(bf16[1,64,128,128]{3,2,1,0:T(8,128)(2,1)} %param.10) | copy-start | bytes 6291460
  0.7 6.3 %collective-permute-start = (s32[64]{0:T(128)}, s32[64]{0:T(128)S(1)}, u32[]{:S(2)}, u32[]{:S(2)}) collective-permute-start(s32[64]{0:T(128)} %bitcast.33), channel_id=1, source_target_pairs={{0,2},{1,3},{2,0},{3,1},{4,6},{5,7},{6,4},{7,5},{8,10},{9,11},{10,... | collective-permute-start | bytes 776 | tf_op jit(solution)/shard_map/ppermute | solution.py:140
  4.8 53.5 %collective-permute-start.3 = (bf16[128,3328]{1,0:T(8,128)(2,1)}, bf16[128,3328]{1,0:T(8,128)(2,1)}, u32[]{:S(2)}, u32[]{:S(2)}) collective-permute-start(bf16[128,3328]{1,0:T(8,128)(2,1)} %own_ref.1), channel_id=1, source_target_pairs={{0,1},{1,0},{2,3},{3,2},{4,5},{5,4},{6,7},{7,6},{8,9},{9,8},{10,11... | collective-permute-start | bytes 2555912 | tf_op jit(solution)/shard_map/ppermute | solution.py:136
  11.3 3.3 %collective-permute-start.1 = (f32[128,128]{1,0:T(8,128)}, f32[128,128]{1,0:T(8,128)}, u32[]{:S(2)}, u32[]{:S(2)}) collective-permute-start(f32[128,128]{1,0:T(8,128)} %pad_maximum_fusion.3), channel_id=1, source_target_pairs={{0,4},{4,0},{8,12},{12,8},{1,5},{5,1},{9,13},{13,9},{2,6},{6,2},{1... | collective-permute-start | bytes 196616 | tf_op jit(solution)/shard_map/ppermute | solution.py:129
  12.3 45.6 %copy-start.3 = (bf16[128,3328]{1,0:T(8,128)(2,1)S(1)}, bf16[128,3328]{1,0:T(8,128)(2,1)}, u32[]{:S(2)}) copy-start(bf16[128,3328]{1,0:T(8,128)(2,1)} %own_ref.1) | copy-start | bytes 2555908
  12.3 29.0 %collective-permute-start.4 = (bf16[12,128,128]{2,1,0:T(8,128)(2,1)}, bf16[12,128,128]{2,1,0:T(8,128)(2,1)}, u32[]{:S(2)}, u32[]{:S(2)}) collective-permute-start(bf16[12,128,128]{2,1,0:T(8,128)(2,1)} %get-tuple-element.34), channel_id=1, source_target_pairs={{0,2},{1,3},{2,0},{3,1},{4,6},{5,7},{6,4},{7,5},{8,10},{9,11},{10,... | collective-permute-start | bytes 1179656 | tf_op jit(solution)/shard_map/ppermute | solution.py:140
  15.6 4.3 %collective-permute-start.2 = (f32[128,128]{1,0:T(8,128)S(1)}, f32[128,128]{1,0:T(8,128)S(1)}, u32[]{:S(2)}, u32[]{:S(2)}) collective-permute-start(f32[128,128]{1,0:T(8,128)S(1)} %fusion.17), channel_id=1, source_target_pairs={{0,8},{4,12},{8,0},{12,4},{1,9},{5,13},{9,1},{13,5},{2,10},{6,14},... | collective-permute-start | bytes 196616 | tf_op jit(solution)/shard_map/ppermute | solution.py:133
  17.9 38.5 %collective-permute-start.5 = (bf16[12,128,128]{2,1,0:T(8,128)(2,1)}, bf16[12,128,128]{2,1,0:T(8,128)(2,1)}, u32[]{:S(2)}, u32[]{:S(2)}) collective-permute-start(bf16[12,128,128]{2,1,0:T(8,128)(2,1)} %get-tuple-element.22), channel_id=1, source_target_pairs={{0,2},{1,3},{2,0},{3,1},{4,6},{5,7},{6,4},{7,5},{8,10},{9,11},{10,... | collective-permute-start | bytes 1179656 | tf_op jit(solution)/shard_map/ppermute | solution.py:140
  19.9 38.3 %copy-start.6 = (s32[1,64]{1,0:T(1,128)S(1)}, s32[1,64]{1,0:T(1,128)}, u32[]{:S(2)}) copy-start(s32[1,64]{1,0:T(1,128)} %param.11) | copy-start | bytes 772
  25.1 33.2 %collective-permute-start.15 = (f32[64,1152]{1,0:T(8,128)}, f32[64,1152]{1,0:T(8,128)}, u32[]{:S(2)}, u32[]{:S(2)}) collective-permute-start(f32[64,1152]{1,0:T(8,128)} %pad_maximum_fusion.2), channel_id=1, source_target_pairs={{0,1},{1,0},{2,3},{3,2},{4,5},{5,4},{6,7},{7,6},{8,9},{9,8},{10,11... | collective-permute-start | bytes 884744 | tf_op jit(solution)/shard_map/ppermute | solution.py:136
  26.7 36.0 %collective-permute-start.7 = (bf16[8,128,128]{2,1,0:T(8,128)(2,1)}, bf16[8,128,128]{2,1,0:T(8,128)(2,1)S(1)}, u32[]{:S(2)}, u32[]{:S(2)}) collective-permute-start(bf16[8,128,128]{2,1,0:T(8,128)(2,1)} %dynamic-slice_bitcast_fusion.2), channel_id=1, source_target_pairs={{0,2},{1,3},{2,0},{3,1},{4,6},{5,7},{6,4},{7,5},{8,10},{9,11},{10,... | collective-permute-start | bytes 786440 | tf_op jit(solution)/shard_map/ppermute | solution.py:140
  41.2 23.0 %collective-permute-start.6 = (bf16[12,128,128]{2,1,0:T(8,128)(2,1)}, bf16[12,128,128]{2,1,0:T(8,128)(2,1)S(1)}, u32[]{:S(2)}, u32[]{:S(2)}) collective-permute-start(bf16[12,128,128]{2,1,0:T(8,128)(2,1)} %collective-permute-done.4.rest_0_), channel_id=1, source_target_pairs={{0,16},{16,0},{1,17},{17,1},{2,18},{18,2},{3,19},{19,3},{4,20},{20... | collective-permute-start | bytes 1179656 | tf_op jit(solution)/shard_map/ppermute | solution.py:143
  56.3 12.3 %collective-permute-start.8 = (bf16[12,128,128]{2,1,0:T(8,128)(2,1)}, bf16[12,128,128]{2,1,0:T(8,128)(2,1)S(1)}, u32[]{:S(2)}, u32[]{:S(2)}) collective-permute-start(bf16[12,128,128]{2,1,0:T(8,128)(2,1)} %collective-permute-done.5.rest_1_), channel_id=1, source_target_pairs={{0,16},{16,0},{1,17},{17,1},{2,18},{18,2},{3,19},{19,3},{4,20},{20... | collective-permute-start | bytes 1179656 | tf_op jit(solution)/shard_map/ppermute | solution.py:143
  58.2 5.0 %copy-start.10 = (f32[64,2048]{1,0:T(8,128)S(1)}, f32[64,2048]{1,0:T(8,128)}, u32[]{:S(2)}) copy-start(f32[64,2048]{1,0:T(8,128)} %copy-done.9) | copy-start | bytes 1572868
  62.7 9.8 %collective-permute-start.9 = (bf16[8,128,128]{2,1,0:T(8,128)(2,1)S(1)}, bf16[8,128,128]{2,1,0:T(8,128)(2,1)S(1)}, u32[]{:S(2)}, u32[]{:S(2)}) collective-permute-start(bf16[8,128,128]{2,1,0:T(8,128)(2,1)S(1)} %collective-permute-done.7.rest_0_), channel_id=1, source_target_pairs={{0,16},{16,0},{1,17},{17,1},{2,18},{18,2},{3,19},{19,3},{4,20},{20... | collective-permute-start | bytes 786440 | tf_op jit(solution)/shard_map/ppermute | solution.py:143
  75.8 3.6 %copy-start.1 = (f32[65,256,128]{2,1,0:T(8,128)}, f32[65,256,128]{2,1,0:T(8,128)S(1)}, u32[]{:S(2)}) copy-start(f32[65,256,128]{2,1,0:T(8,128)S(1)} %get-tuple-element.25.total_ref) | copy-start | bytes 25559044
  75.8 2.9 %collective-permute-start.11 = (bf16[2,16,128,128]{3,2,1,0:T(8,128)(2,1)S(1)}, bf16[2,16,128,128]{3,2,1,0:T(8,128)(2,1)S(1)}, u32[]{:S(2)}, u32[]{:S(2)}) collective-permute-start(bf16[2,16,128,128]{3,2,1,0:T(8,128)(2,1)S(1)} %get-tuple-element.27), channel_id=1, source_target_pairs={{0,4},{4,0},{8,12},{12,8},{1,5},{5,1},{9,13},{13,9},{2,6},{6,2},{1... | collective-permute-start | bytes 3145736 | tf_op jit(solution)/shard_map/ppermute | solution.py:129
  78.0 18.8 %copy-start.7 = (bf16[64,2688]{1,0:T(8,128)(2,1)}, bf16[64,2688]{1,0:T(8,128)(2,1)S(1)}, u32[]{:S(2)}) copy-start(bf16[64,2688]{1,0:T(8,128)(2,1)S(1)} %pad_maximum_fusion.1) | copy-start | bytes 1032196
  78.0 18.8 %collective-permute-start.16 = (bf16[64,2688]{1,0:T(8,128)(2,1)S(1)}, bf16[64,2688]{1,0:T(8,128)(2,1)S(1)}, u32[]{:S(2)}, u32[]{:S(2)}) collective-permute-start(bf16[64,2688]{1,0:T(8,128)(2,1)S(1)} %pad_maximum_fusion.1), channel_id=1, source_target_pairs={{0,2},{1,3},{2,0},{3,1},{4,6},{5,7},{6,4},{7,5},{8,10},{9,11},{10,... | collective-permute-start | bytes 1032200 | tf_op jit(solution)/shard_map/ppermute | solution.py:140
  78.1 21.2 %collective-permute-start.10 = (bf16[2,16,128,128]{3,2,1,0:T(8,128)(2,1)}, bf16[2,16,128,128]{3,2,1,0:T(8,128)(2,1)S(1)}, u32[]{:S(2)}, u32[]{:S(2)}) collective-permute-start(bf16[2,16,128,128]{3,2,1,0:T(8,128)(2,1)} %get-tuple-element.26), channel_id=1, source_target_pairs={{0,4},{4,0},{8,12},{12,8},{1,5},{5,1},{9,13},{13,9},{2,6},{6,2},{1... | collective-permute-start | bytes 3145736 | tf_op jit(solution)/shard_map/ppermute | solution.py:129
  97.8 18.4 %collective-permute-start.17 = (f32[64,2688]{1,0:T(8,128)}, f32[64,2688]{1,0:T(8,128)}, u32[]{:S(2)}, u32[]{:S(2)}) collective-permute-start(f32[64,2688]{1,0:T(8,128)} %convert_add_fusion), channel_id=1, source_target_pairs={{0,1},{1,0},{2,3},{3,2},{4,5},{5,4},{6,7},{7,6},{8,9},{9,8},{10,11... | collective-permute-start | bytes 2064392 | tf_op jit(solution)/shard_map/ppermute | solution.py:136
  97.8 13.7 %collective-permute-start.12 = (bf16[16,128,128]{2,1,0:T(8,128)(2,1)S(1)}, bf16[16,128,128]{2,1,0:T(8,128)(2,1)}, u32[]{:S(2)}, u32[]{:S(2)}) collective-permute-start(bf16[16,128,128]{2,1,0:T(8,128)(2,1)S(1)} %bitcast.32), channel_id=1, source_target_pairs={{0,8},{4,12},{8,0},{12,4},{1,9},{5,13},{9,1},{13,5},{2,10},{6,14},... | collective-permute-start | bytes 1572872 | tf_op jit(solution)/shard_map/ppermute | solution.py:133
  99.3 3.4 %copy-start.2 = (f32[65,256,128]{2,1,0:T(8,128)S(1)}, f32[65,256,128]{2,1,0:T(8,128)}, u32[]{:S(2)}) copy-start(f32[65,256,128]{2,1,0:T(8,128)} %copy-done.1) | copy-start | bytes 25559044
  103.4 12.8 %copy-start.8 = (bf16[64,2688]{1,0:T(8,128)(2,1)S(1)}, bf16[64,2688]{1,0:T(8,128)(2,1)}, u32[]{:S(2)}) copy-start(bf16[64,2688]{1,0:T(8,128)(2,1)} %copy-done.7) | copy-start | bytes 1032196
  103.4 12.8 %copy-start.12 = (bf16[64,2688]{1,0:T(8,128)(2,1)S(1)}, bf16[64,2688]{1,0:T(8,128)(2,1)}, u32[]{:S(2)}) copy-start(bf16[64,2688]{1,0:T(8,128)(2,1)} %copy-done.11) | copy-start | bytes 1032196
  111.5 15.3 %slice-start = ((s8[8519680]{0:T(1024)(128)(4,1)}), s8[4194304]{0:T(1024)(128)(4,1)S(1)}, s32[]{:S(2)}) async-start(s8[8519680]{0:T(1024)(128)(4,1)} %bitcast.28), calls=%async_computation | async-start | bytes 8388608
  111.5 15.3 %slice-start.1 = ((s8[8519680]{0:T(1024)(128)(4,1)}), s8[4194304]{0:T(1024)(128)(4,1)S(1)}, s32[]{:S(2)}) async-start(s8[8519680]{0:T(1024)(128)(4,1)} %bitcast.28), calls=%async_computation.1 | async-start | bytes 8388608
  112.9 13.9 %collective-permute-start.14 = (bf16[16,128,128]{2,1,0:T(8,128)(2,1)S(1)}, bf16[16,128,128]{2,1,0:T(8,128)(2,1)S(1)}, u32[]{:S(2)}, u32[]{:S(2)}) collective-permute-start(bf16[16,128,128]{2,1,0:T(8,128)(2,1)S(1)} %shard_map.99), channel_id=1, source_target_pairs={{0,1},{1,0},{2,3},{3,2},{4,5},{5,4},{6,7},{7,6},{8,9},{9,8},{10,11... | collective-permute-start | bytes 1572872 | tf_op jit(solution)/shard_map/ppermute | solution.py:136
  114.7 12.1 %slice-start.2 = ((s8[8519680]{0:T(1024)(128)(4,1)}), s8[131072]{0:T(1024)(128)(4,1)S(1)}, s32[]{:S(2)}) async-start(s8[8519680]{0:T(1024)(128)(4,1)} %bitcast.28), calls=%async_computation.2 | async-start | bytes 262144
  114.7 12.1 %collective-permute-start.13 = (bf16[16,128,128]{2,1,0:T(8,128)(2,1)S(1)}, bf16[16,128,128]{2,1,0:T(8,128)(2,1)S(1)}, u32[]{:S(2)}, u32[]{:S(2)}) collective-permute-start(bf16[16,128,128]{2,1,0:T(8,128)(2,1)S(1)} %bitcast.31), channel_id=1, source_target_pairs={{0,8},{4,12},{8,0},{12,4},{1,9},{5,13},{9,1},{13,5},{2,10},{6,14},... | collective-permute-start | bytes 1572872 | tf_op jit(solution)/shard_map/ppermute | solution.py:133
  117.5 9.3 %copy-start.5 = (bf16[64,2048]{1,0:T(8,128)(2,1)S(1)}, bf16[64,2048]{1,0:T(8,128)(2,1)}, u32[]{:S(2)}) copy-start(bf16[64,2048]{1,0:T(8,128)(2,1)} %adapter_ref.1) | copy-start | bytes 786436
  (4 other events, 5.0 us)

commit v3 on v2

--- a/solution.py
+++ b/solution.py
@@ -85,9 +85,71 @@
         out_ref[q] = value.astype(BF16)
 
 
-def final_kernel(where_ref, low_ref, adapter_ref, total_ref, core_ref, *rest):
+def ordered_sum(own, received, place):
+    count = len(received) + 1
+    if count == 1:
+        return own
+    if count == 2:
+        return own + received[0]
+    total = None
+    for member in range(count):
+        value = own
+        for d, other in enumerate(received, 1):
+            value = jnp.where(lax.rem(place + (count - d), count) == member, other, value)
+        total = value if total is None else total + value
+    return total
+
+
+CONTRACT_LAST = (((1,), (1,)), ((), ()))
+
+
+def low_rank_kernel(acts_ref, adapter_a_ref, cot_ref, adapter_ref, labels_ref, out_ref):
+    rank = adapter_a_ref.shape[0]
+    signs = (1 - 2 * labels_ref[...]).astype(F32)
+    out_ref[:rank, :] = lax.dot_general(adapter_a_ref[...], acts_ref[...], CONTRACT_LAST, preferred_element_type=F32)
+    out_ref[rank:, :] = signs * lax.dot_general(
+        adapter_ref[...], cot_ref[...], CONTRACT_LAST, preferred_element_type=F32
+    )
+
+
+def own_grad_kernel(where_ref, cot_ref, labels_ref, both_ref, *rest):
+    received, (rounded_ref, pack_ref) = rest[:-2], rest[-2:]
+    feats = cot_ref.shape[1]
+    rounded = ordered_sum(both_ref[...], [ref[...] for ref in received], where_ref[2]).astype(BF16)
+    rounded_ref[...] = rounded
+    rank = rounded.shape[0] // 2
+    signs = (1 - 2 * labels_ref[...]).astype(F32)
+    signed_low = (rounded[:rank].astype(F32) * signs).astype(BF16)
+    grad = jnp.dot(signed_low, cot_ref[...], preferred_element_type=F32)
+    pack_ref[:, :feats] = (adapter_scale * grad).astype(BF16)
+    pack_ref[:, feats:] = rounded[rank:]
+
+
+def pair_grad_kernel(rounded_ref, acts_ref, mate_acts_ref, pack_ref, mate_pack_ref, out_ref):
+    rank, shard_rows = rounded_ref.shape[0] // 2, acts_ref.shape[1]
+    feats = pack_ref.shape[1] - rounded_ref.shape[1]
+    own = jnp.dot(rounded_ref[rank:, :], acts_ref[...], preferred_element_type=F32)
+    mate = jnp.dot(mate_pack_ref[:, feats:], mate_acts_ref[...], preferred_element_type=F32)
+    out_ref[:, :shard_rows] = (adapter_scale * (own + mate)).astype(BF16)
+    out_ref[:, shard_rows:] = (
+        pack_ref[:, :feats].astype(F32) + mate_pack_ref[:, :feats].astype(F32)
+    ).astype(BF16)
+
+
+def grad_sum_kernel(where_ref, own_ref, *rest):
+    received, (in_ref, out_ref) = rest[:-2], rest[-2:]
+    shard_rows = in_ref.shape[1]
+    own, place = own_ref[...].astype(F32), where_ref[3]
+    total = ordered_sum(own, [ref[...].astype(F32) for ref in received], place)
+    in_ref[...] = total[:, :shard_rows]
+    out_ref[...] = total[:, shard_rows:]
+
+
+def final_kernel(where_ref, rounded_ref, adapter_ref, total_ref, core_ref, *rest):
     pieces, out_ref = rest[:-1], rest[-1]
     _, share, tokens, tile = core_ref.shape
+    rank = rounded_ref.shape[0] // 2
+    low = rounded_ref[:rank, :].astype(F32).T.astype(BF16)
     chip = where_ref[2]
     mine = (2 * chip + where_ref[1]) * share
     for q in range(share):
@@ -95,7 +157,7 @@
         for piece in pieces:
             value += piece[q].astype(F32)
         cols = slice(q * tile, (q + 1) * tile)
-        extra = jnp.dot(low_ref[...], adapter_ref[:, cols], preferred_element_type=F32)
+        extra = jnp.dot(low, adapter_ref[:, cols], preferred_element_type=F32)
         out_ref[:, cols] = (value + adapter_scale * extra).astype(BF16)
 
 
@@ -142,15 +204,6 @@
     def part_shift(value, d):
         return lax.ppermute(value, "parts", [(i, (i + d) % n_parts) for i in range(n_parts)])
 
-    def in_order_sum(own, received, place, count):
-        if count == 2:
-            return own.astype(F32) + received[0].astype(F32)
-        stack = jnp.zeros((count,) + own.shape, own.dtype)
-        stack = lax.dynamic_update_index_in_dim(stack, own, place, 0)
-        for d, value in enumerate(received, 1):
-            stack = lax.dynamic_update_index_in_dim(stack, value, lax.rem(place + (count - d), count), 0)
-        return stack.astype(F32).sum(axis=0)
-
     def body(activations, cotangent, forget_labels, kept_blocks, block_ids, adapter_a, output_adapter):
         tokens, shard_rows = activations.shape
         rank = adapter_a.shape[1]
@@ -162,45 +215,44 @@
         part = lax.axis_index("parts")
         row_index = lax.axis_index("row")
         dp_index = lax.axis_index("dp")
-        core, chip = lax.rem(row_index, 2), lax.div(row_index, 2)
-        half_bit, place = lax.rem(dp_index, 2), lax.div(dp_index, 2)
-        where = jnp.stack([part, core, chip]).astype(jnp.int32)
+        where = jnp.stack(
+            [part, lax.rem(row_index, 2), lax.div(row_index, 2), lax.div(dp_index, 2)]
+        ).astype(jnp.int32)
         blocks = kept_blocks[0]
         ids = block_ids[0]
+        labels = forget_labels[None, :]
 
         far_ids = [group_shift(ids, d) for d in range(1, group)]
-        mate_activations = mate_swap(activations)
+        all_ids = far_ids[0] if group == 2 else jnp.concatenate(far_ids)
         held = slots // n_parts
         sizes = [held * k // 32 for k in (12, 12, 8)]
         starts = [sum(sizes[:k]) for k in range(len(sizes))]
         own_share = lax.dynamic_slice_in_dim(blocks, part * held, held, axis=0)
-        all_ids = far_ids[0] if group == 2 else jnp.concatenate(far_ids)
+        shares = [own_share[start:start + size] for start, size in zip(starts, sizes)]
         direct = []
         for d in range(1, group):
-            for start, size in zip(starts, sizes):
-                leaving = own_share[start:start + size]
+            for leaving, start in zip(shares, starts):
                 if start > 0:
                     leaving = after(leaving, all_ids)
                 direct.append((group_shift(leaving, d), ((d - 1) * slots, 0, start)))
-
-        adapter_early = after(adapter_a, all_ids)
-        signs = (1 - 2 * forget_labels).astype(F32)[:, None]
-        low_part = jnp.dot(activations, adapter_early, preferred_element_type=F32)
-        back_part = signs * lax.dot_general(
-            cotangent, after(output_adapter, all_ids), (((1,), (1,)), ((), ())), preferred_element_type=F32
-        )
-        both = jnp.concatenate([low_part, back_part], axis=1)
+        mate_activations = mate_swap(activations)
+
+        adapter_early = after(adapter_a, all_ids, *shares)
+        (both,) = call(
+            low_rank_kernel, (jax.ShapeDtypeStruct((2 * rank, tokens), F32),), (),
+            (activations, adapter_early.T, cotangent, output_adapter, labels), 4 * tokens * rank * shard_rows,
+        )
         both = both + core_swap(both)
-        both = in_order_sum(both, [chip_shift(both, d) for d in range(1, chips)], chip, chips).astype(BF16)
-        low_b, back_b = both[:, :rank], both[:, rank:]
-        contract_tokens = (((0,), (0,)), ((), ()))
-        out_grad = adapter_scale * lax.dot_general(
-            low_b * signs.astype(BF16), cotangent, contract_tokens, preferred_element_type=F32
-        )
-        in_half, out_half = shard_rows // 2, feats // 2
-        out_mine = lax.dynamic_slice_in_dim(out_grad, half_bit * out_half, out_half, axis=1)
-        out_other = lax.dynamic_slice_in_dim(out_grad, (1 - half_bit) * out_half, out_half, axis=1)
-        mate_pack = mate_swap(jnp.concatenate([out_other, back_b.astype(F32).T], axis=1))
+        rounded, pack = call(
+            own_grad_kernel,
+            (
+                jax.ShapeDtypeStruct((2 * rank, tokens), BF16),
+                jax.ShapeDtypeStruct((rank, feats + tokens), BF16),
+            ),
+            (where,), (cotangent, labels, both) + tuple(chip_shift(both, d) for d in range(1, chips)),
+            2 * tokens * rank * feats,
+        )
+        mate_pack = mate_swap(pack)
 
         both_tokens = 2 * tokens
         per_block = 2 * both_tokens * tile * tile
@@ -212,25 +264,21 @@
         )
         swapped = []
         for k, (value, (offset, _, start)) in enumerate(direct):
-            if k == len(direct) - 1:
+            if k == len(direct) - 2:
                 value = after(value, total)
             for e in range(1, n_parts):
                 swapped.append((part_shift(value, e), (offset, e, start)))
 
-        gate = direct[-2][0]
-        mate_pack = after(mate_pack, gate)
-        mate_out, mate_back_b = mate_pack[:, :out_half], mate_pack[:, out_half:].astype(BF16)
-        in_grad = adapter_scale * (
-            lax.dot_general(back_b, activations, contract_tokens, preferred_element_type=F32)
-            + jnp.dot(mate_back_b, mate_activations, preferred_element_type=F32)
-        )
-        in_mine = lax.dynamic_slice_in_dim(in_grad, half_bit * in_half, in_half, axis=1)
-        grads = jnp.concatenate([in_mine, out_mine + mate_out], axis=1).astype(BF16)
+        (grads,) = call(
+            pair_grad_kernel, (jax.ShapeDtypeStruct((rank, shard_rows + feats), BF16),), (),
+            (rounded, activations, mate_activations, pack, after(mate_pack, direct[-2][0])),
+            4 * tokens * rank * shard_rows,
+        )
         grads = after(grads, direct[-1][0])
         far_grads = [group_shift(grads, d) for d in range(1, group)]
 
-        late = [direct[-1]] + swapped[-2 * (n_parts - 1):]
-        early = direct[:-1] + swapped[:-2 * (n_parts - 1)]
+        late = swapped[1 - n_parts:]
+        early = direct + swapped[:1 - n_parts]
 
         def plan(items):
             return dict(places=[item[1] for item in items], parts=n_parts, held=held, col_blocks=col_blocks)
@@ -244,7 +292,8 @@
         )
         send = pltpu.VMEM((chips, share, tokens, tile), BF16)
         total, send_mate, send_own = call(
-            functools.partial(last_kernel, **plan(late)), (total_shape, send, send), (where, all_ids),
+            functools.partial(last_kernel, **plan(late)), (total_shape, send, send),
+            (after(where, grads), all_ids),
             (on_chip(tiles), on_chip(total)) + tuple(item[0] for item in late), work(late), {3: 0},
         )
 
@@ -255,31 +304,29 @@
             )
             if needed:
                 leaving = after(leaving, *needed)
-            return leaving, [chip_shift(leaving[d - 1], d) for d in range(1, chips)]
+            return [chip_shift(leaving[d - 1], d) for d in range(1, chips)]
 
         core_mate = core_swap(send_mate)
         core_own = core_swap(send_own)
-        leaving, mate_pieces = for_chips(tokens, core_mate)
-        far_grads = [after(value, leaving) for value in far_grads]
-        grads = in_order_sum(grads, far_grads, place, group)
-        mate_grads = mate_swap(grads)
+        mate_pieces = for_chips(tokens, core_mate)
         (mate_total,) = call(
             mate_kernel, (pltpu.VMEM((share, tokens, tile), BF16),), (where,),
             (on_chip(total), core_mate) + tuple(mate_pieces), 0,
         )
         from_mate = mate_swap(mate_total)
-        _, own_pieces = for_chips(0, core_own, mate_total)
-        mate_grads = after(mate_grads, mate_total)
-        low_side = jnp.where(half_bit == 0, grads, mate_grads)
-        high_side = jnp.where(half_bit == 0, mate_grads, grads)
-        input_adapter_gradient = jnp.concatenate([low_side[:, :in_half], high_side[:, :in_half]], axis=1).T
-        output_adapter_gradient = jnp.concatenate([low_side[:, in_half:], high_side[:, in_half:]], axis=1)
+        own_pieces = for_chips(0, core_own, mate_total)
+        far_grads = [after(value, mate_total) for value in far_grads]
+        in_grad, out_grad = call(
+            grad_sum_kernel,
+            (jax.ShapeDtypeStruct((rank, shard_rows), F32), jax.ShapeDtypeStruct((rank, feats), F32)),
+            (where,), (grads,) + tuple(far_grads), 0,
+        )
         (projected,) = call(
             final_kernel, (jax.ShapeDtypeStruct((tokens, feats), BF16),), (where,),
-            (low_b, output_adapter, on_chip(total), core_own) + tuple(own_pieces) + (from_mate,),
+            (rounded, output_adapter, on_chip(total), core_own) + tuple(own_pieces) + (from_mate,),
             2 * tokens * rank * feats,
         )
-        return projected, input_adapter_gradient, output_adapter_gradient
+        return projected, in_grad.T, out_grad
 
     return body
 

time: 129 us -> 125 us (0.969)
  waiting for transfers between devices: 66.9 us -> 77.8 us
  other arithmetic: 10 us -> 0.92 us
  matrix products: 5.72 us -> 0 us
  Pallas kernels: 15.4 us -> 18.4 us
  local copies, waits for them, and re-layouts: 8.19 us -> 6.52 us
  starting transfers between devices: 21.4 us -> 20 us
    ppermute x4 -> x3, waiting for transfers between devices: 0.01 us -> 12 us  [mate_swap(): return lax.ppermute(value, 'dp', [(i, i ^ 1) for i in range(n_dp)])]
    ppermute x5, waiting for transfers between devices: 45 us -> 51.1 us  [group_shift(): return lax.ppermute(value, 'dp', pairs)]
    dot_general x5 -> x0, matrix products: 5.72 us -> none  [the longest x1 2.1 us: body(): jnp.dot(mate_back_b, mate_activations, preferred_element_type=F32)]
    ppermute x3, waiting for transfers between devices: 16.9 us -> 11.3 us  [chip_shift(): return lax.ppermute(value, 'row', pairs)]
    ppermute x3, waiting for transfers between devices: 5.04 us -> 0.01 us  [part_shift(): lax.ppermute(value, 'parts', [(i, (i + d) % n_parts) for i in range(n_par...]
    ppermute x3, waiting for transfers between devices: 0.01 us -> 3.44 us  [core_swap(): return lax.ppermute(value, 'row', [(i, i ^ 1) for i in range(n_row)])]
    concatenate x4 -> x0, other arithmetic: 3.28 us -> none  [the longest x1 1.71 us: body(): jnp.concatenate([out_other, back_b.astype(F32).T], axis=1)]
    pallas_call x7 -> x11, Pallas kernels: 15.4 us -> 18.4 us  [call(): pl.pallas_call(kernel, out_shape=outs, in_specs=[smem] * len(scalars) + [...]
  transfers between devices with their start and end apart: 18 -> 17, of which waited for: 8 -> 9; matrix products, arithmetic and copies ran while one was open for 15% -> 4% of each run, Pallas kernels for 8% -> 12%
where the time goes in v3:
time: 125 us; the launch traced here: 124 us
  waiting for transfers between devices  77.8 us (62%)
  starting transfers between devices  20 us (16%)
  Pallas kernels  18.4 us (15%)
  local copies, waits for them, and re-layouts  6.52 us (5%)
    ppermute x5, waiting for transfers between devices, group_shift(): return lax.ppermute(value, 'dp', pairs)  51.1 us
    pallas_call x11, Pallas kernels, call(): pl.pallas_call(kernel, out_shape=outs, in_specs=[smem] * len(scalars) + [...  18.4 us
    ppermute x3, waiting for transfers between devices, mate_swap(): return lax.ppermute(value, 'dp', [(i, i ^ 1) for i in range(n_dp)])  12 us
    ppermute x3, waiting for transfers between devices, chip_shift(): return lax.ppermute(value, 'row', pairs)  11.3 us
    ppermute x5, starting transfers between devices, group_shift(): return lax.ppermute(value, 'dp', pairs)  6.92 us
    ppermute x3, starting transfers between devices, chip_shift(): return lax.ppermute(value, 'row', pairs)  4.67 us
    ppermute x3, starting transfers between devices, part_shift(): lax.ppermute(value, 'parts', [(i, (i + d) % n_parts) for i in range(n_par...  4.56 us
    slice x2, local copies, waits for them, and re-layouts, body(): own_share[start:start + size]  3.88 us
  transfers between devices with their start and end apart: 17, of which 9 were waited for; matrix products, arithmetic and copies ran while one was open for 4% of the time, Pallas kernels for 12%

profile of v3, /device:TPU:0, one launch (start us, length us, event | category | flops | bytes accessed | tf_op | source)
XLA Modules:
  0.0 124.4 jit_solution(6220560431495275932)
XLA Ops:
  0.6 3.1 %collective-permute-start.3 = (bf16[128,3328]{1,0:T(8,128)(2,1)}, bf16[128,3328]{1,0:T(8,128)(2,1)}, u32[]{:S(2)}, u32[]{:S(2)}) collective-permute-start(bf16[128,3328]{1,0:T(8,128)(2,1)} %own_ref.1), channel_id=1, source_target_pairs={{0,1},{1,0},{2,3},{3,2},{4,5},{5,4},{6,7},{7,6},{8,9},{9,8},{10,11... | collective-permute-start | bytes 2555912 | tf_op jit(solution)/shard_map/ppermute | solution.py:198
  3.7 2.2 %dynamic-slice_bitcast_fusion = (bf16[12,128,128]{2,1,0:T(8,128)(2,1)}, bf16[12,128,128]{2,1,0:T(8,128)(2,1)}) fusion(bf16[1,64,128,128]{3,2,1,0:T(8,128)(2,1)} %param.10, s32[]{:T(128)S(6)} %add.11, s32[]{:T(128)S(6)} %select_n.3), kind=kLoop, calls=%fused_computation | loop fusion | bytes 1572872 | tf_op jit(solution)/shard_map/slice | solution.py:231
  6.0 2.6 %collective-permute-start.7 = (bf16[12,128,128]{2,1,0:T(8,128)(2,1)}, bf16[12,128,128]{2,1,0:T(8,128)(2,1)}, u32[]{:S(2)}, u32[]{:S(2)}) collective-permute-start(bf16[12,128,128]{2,1,0:T(8,128)(2,1)} %get-tuple-element.40), channel_id=1, source_target_pairs={{0,2},{1,3},{2,0},{3,1},{4,6},{5,7},{6,4},{7,5},{8,10},{9,11},{10,... | collective-permute-start | bytes 1179656 | tf_op jit(solution)/shard_map/ppermute | solution.py:202
  8.9 21.8 %collective-permute-done.ids_ref = s32[64]{0:T(128)S(1)} collective-permute-done((s32[64]{0:T(128)}, s32[64]{0:T(128)S(1)}, u32[]{:S(2)}, u32[]{:S(2)}) %collective-permute-start) | collective-permute-done | bytes 288 | tf_op jit(solution)/shard_map/ppermute | solution.py:202
  30.7 3.4 %collective-permute-start.5 = (bf16[12,128,128]{2,1,0:T(8,128)(2,1)}, bf16[12,128,128]{2,1,0:T(8,128)(2,1)}, u32[]{:S(2)}, u32[]{:S(2)}) collective-permute-start(bf16[12,128,128]{2,1,0:T(8,128)(2,1)} %get-tuple-element.24), channel_id=1, source_target_pairs={{0,2},{1,3},{2,0},{3,1},{4,6},{5,7},{6,4},{7,5},{8,10},{9,11},{10,... | collective-permute-start | bytes 1179656 | tf_op jit(solution)/shard_map/ppermute | solution.py:202
  34.1 1.7 %dynamic-slice_bitcast_fusion.2 = bf16[8,128,128]{2,1,0:T(8,128)(2,1)} fusion(bf16[1,64,128,128]{3,2,1,0:T(8,128)(2,1)} %param.10, s32[]{:T(128)S(6)} %add.12), kind=kLoop, calls=%fused_computation.2 | loop fusion | bytes 524292 | tf_op jit(solution)/shard_map/slice | solution.py:231
  35.8 0.9 copy-done.3
  36.7 1.0 copy-done.5
  37.7 0.7 copy-done.6
  39.1 1.3 %collective-permute-done.1 = f32[128,128]{1,0:T(8,128)} collective-permute-done((f32[128,128]{1,0:T(8,128)S(1)}, f32[128,128]{1,0:T(8,128)}, u32[]{:S(2)}, u32[]{:S(2)}) %collective-permute-start.1) | collective-permute-done | bytes 65568 | tf_op jit(solution)/shard_map/ppermute | solution.py:191
  40.4 0.8 add.7.both_ref
  41.3 1.5 %collective-permute-start.2 = (f32[128,128]{1,0:T(8,128)S(1)}, f32[128,128]{1,0:T(8,128)S(1)}, u32[]{:S(2)}, u32[]{:S(2)}) collective-permute-start(f32[128,128]{1,0:T(8,128)S(1)} %add.7.both_ref), channel_id=1, source_target_pairs={{0,8},{4,12},{8,0},{12,4},{1,9},{5,13},{9,1},{13,5},{2,10},{6,14},... | collective-permute-start | bytes 196616 | tf_op jit(solution)/shard_map/ppermute | solution.py:195
  42.8 1.5 %collective-permute-start.8 = (bf16[12,128,128]{2,1,0:T(8,128)(2,1)}, bf16[12,128,128]{2,1,0:T(8,128)(2,1)S(1)}, u32[]{:S(2)}, u32[]{:S(2)}) collective-permute-start(bf16[12,128,128]{2,1,0:T(8,128)(2,1)} %collective-permute-done.7.rest_0_), channel_id=1, source_target_pairs={{0,16},{16,0},{1,17},{17,1},{2,18},{18,2},{3,19},{19,3},{4,20},{20... | collective-permute-start | bytes 1179656 | tf_op jit(solution)/shard_map/ppermute | solution.py:205
  44.4 4.4 %shard_map.97 = (f32[65,256,128]{2,1,0:T(8,128)S(1)}, bf16[26,256,128]{2,1,0:T(8,128)(2,1)S(1)}) custom-call(s32[64]{0:T(128)S(1)} %bitcast.24, bf16[128,3328]{1,0:T(8,128)(2,1)S(1)} %copy-done, bf16[128,3328]{1,0:T(8,128)(2,1)} %collective-permute-done.3.mate_acts_ref.mate_ref, bf16[64,128,128]{2,1,0:T(8,128)(2,1)S(1)} %bitcast.17), custom_call_target="tpu_custom_call" | custom-call | flops 536870912 | bytes 1048576 | tf_op jit(solution)/shard_map/pallas_call | solution.py:167
  48.7 9.7 %collective-permute-done.5.rest_1_ = bf16[12,128,128]{2,1,0:T(8,128)(2,1)} collective-permute-done((bf16[12,128,128]{2,1,0:T(8,128)(2,1)}, bf16[12,128,128]{2,1,0:T(8,128)(2,1)}, u32[]{:S(2)}, u32[]{:S(2)}) %collective-permute-start.5) | collective-permute-done | bytes 393248 | tf_op jit(solution)/shard_map/ppermute | solution.py:202
  58.5 1.5 %collective-permute-start.9 = (bf16[12,128,128]{2,1,0:T(8,128)(2,1)}, bf16[12,128,128]{2,1,0:T(8,128)(2,1)S(1)}, u32[]{:S(2)}, u32[]{:S(2)}) collective-permute-start(bf16[12,128,128]{2,1,0:T(8,128)(2,1)} %collective-permute-done.5.rest_1_), channel_id=1, source_target_pairs={{0,16},{16,0},{1,17},{17,1},{2,18},{18,2},{3,19},{19,3},{4,20},{20... | collective-permute-start | bytes 1179656 | tf_op jit(solution)/shard_map/ppermute | solution.py:205
  60.1 0.8 shard_map.95
  60.9 1.5 %collective-permute-done.6.rest_2_ = bf16[8,128,128]{2,1,0:T(8,128)(2,1)} collective-permute-done((bf16[8,128,128]{2,1,0:T(8,128)(2,1)}, bf16[8,128,128]{2,1,0:T(8,128)(2,1)}, u32[]{:S(2)}, u32[]{:S(2)}) %collective-permute-start.6) | collective-permute-done | bytes 262176 | tf_op jit(solution)/shard_map/ppermute | solution.py:202
  62.4 1.5 %collective-permute-start.10 = (bf16[8,128,128]{2,1,0:T(8,128)(2,1)}, bf16[8,128,128]{2,1,0:T(8,128)(2,1)S(1)}, u32[]{:S(2)}, u32[]{:S(2)}) collective-permute-start(bf16[8,128,128]{2,1,0:T(8,128)(2,1)} %collective-permute-done.6.rest_2_), channel_id=1, source_target_pairs={{0,16},{16,0},{1,17},{17,1},{2,18},{18,2},{3,19},{19,3},{4,20},{20... | collective-permute-start | bytes 786440 | tf_op jit(solution)/shard_map/ppermute | solution.py:205
  63.9 4.2 %collective-permute-done.4.mate_pack_ref = bf16[64,2176]{1,0:T(8,128)(2,1)S(1)} collective-permute-done((bf16[64,2176]{1,0:T(8,128)(2,1)S(1)}, bf16[64,2176]{1,0:T(8,128)(2,1)S(1)}, u32[]{:S(2)}, u32[]{:S(2)}) %collective-permute-start.4) | collective-permute-done | bytes 278560 | tf_op jit(solution)/shard_map/ppermute | solution.py:198
  68.1 1.6 %shard_map.96.own_ref = bf16[64,5376]{1,0:T(8,128)(2,1)S(1)} custom-call(bf16[128,128]{1,0:T(8,128)(2,1)S(1)} %get-tuple-element.22.rounded_ref, bf16[128,3328]{1,0:T(8,128)(2,1)S(1)} %copy-done, bf16[128,3328]{1,0:T(8,128)(2,1)} %collective-permute-done.3.mate_acts_ref.mate_ref, bf16[64,2176]{1,0:T(8,128)(2,1)S(1)} %get-tuple-element.23.pack_ref, ...), custom_call_target="tpu_custom_call" | custom-call | flops 109051904 | bytes 1048576 | tf_op jit(solution)/shard_map/pallas_call | solution.py:167
  69.8 4.4 %shard_map.98.old_ref = f32[65,256,128]{2,1,0:T(8,128)S(1)} custom-call(s32[4]{0:T(128)S(1)} %pad_add_fusion.where_ref, s32[64]{0:T(128)S(1)} %collective-permute-done.ids_ref, bf16[26,256,128]{2,1,0:T(8,128)(2,1)S(1)} %get-tuple-element.29.tiles_ref, f32[65,256,128]{2,1,0:T(8,128)S(1)} %get-tuple-element.30.old_ref, ...), custom_call_target="tpu_custom_call", output_to_operand_aliasing={{}: (3, {})} | custom-call | flops 469762048 | bytes 1048576 | tf_op jit(solution)/shard_map/pallas_call | solution.py:167
  74.2 1.2 shard_map.99
  76.0 2.1 %collective-permute-done.12.core_ref = bf16[2,16,128,128]{3,2,1,0:T(8,128)(2,1)S(1)} collective-permute-done((bf16[2,16,128,128]{3,2,1,0:T(8,128)(2,1)S(1)}, bf16[2,16,128,128]{3,2,1,0:T(8,128)(2,1)S(1)}, u32[]{:S(2)}, u32[]{:S(2)}) %collective-permute-start.12) | collective-permute-done | bytes 1048608 | tf_op jit(solution)/shard_map/ppermute | solution.py:191
  78.8 1.6 %collective-permute-start.13 = (bf16[16,128,128]{2,1,0:T(8,128)(2,1)S(1)}, bf16[16,128,128]{2,1,0:T(8,128)(2,1)S(1)}, u32[]{:S(2)}, u32[]{:S(2)}) collective-permute-start(bf16[16,128,128]{2,1,0:T(8,128)(2,1)S(1)} %bitcast.19), channel_id=1, source_target_pairs={{0,8},{4,12},{8,0},{12,4},{1,9},{5,13},{9,1},{13,5},{2,10},{6,14},... | collective-permute-start | bytes 1572872 | tf_op jit(solution)/shard_map/ppermute | solution.py:195
  81.5 11.3 %collective-permute-done.13.rest_0_ = bf16[16,128,128]{2,1,0:T(8,128)(2,1)S(1)} collective-permute-done((bf16[16,128,128]{2,1,0:T(8,128)(2,1)S(1)}, bf16[16,128,128]{2,1,0:T(8,128)(2,1)S(1)}, u32[]{:S(2)}, u32[]{:S(2)}) %collective-permute-start.13) | collective-permute-done | bytes 524320 | tf_op jit(solution)/shard_map/ppermute | solution.py:195
  92.8 0.7 shard_map.102
  93.5 1.6 %collective-permute-start.14 = (bf16[16,128,128]{2,1,0:T(8,128)(2,1)S(1)}, bf16[16,128,128]{2,1,0:T(8,128)(2,1)S(1)}, u32[]{:S(2)}, u32[]{:S(2)}) collective-permute-start(bf16[16,128,128]{2,1,0:T(8,128)(2,1)S(1)} %bitcast.18), channel_id=1, source_target_pairs={{0,8},{4,12},{8,0},{12,4},{1,9},{5,13},{9,1},{13,5},{2,10},{6,14},... | collective-permute-start | bytes 1572872 | tf_op jit(solution)/shard_map/ppermute | solution.py:195
  95.1 18.0 %collective-permute-done.16.rest_0_ = bf16[64,5376]{1,0:T(8,128)(2,1)S(1)} collective-permute-done((bf16[64,5376]{1,0:T(8,128)(2,1)S(1)}, bf16[64,5376]{1,0:T(8,128)(2,1)S(1)}, u32[]{:S(2)}, u32[]{:S(2)}) %collective-permute-start.16) | collective-permute-done | bytes 688160 | tf_op jit(solution)/shard_map/ppermute | solution.py:202
  113.1 1.7 %shard_map.104 = (f32[64,3328]{1,0:T(8,128)}, f32[64,2048]{1,0:T(8,128)}) custom-call(s32[4]{0:T(128)S(1)} %pad_add_fusion.where_ref, bf16[64,5376]{1,0:T(8,128)(2,1)S(1)} %shard_map.96.own_ref, bf16[64,5376]{1,0:T(8,128)(2,1)S(1)} %collective-permute-done.16.rest_0_), custom_call_target="tpu_custom_call" | custom-call | bytes 1048576 | tf_op jit(solution)/shard_map/pallas_call | solution.py:167
  114.8 7.8 %collective-permute-done.15.rest_1_ = bf16[16,128,128]{2,1,0:T(8,128)(2,1)S(1)} collective-permute-done((bf16[16,128,128]{2,1,0:T(8,128)(2,1)S(1)}, bf16[16,128,128]{2,1,0:T(8,128)(2,1)S(1)}, u32[]{:S(2)}, u32[]{:S(2)}) %collective-permute-start.15) | collective-permute-done | bytes 524320 | tf_op jit(solution)/shard_map/ppermute | solution.py:198
  122.6 1.8 %shard_map.103 = bf16[128,2048]{1,0:T(8,128)(2,1)} custom-call(s32[4]{0:T(128)S(1)} %pad_add_fusion.where_ref, bf16[128,128]{1,0:T(8,128)(2,1)S(1)} %get-tuple-element.22.rounded_ref, bf16[64,2048]{1,0:T(8,128)(2,1)S(1)} %copy-done.4, f32[65,256,128]{2,1,0:T(8,128)S(1)} %get-tuple-element.32.total_ref, ...), custom_call_target="tpu_custom_call" | custom-call | flops 33554432 | bytes 1048576 | tf_op jit(solution)/shard_map/pallas_call | solution.py:167
  (35 shorter events, 3.7 us)
Async XLA Ops:
  0.6 35.1 %copy-start = (bf16[128,3328]{1,0:T(8,128)(2,1)S(1)}, bf16[128,3328]{1,0:T(8,128)(2,1)}, u32[]{:S(2)}) copy-start(bf16[128,3328]{1,0:T(8,128)(2,1)} %own_ref.1) | copy-start | bytes 2555908
  0.6 35.1 %copy-start.2 = (bf16[128,2048]{1,0:T(8,128)(2,1)S(1)}, bf16[128,2048]{1,0:T(8,128)(2,1)}, u32[]{:S(2)}) copy-start(bf16[128,2048]{1,0:T(8,128)(2,1)} %cot_ref.3) | copy-start | bytes 1572868
  0.6 43.7 %collective-permute-start.3 = (bf16[128,3328]{1,0:T(8,128)(2,1)}, bf16[128,3328]{1,0:T(8,128)(2,1)}, u32[]{:S(2)}, u32[]{:S(2)}) collective-permute-start(bf16[128,3328]{1,0:T(8,128)(2,1)} %own_ref.1), channel_id=1, source_target_pairs={{0,1},{1,0},{2,3},{3,2},{4,5},{5,4},{6,7},{7,6},{8,9},{9,8},{10,11... | collective-permute-start | bytes 2555912 | tf_op jit(solution)/shard_map/ppermute | solution.py:198
  3.7 40.6 %copy-start.1 = (bf16[1,64,128,128]{3,2,1,0:T(8,128)(2,1)S(1)}, bf16[1,64,128,128]{3,2,1,0:T(8,128)(2,1)}, u32[]{:S(2)}) copy-start(bf16[1,64,128,128]{3,2,1,0:T(8,128)(2,1)} %param.10) | copy-start | bytes 6291460
  6.0 36.9 %collective-permute-start.7 = (bf16[12,128,128]{2,1,0:T(8,128)(2,1)}, bf16[12,128,128]{2,1,0:T(8,128)(2,1)}, u32[]{:S(2)}, u32[]{:S(2)}) collective-permute-start(bf16[12,128,128]{2,1,0:T(8,128)(2,1)} %get-tuple-element.40), channel_id=1, source_target_pairs={{0,2},{1,3},{2,0},{3,1},{4,6},{5,7},{6,4},{7,5},{8,10},{9,11},{10,... | collective-permute-start | bytes 1179656 | tf_op jit(solution)/shard_map/ppermute | solution.py:202
  8.5 22.1 %collective-permute-start = (s32[64]{0:T(128)}, s32[64]{0:T(128)S(1)}, u32[]{:S(2)}, u32[]{:S(2)}) collective-permute-start(s32[64]{0:T(128)} %bitcast.23), channel_id=1, source_target_pairs={{0,2},{1,3},{2,0},{3,1},{4,6},{5,7},{6,4},{7,5},{8,10},{9,11},{10,... | collective-permute-start | bytes 776 | tf_op jit(solution)/shard_map/ppermute | solution.py:202
  30.7 27.8 %collective-permute-start.5 = (bf16[12,128,128]{2,1,0:T(8,128)(2,1)}, bf16[12,128,128]{2,1,0:T(8,128)(2,1)}, u32[]{:S(2)}, u32[]{:S(2)}) collective-permute-start(bf16[12,128,128]{2,1,0:T(8,128)(2,1)} %get-tuple-element.24), channel_id=1, source_target_pairs={{0,2},{1,3},{2,0},{3,1},{4,6},{5,7},{6,4},{7,5},{8,10},{9,11},{10,... | collective-permute-start | bytes 1179656 | tf_op jit(solution)/shard_map/ppermute | solution.py:202
  35.7 1.0 copy-start.3
  36.7 1.0 copy-start.5
  37.7 0.7 copy-start.6
  38.4 6.0 %copy-start.8 = (s32[1,64]{1,0:T(1,128)S(1)}, s32[1,64]{1,0:T(1,128)}, u32[]{:S(2)}) copy-start(s32[1,64]{1,0:T(1,128)} %param.11) | copy-start | bytes 772
  39.0 21.1 %copy-start.7 = (s32[128]{0:T(128)S(1)}, s32[128]{0:T(128)}, u32[]{:S(2)}) copy-start(s32[128]{0:T(128)} %param.9) | copy-start | bytes 1540
  39.0 1.5 %collective-permute-start.1 = (f32[128,128]{1,0:T(8,128)S(1)}, f32[128,128]{1,0:T(8,128)}, u32[]{:S(2)}, u32[]{:S(2)}) collective-permute-start(f32[128,128]{1,0:T(8,128)S(1)} %shard_map.94), channel_id=1, source_target_pairs={{0,4},{4,0},{8,12},{12,8},{1,5},{5,1},{9,13},{13,9},{2,6},{6,2},{1... | collective-permute-start | bytes 196616 | tf_op jit(solution)/shard_map/ppermute | solution.py:191
  39.1 23.3 %collective-permute-start.6 = (bf16[8,128,128]{2,1,0:T(8,128)(2,1)}, bf16[8,128,128]{2,1,0:T(8,128)(2,1)}, u32[]{:S(2)}, u32[]{:S(2)}) collective-permute-start(bf16[8,128,128]{2,1,0:T(8,128)(2,1)} %dynamic-slice_bitcast_fusion.2), channel_id=1, source_target_pairs={{0,2},{1,3},{2,0},{3,1},{4,6},{5,7},{6,4},{7,5},{8,10},{9,11},{10,... | collective-permute-start | bytes 786440 | tf_op jit(solution)/shard_map/ppermute | solution.py:202
  41.3 18.8 %collective-permute-start.2 = (f32[128,128]{1,0:T(8,128)S(1)}, f32[128,128]{1,0:T(8,128)S(1)}, u32[]{:S(2)}, u32[]{:S(2)}) collective-permute-start(f32[128,128]{1,0:T(8,128)S(1)} %add.7.both_ref), channel_id=1, source_target_pairs={{0,8},{4,12},{8,0},{12,4},{1,9},{5,13},{9,1},{13,5},{2,10},{6,14},... | collective-permute-start | bytes 196616 | tf_op jit(solution)/shard_map/ppermute | solution.py:195
  42.8 26.9 %collective-permute-start.8 = (bf16[12,128,128]{2,1,0:T(8,128)(2,1)}, bf16[12,128,128]{2,1,0:T(8,128)(2,1)S(1)}, u32[]{:S(2)}, u32[]{:S(2)}) collective-permute-start(bf16[12,128,128]{2,1,0:T(8,128)(2,1)} %collective-permute-done.7.rest_0_), channel_id=1, source_target_pairs={{0,16},{16,0},{1,17},{17,1},{2,18},{18,2},{3,19},{19,3},{4,20},{20... | collective-permute-start | bytes 1179656 | tf_op jit(solution)/shard_map/ppermute | solution.py:205
  58.5 11.3 %collective-permute-start.9 = (bf16[12,128,128]{2,1,0:T(8,128)(2,1)}, bf16[12,128,128]{2,1,0:T(8,128)(2,1)S(1)}, u32[]{:S(2)}, u32[]{:S(2)}) collective-permute-start(bf16[12,128,128]{2,1,0:T(8,128)(2,1)} %collective-permute-done.5.rest_1_), channel_id=1, source_target_pairs={{0,16},{16,0},{1,17},{17,1},{2,18},{18,2},{3,19},{19,3},{4,20},{20... | collective-permute-start | bytes 1179656 | tf_op jit(solution)/shard_map/ppermute | solution.py:205
  60.8 7.3 %collective-permute-start.4 = (bf16[64,2176]{1,0:T(8,128)(2,1)S(1)}, bf16[64,2176]{1,0:T(8,128)(2,1)S(1)}, u32[]{:S(2)}, u32[]{:S(2)}) collective-permute-start(bf16[64,2176]{1,0:T(8,128)(2,1)S(1)} %get-tuple-element.23.pack_ref), channel_id=1, source_target_pairs={{0,1},{1,0},{2,3},{3,2},{4,5},{5,4},{6,7},{7,6},{8,9},{9,8},{10,11... | collective-permute-start | bytes 835592 | tf_op jit(solution)/shard_map/ppermute | solution.py:198
  62.4 11.8 %collective-permute-start.10 = (bf16[8,128,128]{2,1,0:T(8,128)(2,1)}, bf16[8,128,128]{2,1,0:T(8,128)(2,1)S(1)}, u32[]{:S(2)}, u32[]{:S(2)}) collective-permute-start(bf16[8,128,128]{2,1,0:T(8,128)(2,1)} %collective-permute-done.6.rest_2_), channel_id=1, source_target_pairs={{0,16},{16,0},{1,17},{17,1},{2,18},{18,2},{3,19},{19,3},{4,20},{20... | collective-permute-start | bytes 786440 | tf_op jit(solution)/shard_map/ppermute | solution.py:205
  75.4 2.7 %collective-permute-start.12 = (bf16[2,16,128,128]{3,2,1,0:T(8,128)(2,1)S(1)}, bf16[2,16,128,128]{3,2,1,0:T(8,128)(2,1)S(1)}, u32[]{:S(2)}, u32[]{:S(2)}) collective-permute-start(bf16[2,16,128,128]{3,2,1,0:T(8,128)(2,1)S(1)} %get-tuple-element.34), channel_id=1, source_target_pairs={{0,4},{4,0},{8,12},{12,8},{1,5},{5,1},{9,13},{13,9},{2,6},{6,2},{1... | collective-permute-start | bytes 3145736 | tf_op jit(solution)/shard_map/ppermute | solution.py:191
  75.5 5.4 %collective-permute-start.11 = (bf16[2,16,128,128]{3,2,1,0:T(8,128)(2,1)S(1)}, bf16[2,16,128,128]{3,2,1,0:T(8,128)(2,1)S(1)}, u32[]{:S(2)}, u32[]{:S(2)}) collective-permute-start(bf16[2,16,128,128]{3,2,1,0:T(8,128)(2,1)S(1)} %get-tuple-element.33), channel_id=1, source_target_pairs={{0,4},{4,0},{8,12},{12,8},{1,5},{5,1},{9,13},{13,9},{2,6},{6,2},{1... | collective-permute-start | bytes 3145736 | tf_op jit(solution)/shard_map/ppermute | solution.py:191
  78.8 14.0 %collective-permute-start.13 = (bf16[16,128,128]{2,1,0:T(8,128)(2,1)S(1)}, bf16[16,128,128]{2,1,0:T(8,128)(2,1)S(1)}, u32[]{:S(2)}, u32[]{:S(2)}) collective-permute-start(bf16[16,128,128]{2,1,0:T(8,128)(2,1)S(1)} %bitcast.19), channel_id=1, source_target_pairs={{0,8},{4,12},{8,0},{12,4},{1,9},{5,13},{9,1},{13,5},{2,10},{6,14},... | collective-permute-start | bytes 1572872 | tf_op jit(solution)/shard_map/ppermute | solution.py:195
  80.3 32.8 %collective-permute-start.16 = (bf16[64,5376]{1,0:T(8,128)(2,1)S(1)}, bf16[64,5376]{1,0:T(8,128)(2,1)S(1)}, u32[]{:S(2)}, u32[]{:S(2)}) collective-permute-start(bf16[64,5376]{1,0:T(8,128)(2,1)S(1)} %shard_map.96.own_ref), channel_id=1, source_target_pairs={{0,2},{1,3},{2,0},{3,1},{4,6},{5,7},{6,4},{7,5},{8,10},{9,11},{10,... | collective-permute-start | bytes 2064392 | tf_op jit(solution)/shard_map/ppermute | solution.py:202
  81.5 41.1 %copy-start.4 = (bf16[64,2048]{1,0:T(8,128)(2,1)S(1)}, bf16[64,2048]{1,0:T(8,128)(2,1)}, u32[]{:S(2)}) copy-start(bf16[64,2048]{1,0:T(8,128)(2,1)} %adapter_ref.3) | copy-start | bytes 786436
  93.5 21.3 %collective-permute-start.14 = (bf16[16,128,128]{2,1,0:T(8,128)(2,1)S(1)}, bf16[16,128,128]{2,1,0:T(8,128)(2,1)S(1)}, u32[]{:S(2)}, u32[]{:S(2)}) collective-permute-start(bf16[16,128,128]{2,1,0:T(8,128)(2,1)S(1)} %bitcast.18), channel_id=1, source_target_pairs={{0,8},{4,12},{8,0},{12,4},{1,9},{5,13},{9,1},{13,5},{2,10},{6,14},... | collective-permute-start | bytes 1572872 | tf_op jit(solution)/shard_map/ppermute | solution.py:195
  95.1 27.5 %collective-permute-start.15 = (bf16[16,128,128]{2,1,0:T(8,128)(2,1)S(1)}, bf16[16,128,128]{2,1,0:T(8,128)(2,1)S(1)}, u32[]{:S(2)}, u32[]{:S(2)}) collective-permute-start(bf16[16,128,128]{2,1,0:T(8,128)(2,1)S(1)} %shard_map.102), channel_id=1, source_target_pairs={{0,1},{1,0},{2,3},{3,2},{4,5},{5,4},{6,7},{7,6},{8,9},{9,8},{10,11... | collective-permute-start | bytes 1572872 | tf_op jit(solution)/shard_map/ppermute | solution.py:198

commit v4 on v3

--- a/solution.py
+++ b/solution.py
@@ -31,21 +31,23 @@
     lax.fori_loop(0, count // unroll, one, 0)
 
 
-def first_kernel(ids_ref, own_ref, mate_ref, blocks_ref, total_ref, tiles_ref, *, col_blocks):
+def add_arrivals(where_ref, ids_ref, tiles_ref, blocks, total_ref, places, parts, held, col_blocks):
+    for blocks_ref, (offset, shift, start) in zip(blocks, places):
+        source = lax.rem(where_ref[0] + (parts - shift), parts)
+        base = offset + source * held + start
+        add_blocks(total_ref, tiles_ref, blocks_ref, ids_ref, base, col_blocks, 2)
+
+
+def first_kernel(where_ref, own_ids_ref, ids_ref, own_ref, mate_ref, own_blocks_ref, *rest, **plan):
+    blocks, (total_ref, tiles_ref) = rest[:-2], rest[-2:]
     row_blocks, _, tile = tiles_ref.shape
     tokens = own_ref.shape[0]
     total_ref[...] = jnp.zeros_like(total_ref)
     for i in range(row_blocks):
         tiles_ref[i, :tokens, :] = own_ref[:, i * tile:(i + 1) * tile]
         tiles_ref[i, tokens:, :] = mate_ref[:, i * tile:(i + 1) * tile]
-    add_blocks(total_ref, tiles_ref, blocks_ref, ids_ref, 0, col_blocks, 8)
-
-
-def add_arrivals(where_ref, ids_ref, tiles_ref, blocks, total_ref, places, parts, held, col_blocks):
-    for blocks_ref, (offset, shift, start) in zip(blocks, places):
-        source = lax.rem(where_ref[0] + (parts - shift), parts)
-        base = offset + source * held + start
-        add_blocks(total_ref, tiles_ref, blocks_ref, ids_ref, base, col_blocks, 4)
+    add_blocks(total_ref, tiles_ref, own_blocks_ref, own_ids_ref, 0, plan["col_blocks"], 8)
+    add_arrivals(where_ref, ids_ref, tiles_ref, blocks, total_ref, **plan)
 
 
 def more_kernel(where_ref, ids_ref, tiles_ref, old_ref, *rest, **plan):
@@ -125,24 +127,31 @@
     pack_ref[:, feats:] = rounded[rank:]
 
 
-def pair_grad_kernel(rounded_ref, acts_ref, mate_acts_ref, pack_ref, mate_pack_ref, out_ref):
+def pair_grad_kernel(where_ref, rounded_ref, acts_ref, mate_acts_ref, pack_ref, mate_pack_ref, half_ref):
     rank, shard_rows = rounded_ref.shape[0] // 2, acts_ref.shape[1]
     feats = pack_ref.shape[1] - rounded_ref.shape[1]
-    own = jnp.dot(rounded_ref[rank:, :], acts_ref[...], preferred_element_type=F32)
-    mate = jnp.dot(mate_pack_ref[:, feats:], mate_acts_ref[...], preferred_element_type=F32)
-    out_ref[:, :shard_rows] = (adapter_scale * (own + mate)).astype(BF16)
-    out_ref[:, shard_rows:] = (
-        pack_ref[:, :feats].astype(F32) + mate_pack_ref[:, :feats].astype(F32)
-    ).astype(BF16)
-
-
-def grad_sum_kernel(where_ref, own_ref, *rest):
-    received, (in_ref, out_ref) = rest[:-2], rest[-2:]
-    shard_rows = in_ref.shape[1]
-    own, place = own_ref[...].astype(F32), where_ref[3]
-    total = ordered_sum(own, [ref[...].astype(F32) for ref in received], place)
-    in_ref[...] = total[:, :shard_rows]
-    out_ref[...] = total[:, shard_rows:]
+    in_half, out_half = shard_rows // 2, feats // 2
+    back, mate_back = rounded_ref[rank:, :], mate_pack_ref[:, feats:]
+    for bit in range(2):
+        @pl.when(where_ref[3] == bit)
+        def _():
+            cols = slice(bit * in_half, (bit + 1) * in_half)
+            grad = jnp.dot(back, acts_ref[:, cols], preferred_element_type=F32)
+            grad += jnp.dot(mate_back, mate_acts_ref[:, cols], preferred_element_type=F32)
+            half_ref[:, :in_half] = (adapter_scale * grad).astype(BF16)
+            cols = slice(bit * out_half, (bit + 1) * out_half)
+            grad = pack_ref[:, cols].astype(F32) + mate_pack_ref[:, cols].astype(F32)
+            half_ref[:, in_half:] = grad.astype(BF16)
+
+
+def grad_sum_kernel(halves_ref, in_ref, out_ref):
+    in_half, out_half = in_ref.shape[1] // 2, out_ref.shape[1] // 2
+    for bit in range(2):
+        total = halves_ref[bit].astype(F32)
+        for member in range(2 + bit, halves_ref.shape[0], 2):
+            total += halves_ref[member].astype(F32)
+        in_ref[:, bit * in_half:(bit + 1) * in_half] = total[:, :in_half]
+        out_ref[:, bit * out_half:(bit + 1) * out_half] = total[:, in_half:]
 
 
 def final_kernel(where_ref, rounded_ref, adapter_ref, total_ref, core_ref, *rest):
@@ -161,7 +170,7 @@
         out_ref[:, cols] = (value + adapter_scale * extra).astype(BF16)
 
 
-def call(kernel, outs, scalars, arrays, flops, aliases=None):
+def call(kernel, outs, scalars, arrays, aliases=None):
     smem = pl.BlockSpec(memory_space=pltpu.SMEM)
     vmem = pl.BlockSpec(memory_space=pltpu.VMEM)
     return pl.pallas_call(
@@ -170,7 +179,7 @@
         in_specs=[smem] * len(scalars) + [vmem] * len(arrays),
         out_specs=tuple(vmem for _ in outs),
         input_output_aliases=aliases or {},
-        cost_estimate=pl.CostEstimate(flops=flops, transcendentals=0, bytes_accessed=1 << 20),
+        cost_estimate=pl.CostEstimate(flops=0, transcendentals=0, bytes_accessed=0),
         compiler_params=pltpu.CompilerParams(vmem_limit_bytes=4 * 1024 * 1024),
     )(*scalars, *arrays)
 
@@ -216,91 +225,88 @@
         row_index = lax.axis_index("row")
         dp_index = lax.axis_index("dp")
         where = jnp.stack(
-            [part, lax.rem(row_index, 2), lax.div(row_index, 2), lax.div(dp_index, 2)]
+            [part, lax.rem(row_index, 2), lax.div(row_index, 2), lax.rem(dp_index, 2)]
         ).astype(jnp.int32)
         blocks = kept_blocks[0]
         ids = block_ids[0]
         labels = forget_labels[None, :]
 
+        soon = core_swap(ids)
         far_ids = [group_shift(ids, d) for d in range(1, group)]
         all_ids = far_ids[0] if group == 2 else jnp.concatenate(far_ids)
         held = slots // n_parts
-        sizes = [held * k // 32 for k in (12, 12, 8)]
+        sizes = [held * k // 32 for k in (14, 10, 8)]
         starts = [sum(sizes[:k]) for k in range(len(sizes))]
-        own_share = lax.dynamic_slice_in_dim(blocks, part * held, held, axis=0)
-        shares = [own_share[start:start + size] for start, size in zip(starts, sizes)]
-        direct = []
-        for d in range(1, group):
-            for leaving, start in zip(shares, starts):
-                if start > 0:
-                    leaving = after(leaving, all_ids)
-                direct.append((group_shift(leaving, d), ((d - 1) * slots, 0, start)))
-        mate_activations = mate_swap(activations)
-
-        adapter_early = after(adapter_a, all_ids, *shares)
+
+        def leaving_chunk(k):
+            chunk = lax.dynamic_slice_in_dim(blocks, part * held + starts[k], sizes[k], axis=0)
+            return chunk if k == 0 else after(chunk, soon)
+
+        direct = [
+            (group_shift(leaving_chunk(k), d), ((d - 1) * slots, 0, starts[k]))
+            for d in range(1, group) for k in range(len(starts))
+        ]
+        mate_activations = mate_swap(after(activations, soon))
+
         (both,) = call(
             low_rank_kernel, (jax.ShapeDtypeStruct((2 * rank, tokens), F32),), (),
-            (activations, adapter_early.T, cotangent, output_adapter, labels), 4 * tokens * rank * shard_rows,
+            (activations, after(adapter_a, direct[0][0]).T, cotangent, output_adapter, labels),
         )
         both = both + core_swap(both)
+        both_later = after(both, direct[1][0])
+        swapped = [
+            (part_shift(value, e), (offset, e, start))
+            for value, (offset, _, start) in direct for e in range(1, n_parts)
+        ]
+
+        def plan(items):
+            return dict(places=[item[1] for item in items], parts=n_parts, held=held, col_blocks=col_blocks)
+
+        def values(items):
+            return tuple(item[0] for item in items)
+
+        chunks, copies = len(direct), n_parts - 1
+        first = []
+        more = direct + swapped[:copies * (chunks - 1)]
+        last = swapped[copies * (chunks - 1):]
+        total_shape = pltpu.VMEM((col_blocks + 1, 2 * tokens, tile), F32)
+        total, tiles = call(
+            functools.partial(first_kernel, **plan(first)),
+            (total_shape, pltpu.VMEM((row_blocks, 2 * tokens, tile), BF16)),
+            (where, ids, ids), (activations, mate_activations, blocks) + values(first),
+        )
+
         rounded, pack = call(
             own_grad_kernel,
             (
                 jax.ShapeDtypeStruct((2 * rank, tokens), BF16),
                 jax.ShapeDtypeStruct((rank, feats + tokens), BF16),
             ),
-            (where,), (cotangent, labels, both) + tuple(chip_shift(both, d) for d in range(1, chips)),
-            2 * tokens * rank * feats,
+            (after(where, total),), (cotangent, labels, both) + tuple(chip_shift(both_later, d) for d in range(1, chips)),
         )
         mate_pack = mate_swap(pack)
 
-        both_tokens = 2 * tokens
-        per_block = 2 * both_tokens * tile * tile
-        total_shape = pltpu.VMEM((col_blocks + 1, both_tokens, tile), F32)
-        total, tiles = call(
-            functools.partial(first_kernel, col_blocks=col_blocks),
-            (total_shape, pltpu.VMEM((row_blocks, both_tokens, tile), BF16)),
-            (ids,), (activations, mate_activations, blocks), slots * per_block,
-        )
-        swapped = []
-        for k, (value, (offset, _, start)) in enumerate(direct):
-            if k == len(direct) - 2:
-                value = after(value, total)
-            for e in range(1, n_parts):
-                swapped.append((part_shift(value, e), (offset, e, start)))
-
-        (grads,) = call(
-            pair_grad_kernel, (jax.ShapeDtypeStruct((rank, shard_rows + feats), BF16),), (),
-            (rounded, activations, mate_activations, pack, after(mate_pack, direct[-2][0])),
-            4 * tokens * rank * shard_rows,
-        )
-        grads = after(grads, direct[-1][0])
-        far_grads = [group_shift(grads, d) for d in range(1, group)]
-
-        late = swapped[1 - n_parts:]
-        early = direct + swapped[:1 - n_parts]
-
-        def plan(items):
-            return dict(places=[item[1] for item in items], parts=n_parts, held=held, col_blocks=col_blocks)
-
-        def work(items):
-            return sum(item[0].shape[0] for item in items) * per_block
+        (half_grads,) = call(
+            pair_grad_kernel, (jax.ShapeDtypeStruct((rank, (shard_rows + feats) // 2), BF16),),
+            (where,), (rounded, activations, mate_activations, pack, mate_pack),
+        )
+        half_grads = after(half_grads, direct[-1][0])
+        halves = lax.all_gather(half_grads, "dp")
 
         (total,) = call(
-            functools.partial(more_kernel, **plan(early)), (total_shape,), (where, all_ids),
-            (on_chip(tiles), on_chip(total)) + tuple(item[0] for item in early), work(early), {3: 0},
+            functools.partial(more_kernel, **plan(more)), (total_shape,), (where, all_ids),
+            (on_chip(tiles), on_chip(total)) + values(more), {3: 0},
         )
         send = pltpu.VMEM((chips, share, tokens, tile), BF16)
         total, send_mate, send_own = call(
-            functools.partial(last_kernel, **plan(late)), (total_shape, send, send),
-            (after(where, grads), all_ids),
-            (on_chip(tiles), on_chip(total)) + tuple(item[0] for item in late), work(late), {3: 0},
-        )
-
-        def for_chips(first, core_got, *needed):
+            functools.partial(last_kernel, **plan(last)), (total_shape, send, send),
+            (after(where, half_grads), all_ids), (on_chip(tiles), on_chip(total)) + values(last), {3: 0},
+        )
+
+        def for_chips(first, core_got, where, *needed):
             (leaving,) = call(
                 functools.partial(chip_kernel, first=first),
-                (pltpu.VMEM((chips - 1, share, tokens, tile), BF16),), (where,), (on_chip(total), core_got), 0,
+                (pltpu.VMEM((chips - 1, share, tokens, tile), BF16),), (where,), (on_chip(total), core_got),
             )
             if needed:
                 leaving = after(leaving, *needed)
@@ -308,23 +314,21 @@
 
         core_mate = core_swap(send_mate)
         core_own = core_swap(send_own)
-        mate_pieces = for_chips(tokens, core_mate)
+        mate_pieces = for_chips(tokens, core_mate, where)
         (mate_total,) = call(
             mate_kernel, (pltpu.VMEM((share, tokens, tile), BF16),), (where,),
-            (on_chip(total), core_mate) + tuple(mate_pieces), 0,
+            (on_chip(total), core_mate) + tuple(mate_pieces),
         )
         from_mate = mate_swap(mate_total)
-        own_pieces = for_chips(0, core_own, mate_total)
-        far_grads = [after(value, mate_total) for value in far_grads]
+        own_pieces = for_chips(0, core_own, where, mate_total)
         in_grad, out_grad = call(
             grad_sum_kernel,
             (jax.ShapeDtypeStruct((rank, shard_rows), F32), jax.ShapeDtypeStruct((rank, feats), F32)),
-            (where,), (grads,) + tuple(far_grads), 0,
+            (), (after(halves, mate_total),),
         )
         (projected,) = call(
             final_kernel, (jax.ShapeDtypeStruct((tokens, feats), BF16),), (where,),
             (rounded, output_adapter, on_chip(total), core_own) + tuple(own_pieces) + (from_mate,),
-            2 * tokens * rank * feats,
         )
         return projected, in_grad.T, out_grad
 

time: 125 us -> 150 us (1.20)
  local copies, waits for them, and re-layouts: 6.52 us -> 26.3 us
  between operations: 0.82 us -> 14.2 us
  waiting for transfers between devices: 77.8 us -> 66.5 us
  Pallas kernels: 18.4 us -> 21.2 us
  starting transfers between devices: 20 us -> 21.5 us
    unnamed x18 -> x32, local copies, waits for them, and re-layouts: 2.64 us -> 21.9 us
    ppermute x5 -> x4, waiting for transfers between devices: 51.1 us -> 34.3 us  [group_shift(): return lax.ppermute(value, 'dp', pairs)]
    all_gather x0 -> x1, waiting for transfers between devices: none -> 11.3 us  [body(): halves = lax.all_gather(half_grads, 'dp')]
    ppermute x3, waiting for transfers between devices: 12 us -> 4.96 us  [mate_swap(): return lax.ppermute(value, 'dp', [(i, i ^ 1) for i in range(n_dp)])]
    dynamic_slice x0 -> x3, local copies, waits for them, and re-layouts: none -> 4.45 us  [leaving_chunk(): lax.dynamic_slice_in_dim(blocks, part * held + starts[k], sizes[k], axis=0)]
    slice x2 -> x0, local copies, waits for them, and re-layouts: 3.88 us -> none  [body(): own_share[start:start + size]]
    pallas_call x11, Pallas kernels: 18.4 us -> 21.2 us  [call(): pl.pallas_call(kernel, out_shape=outs, in_specs=[smem] * len(scalars) + [...]
    ppermute x3, starting transfers between devices: 3.16 us -> 5.42 us  [mate_swap(): return lax.ppermute(value, 'dp', [(i, i ^ 1) for i in range(n_dp)])]
  transfers between devices with their start and end apart: 17 -> 18, of which waited for: 9 -> 8; matrix products, arithmetic and copies ran while one was open for 4% -> 3% of each run, Pallas kernels for 12% -> 11%
where the time goes in v4:
time: 150 us
  waiting for transfers between devices  66.5 us (44%)
  local copies, waits for them, and re-layouts  26.3 us (18%)
  starting transfers between devices  21.5 us (14%)
  Pallas kernels  21.2 us (14%)
  between operations  14.2 us (9%)
    ppermute x4, waiting for transfers between devices, group_shift(): return lax.ppermute(value, 'dp', pairs)  34.3 us
    unnamed x32, local copies, waits for them, and re-layouts  21.9 us
    pallas_call x11, Pallas kernels, call(): pl.pallas_call(kernel, out_shape=outs, in_specs=[smem] * len(scalars) + [...  21.2 us
    ppermute x3, waiting for transfers between devices, chip_shift(): return lax.ppermute(value, 'row', pairs)  12.7 us
    all_gather x1, waiting for transfers between devices, body(): halves = lax.all_gather(half_grads, 'dp')  11.3 us
    ppermute x4, starting transfers between devices, group_shift(): return lax.ppermute(value, 'dp', pairs)  8.54 us
    ppermute x3, starting transfers between devices, mate_swap(): return lax.ppermute(value, 'dp', [(i, i ^ 1) for i in range(n_dp)])  5.42 us
    ppermute x3, waiting for transfers between devices, mate_swap(): return lax.ppermute(value, 'dp', [(i, i ^ 1) for i in range(n_dp)])  4.96 us
  transfers between devices with their start and end apart: 18, of which 8 were waited for; matrix products, arithmetic and copies ran while one was open for 3% of the time, Pallas kernels for 11%

profile of v4, /device:TPU:0, one launch (start us, length us, event | category | flops | bytes accessed | tf_op | source)
XLA Modules:
  0.0 149.9 jit_solution(3162243785845156715)
XLA Ops:
  8.7 2.9 %collective-permute-start.1 = (bf16[128,3328]{1,0:T(8,128)(2,1)}, bf16[128,3328]{1,0:T(8,128)(2,1)S(1)}, u32[]{:S(2)}, u32[]{:S(2)}) collective-permute-start(bf16[128,3328]{1,0:T(8,128)(2,1)} %acts_ref.3), channel_id=1, source_target_pairs={{0,1},{1,0},{2,3},{3,2},{4,5},{5,4},{6,7},{7,6},{8,9},{9,8},{10,11... | collective-permute-start | bytes 2555912 | tf_op jit(solution)/shard_map/ppermute | solution.py:207
  11.6 1.1 dynamic-slice_bitcast_fusion
  12.7 2.7 %collective-permute-start.2 = (bf16[14,128,128]{2,1,0:T(8,128)(2,1)S(1)}, bf16[14,128,128]{2,1,0:T(8,128)(2,1)}, u32[]{:S(2)}, u32[]{:S(2)}) collective-permute-start(bf16[14,128,128]{2,1,0:T(8,128)(2,1)S(1)} %dynamic-slice_bitcast_fusion), channel_id=1, source_target_pairs={{0,2},{1,3},{2,0},{3,1},{4,6},{5,7},{6,4},{7,5},{8,10},{9,11},{10,... | collective-permute-start | bytes 1376264 | tf_op jit(solution)/shard_map/ppermute | solution.py:211
  15.3 1.7 %dynamic-slice_bitcast_fusion.1 = bf16[10,128,128]{2,1,0:T(8,128)(2,1)} fusion(bf16[1,64,128,128]{3,2,1,0:T(8,128)(2,1)} %param.10, s32[]{:T(128)S(6)} %select_n.10), kind=kLoop, calls=%fused_computation.1 | loop fusion | bytes 655364 | tf_op jit(solution)/shard_map/dynamic_slice | solution.py:242
  17.4 1.7 %dynamic-slice_bitcast_fusion.2 = bf16[8,128,128]{2,1,0:T(8,128)(2,1)} fusion(bf16[1,64,128,128]{3,2,1,0:T(8,128)(2,1)} %param.10, s32[]{:T(128)S(6)} %select_n.11), kind=kLoop, calls=%fused_computation.2 | loop fusion | bytes 524292 | tf_op jit(solution)/shard_map/dynamic_slice | solution.py:242
  19.1 2.6 %collective-permute-start.7 = (bf16[8,128,128]{2,1,0:T(8,128)(2,1)}, bf16[8,128,128]{2,1,0:T(8,128)(2,1)}, u32[]{:S(2)}, u32[]{:S(2)}) collective-permute-start(bf16[8,128,128]{2,1,0:T(8,128)(2,1)} %dynamic-slice_bitcast_fusion.2), channel_id=1, source_target_pairs={{0,2},{1,3},{2,0},{3,1},{4,6},{5,7},{6,4},{7,5},{8,10},{9,11},{10,... | collective-permute-start | bytes 786440 | tf_op jit(solution)/shard_map/ppermute | solution.py:211
  21.6 19.3 %collective-permute-done.2.rest_0_ = bf16[14,128,128]{2,1,0:T(8,128)(2,1)} collective-permute-done((bf16[14,128,128]{2,1,0:T(8,128)(2,1)S(1)}, bf16[14,128,128]{2,1,0:T(8,128)(2,1)}, u32[]{:S(2)}, u32[]{:S(2)}) %collective-permute-start.2) | collective-permute-done | bytes 458784 | tf_op jit(solution)/shard_map/ppermute | solution.py:211
  41.0 1.5 %collective-permute-start.9 = (bf16[14,128,128]{2,1,0:T(8,128)(2,1)}, bf16[14,128,128]{2,1,0:T(8,128)(2,1)}, u32[]{:S(2)}, u32[]{:S(2)}) collective-permute-start(bf16[14,128,128]{2,1,0:T(8,128)(2,1)} %collective-permute-done.2.rest_0_), channel_id=1, source_target_pairs={{0,16},{16,0},{1,17},{17,1},{2,18},{18,2},{3,19},{19,3},{4,20},{20... | collective-permute-start | bytes 1376264 | tf_op jit(solution)/shard_map/ppermute | solution.py:214
  43.2 13.4 %collective-permute-done.4.rest_1_ = bf16[10,128,128]{2,1,0:T(8,128)(2,1)} collective-permute-done((bf16[10,128,128]{2,1,0:T(8,128)(2,1)}, bf16[10,128,128]{2,1,0:T(8,128)(2,1)}, u32[]{:S(2)}, u32[]{:S(2)}) %collective-permute-start.4) | collective-permute-done | bytes 327712 | tf_op jit(solution)/shard_map/ppermute | solution.py:211
  56.6 1.5 %collective-permute-start.10 = (bf16[10,128,128]{2,1,0:T(8,128)(2,1)}, bf16[10,128,128]{2,1,0:T(8,128)(2,1)S(1)}, u32[]{:S(2)}, u32[]{:S(2)}) collective-permute-start(bf16[10,128,128]{2,1,0:T(8,128)(2,1)} %collective-permute-done.4.rest_1_), channel_id=1, source_target_pairs={{0,16},{16,0},{1,17},{17,1},{2,18},{18,2},{3,19},{19,3},{4,20},{20... | collective-permute-start | bytes 983048 | tf_op jit(solution)/shard_map/ppermute | solution.py:214
  58.2 1.6 %collective-permute-start.5 = (f32[128,128]{1,0:T(8,128)S(1)}, f32[128,128]{1,0:T(8,128)S(1)}, u32[]{:S(2)}, u32[]{:S(2)}) collective-permute-start(f32[128,128]{1,0:T(8,128)S(1)} %add.23.both_ref), channel_id=1, source_target_pairs={{0,8},{4,12},{8,0},{12,4},{1,9},{5,13},{9,1},{13,5},{2,10},{6,14},... | collective-permute-start | bytes 196616 | tf_op jit(solution)/shard_map/ppermute | solution.py:204
  59.8 1.6 %copy-done.6 = bf16[1,64,128,128]{3,2,1,0:T(8,128)(2,1)S(1)} copy-done((bf16[1,64,128,128]{3,2,1,0:T(8,128)(2,1)S(1)}, bf16[1,64,128,128]{3,2,1,0:T(8,128)(2,1)}, u32[]{:S(2)}) %copy-start.6) | copy-done | bytes 2097176
  61.4 3.8 %shard_map.94 = (f32[65,256,128]{2,1,0:T(8,128)S(1)}, bf16[26,256,128]{2,1,0:T(8,128)(2,1)S(1)}) custom-call(s32[4]{0:T(128)S(1)} %pad_add_fusion.where_ref, s32[64]{0:T(128)S(1)} %bitcast.26, s32[64]{0:T(128)S(1)} %bitcast.27, bf16[128,3328]{1,0:T(8,128)(2,1)S(1)} %copy-done.5, bf16[128,3328]{1,0:T(8,128)(2,1)S(1)} %collective-permute-done.1.mate_ref.mate_acts_ref, ...), custom_call_target="tpu_custom_call" | custom-call | tf_op jit(solution)/shard_map/pallas_call | solution.py:176
  65.2 1.0 copy-done.8
  67.7 3.0 %collective-permute-start.8 = (s32[64]{0:T(128)S(1)}, s32[64]{0:T(128)S(1)}, u32[]{:S(2)}, u32[]{:S(2)}) collective-permute-start(s32[64]{0:T(128)S(1)} %bitcast.28), channel_id=1, source_target_pairs={{0,2},{1,3},{2,0},{3,1},{4,6},{5,7},{6,4},{7,5},{8,10},{9,11},{10,... | collective-permute-start | bytes 776 | tf_op jit(solution)/shard_map/ppermute | solution.py:211
  70.6 1.5 %collective-permute-done.8.ids_ref = s32[64]{0:T(128)S(1)} collective-permute-done((s32[64]{0:T(128)S(1)}, s32[64]{0:T(128)S(1)}, u32[]{:S(2)}, u32[]{:S(2)}) %collective-permute-start.8) | collective-permute-done | bytes 288 | tf_op jit(solution)/shard_map/ppermute | solution.py:211
  72.2 6.5 %shard_map.98.old_ref = f32[65,256,128]{2,1,0:T(8,128)S(1)} custom-call(s32[4]{0:T(128)S(1)} %pad_add_fusion.where_ref, s32[64]{0:T(128)S(1)} %collective-permute-done.8.ids_ref, bf16[26,256,128]{2,1,0:T(8,128)(2,1)S(1)} %get-tuple-element.33.tiles_ref, f32[65,256,128]{2,1,0:T(8,128)S(1)} %get-tuple-element.23.old_ref, ...), custom_call_target="tpu_custom_call", output_to_operand_aliasing={{}: (3, {})} | custom-call | tf_op jit(solution)/shard_map/pallas_call | solution.py:176
  78.7 3.3 %copy-done = f32[65,256,128]{2,1,0:T(8,128)} copy-done((f32[65,256,128]{2,1,0:T(8,128)}, f32[65,256,128]{2,1,0:T(8,128)S(1)}, u32[]{:S(2)}) %copy-start) | copy-done | bytes 8519704
  82.0 1.6 %shard_map.97 = bf16[64,2688]{1,0:T(8,128)(2,1)} custom-call(s32[4]{0:T(128)S(1)} %pad_add_fusion.where_ref, bf16[128,128]{1,0:T(8,128)(2,1)S(1)} %get-tuple-element.28.rounded_ref, bf16[128,3328]{1,0:T(8,128)(2,1)S(1)} %copy-done.5, bf16[128,3328]{1,0:T(8,128)(2,1)S(1)} %collective-permute-done.1.mate_ref.mate_acts_ref, ...), custom_call_target="tpu_custom_call" | custom-call | tf_op jit(solution)/shard_map/pallas_call | solution.py:176
  83.6 3.4 %copy-done.1 = f32[65,256,128]{2,1,0:T(8,128)S(1)} copy-done((f32[65,256,128]{2,1,0:T(8,128)S(1)}, f32[65,256,128]{2,1,0:T(8,128)}, u32[]{:S(2)}) %copy-start.1) | copy-done | bytes 8519704
  87.0 2.9 %shard_map.99 = (f32[65,256,128]{2,1,0:T(8,128)S(1)}, bf16[2,16,128,128]{3,2,1,0:T(8,128)(2,1)}, bf16[2,16,128,128]{3,2,1,0:T(8,128)(2,1)S(1)}) custom-call(s32[4]{0:T(128)S(1)} %pad_add_fusion.where_ref, s32[64]{0:T(128)S(1)} %collective-permute-done.8.ids_ref, ...), custom_call_target="tpu_custom_call", output_to_operand_aliasing={{0}: (3, {})} | custom-call | tf_op jit(solution)/shard_map/pallas_call | solution.py:176
  89.9 3.3 %copy-done.2 = f32[65,256,128]{2,1,0:T(8,128)} copy-done((f32[65,256,128]{2,1,0:T(8,128)}, f32[65,256,128]{2,1,0:T(8,128)S(1)}, u32[]{:S(2)}) %copy-start.2) | copy-done | bytes 8519704
  94.8 2.3 %collective-permute-done.13.core_ref = bf16[2,16,128,128]{3,2,1,0:T(8,128)(2,1)S(1)} collective-permute-done((bf16[2,16,128,128]{3,2,1,0:T(8,128)(2,1)}, bf16[2,16,128,128]{3,2,1,0:T(8,128)(2,1)S(1)}, u32[]{:S(2)}, u32[]{:S(2)}) %collective-permute-start.13) | collective-permute-done | bytes 1048608 | tf_op jit(solution)/shard_map/ppermute | solution.py:200
  97.1 3.4 %copy-done.3 = f32[65,256,128]{2,1,0:T(8,128)S(1)} copy-done((f32[65,256,128]{2,1,0:T(8,128)S(1)}, f32[65,256,128]{2,1,0:T(8,128)}, u32[]{:S(2)}) %copy-start.3) | copy-done | bytes 8519704
  102.5 12.7 %collective-permute-done.14.rest_0_ = bf16[16,128,128]{2,1,0:T(8,128)(2,1)S(1)} collective-permute-done((bf16[16,128,128]{2,1,0:T(8,128)(2,1)S(1)}, bf16[16,128,128]{2,1,0:T(8,128)(2,1)S(1)}, u32[]{:S(2)}, u32[]{:S(2)}) %collective-permute-start.14) | collective-permute-done | bytes 524320 | tf_op jit(solution)/shard_map/ppermute | solution.py:204
  116.6 2.5 %collective-permute-start.16 = (bf16[16,128,128]{2,1,0:T(8,128)(2,1)S(1)}, bf16[16,128,128]{2,1,0:T(8,128)(2,1)S(1)}, u32[]{:S(2)}, u32[]{:S(2)}) collective-permute-start(bf16[16,128,128]{2,1,0:T(8,128)(2,1)S(1)} %shard_map.102), channel_id=1, source_target_pairs={{0,1},{1,0},{2,3},{3,2},{4,5},{5,4},{6,7},{7,6},{8,9},{9,8},{10,11... | collective-permute-start | bytes 1572872 | tf_op jit(solution)/shard_map/ppermute | solution.py:207
  119.0 11.3 %all-gather.3.cloned.1.call-done = bf16[256,2688]{1,0:T(8,128)(2,1)} async-done(((bf16[64,2688]{1,0:T(8,128)(2,1)}), bf16[256,2688]{1,0:T(8,128)(2,1)}) %all-gather.3.cloned.1.call-update) | async-done | bytes 1376272 | tf_op jit(solution)/shard_map/all_gather | solution.py:294
  130.3 1.3 copy-done.9
  131.7 1.2 shard_map.104
  132.8 5.0 %collective-permute-done.16.rest_1_ = bf16[16,128,128]{2,1,0:T(8,128)(2,1)S(1)} collective-permute-done((bf16[16,128,128]{2,1,0:T(8,128)(2,1)S(1)}, bf16[16,128,128]{2,1,0:T(8,128)(2,1)S(1)}, u32[]{:S(2)}, u32[]{:S(2)}) %collective-permute-start.16) | collective-permute-done | bytes 524320 | tf_op jit(solution)/shard_map/ppermute | solution.py:207
  137.8 3.4 %copy-done.4 = f32[65,256,128]{2,1,0:T(8,128)S(1)} copy-done((f32[65,256,128]{2,1,0:T(8,128)S(1)}, f32[65,256,128]{2,1,0:T(8,128)}, u32[]{:S(2)}) %copy-start.4) | copy-done | bytes 8519704
  141.2 1.8 %shard_map.103 = bf16[128,2048]{1,0:T(8,128)(2,1)} custom-call(s32[4]{0:T(128)S(1)} %pad_add_fusion.where_ref, bf16[128,128]{1,0:T(8,128)(2,1)S(1)} %get-tuple-element.28.rounded_ref, bf16[64,2048]{1,0:T(8,128)(2,1)S(1)} %copy-done.11, f32[65,256,128]{2,1,0:T(8,128)S(1)} %copy-done.4, bf16[2,16,128,128]{3,2,1,0:T(8,128)(2,1)S(1)} %collective-permute-done.12.core_ref, ...), custom_call_target="tpu_custom_call" | custom-call | tf_op jit(solution)/shard_map/pallas_call | solution.py:176
  (53 shorter events, 8.9 us)
Async XLA Ops:
  7.2 35.4 %copy-start.5 = (bf16[128,3328]{1,0:T(8,128)(2,1)S(1)}, bf16[128,3328]{1,0:T(8,128)(2,1)}, u32[]{:S(2)}) copy-start(bf16[128,3328]{1,0:T(8,128)(2,1)} %acts_ref.3) | copy-start | bytes 2555908
  7.2 35.3 %copy-start.12 = (bf16[3328,64]{0,1:T(8,128)(2,1)S(1)}, bf16[3328,64]{0,1:T(8,128)(2,1)}, u32[]{:S(2)}) copy-start(bf16[3328,64]{0,1:T(8,128)(2,1)} %param.12) | copy-start | bytes 1277956
  7.2 35.3 %copy-start.13 = (s32[128]{0:T(128)S(1)}, s32[128]{0:T(128)}, u32[]{:S(2)}) copy-start(s32[128]{0:T(128)} %param.9) | copy-start | bytes 1540
  7.2 35.3 %copy-start.10 = (bf16[64,2048]{1,0:T(8,128)(2,1)S(1)}, bf16[64,2048]{1,0:T(8,128)(2,1)}, u32[]{:S(2)}) copy-start(bf16[64,2048]{1,0:T(8,128)(2,1)} %adapter_ref.3) | copy-start | bytes 786436
  7.2 35.3 %copy-start.7 = (bf16[128,2048]{1,0:T(8,128)(2,1)S(1)}, bf16[128,2048]{1,0:T(8,128)(2,1)}, u32[]{:S(2)}) copy-start(bf16[128,2048]{1,0:T(8,128)(2,1)} %cot_ref.3) | copy-start | bytes 1572868
  7.2 123.1 %all-gather.3.cloned.1.call-start = ((), (), s32[]{:S(2)}) async-start(), calls=%async_computation | async-start | bytes 1720320 | tf_op jit(solution)/shard_map/all_gather | solution.py:294
  7.3 1.5 collective-permute-start
  8.7 51.1 %collective-permute-start.1 = (bf16[128,3328]{1,0:T(8,128)(2,1)}, bf16[128,3328]{1,0:T(8,128)(2,1)S(1)}, u32[]{:S(2)}, u32[]{:S(2)}) collective-permute-start(bf16[128,3328]{1,0:T(8,128)(2,1)} %acts_ref.3), channel_id=1, source_target_pairs={{0,1},{1,0},{2,3},{3,2},{4,5},{5,4},{6,7},{7,6},{8,9},{9,8},{10,11... | collective-permute-start | bytes 2555912 | tf_op jit(solution)/shard_map/ppermute | solution.py:207
  11.6 48.2 %copy-start.14 = (s32[1,64]{1,0:T(1,128)S(1)}, s32[1,64]{1,0:T(1,128)}, u32[]{:S(2)}) copy-start(s32[1,64]{1,0:T(1,128)} %param.11) | copy-start | bytes 772
  12.7 28.3 %collective-permute-start.2 = (bf16[14,128,128]{2,1,0:T(8,128)(2,1)S(1)}, bf16[14,128,128]{2,1,0:T(8,128)(2,1)}, u32[]{:S(2)}, u32[]{:S(2)}) collective-permute-start(bf16[14,128,128]{2,1,0:T(8,128)(2,1)S(1)} %dynamic-slice_bitcast_fusion), channel_id=1, source_target_pairs={{0,2},{1,3},{2,0},{3,1},{4,6},{5,7},{6,4},{7,5},{8,10},{9,11},{10,... | collective-permute-start | bytes 1376264 | tf_op jit(solution)/shard_map/ppermute | solution.py:211
  17.1 39.6 %collective-permute-start.4 = (bf16[10,128,128]{2,1,0:T(8,128)(2,1)}, bf16[10,128,128]{2,1,0:T(8,128)(2,1)}, u32[]{:S(2)}, u32[]{:S(2)}) collective-permute-start(bf16[10,128,128]{2,1,0:T(8,128)(2,1)} %dynamic-slice_bitcast_fusion.1), channel_id=1, source_target_pairs={{0,2},{1,3},{2,0},{3,1},{4,6},{5,7},{6,4},{7,5},{8,10},{9,11},{10,... | collective-permute-start | bytes 983048 | tf_op jit(solution)/shard_map/ppermute | solution.py:211
  19.1 48.0 %collective-permute-start.7 = (bf16[8,128,128]{2,1,0:T(8,128)(2,1)}, bf16[8,128,128]{2,1,0:T(8,128)(2,1)}, u32[]{:S(2)}, u32[]{:S(2)}) collective-permute-start(bf16[8,128,128]{2,1,0:T(8,128)(2,1)} %dynamic-slice_bitcast_fusion.2), channel_id=1, source_target_pairs={{0,2},{1,3},{2,0},{3,1},{4,6},{5,7},{6,4},{7,5},{8,10},{9,11},{10,... | collective-permute-start | bytes 786440 | tf_op jit(solution)/shard_map/ppermute | solution.py:211
  41.0 31.2 %collective-permute-start.9 = (bf16[14,128,128]{2,1,0:T(8,128)(2,1)}, bf16[14,128,128]{2,1,0:T(8,128)(2,1)}, u32[]{:S(2)}, u32[]{:S(2)}) collective-permute-start(bf16[14,128,128]{2,1,0:T(8,128)(2,1)} %collective-permute-done.2.rest_0_), channel_id=1, source_target_pairs={{0,16},{16,0},{1,17},{17,1},{2,18},{18,2},{3,19},{19,3},{4,20},{20... | collective-permute-start | bytes 1376264 | tf_op jit(solution)/shard_map/ppermute | solution.py:214
  43.1 15.0 %collective-permute-start.3 = (f32[128,128]{1,0:T(8,128)S(1)}, f32[128,128]{1,0:T(8,128)S(1)}, u32[]{:S(2)}, u32[]{:S(2)}) collective-permute-start(f32[128,128]{1,0:T(8,128)S(1)} %shard_map.95), channel_id=1, source_target_pairs={{0,4},{4,0},{8,12},{12,8},{1,5},{5,1},{9,13},{13,9},{2,6},{6,2},{1... | collective-permute-start | bytes 196616 | tf_op jit(solution)/shard_map/ppermute | solution.py:200
  56.6 15.5 %collective-permute-start.10 = (bf16[10,128,128]{2,1,0:T(8,128)(2,1)}, bf16[10,128,128]{2,1,0:T(8,128)(2,1)S(1)}, u32[]{:S(2)}, u32[]{:S(2)}) collective-permute-start(bf16[10,128,128]{2,1,0:T(8,128)(2,1)} %collective-permute-done.4.rest_1_), channel_id=1, source_target_pairs={{0,16},{16,0},{1,17},{17,1},{2,18},{18,2},{3,19},{19,3},{4,20},{20... | collective-permute-start | bytes 983048 | tf_op jit(solution)/shard_map/ppermute | solution.py:214
  58.2 7.0 %collective-permute-start.5 = (f32[128,128]{1,0:T(8,128)S(1)}, f32[128,128]{1,0:T(8,128)S(1)}, u32[]{:S(2)}, u32[]{:S(2)}) collective-permute-start(f32[128,128]{1,0:T(8,128)S(1)} %add.23.both_ref), channel_id=1, source_target_pairs={{0,8},{4,12},{8,0},{12,4},{1,9},{5,13},{9,1},{13,5},{2,10},{6,14},... | collective-permute-start | bytes 196616 | tf_op jit(solution)/shard_map/ppermute | solution.py:204
  59.8 1.6 %copy-start.6 = (bf16[1,64,128,128]{3,2,1,0:T(8,128)(2,1)S(1)}, bf16[1,64,128,128]{3,2,1,0:T(8,128)(2,1)}, u32[]{:S(2)}) copy-start(bf16[1,64,128,128]{3,2,1,0:T(8,128)(2,1)} %param.10) | copy-start | bytes 6291460
  67.0 15.0 %collective-permute-start.6 = (bf16[64,2176]{1,0:T(8,128)(2,1)S(1)}, bf16[64,2176]{1,0:T(8,128)(2,1)S(1)}, u32[]{:S(2)}, u32[]{:S(2)}) collective-permute-start(bf16[64,2176]{1,0:T(8,128)(2,1)S(1)} %get-tuple-element.29.pack_ref), channel_id=1, source_target_pairs={{0,1},{1,0},{2,3},{3,2},{4,5},{5,4},{6,7},{7,6},{8,9},{9,8},{10,11... | collective-permute-start | bytes 835592 | tf_op jit(solution)/shard_map/ppermute | solution.py:207
  67.1 16.5 %collective-permute-start.11 = (bf16[8,128,128]{2,1,0:T(8,128)(2,1)}, bf16[8,128,128]{2,1,0:T(8,128)(2,1)}, u32[]{:S(2)}, u32[]{:S(2)}) collective-permute-start(bf16[8,128,128]{2,1,0:T(8,128)(2,1)} %collective-permute-done.7.rest_2_), channel_id=1, source_target_pairs={{0,16},{16,0},{1,17},{17,1},{2,18},{18,2},{3,19},{19,3},{4,20},{20... | collective-permute-start | bytes 786440 | tf_op jit(solution)/shard_map/ppermute | solution.py:214
  67.7 4.5 %collective-permute-start.8 = (s32[64]{0:T(128)S(1)}, s32[64]{0:T(128)S(1)}, u32[]{:S(2)}, u32[]{:S(2)}) collective-permute-start(s32[64]{0:T(128)S(1)} %bitcast.28), channel_id=1, source_target_pairs={{0,2},{1,3},{2,0},{3,1},{4,6},{5,7},{6,4},{7,5},{8,10},{9,11},{10,... | collective-permute-start | bytes 776 | tf_op jit(solution)/shard_map/ppermute | solution.py:211
  78.7 3.3 %copy-start = (f32[65,256,128]{2,1,0:T(8,128)}, f32[65,256,128]{2,1,0:T(8,128)S(1)}, u32[]{:S(2)}) copy-start(f32[65,256,128]{2,1,0:T(8,128)S(1)} %shard_map.98.old_ref) | copy-start | bytes 25559044
  83.6 3.4 %copy-start.1 = (f32[65,256,128]{2,1,0:T(8,128)S(1)}, f32[65,256,128]{2,1,0:T(8,128)}, u32[]{:S(2)}) copy-start(f32[65,256,128]{2,1,0:T(8,128)} %copy-done) | copy-start | bytes 25559044
  89.9 3.3 %copy-start.2 = (f32[65,256,128]{2,1,0:T(8,128)}, f32[65,256,128]{2,1,0:T(8,128)S(1)}, u32[]{:S(2)}) copy-start(f32[65,256,128]{2,1,0:T(8,128)S(1)} %get-tuple-element.34.total_ref) | copy-start | bytes 25559044
  94.2 2.9 %collective-permute-start.13 = (bf16[2,16,128,128]{3,2,1,0:T(8,128)(2,1)}, bf16[2,16,128,128]{3,2,1,0:T(8,128)(2,1)S(1)}, u32[]{:S(2)}, u32[]{:S(2)}) collective-permute-start(bf16[2,16,128,128]{3,2,1,0:T(8,128)(2,1)} %get-tuple-element.36), channel_id=1, source_target_pairs={{0,4},{4,0},{8,12},{12,8},{1,5},{5,1},{9,13},{13,9},{2,6},{6,2},{1... | collective-permute-start | bytes 3145736 | tf_op jit(solution)/shard_map/ppermute | solution.py:200
  94.2 7.5 %collective-permute-start.12 = (bf16[2,16,128,128]{3,2,1,0:T(8,128)(2,1)}, bf16[2,16,128,128]{3,2,1,0:T(8,128)(2,1)S(1)}, u32[]{:S(2)}, u32[]{:S(2)}) collective-permute-start(bf16[2,16,128,128]{3,2,1,0:T(8,128)(2,1)} %copy-done.15), channel_id=1, source_target_pairs={{0,4},{4,0},{8,12},{12,8},{1,5},{5,1},{9,13},{13,9},{2,6},{6,2},{1... | collective-permute-start | bytes 3145736 | tf_op jit(solution)/shard_map/ppermute | solution.py:200
  97.1 3.4 %copy-start.3 = (f32[65,256,128]{2,1,0:T(8,128)S(1)}, f32[65,256,128]{2,1,0:T(8,128)}, u32[]{:S(2)}) copy-start(f32[65,256,128]{2,1,0:T(8,128)} %copy-done.2) | copy-start | bytes 25559044
  101.2 14.0 %collective-permute-start.14 = (bf16[16,128,128]{2,1,0:T(8,128)(2,1)S(1)}, bf16[16,128,128]{2,1,0:T(8,128)(2,1)S(1)}, u32[]{:S(2)}, u32[]{:S(2)}) collective-permute-start(bf16[16,128,128]{2,1,0:T(8,128)(2,1)S(1)} %bitcast.21), channel_id=1, source_target_pairs={{0,8},{4,12},{8,0},{12,4},{1,9},{5,13},{9,1},{13,5},{2,10},{6,14},... | collective-permute-start | bytes 1572872 | tf_op jit(solution)/shard_map/ppermute | solution.py:204
  102.5 35.3 %copy-start.11 = (bf16[64,2048]{1,0:T(8,128)(2,1)S(1)}, bf16[64,2048]{1,0:T(8,128)(2,1)}, u32[]{:S(2)}) copy-start(bf16[64,2048]{1,0:T(8,128)(2,1)} %adapter_ref.3) | copy-start | bytes 786436
  116.0 16.9 %collective-permute-start.15 = (bf16[16,128,128]{2,1,0:T(8,128)(2,1)S(1)}, bf16[16,128,128]{2,1,0:T(8,128)(2,1)S(1)}, u32[]{:S(2)}, u32[]{:S(2)}) collective-permute-start(bf16[16,128,128]{2,1,0:T(8,128)(2,1)S(1)} %bitcast.20), channel_id=1, source_target_pairs={{0,8},{4,12},{8,0},{12,4},{1,9},{5,13},{9,1},{13,5},{2,10},{6,14},... | collective-permute-start | bytes 1572872 | tf_op jit(solution)/shard_map/ppermute | solution.py:204
  116.6 21.3 %collective-permute-start.16 = (bf16[16,128,128]{2,1,0:T(8,128)(2,1)S(1)}, bf16[16,128,128]{2,1,0:T(8,128)(2,1)S(1)}, u32[]{:S(2)}, u32[]{:S(2)}) collective-permute-start(bf16[16,128,128]{2,1,0:T(8,128)(2,1)S(1)} %shard_map.102), channel_id=1, source_target_pairs={{0,1},{1,0},{2,3},{3,2},{4,5},{5,4},{6,7},{7,6},{8,9},{9,8},{10,11... | collective-permute-start | bytes 1572872 | tf_op jit(solution)/shard_map/ppermute | solution.py:207
  130.3 1.3 copy-start.9
  137.8 3.4 %copy-start.4 = (f32[65,256,128]{2,1,0:T(8,128)S(1)}, f32[65,256,128]{2,1,0:T(8,128)}, u32[]{:S(2)}) copy-start(f32[65,256,128]{2,1,0:T(8,128)} %copy-done.2) | copy-start | bytes 25559044
  (2 other events, 2.0 us)
Sparse Core Ops, SparseCore 0:
  94.4 35.9 all-gather.2

commit v5 on v4

--- a/solution.py
+++ b/solution.py
@@ -35,7 +35,7 @@
     for blocks_ref, (offset, shift, start) in zip(blocks, places):
         source = lax.rem(where_ref[0] + (parts - shift), parts)
         base = offset + source * held + start
-        add_blocks(total_ref, tiles_ref, blocks_ref, ids_ref, base, col_blocks, 2)
+        add_blocks(total_ref, tiles_ref, blocks_ref, ids_ref, base, col_blocks, 4)
 
 
 def first_kernel(where_ref, own_ids_ref, ids_ref, own_ref, mate_ref, own_blocks_ref, *rest, **plan):
@@ -127,31 +127,46 @@
     pack_ref[:, feats:] = rounded[rank:]
 
 
-def pair_grad_kernel(where_ref, rounded_ref, acts_ref, mate_acts_ref, pack_ref, mate_pack_ref, half_ref):
+def pair_grad_kernel(
+    where_ref, rounded_ref, acts_ref, mate_acts_ref, pack_ref, mate_pack_ref, half_ref, other_ref
+):
     rank, shard_rows = rounded_ref.shape[0] // 2, acts_ref.shape[1]
     feats = pack_ref.shape[1] - rounded_ref.shape[1]
     in_half, out_half = shard_rows // 2, feats // 2
     back, mate_back = rounded_ref[rank:, :], mate_pack_ref[:, feats:]
+
+    def fill(bit, out_ref):
+        cols = slice(bit * in_half, (bit + 1) * in_half)
+        grad = jnp.dot(back, acts_ref[:, cols], preferred_element_type=F32)
+        grad = grad + jnp.dot(mate_back, mate_acts_ref[:, cols], preferred_element_type=F32)
+        out_ref[:, :in_half] = (adapter_scale * grad).astype(BF16)
+        cols = slice(bit * out_half, (bit + 1) * out_half)
+        grad = pack_ref[:, cols].astype(F32) + mate_pack_ref[:, cols].astype(F32)
+        out_ref[:, in_half:] = grad.astype(BF16)
+
     for bit in range(2):
         @pl.when(where_ref[3] == bit)
         def _():
-            cols = slice(bit * in_half, (bit + 1) * in_half)
-            grad = jnp.dot(back, acts_ref[:, cols], preferred_element_type=F32)
-            grad += jnp.dot(mate_back, mate_acts_ref[:, cols], preferred_element_type=F32)
-            half_ref[:, :in_half] = (adapter_scale * grad).astype(BF16)
-            cols = slice(bit * out_half, (bit + 1) * out_half)
-            grad = pack_ref[:, cols].astype(F32) + mate_pack_ref[:, cols].astype(F32)
-            half_ref[:, in_half:] = grad.astype(BF16)
-
-
-def grad_sum_kernel(halves_ref, in_ref, out_ref):
+            fill(bit, half_ref)
+            fill(1 - bit, other_ref)
+
+
+def grad_sum_kernel(where_ref, half_ref, other_ref, *rest):
+    received, (in_ref, out_ref) = rest[:-2], rest[-2:]
     in_half, out_half = in_ref.shape[1] // 2, out_ref.shape[1] // 2
-    for bit in range(2):
-        total = halves_ref[bit].astype(F32)
-        for member in range(2 + bit, halves_ref.shape[0], 2):
-            total += halves_ref[member].astype(F32)
+    count = len(received) // 2
+    place = where_ref[4]
+
+    def add(bit, own_ref, halves):
+        total = ordered_sum(own_ref[...].astype(F32), [ref[...].astype(F32) for ref in halves], place)
         in_ref[:, bit * in_half:(bit + 1) * in_half] = total[:, :in_half]
         out_ref[:, bit * out_half:(bit + 1) * out_half] = total[:, in_half:]
+
+    for bit in range(2):
+        @pl.when(where_ref[3] == bit)
+        def _():
+            add(bit, half_ref, received[:count])
+            add(1 - bit, other_ref, received[count:])
 
 
 def final_kernel(where_ref, rounded_ref, adapter_ref, total_ref, core_ref, *rest):
@@ -225,7 +240,7 @@
         row_index = lax.axis_index("row")
         dp_index = lax.axis_index("dp")
         where = jnp.stack(
-            [part, lax.rem(row_index, 2), lax.div(row_index, 2), lax.rem(dp_index, 2)]
+            [part, lax.rem(row_index, 2), lax.div(row_index, 2), lax.rem(dp_index, 2), lax.div(dp_index, 2)]
         ).astype(jnp.int32)
         blocks = kept_blocks[0]
         ids = block_ids[0]
@@ -235,7 +250,7 @@
         far_ids = [group_shift(ids, d) for d in range(1, group)]
         all_ids = far_ids[0] if group == 2 else jnp.concatenate(far_ids)
         held = slots // n_parts
-        sizes = [held * k // 32 for k in (14, 10, 8)]
+        sizes = [held * k // 32 for k in (12, 12, 8)]
         starts = [sum(sizes[:k]) for k in range(len(sizes))]
 
         def leaving_chunk(k):
@@ -286,12 +301,12 @@
         )
         mate_pack = mate_swap(pack)
 
-        (half_grads,) = call(
-            pair_grad_kernel, (jax.ShapeDtypeStruct((rank, (shard_rows + feats) // 2), BF16),),
-            (where,), (rounded, activations, mate_activations, pack, mate_pack),
+        half_shape = jax.ShapeDtypeStruct((rank, (shard_rows + feats) // 2), BF16)
+        half_grads, other_grads = call(
+            pair_grad_kernel, (half_shape, half_shape), (where,), (rounded, activations, mate_activations, pack, mate_pack),
         )
         half_grads = after(half_grads, direct[-1][0])
-        halves = lax.all_gather(half_grads, "dp")
+        far_grads = [group_shift(half_grads, d) for d in range(1, group)]
 
         (total,) = call(
             functools.partial(more_kernel, **plan(more)), (total_shape,), (where, all_ids),
@@ -321,10 +336,11 @@
         )
         from_mate = mate_swap(mate_total)
         own_pieces = for_chips(0, core_own, where, mate_total)
+        from_mate_grads = [mate_swap(value) for value in far_grads]
         in_grad, out_grad = call(
             grad_sum_kernel,
             (jax.ShapeDtypeStruct((rank, shard_rows), F32), jax.ShapeDtypeStruct((rank, feats), F32)),
-            (), (after(halves, mate_total),),
+            (where,), (half_grads, other_grads) + tuple(far_grads) + tuple(after(value, mate_total) for value in from_mate_grads),
         )
         (projected,) = call(
             final_kernel, (jax.ShapeDtypeStruct((tokens, feats), BF16),), (where,),

time: 150 us -> 118 us (0.79)
  local copies, waits for them, and re-layouts: 26.3 us -> 6.61 us
  between operations: 14.2 us -> 0.82 us
  starting transfers between devices: 21.5 us -> 24.4 us
  Pallas kernels: 21.2 us -> 19.2 us
    unnamed x32 -> x18, local copies, waits for them, and re-layouts: 21.9 us -> 2.64 us
    ppermute x3 -> x4, waiting for transfers between devices: 4.96 us -> 18.5 us  [mate_swap(): return lax.ppermute(value, 'dp', [(i, i ^ 1) for i in range(n_dp)])]
    all_gather x1 -> x0, waiting for transfers between devices: 11.3 us -> none  [body(): halves = lax.all_gather(half_grads, 'dp')]
    ppermute x3, waiting for transfers between devices: 12.7 us -> 9.82 us  [chip_shift(): return lax.ppermute(value, 'row', pairs)]
    ppermute x4 -> x5, starting transfers between devices: 8.54 us -> 11.4 us  [group_shift(): return lax.ppermute(value, 'dp', pairs)]
    pallas_call x11, Pallas kernels: 21.2 us -> 19.2 us  [call(): pl.pallas_call(kernel, out_shape=outs, in_specs=[smem] * len(scalars) + [...]
    dynamic_slice x3 -> x2, local copies, waits for them, and re-layouts: 4.45 us -> 3.88 us  [leaving_chunk(): lax.dynamic_slice_in_dim(blocks, part * held + starts[k], sizes[k], axis=0)]
    ppermute x4 -> x5, waiting for transfers between devices: 34.3 us -> 34.8 us  [group_shift(): return lax.ppermute(value, 'dp', pairs)]
  transfers between devices with their start and end apart: 18 -> 19, of which waited for: 8 -> 8; matrix products, arithmetic and copies ran while one was open for 3% -> 3% of each run, Pallas kernels for 11% -> 14%
where the time goes in v5:
time: 118 us; the launch traced here: 117 us
  waiting for transfers between devices  66.2 us (56%)
  starting transfers between devices  24.4 us (21%)
  Pallas kernels  19.2 us (16%)
  local copies, waits for them, and re-layouts  6.61 us (6%)
    ppermute x5, waiting for transfers between devices, group_shift(): return lax.ppermute(value, 'dp', pairs)  34.8 us
    pallas_call x11, Pallas kernels, call(): pl.pallas_call(kernel, out_shape=outs, in_specs=[smem] * len(scalars) + [...  19.2 us
    ppermute x4, waiting for transfers between devices, mate_swap(): return lax.ppermute(value, 'dp', [(i, i ^ 1) for i in range(n_dp)])  18.5 us
    ppermute x5, starting transfers between devices, group_shift(): return lax.ppermute(value, 'dp', pairs)  11.4 us
    ppermute x3, waiting for transfers between devices, chip_shift(): return lax.ppermute(value, 'row', pairs)  9.82 us
    ppermute x4, starting transfers between devices, mate_swap(): return lax.ppermute(value, 'dp', [(i, i ^ 1) for i in range(n_dp)])  5.42 us
    dynamic_slice x2, local copies, waits for them, and re-layouts, leaving_chunk(): lax.dynamic_slice_in_dim(blocks, part * held + starts[k], sizes[k], axis=0)  3.88 us
    ppermute x3, starting transfers between devices, part_shift(): lax.ppermute(value, 'parts', [(i, (i + d) % n_parts) for i in range(n_par...  3.68 us
  transfers between devices with their start and end apart: 19, of which 8 were waited for; matrix products, arithmetic and copies ran while one was open for 3% of the time, Pallas kernels for 14%

profile of v5, /device:TPU:0, one launch (start us, length us, event | category | flops | bytes accessed | tf_op | source)
XLA Modules:
  0.0 117.2 jit_solution(3823908886784337299)
XLA Ops:
  1.2 1.0 collective-permute-done
  2.1 2.9 %collective-permute-start.1 = (bf16[128,3328]{1,0:T(8,128)(2,1)}, bf16[128,3328]{1,0:T(8,128)(2,1)}, u32[]{:S(2)}, u32[]{:S(2)}) collective-permute-start(bf16[128,3328]{1,0:T(8,128)(2,1)} %acts_ref.3), channel_id=1, source_target_pairs={{0,1},{1,0},{2,3},{3,2},{4,5},{5,4},{6,7},{7,6},{8,9},{9,8},{10,11... | collective-permute-start | bytes 2555912 | tf_op jit(solution)/shard_map/ppermute | solution.py:222
  5.0 2.2 %dynamic-slice_bitcast_fusion = (bf16[12,128,128]{2,1,0:T(8,128)(2,1)}, bf16[12,128,128]{2,1,0:T(8,128)(2,1)}) fusion(bf16[1,64,128,128]{3,2,1,0:T(8,128)(2,1)} %param.10, s32[]{:T(128)S(6)} %select_n.10, s32[]{:T(128)S(6)} %select_n.9), kind=kLoop, calls=%fused_computation | loop fusion | bytes 1572872 | tf_op jit(solution)/shard_map/dynamic_slice | solution.py:257
  7.2 2.6 %collective-permute-start.2 = (bf16[12,128,128]{2,1,0:T(8,128)(2,1)}, bf16[12,128,128]{2,1,0:T(8,128)(2,1)}, u32[]{:S(2)}, u32[]{:S(2)}) collective-permute-start(bf16[12,128,128]{2,1,0:T(8,128)(2,1)} %get-tuple-element.46), channel_id=1, source_target_pairs={{0,2},{1,3},{2,0},{3,1},{4,6},{5,7},{6,4},{7,5},{8,10},{9,11},{10,... | collective-permute-start | bytes 1179656 | tf_op jit(solution)/shard_map/ppermute | solution.py:226
  10.1 1.7 %dynamic-slice_bitcast_fusion.2 = bf16[8,128,128]{2,1,0:T(8,128)(2,1)} fusion(bf16[1,64,128,128]{3,2,1,0:T(8,128)(2,1)} %param.10, s32[]{:T(128)S(6)} %select_n.11), kind=kLoop, calls=%fused_computation.2 | loop fusion | bytes 524292 | tf_op jit(solution)/shard_map/dynamic_slice | solution.py:257
  11.8 2.6 %collective-permute-start.7 = (bf16[8,128,128]{2,1,0:T(8,128)(2,1)}, bf16[8,128,128]{2,1,0:T(8,128)(2,1)}, u32[]{:S(2)}, u32[]{:S(2)}) collective-permute-start(bf16[8,128,128]{2,1,0:T(8,128)(2,1)} %dynamic-slice_bitcast_fusion.2), channel_id=1, source_target_pairs={{0,2},{1,3},{2,0},{3,1},{4,6},{5,7},{6,4},{7,5},{8,10},{9,11},{10,... | collective-permute-start | bytes 786440 | tf_op jit(solution)/shard_map/ppermute | solution.py:226
  14.4 18.7 %collective-permute-done.2.rest_0_ = bf16[12,128,128]{2,1,0:T(8,128)(2,1)} collective-permute-done((bf16[12,128,128]{2,1,0:T(8,128)(2,1)}, bf16[12,128,128]{2,1,0:T(8,128)(2,1)}, u32[]{:S(2)}, u32[]{:S(2)}) %collective-permute-start.2) | collective-permute-done | bytes 393248 | tf_op jit(solution)/shard_map/ppermute | solution.py:226
  33.1 0.9 copy-done.3
  34.0 1.0 copy-done.5
  35.1 0.7 copy-done.6
  36.4 1.6 %collective-permute-start.9 = (bf16[12,128,128]{2,1,0:T(8,128)(2,1)}, bf16[12,128,128]{2,1,0:T(8,128)(2,1)}, u32[]{:S(2)}, u32[]{:S(2)}) collective-permute-start(bf16[12,128,128]{2,1,0:T(8,128)(2,1)} %collective-permute-done.2.rest_0_), channel_id=1, source_target_pairs={{0,16},{16,0},{1,17},{17,1},{2,18},{18,2},{3,19},{19,3},{4,20},{20... | collective-permute-start | bytes 1179656 | tf_op jit(solution)/shard_map/ppermute | solution.py:229
  38.0 13.3 %collective-permute-done.4.rest_1_ = bf16[12,128,128]{2,1,0:T(8,128)(2,1)} collective-permute-done((bf16[12,128,128]{2,1,0:T(8,128)(2,1)}, bf16[12,128,128]{2,1,0:T(8,128)(2,1)}, u32[]{:S(2)}, u32[]{:S(2)}) %collective-permute-start.4) | collective-permute-done | bytes 393248 | tf_op jit(solution)/shard_map/ppermute | solution.py:226
  51.3 1.5 %collective-permute-start.10 = (bf16[12,128,128]{2,1,0:T(8,128)(2,1)}, bf16[12,128,128]{2,1,0:T(8,128)(2,1)}, u32[]{:S(2)}, u32[]{:S(2)}) collective-permute-start(bf16[12,128,128]{2,1,0:T(8,128)(2,1)} %collective-permute-done.4.rest_1_), channel_id=1, source_target_pairs={{0,16},{16,0},{1,17},{17,1},{2,18},{18,2},{3,19},{19,3},{4,20},{20... | collective-permute-start | bytes 1179656 | tf_op jit(solution)/shard_map/ppermute | solution.py:229
  52.9 1.6 %collective-permute-start.5 = (f32[128,128]{1,0:T(8,128)S(1)}, f32[128,128]{1,0:T(8,128)}, u32[]{:S(2)}, u32[]{:S(2)}) collective-permute-start(f32[128,128]{1,0:T(8,128)S(1)} %add.23.both_ref), channel_id=1, source_target_pairs={{0,8},{4,12},{8,0},{12,4},{1,9},{5,13},{9,1},{13,5},{2,10},{6,14},... | collective-permute-start | bytes 196616 | tf_op jit(solution)/shard_map/ppermute | solution.py:219
  54.5 4.4 %shard_map.94 = (f32[65,256,128]{2,1,0:T(8,128)S(1)}, bf16[26,256,128]{2,1,0:T(8,128)(2,1)S(1)}) custom-call(s32[5]{0:T(128)S(1)} %stack.23.where_ref, s32[64]{0:T(128)S(1)} %bitcast.25, s32[64]{0:T(128)S(1)} %bitcast.26, bf16[128,3328]{1,0:T(8,128)(2,1)S(1)} %copy-done, bf16[128,3328]{1,0:T(8,128)(2,1)} %collective-permute-done.1.mate_ref.mate_acts_ref, ...), custom_call_target="tpu_custom_call" | custom-call | tf_op jit(solution)/shard_map/pallas_call | solution.py:191
  58.9 1.1 shard_map.96
  60.7 3.0 %collective-permute-start.8 = (s32[64]{0:T(128)S(1)}, s32[64]{0:T(128)S(1)}, u32[]{:S(2)}, u32[]{:S(2)}) collective-permute-start(s32[64]{0:T(128)S(1)} %bitcast.27), channel_id=1, source_target_pairs={{0,2},{1,3},{2,0},{3,1},{4,6},{5,7},{6,4},{7,5},{8,10},{9,11},{10,... | collective-permute-start | bytes 776 | tf_op jit(solution)/shard_map/ppermute | solution.py:226
  63.6 1.5 %collective-permute-done.8.ids_ref = s32[64]{0:T(128)S(1)} collective-permute-done((s32[64]{0:T(128)S(1)}, s32[64]{0:T(128)S(1)}, u32[]{:S(2)}, u32[]{:S(2)}) %collective-permute-start.8) | collective-permute-done | bytes 288 | tf_op jit(solution)/shard_map/ppermute | solution.py:226
  65.2 4.6 %shard_map.98.old_ref = f32[65,256,128]{2,1,0:T(8,128)S(1)} custom-call(s32[5]{0:T(128)S(1)} %stack.23.where_ref, s32[64]{0:T(128)S(1)} %collective-permute-done.8.ids_ref, bf16[26,256,128]{2,1,0:T(8,128)(2,1)S(1)} %get-tuple-element.36.tiles_ref, f32[65,256,128]{2,1,0:T(8,128)S(1)} %get-tuple-element.25.old_ref, ...), custom_call_target="tpu_custom_call", output_to_operand_aliasing={{}: (3, {})} | custom-call | tf_op jit(solution)/shard_map/pallas_call | solution.py:191
  69.8 1.6 %shard_map.97 = (bf16[64,2688]{1,0:T(8,128)(2,1)S(1)}, bf16[64,2688]{1,0:T(8,128)(2,1)S(1)}) custom-call(s32[5]{0:T(128)S(1)} %stack.23.where_ref, bf16[128,128]{1,0:T(8,128)(2,1)S(1)} %get-tuple-element.30.rounded_ref, bf16[128,3328]{1,0:T(8,128)(2,1)S(1)} %copy-done, bf16[128,3328]{1,0:T(8,128)(2,1)} %collective-permute-done.1.mate_ref.mate_acts_ref, ...), custom_call_target="tpu_custom_call" | custom-call | tf_op jit(solution)/shard_map/pallas_call | solution.py:191
  71.4 1.2 %shard_map.99 = (f32[65,256,128]{2,1,0:T(8,128)S(1)}, bf16[2,16,128,128]{3,2,1,0:T(8,128)(2,1)S(1)}, bf16[2,16,128,128]{3,2,1,0:T(8,128)(2,1)S(1)}) custom-call(s32[5]{0:T(128)S(1)} %stack.23.where_ref, s32[64]{0:T(128)S(1)} %collective-permute-done.8.ids_ref, ...), custom_call_target="tpu_custom_call", output_to_operand_aliasing={{0}: (3, {})} | custom-call | tf_op jit(solution)/shard_map/pallas_call | solution.py:191
  73.2 2.1 %collective-permute-done.13.core_ref = bf16[2,16,128,128]{3,2,1,0:T(8,128)(2,1)S(1)} collective-permute-done((bf16[2,16,128,128]{3,2,1,0:T(8,128)(2,1)S(1)}, bf16[2,16,128,128]{3,2,1,0:T(8,128)(2,1)S(1)}, u32[]{:S(2)}, u32[]{:S(2)}) %collective-permute-start.13) | collective-permute-done | bytes 1048608 | tf_op jit(solution)/shard_map/ppermute | solution.py:215
  75.4 0.7 shard_map.101
  76.7 2.9 %collective-permute-start.17 = (bf16[64,2688]{1,0:T(8,128)(2,1)S(1)}, bf16[64,2688]{1,0:T(8,128)(2,1)S(1)}, u32[]{:S(2)}, u32[]{:S(2)}) collective-permute-start(bf16[64,2688]{1,0:T(8,128)(2,1)S(1)} %get-tuple-element.34.half_ref), channel_id=1, source_target_pairs={{0,2},{1,3},{2,0},{3,1},{4,6},{5,7},{6,4},{7,5},{8,10},{9,11},{10,... | collective-permute-start | bytes 1032200 | tf_op jit(solution)/shard_map/ppermute | solution.py:226
  79.6 0.7 shard_map.100
  80.3 9.8 %collective-permute-done.14.rest_0_ = bf16[16,128,128]{2,1,0:T(8,128)(2,1)S(1)} collective-permute-done((bf16[16,128,128]{2,1,0:T(8,128)(2,1)S(1)}, bf16[16,128,128]{2,1,0:T(8,128)(2,1)S(1)}, u32[]{:S(2)}, u32[]{:S(2)}) %collective-permute-start.14) | collective-permute-done | bytes 524320 | tf_op jit(solution)/shard_map/ppermute | solution.py:219
  90.1 0.7 shard_map.102
  91.4 2.5 %collective-permute-start.16 = (bf16[16,128,128]{2,1,0:T(8,128)(2,1)S(1)}, bf16[16,128,128]{2,1,0:T(8,128)(2,1)S(1)}, u32[]{:S(2)}, u32[]{:S(2)}) collective-permute-start(bf16[16,128,128]{2,1,0:T(8,128)(2,1)S(1)} %shard_map.102), channel_id=1, source_target_pairs={{0,1},{1,0},{2,3},{3,2},{4,5},{5,4},{6,7},{7,6},{8,9},{9,8},{10,11... | collective-permute-start | bytes 1572872 | tf_op jit(solution)/shard_map/ppermute | solution.py:222
  93.9 1.3 %collective-permute-done.17.rest_0_ = bf16[64,2688]{1,0:T(8,128)(2,1)S(1)} collective-permute-done((bf16[64,2688]{1,0:T(8,128)(2,1)S(1)}, bf16[64,2688]{1,0:T(8,128)(2,1)S(1)}, u32[]{:S(2)}, u32[]{:S(2)}) %collective-permute-start.17) | collective-permute-done | bytes 344096 | tf_op jit(solution)/shard_map/ppermute | solution.py:226
  95.1 18.5 %collective-permute-done.18.rest_1_ = bf16[64,2688]{1,0:T(8,128)(2,1)S(1)} collective-permute-done((bf16[64,2688]{1,0:T(8,128)(2,1)S(1)}, bf16[64,2688]{1,0:T(8,128)(2,1)S(1)}, u32[]{:S(2)}, u32[]{:S(2)}) %collective-permute-start.18) | collective-permute-done | bytes 344096 | tf_op jit(solution)/shard_map/ppermute | solution.py:222
  113.6 1.8 %shard_map.104 = (f32[64,3328]{1,0:T(8,128)}, f32[64,2048]{1,0:T(8,128)}) custom-call(s32[5]{0:T(128)S(1)} %stack.23.where_ref, bf16[64,2688]{1,0:T(8,128)(2,1)S(1)} %get-tuple-element.34.half_ref, bf16[64,2688]{1,0:T(8,128)(2,1)S(1)} %get-tuple-element.41.other_ref, bf16[64,2688]{1,0:T(8,128)(2,1)S(1)} %collective-permute-done.17.rest_0_, ...), custom_call_target="tpu_custom_call" | custom-call | tf_op jit(solution)/shard_map/pallas_call | solution.py:191
  115.4 1.8 %shard_map.103 = bf16[128,2048]{1,0:T(8,128)(2,1)} custom-call(s32[5]{0:T(128)S(1)} %stack.23.where_ref, bf16[128,128]{1,0:T(8,128)(2,1)S(1)} %get-tuple-element.30.rounded_ref, bf16[64,2048]{1,0:T(8,128)(2,1)S(1)} %copy-done.4, f32[65,256,128]{2,1,0:T(8,128)S(1)} %get-tuple-element.37.total_ref, ...), custom_call_target="tpu_custom_call" | custom-call | tf_op jit(solution)/shard_map/pallas_call | solution.py:191
  (39 shorter events, 4.1 us)
Async XLA Ops:
  0.6 32.5 %copy-start = (bf16[128,3328]{1,0:T(8,128)(2,1)S(1)}, bf16[128,3328]{1,0:T(8,128)(2,1)}, u32[]{:S(2)}) copy-start(bf16[128,3328]{1,0:T(8,128)(2,1)} %acts_ref.3) | copy-start | bytes 2555908
  0.6 32.4 %copy-start.2 = (bf16[128,2048]{1,0:T(8,128)(2,1)S(1)}, bf16[128,2048]{1,0:T(8,128)(2,1)}, u32[]{:S(2)}) copy-start(bf16[128,2048]{1,0:T(8,128)(2,1)} %cot_ref.3) | copy-start | bytes 1572868
  0.6 1.5 %collective-permute-start = (s32[64]{0:T(128)}, s32[64]{0:T(128)S(1)}, u32[]{:S(2)}, u32[]{:S(2)}) collective-permute-start(s32[64]{0:T(128)} %bitcast.24), channel_id=1, source_target_pairs={{0,4},{4,0},{8,12},{12,8},{1,5},{5,1},{9,13},{13,9},{2,6},{6,2},{1... | collective-permute-start | bytes 776 | tf_op jit(solution)/shard_map/ppermute | solution.py:215
  2.1 52.4 %collective-permute-start.1 = (bf16[128,3328]{1,0:T(8,128)(2,1)}, bf16[128,3328]{1,0:T(8,128)(2,1)}, u32[]{:S(2)}, u32[]{:S(2)}) collective-permute-start(bf16[128,3328]{1,0:T(8,128)(2,1)} %acts_ref.3), channel_id=1, source_target_pairs={{0,1},{1,0},{2,3},{3,2},{4,5},{5,4},{6,7},{7,6},{8,9},{9,8},{10,11... | collective-permute-start | bytes 2555912 | tf_op jit(solution)/shard_map/ppermute | solution.py:222
  5.0 49.5 %copy-start.1 = (bf16[1,64,128,128]{3,2,1,0:T(8,128)(2,1)S(1)}, bf16[1,64,128,128]{3,2,1,0:T(8,128)(2,1)}, u32[]{:S(2)}) copy-start(bf16[1,64,128,128]{3,2,1,0:T(8,128)(2,1)} %param.10) | copy-start | bytes 6291460
  7.2 25.9 %collective-permute-start.2 = (bf16[12,128,128]{2,1,0:T(8,128)(2,1)}, bf16[12,128,128]{2,1,0:T(8,128)(2,1)}, u32[]{:S(2)}, u32[]{:S(2)}) collective-permute-start(bf16[12,128,128]{2,1,0:T(8,128)(2,1)} %get-tuple-element.46), channel_id=1, source_target_pairs={{0,2},{1,3},{2,0},{3,1},{4,6},{5,7},{6,4},{7,5},{8,10},{9,11},{10,... | collective-permute-start | bytes 1179656 | tf_op jit(solution)/shard_map/ppermute | solution.py:226
  9.8 41.5 %collective-permute-start.4 = (bf16[12,128,128]{2,1,0:T(8,128)(2,1)}, bf16[12,128,128]{2,1,0:T(8,128)(2,1)}, u32[]{:S(2)}, u32[]{:S(2)}) collective-permute-start(bf16[12,128,128]{2,1,0:T(8,128)(2,1)} %get-tuple-element.28), channel_id=1, source_target_pairs={{0,2},{1,3},{2,0},{3,1},{4,6},{5,7},{6,4},{7,5},{8,10},{9,11},{10,... | collective-permute-start | bytes 1179656 | tf_op jit(solution)/shard_map/ppermute | solution.py:226
  11.8 48.3 %collective-permute-start.7 = (bf16[8,128,128]{2,1,0:T(8,128)(2,1)}, bf16[8,128,128]{2,1,0:T(8,128)(2,1)}, u32[]{:S(2)}, u32[]{:S(2)}) collective-permute-start(bf16[8,128,128]{2,1,0:T(8,128)(2,1)} %dynamic-slice_bitcast_fusion.2), channel_id=1, source_target_pairs={{0,2},{1,3},{2,0},{3,1},{4,6},{5,7},{6,4},{7,5},{8,10},{9,11},{10,... | collective-permute-start | bytes 786440 | tf_op jit(solution)/shard_map/ppermute | solution.py:226
  33.1 1.0 copy-start.3
  34.0 1.0 copy-start.5
  35.0 0.7 copy-start.6
  35.7 18.8 %copy-start.8 = (s32[1,64]{1,0:T(1,128)S(1)}, s32[1,64]{1,0:T(1,128)}, u32[]{:S(2)}) copy-start(s32[1,64]{1,0:T(1,128)} %param.11) | copy-start | bytes 772
  36.3 22.6 %copy-start.7 = (s32[128]{0:T(128)S(1)}, s32[128]{0:T(128)}, u32[]{:S(2)}) copy-start(s32[128]{0:T(128)} %param.9) | copy-start | bytes 1540
  36.3 16.5 %collective-permute-start.3 = (f32[128,128]{1,0:T(8,128)S(1)}, f32[128,128]{1,0:T(8,128)S(1)}, u32[]{:S(2)}, u32[]{:S(2)}) collective-permute-start(f32[128,128]{1,0:T(8,128)S(1)} %shard_map.95), channel_id=1, source_target_pairs={{0,4},{4,0},{8,12},{12,8},{1,5},{5,1},{9,13},{13,9},{2,6},{6,2},{1... | collective-permute-start | bytes 196616 | tf_op jit(solution)/shard_map/ppermute | solution.py:215
  36.4 28.8 %collective-permute-start.9 = (bf16[12,128,128]{2,1,0:T(8,128)(2,1)}, bf16[12,128,128]{2,1,0:T(8,128)(2,1)}, u32[]{:S(2)}, u32[]{:S(2)}) collective-permute-start(bf16[12,128,128]{2,1,0:T(8,128)(2,1)} %collective-permute-done.2.rest_0_), channel_id=1, source_target_pairs={{0,16},{16,0},{1,17},{17,1},{2,18},{18,2},{3,19},{19,3},{4,20},{20... | collective-permute-start | bytes 1179656 | tf_op jit(solution)/shard_map/ppermute | solution.py:229
  51.3 13.8 %collective-permute-start.10 = (bf16[12,128,128]{2,1,0:T(8,128)(2,1)}, bf16[12,128,128]{2,1,0:T(8,128)(2,1)}, u32[]{:S(2)}, u32[]{:S(2)}) collective-permute-start(bf16[12,128,128]{2,1,0:T(8,128)(2,1)} %collective-permute-done.4.rest_1_), channel_id=1, source_target_pairs={{0,16},{16,0},{1,17},{17,1},{2,18},{18,2},{3,19},{19,3},{4,20},{20... | collective-permute-start | bytes 1179656 | tf_op jit(solution)/shard_map/ppermute | solution.py:229
  52.9 6.1 %collective-permute-start.5 = (f32[128,128]{1,0:T(8,128)S(1)}, f32[128,128]{1,0:T(8,128)}, u32[]{:S(2)}, u32[]{:S(2)}) collective-permute-start(f32[128,128]{1,0:T(8,128)S(1)} %add.23.both_ref), channel_id=1, source_target_pairs={{0,8},{4,12},{8,0},{12,4},{1,9},{5,13},{9,1},{13,5},{2,10},{6,14},... | collective-permute-start | bytes 196616 | tf_op jit(solution)/shard_map/ppermute | solution.py:219
  60.0 9.8 %collective-permute-start.6 = (bf16[64,2176]{1,0:T(8,128)(2,1)S(1)}, bf16[64,2176]{1,0:T(8,128)(2,1)S(1)}, u32[]{:S(2)}, u32[]{:S(2)}) collective-permute-start(bf16[64,2176]{1,0:T(8,128)(2,1)S(1)} %get-tuple-element.31.pack_ref), channel_id=1, source_target_pairs={{0,1},{1,0},{2,3},{3,2},{4,5},{5,4},{6,7},{7,6},{8,9},{9,8},{10,11... | collective-permute-start | bytes 835592 | tf_op jit(solution)/shard_map/ppermute | solution.py:222
  60.1 11.3 %collective-permute-start.11 = (bf16[8,128,128]{2,1,0:T(8,128)(2,1)}, bf16[8,128,128]{2,1,0:T(8,128)(2,1)S(1)}, u32[]{:S(2)}, u32[]{:S(2)}) collective-permute-start(bf16[8,128,128]{2,1,0:T(8,128)(2,1)} %collective-permute-done.7.rest_2_), channel_id=1, source_target_pairs={{0,16},{16,0},{1,17},{17,1},{2,18},{18,2},{3,19},{19,3},{4,20},{20... | collective-permute-start | bytes 786440 | tf_op jit(solution)/shard_map/ppermute | solution.py:229
  60.7 4.5 %collective-permute-start.8 = (s32[64]{0:T(128)S(1)}, s32[64]{0:T(128)S(1)}, u32[]{:S(2)}, u32[]{:S(2)}) collective-permute-start(s32[64]{0:T(128)S(1)} %bitcast.27), channel_id=1, source_target_pairs={{0,2},{1,3},{2,0},{3,1},{4,6},{5,7},{6,4},{7,5},{8,10},{9,11},{10,... | collective-permute-start | bytes 776 | tf_op jit(solution)/shard_map/ppermute | solution.py:226
  72.6 2.7 %collective-permute-start.13 = (bf16[2,16,128,128]{3,2,1,0:T(8,128)(2,1)S(1)}, bf16[2,16,128,128]{3,2,1,0:T(8,128)(2,1)S(1)}, u32[]{:S(2)}, u32[]{:S(2)}) collective-permute-start(bf16[2,16,128,128]{3,2,1,0:T(8,128)(2,1)S(1)} %get-tuple-element.39), channel_id=1, source_target_pairs={{0,4},{4,0},{8,12},{12,8},{1,5},{5,1},{9,13},{13,9},{2,6},{6,2},{1... | collective-permute-start | bytes 3145736 | tf_op jit(solution)/shard_map/ppermute | solution.py:215
  72.7 6.9 %collective-permute-start.12 = (bf16[2,16,128,128]{3,2,1,0:T(8,128)(2,1)S(1)}, bf16[2,16,128,128]{3,2,1,0:T(8,128)(2,1)S(1)}, u32[]{:S(2)}, u32[]{:S(2)}) collective-permute-start(bf16[2,16,128,128]{3,2,1,0:T(8,128)(2,1)S(1)} %get-tuple-element.38), channel_id=1, source_target_pairs={{0,4},{4,0},{8,12},{12,8},{1,5},{5,1},{9,13},{13,9},{2,6},{6,2},{1... | collective-permute-start | bytes 3145736 | tf_op jit(solution)/shard_map/ppermute | solution.py:215
  76.1 14.0 %collective-permute-start.14 = (bf16[16,128,128]{2,1,0:T(8,128)(2,1)S(1)}, bf16[16,128,128]{2,1,0:T(8,128)(2,1)S(1)}, u32[]{:S(2)}, u32[]{:S(2)}) collective-permute-start(bf16[16,128,128]{2,1,0:T(8,128)(2,1)S(1)} %bitcast.20), channel_id=1, source_target_pairs={{0,8},{4,12},{8,0},{12,4},{1,9},{5,13},{9,1},{13,5},{2,10},{6,14},... | collective-permute-start | bytes 1572872 | tf_op jit(solution)/shard_map/ppermute | solution.py:219
  76.7 18.5 %collective-permute-start.17 = (bf16[64,2688]{1,0:T(8,128)(2,1)S(1)}, bf16[64,2688]{1,0:T(8,128)(2,1)S(1)}, u32[]{:S(2)}, u32[]{:S(2)}) collective-permute-start(bf16[64,2688]{1,0:T(8,128)(2,1)S(1)} %get-tuple-element.34.half_ref), channel_id=1, source_target_pairs={{0,2},{1,3},{2,0},{3,1},{4,6},{5,7},{6,4},{7,5},{8,10},{9,11},{10,... | collective-permute-start | bytes 1032200 | tf_op jit(solution)/shard_map/ppermute | solution.py:226
  80.3 35.1 %copy-start.4 = (bf16[64,2048]{1,0:T(8,128)(2,1)S(1)}, bf16[64,2048]{1,0:T(8,128)(2,1)}, u32[]{:S(2)}) copy-start(bf16[64,2048]{1,0:T(8,128)(2,1)} %adapter_ref.3) | copy-start | bytes 786436
  90.8 24.6 %collective-permute-start.15 = (bf16[16,128,128]{2,1,0:T(8,128)(2,1)S(1)}, bf16[16,128,128]{2,1,0:T(8,128)(2,1)S(1)}, u32[]{:S(2)}, u32[]{:S(2)}) collective-permute-start(bf16[16,128,128]{2,1,0:T(8,128)(2,1)S(1)} %bitcast.19), channel_id=1, source_target_pairs={{0,8},{4,12},{8,0},{12,4},{1,9},{5,13},{9,1},{13,5},{2,10},{6,14},... | collective-permute-start | bytes 1572872 | tf_op jit(solution)/shard_map/ppermute | solution.py:219
  91.4 24.0 %collective-permute-start.16 = (bf16[16,128,128]{2,1,0:T(8,128)(2,1)S(1)}, bf16[16,128,128]{2,1,0:T(8,128)(2,1)S(1)}, u32[]{:S(2)}, u32[]{:S(2)}) collective-permute-start(bf16[16,128,128]{2,1,0:T(8,128)(2,1)S(1)} %shard_map.102), channel_id=1, source_target_pairs={{0,1},{1,0},{2,3},{3,2},{4,5},{5,4},{6,7},{7,6},{8,9},{9,8},{10,11... | collective-permute-start | bytes 1572872 | tf_op jit(solution)/shard_map/ppermute | solution.py:222
  95.1 18.5 %collective-permute-start.18 = (bf16[64,2688]{1,0:T(8,128)(2,1)S(1)}, bf16[64,2688]{1,0:T(8,128)(2,1)S(1)}, u32[]{:S(2)}, u32[]{:S(2)}) collective-permute-start(bf16[64,2688]{1,0:T(8,128)(2,1)S(1)} %collective-permute-done.17.rest_0_), channel_id=1, source_target_pairs={{0,1},{1,0},{2,3},{3,2},{4,5},{5,4},{6,7},{7,6},{8,9},{9,8},{10,11... | collective-permute-start | bytes 1032200 | tf_op jit(solution)/shard_map/ppermute | solution.py:222

commit v6 on v5

--- a/solution.py
+++ b/solution.py
@@ -15,8 +15,9 @@
 BF16 = jnp.bfloat16
 
 
-def add_blocks(total_ref, tiles_ref, blocks_ref, ids_ref, base, col_blocks, unroll):
+def add_blocks(total_ref, tiles_ref, blocks_ref, ids_ref, base, col_blocks):
     count = blocks_ref.shape[0]
+    unroll = max(u for u in range(1, 9) if count % u == 0)
 
     def one(step, carry):
         for u in range(unroll):
@@ -35,7 +36,7 @@
     for blocks_ref, (offset, shift, start) in zip(blocks, places):
         source = lax.rem(where_ref[0] + (parts - shift), parts)
         base = offset + source * held + start
-        add_blocks(total_ref, tiles_ref, blocks_ref, ids_ref, base, col_blocks, 4)
+        add_blocks(total_ref, tiles_ref, blocks_ref, ids_ref, base, col_blocks)
 
 
 def first_kernel(where_ref, own_ids_ref, ids_ref, own_ref, mate_ref, own_blocks_ref, *rest, **plan):
@@ -46,7 +47,7 @@
     for i in range(row_blocks):
         tiles_ref[i, :tokens, :] = own_ref[:, i * tile:(i + 1) * tile]
         tiles_ref[i, tokens:, :] = mate_ref[:, i * tile:(i + 1) * tile]
-    add_blocks(total_ref, tiles_ref, own_blocks_ref, own_ids_ref, 0, plan["col_blocks"], 8)
+    add_blocks(total_ref, tiles_ref, own_blocks_ref, own_ids_ref, 0, plan["col_blocks"])
     add_arrivals(where_ref, ids_ref, tiles_ref, blocks, total_ref, **plan)
 
 
@@ -65,26 +66,26 @@
             send_own[chip, q] = total_ref[other + q, :tokens, :].astype(BF16)
 
 
-def chip_kernel(where_ref, total_ref, core_ref, leaving_ref, *, first):
+def chip_kernel(where_ref, total_ref, core_ref, leaving_ref, *, first, blocks):
     chips, share, tokens, _ = core_ref.shape
     for d in range(1, chips):
         to_chip = lax.rem(where_ref[2] + d, chips)
         mine = (2 * to_chip + where_ref[1]) * share
-        for q in range(share):
+        for k, q in enumerate(blocks):
             value = total_ref[mine + q, first:first + tokens, :] + core_ref[to_chip, q].astype(F32)
-            leaving_ref[d - 1, q] = value.astype(BF16)
-
-
-def mate_kernel(where_ref, total_ref, core_ref, *rest):
+            leaving_ref[d - 1, k] = value.astype(BF16)
+
+
+def mate_kernel(where_ref, total_ref, core_ref, *rest, blocks):
     pieces, out_ref = rest[:-1], rest[-1]
     _, share, tokens, _ = core_ref.shape
     chip = where_ref[2]
     mine = (2 * chip + where_ref[1]) * share
-    for q in range(share):
+    for k, q in enumerate(blocks):
         value = total_ref[mine + q, tokens:, :] + core_ref[chip, q].astype(F32)
         for piece in pieces:
-            value += piece[q].astype(F32)
-        out_ref[q] = value.astype(BF16)
+            value += piece[k].astype(F32)
+        out_ref[k] = value.astype(BF16)
 
 
 def ordered_sum(own, received, place):
@@ -169,20 +170,29 @@
             add(1 - bit, other_ref, received[count:])
 
 
-def final_kernel(where_ref, rounded_ref, adapter_ref, total_ref, core_ref, *rest):
-    pieces, out_ref = rest[:-1], rest[-1]
+def near_kernel(where_ref, rounded_ref, adapter_ref, total_ref, core_ref, *rest):
+    from_mate, near_ref = rest[:-1], rest[-1]
     _, share, tokens, tile = core_ref.shape
     rank = rounded_ref.shape[0] // 2
     low = rounded_ref[:rank, :].astype(F32).T.astype(BF16)
     chip = where_ref[2]
     mine = (2 * chip + where_ref[1]) * share
+    size = from_mate[0].shape[0]
     for q in range(share):
         value = total_ref[mine + q, :tokens, :] + core_ref[chip, q].astype(F32)
+        value += from_mate[q // size][q % size].astype(F32)
+        extra = jnp.dot(low, adapter_ref[:, q * tile:(q + 1) * tile], preferred_element_type=F32)
+        near_ref[q] = value + adapter_scale * extra
+
+
+def final_kernel(near_ref, *rest):
+    pieces, out_ref = rest[:-1], rest[-1]
+    share, _, tile = near_ref.shape
+    for q in range(share):
+        value = near_ref[q]
         for piece in pieces:
             value += piece[q].astype(F32)
-        cols = slice(q * tile, (q + 1) * tile)
-        extra = jnp.dot(low, adapter_ref[:, cols], preferred_element_type=F32)
-        out_ref[:, cols] = (value + adapter_scale * extra).astype(BF16)
+        out_ref[:, q * tile:(q + 1) * tile] = value.astype(BF16)
 
 
 def call(kernel, outs, scalars, arrays, aliases=None):
@@ -246,22 +256,23 @@
         ids = block_ids[0]
         labels = forget_labels[None, :]
 
-        soon = core_swap(ids)
         far_ids = [group_shift(ids, d) for d in range(1, group)]
         all_ids = far_ids[0] if group == 2 else jnp.concatenate(far_ids)
         held = slots // n_parts
-        sizes = [held * k // 32 for k in (12, 12, 8)]
+        sizes = [held * k // 32 for k in (16, 10, 6)]
         starts = [sum(sizes[:k]) for k in range(len(sizes))]
 
         def leaving_chunk(k):
-            chunk = lax.dynamic_slice_in_dim(blocks, part * held + starts[k], sizes[k], axis=0)
-            return chunk if k == 0 else after(chunk, soon)
-
+            return lax.dynamic_slice_in_dim(blocks, part * held + starts[k], sizes[k], axis=0)
+
+        first_chunk = leaving_chunk(0)
+        soon = core_swap(after(ids, first_chunk))
+        leaving_chunks = [first_chunk] + [after(leaving_chunk(k), soon) for k in range(1, len(starts))]
         direct = [
-            (group_shift(leaving_chunk(k), d), ((d - 1) * slots, 0, starts[k]))
+            (group_shift(leaving_chunks[k], d), ((d - 1) * slots, 0, starts[k]))
             for d in range(1, group) for k in range(len(starts))
         ]
-        mate_activations = mate_swap(after(activations, soon))
+        mate_activations = mate_swap(activations)
 
         (both,) = call(
             low_rank_kernel, (jax.ShapeDtypeStruct((2 * rank, tokens), F32),), (),
@@ -305,7 +316,6 @@
         half_grads, other_grads = call(
             pair_grad_kernel, (half_shape, half_shape), (where,), (rounded, activations, mate_activations, pack, mate_pack),
         )
-        half_grads = after(half_grads, direct[-1][0])
         far_grads = [group_shift(half_grads, d) for d in range(1, group)]
 
         (total,) = call(
@@ -318,33 +328,39 @@
             (after(where, half_grads), all_ids), (on_chip(tiles), on_chip(total)) + values(last), {3: 0},
         )
 
-        def for_chips(first, core_got, where, *needed):
+        def for_chips(first, core_got, where, blocks):
             (leaving,) = call(
-                functools.partial(chip_kernel, first=first),
-                (pltpu.VMEM((chips - 1, share, tokens, tile), BF16),), (where,), (on_chip(total), core_got),
+                functools.partial(chip_kernel, first=first, blocks=blocks),
+                (pltpu.VMEM((chips - 1, len(blocks), tokens, tile), BF16),),
+                (where,), (on_chip(total), core_got),
             )
-            if needed:
-                leaving = after(leaving, *needed)
             return [chip_shift(leaving[d - 1], d) for d in range(1, chips)]
 
         core_mate = core_swap(send_mate)
         core_own = core_swap(send_own)
-        mate_pieces = for_chips(tokens, core_mate, where)
-        (mate_total,) = call(
-            mate_kernel, (pltpu.VMEM((share, tokens, tile), BF16),), (where,),
-            (on_chip(total), core_mate) + tuple(mate_pieces),
-        )
-        from_mate = mate_swap(mate_total)
-        own_pieces = for_chips(0, core_own, where, mate_total)
-        from_mate_grads = [mate_swap(value) for value in far_grads]
+        halves = [tuple(range(share // 2)), tuple(range(share // 2, share))]
+        mate_pieces = [for_chips(tokens, core_mate, where, part_blocks) for part_blocks in halves]
+        mate_totals = []
+        for part_blocks, got in zip(halves, mate_pieces):
+            mate_totals += call(
+                functools.partial(mate_kernel, blocks=part_blocks),
+                (pltpu.VMEM((len(part_blocks), tokens, tile), BF16),), (where,),
+                (on_chip(total), core_mate) + tuple(got),
+            )
+        from_mate = [mate_swap(value) for value in mate_totals]
+        own_pieces = for_chips(0, core_own, after(where, mate_totals[0]), tuple(range(share)))
+        from_mate_grads = [mate_swap(after(value, *from_mate)) for value in far_grads]
         in_grad, out_grad = call(
             grad_sum_kernel,
             (jax.ShapeDtypeStruct((rank, shard_rows), F32), jax.ShapeDtypeStruct((rank, feats), F32)),
-            (where,), (half_grads, other_grads) + tuple(far_grads) + tuple(after(value, mate_total) for value in from_mate_grads),
+            (where,), (half_grads, other_grads) + tuple(far_grads) + tuple(from_mate_grads),
+        )
+        (near,) = call(
+            near_kernel, (pltpu.VMEM((share, tokens, tile), F32),), (where,),
+            (rounded, output_adapter, on_chip(total), core_own) + tuple(from_mate),
         )
         (projected,) = call(
-            final_kernel, (jax.ShapeDtypeStruct((tokens, feats), BF16),), (where,),
-            (rounded, output_adapter, on_chip(total), core_own) + tuple(own_pieces) + (from_mate,),
+            final_kernel, (jax.ShapeDtypeStruct((tokens, feats), BF16),), (), (on_chip(near),) + tuple(own_pieces),
         )
         return projected, in_grad.T, out_grad
 

time: 118 us -> 108 us (0.915)
  waiting for transfers between devices: 66.2 us -> 53.6 us
  starting transfers between devices: 24.4 us -> 26.7 us
    ppermute x4 -> x5, waiting for transfers between devices: 18.5 us -> 12.6 us  [mate_swap(): return lax.ppermute(value, 'dp', [(i, i ^ 1) for i in range(n_dp)])]
    ppermute x5, waiting for transfers between devices: 34.8 us -> 31.7 us  [group_shift(): return lax.ppermute(value, 'dp', pairs)]
    ppermute x3 -> x4, waiting for transfers between devices: 9.82 us -> 7.19 us  [chip_shift(): return lax.ppermute(value, 'row', pairs)]
    ppermute x4 -> x5, starting transfers between devices: 5.42 us -> 7.75 us  [mate_swap(): return lax.ppermute(value, 'dp', [(i, i ^ 1) for i in range(n_dp)])]
    ppermute x3 -> x4, starting transfers between devices: 2.76 us -> 4.31 us  [chip_shift(): return lax.ppermute(value, 'row', pairs)]
    unnamed x18 -> x20, local copies, waits for them, and re-layouts: 2.64 us -> 3.68 us
    dynamic_slice x2 -> x3, local copies, waits for them, and re-layouts: 3.88 us -> 3.5 us  [leaving_chunk(): lax.dynamic_slice_in_dim(blocks, part * held + starts[k], sizes[k], axis=0)]
    pallas_call x11 -> x14, Pallas kernels: 19.2 us -> 19.4 us  [call(): pl.pallas_call(kernel, out_shape=outs, in_specs=[smem] * len(scalars) + [...]
  transfers between devices with their start and end apart: 19 -> 21, of which waited for: 8 -> 11; matrix products, arithmetic and copies ran while one was open for 3% -> 3% of each run, Pallas kernels for 14% -> 15%
where the time goes in v6:
time: 108 us
  waiting for transfers between devices  53.6 us (50%)
  starting transfers between devices  26.7 us (25%)
  Pallas kernels  19.4 us (18%)
  local copies, waits for them, and re-layouts  7.26 us (7%)
    ppermute x5, waiting for transfers between devices, group_shift(): return lax.ppermute(value, 'dp', pairs)  31.7 us
    pallas_call x14, Pallas kernels, call(): pl.pallas_call(kernel, out_shape=outs, in_specs=[smem] * len(scalars) + [...  19.4 us
    ppermute x5, waiting for transfers between devices, mate_swap(): return lax.ppermute(value, 'dp', [(i, i ^ 1) for i in range(n_dp)])  12.6 us
    ppermute x5, starting transfers between devices, group_shift(): return lax.ppermute(value, 'dp', pairs)  10.7 us
    ppermute x5, starting transfers between devices, mate_swap(): return lax.ppermute(value, 'dp', [(i, i ^ 1) for i in range(n_dp)])  7.75 us
    ppermute x4, waiting for transfers between devices, chip_shift(): return lax.ppermute(value, 'row', pairs)  7.19 us
    ppermute x4, starting transfers between devices, chip_shift(): return lax.ppermute(value, 'row', pairs)  4.31 us
    unnamed x20, local copies, waits for them, and re-layouts  3.68 us
  transfers between devices with their start and end apart: 21, of which 11 were waited for; matrix products, arithmetic and copies ran while one was open for 3% of the time, Pallas kernels for 15%

profile of v6, /device:TPU:0, one launch (start us, length us, event | category | flops | bytes accessed | tf_op | source)
XLA Modules:
  0.0 107.8 jit_solution(15980052249433055994)
XLA Ops:
  0.7 3.1 %collective-permute-start = (bf16[128,3328]{1,0:T(8,128)(2,1)}, bf16[128,3328]{1,0:T(8,128)(2,1)}, u32[]{:S(2)}, u32[]{:S(2)}) collective-permute-start(bf16[128,3328]{1,0:T(8,128)(2,1)} %acts_ref.3), channel_id=1, source_target_pairs={{0,1},{1,0},{2,3},{3,2},{4,5},{5,4},{6,7},{7,6},{8,9},{9,8},{10,11... | collective-permute-start | bytes 2555912 | tf_op jit(solution)/shard_map/ppermute | solution.py:232
  3.7 1.1 dynamic-slice_bitcast_fusion
  4.8 2.7 %collective-permute-start.1 = (bf16[16,128,128]{2,1,0:T(8,128)(2,1)S(1)}, bf16[16,128,128]{2,1,0:T(8,128)(2,1)}, u32[]{:S(2)}, u32[]{:S(2)}) collective-permute-start(bf16[16,128,128]{2,1,0:T(8,128)(2,1)S(1)} %dynamic-slice_bitcast_fusion), channel_id=1, source_target_pairs={{0,2},{1,3},{2,0},{3,1},{4,6},{5,7},{6,4},{7,5},{8,10},{9,11},{10,... | collective-permute-start | bytes 1572872 | tf_op jit(solution)/shard_map/ppermute | solution.py:236
  7.5 1.7 %dynamic-slice_bitcast_fusion.1 = bf16[10,128,128]{2,1,0:T(8,128)(2,1)} fusion(bf16[1,64,128,128]{3,2,1,0:T(8,128)(2,1)} %param.10, s32[]{:T(128)S(6)} %select_n.10), kind=kLoop, calls=%fused_computation.1 | loop fusion | bytes 655364 | tf_op jit(solution)/shard_map/dynamic_slice | solution.py:266
  9.5 25.0 %collective-permute-done.1.rest_0_ = bf16[16,128,128]{2,1,0:T(8,128)(2,1)} collective-permute-done((bf16[16,128,128]{2,1,0:T(8,128)(2,1)S(1)}, bf16[16,128,128]{2,1,0:T(8,128)(2,1)}, u32[]{:S(2)}, u32[]{:S(2)}) %collective-permute-start.1) | collective-permute-done | bytes 524320 | tf_op jit(solution)/shard_map/ppermute | solution.py:236
  34.6 1.5 %collective-permute-start.9 = (bf16[16,128,128]{2,1,0:T(8,128)(2,1)}, bf16[16,128,128]{2,1,0:T(8,128)(2,1)}, u32[]{:S(2)}, u32[]{:S(2)}) collective-permute-start(bf16[16,128,128]{2,1,0:T(8,128)(2,1)} %collective-permute-done.1.rest_0_), channel_id=1, source_target_pairs={{0,16},{16,0},{1,17},{17,1},{2,18},{18,2},{3,19},{19,3},{4,20},{20... | collective-permute-start | bytes 1572872 | tf_op jit(solution)/shard_map/ppermute | solution.py:239
  36.1 1.0 copy-done.2
  38.1 1.0 copy-done.6
  41.2 3.5 %collective-permute-start.8 = (bf16[6,128,128]{2,1,0:T(8,128)(2,1)}, bf16[6,128,128]{2,1,0:T(8,128)(2,1)}, u32[]{:S(2)}, u32[]{:S(2)}) collective-permute-start(bf16[6,128,128]{2,1,0:T(8,128)(2,1)} %dynamic-slice_bitcast_fusion.2), channel_id=1, source_target_pairs={{0,2},{1,3},{2,0},{3,1},{4,6},{5,7},{6,4},{7,5},{8,10},{9,11},{10,... | collective-permute-start | bytes 589832 | tf_op jit(solution)/shard_map/ppermute | solution.py:236
  44.7 1.6 %collective-permute-start.5 = (f32[128,128]{1,0:T(8,128)S(1)}, f32[128,128]{1,0:T(8,128)}, u32[]{:S(2)}, u32[]{:S(2)}) collective-permute-start(f32[128,128]{1,0:T(8,128)S(1)} %add.23.both_ref), channel_id=1, source_target_pairs={{0,8},{4,12},{8,0},{12,4},{1,9},{5,13},{9,1},{13,5},{2,10},{6,14},... | collective-permute-start | bytes 196616 | tf_op jit(solution)/shard_map/ppermute | solution.py:229
  46.3 1.3 %collective-permute-start.10 = (bf16[10,128,128]{2,1,0:T(8,128)(2,1)}, bf16[10,128,128]{2,1,0:T(8,128)(2,1)}, u32[]{:S(2)}, u32[]{:S(2)}) collective-permute-start(bf16[10,128,128]{2,1,0:T(8,128)(2,1)} %collective-permute-done.4.rest_1_), channel_id=1, source_target_pairs={{0,16},{16,0},{1,17},{17,1},{2,18},{18,2},{3,19},{19,3},{4,20},{20... | collective-permute-start | bytes 983048 | tf_op jit(solution)/shard_map/ppermute | solution.py:239
  47.7 4.4 %shard_map.94 = (f32[65,256,128]{2,1,0:T(8,128)S(1)}, bf16[26,256,128]{2,1,0:T(8,128)(2,1)S(1)}) custom-call(s32[5]{0:T(128)S(1)} %stack.23.where_ref, s32[64]{0:T(128)S(1)} %bitcast.27, s32[64]{0:T(128)S(1)} %bitcast.28, bf16[128,3328]{1,0:T(8,128)(2,1)S(1)} %copy-done, bf16[128,3328]{1,0:T(8,128)(2,1)} %collective-permute-done.mate_ref.mate_acts_ref, ...), custom_call_target="tpu_custom_call" | custom-call | tf_op jit(solution)/shard_map/pallas_call | solution.py:201
  52.1 1.1 shard_map.96
  53.3 1.5 %collective-permute-done.8.rest_2_ = bf16[6,128,128]{2,1,0:T(8,128)(2,1)} collective-permute-done((bf16[6,128,128]{2,1,0:T(8,128)(2,1)}, bf16[6,128,128]{2,1,0:T(8,128)(2,1)}, u32[]{:S(2)}, u32[]{:S(2)}) %collective-permute-start.8) | collective-permute-done | bytes 196640 | tf_op jit(solution)/shard_map/ppermute | solution.py:236
  55.3 1.7 %collective-permute-start.7 = (s32[64]{0:T(128)S(1)}, s32[64]{0:T(128)S(1)}, u32[]{:S(2)}, u32[]{:S(2)}) collective-permute-start(s32[64]{0:T(128)S(1)} %bitcast.29), channel_id=1, source_target_pairs={{0,2},{1,3},{2,0},{3,1},{4,6},{5,7},{6,4},{7,5},{8,10},{9,11},{10,... | collective-permute-start | bytes 776 | tf_op jit(solution)/shard_map/ppermute | solution.py:236
  57.0 2.7 %collective-permute-done.7.ids_ref = s32[64]{0:T(128)S(1)} collective-permute-done((s32[64]{0:T(128)S(1)}, s32[64]{0:T(128)S(1)}, u32[]{:S(2)}, u32[]{:S(2)}) %collective-permute-start.7) | collective-permute-done | bytes 288 | tf_op jit(solution)/shard_map/ppermute | solution.py:236
  59.7 3.9 %shard_map.98.old_ref = f32[65,256,128]{2,1,0:T(8,128)S(1)} custom-call(s32[5]{0:T(128)S(1)} %stack.23.where_ref, s32[64]{0:T(128)S(1)} %collective-permute-done.7.ids_ref, bf16[26,256,128]{2,1,0:T(8,128)(2,1)S(1)} %get-tuple-element.33.tiles_ref, f32[65,256,128]{2,1,0:T(8,128)S(1)} %get-tuple-element.23.old_ref, ...), custom_call_target="tpu_custom_call", output_to_operand_aliasing={{}: (3, {})} | custom-call | tf_op jit(solution)/shard_map/pallas_call | solution.py:201
  63.6 1.6 %shard_map.97 = (bf16[64,2688]{1,0:T(8,128)(2,1)S(1)}, bf16[64,2688]{1,0:T(8,128)(2,1)S(1)}) custom-call(s32[5]{0:T(128)S(1)} %stack.23.where_ref, bf16[128,128]{1,0:T(8,128)(2,1)S(1)} %get-tuple-element.29.rounded_ref, bf16[128,3328]{1,0:T(8,128)(2,1)S(1)} %copy-done, bf16[128,3328]{1,0:T(8,128)(2,1)} %collective-permute-done.mate_ref.mate_acts_ref, ...), custom_call_target="tpu_custom_call" | custom-call | tf_op jit(solution)/shard_map/pallas_call | solution.py:201
  65.3 1.0 shard_map.99
  66.9 2.1 %collective-permute-done.13.core_ref = bf16[2,16,128,128]{3,2,1,0:T(8,128)(2,1)S(1)} collective-permute-done((bf16[2,16,128,128]{3,2,1,0:T(8,128)(2,1)S(1)}, bf16[2,16,128,128]{3,2,1,0:T(8,128)(2,1)S(1)}, u32[]{:S(2)}, u32[]{:S(2)}) %collective-permute-start.13) | collective-permute-done | bytes 1048608 | tf_op jit(solution)/shard_map/ppermute | solution.py:225
  69.6 1.6 %collective-permute-start.14 = (bf16[8,128,128]{2,1,0:T(8,128)(2,1)S(1)}, bf16[8,128,128]{2,1,0:T(8,128)(2,1)S(1)}, u32[]{:S(2)}, u32[]{:S(2)}) collective-permute-start(bf16[8,128,128]{2,1,0:T(8,128)(2,1)S(1)} %bitcast.23), channel_id=1, source_target_pairs={{0,8},{4,12},{8,0},{12,4},{1,9},{5,13},{9,1},{13,5},{2,10},{6,14},... | collective-permute-start | bytes 786440 | tf_op jit(solution)/shard_map/ppermute | solution.py:229
  72.4 2.4 %collective-permute-start.19 = (bf16[64,2688]{1,0:T(8,128)(2,1)S(1)}, bf16[64,2688]{1,0:T(8,128)(2,1)S(1)}, u32[]{:S(2)}, u32[]{:S(2)}) collective-permute-start(bf16[64,2688]{1,0:T(8,128)(2,1)S(1)} %get-tuple-element.31.half_ref), channel_id=1, source_target_pairs={{0,2},{1,3},{2,0},{3,1},{4,6},{5,7},{6,4},{7,5},{8,10},{9,11},{10,... | collective-permute-start | bytes 1032200 | tf_op jit(solution)/shard_map/ppermute | solution.py:236
  74.8 4.0 %collective-permute-done.14.rest_0_ = bf16[8,128,128]{2,1,0:T(8,128)(2,1)S(1)} collective-permute-done((bf16[8,128,128]{2,1,0:T(8,128)(2,1)S(1)}, bf16[8,128,128]{2,1,0:T(8,128)(2,1)S(1)}, u32[]{:S(2)}, u32[]{:S(2)}) %collective-permute-start.14) | collective-permute-done | bytes 262176 | tf_op jit(solution)/shard_map/ppermute | solution.py:229
  79.5 2.3 %collective-permute-start.15 = (bf16[8,128,128]{2,1,0:T(8,128)(2,1)S(1)}, bf16[8,128,128]{2,1,0:T(8,128)(2,1)S(1)}, u32[]{:S(2)}, u32[]{:S(2)}) collective-permute-start(bf16[8,128,128]{2,1,0:T(8,128)(2,1)S(1)} %shard_map.101), channel_id=1, source_target_pairs={{0,1},{1,0},{2,3},{3,2},{4,5},{5,4},{6,7},{7,6},{8,9},{9,8},{10,11... | collective-permute-start | bytes 786440 | tf_op jit(solution)/shard_map/ppermute | solution.py:232
  81.8 1.9 %collective-permute-done.16.rest_0_ = bf16[8,128,128]{2,1,0:T(8,128)(2,1)S(1)} collective-permute-done((bf16[8,128,128]{2,1,0:T(8,128)(2,1)S(1)}, bf16[8,128,128]{2,1,0:T(8,128)(2,1)S(1)}, u32[]{:S(2)}, u32[]{:S(2)}) %collective-permute-start.16) | collective-permute-done | bytes 262176 | tf_op jit(solution)/shard_map/ppermute | solution.py:229
  84.3 2.3 %collective-permute-start.17 = (bf16[8,128,128]{2,1,0:T(8,128)(2,1)S(1)}, bf16[8,128,128]{2,1,0:T(8,128)(2,1)S(1)}, u32[]{:S(2)}, u32[]{:S(2)}) collective-permute-start(bf16[8,128,128]{2,1,0:T(8,128)(2,1)S(1)} %shard_map.103), channel_id=1, source_target_pairs={{0,1},{1,0},{2,3},{3,2},{4,5},{5,4},{6,7},{7,6},{8,9},{9,8},{10,11... | collective-permute-start | bytes 786440 | tf_op jit(solution)/shard_map/ppermute | solution.py:232
  87.9 2.4 %collective-permute-done.19.rest_0_ = bf16[64,2688]{1,0:T(8,128)(2,1)S(1)} collective-permute-done((bf16[64,2688]{1,0:T(8,128)(2,1)S(1)}, bf16[64,2688]{1,0:T(8,128)(2,1)S(1)}, u32[]{:S(2)}, u32[]{:S(2)}) %collective-permute-start.19) | collective-permute-done | bytes 344096 | tf_op jit(solution)/shard_map/ppermute | solution.py:236
  90.3 4.0 %collective-permute-done.15.rest_0_ = bf16[8,128,128]{2,1,0:T(8,128)(2,1)S(1)} collective-permute-done((bf16[8,128,128]{2,1,0:T(8,128)(2,1)S(1)}, bf16[8,128,128]{2,1,0:T(8,128)(2,1)S(1)}, u32[]{:S(2)}, u32[]{:S(2)}) %collective-permute-start.15) | collective-permute-done | bytes 262176 | tf_op jit(solution)/shard_map/ppermute | solution.py:232
  94.3 3.6 %collective-permute-done.17.rest_1_ = bf16[8,128,128]{2,1,0:T(8,128)(2,1)S(1)} collective-permute-done((bf16[8,128,128]{2,1,0:T(8,128)(2,1)S(1)}, bf16[8,128,128]{2,1,0:T(8,128)(2,1)S(1)}, u32[]{:S(2)}, u32[]{:S(2)}) %collective-permute-start.17) | collective-permute-done | bytes 262176 | tf_op jit(solution)/shard_map/ppermute | solution.py:232
  98.9 1.3 %collective-permute-done.18.rest_0_ = bf16[16,128,128]{2,1,0:T(8,128)(2,1)S(1)} collective-permute-done((bf16[16,128,128]{2,1,0:T(8,128)(2,1)S(1)}, bf16[16,128,128]{2,1,0:T(8,128)(2,1)S(1)}, u32[]{:S(2)}, u32[]{:S(2)}) %collective-permute-start.18) | collective-permute-done | bytes 524320 | tf_op jit(solution)/shard_map/ppermute | solution.py:229
  101.1 5.0 %collective-permute-done.20.rest_1_ = bf16[64,2688]{1,0:T(8,128)(2,1)S(1)} collective-permute-done((bf16[64,2688]{1,0:T(8,128)(2,1)S(1)}, bf16[64,2688]{1,0:T(8,128)(2,1)S(1)}, u32[]{:S(2)}, u32[]{:S(2)}) %collective-permute-start.20) | collective-permute-done | bytes 344096 | tf_op jit(solution)/shard_map/ppermute | solution.py:232
  106.1 1.8 %shard_map.107 = (f32[64,3328]{1,0:T(8,128)}, f32[64,2048]{1,0:T(8,128)}) custom-call(s32[5]{0:T(128)S(1)} %stack.23.where_ref, bf16[64,2688]{1,0:T(8,128)(2,1)S(1)} %get-tuple-element.31.half_ref, bf16[64,2688]{1,0:T(8,128)(2,1)S(1)} %get-tuple-element.39.other_ref, bf16[64,2688]{1,0:T(8,128)(2,1)S(1)} %collective-permute-done.19.rest_0_, ...), custom_call_target="tpu_custom_call" | custom-call | tf_op jit(solution)/shard_map/pallas_call | solution.py:201
  (49 shorter events, 10.8 us)
Async XLA Ops:
  0.6 35.5 %copy-start = (bf16[128,3328]{1,0:T(8,128)(2,1)S(1)}, bf16[128,3328]{1,0:T(8,128)(2,1)}, u32[]{:S(2)}) copy-start(bf16[128,3328]{1,0:T(8,128)(2,1)} %acts_ref.3) | copy-start | bytes 2555908
  0.6 39.8 %copy-start.1 = (bf16[1,64,128,128]{3,2,1,0:T(8,128)(2,1)S(1)}, bf16[1,64,128,128]{3,2,1,0:T(8,128)(2,1)}, u32[]{:S(2)}) copy-start(bf16[1,64,128,128]{3,2,1,0:T(8,128)(2,1)} %param.10) | copy-start | bytes 6291460
  0.7 47.0 %collective-permute-start = (bf16[128,3328]{1,0:T(8,128)(2,1)}, bf16[128,3328]{1,0:T(8,128)(2,1)}, u32[]{:S(2)}, u32[]{:S(2)}) collective-permute-start(bf16[128,3328]{1,0:T(8,128)(2,1)} %acts_ref.3), channel_id=1, source_target_pairs={{0,1},{1,0},{2,3},{3,2},{4,5},{5,4},{6,7},{7,6},{8,9},{9,8},{10,11... | collective-permute-start | bytes 2555912 | tf_op jit(solution)/shard_map/ppermute | solution.py:232
  4.8 29.8 %collective-permute-start.1 = (bf16[16,128,128]{2,1,0:T(8,128)(2,1)S(1)}, bf16[16,128,128]{2,1,0:T(8,128)(2,1)}, u32[]{:S(2)}, u32[]{:S(2)}) collective-permute-start(bf16[16,128,128]{2,1,0:T(8,128)(2,1)S(1)} %dynamic-slice_bitcast_fusion), channel_id=1, source_target_pairs={{0,2},{1,3},{2,0},{3,1},{4,6},{5,7},{6,4},{7,5},{8,10},{9,11},{10,... | collective-permute-start | bytes 1572872 | tf_op jit(solution)/shard_map/ppermute | solution.py:236
  7.5 1.7 %collective-permute-start.3 = (s32[64]{0:T(128)}, s32[64]{0:T(128)S(1)}, u32[]{:S(2)}, u32[]{:S(2)}) collective-permute-start(s32[64]{0:T(128)} %bitcast.26), channel_id=1, source_target_pairs={{0,4},{4,0},{8,12},{12,8},{1,5},{5,1},{9,13},{13,9},{2,6},{6,2},{1... | collective-permute-start | bytes 776 | tf_op jit(solution)/shard_map/ppermute | solution.py:225
  9.2 35.5 %collective-permute-start.4 = (bf16[10,128,128]{2,1,0:T(8,128)(2,1)}, bf16[10,128,128]{2,1,0:T(8,128)(2,1)}, u32[]{:S(2)}, u32[]{:S(2)}) collective-permute-start(bf16[10,128,128]{2,1,0:T(8,128)(2,1)} %dynamic-slice_bitcast_fusion.1), channel_id=1, source_target_pairs={{0,2},{1,3},{2,0},{3,1},{4,6},{5,7},{6,4},{7,5},{8,10},{9,11},{10,... | collective-permute-start | bytes 983048 | tf_op jit(solution)/shard_map/ppermute | solution.py:236
  34.6 25.1 %collective-permute-start.9 = (bf16[16,128,128]{2,1,0:T(8,128)(2,1)}, bf16[16,128,128]{2,1,0:T(8,128)(2,1)}, u32[]{:S(2)}, u32[]{:S(2)}) collective-permute-start(bf16[16,128,128]{2,1,0:T(8,128)(2,1)} %collective-permute-done.1.rest_0_), channel_id=1, source_target_pairs={{0,16},{16,0},{1,17},{17,1},{2,18},{18,2},{3,19},{19,3},{4,20},{20... | collective-permute-start | bytes 1572872 | tf_op jit(solution)/shard_map/ppermute | solution.py:239
  36.1 1.0 copy-start.2
  37.1 0.9 copy-start.4
  38.1 1.0 copy-start.6
  39.1 0.7 copy-start.7
  39.8 7.9 %copy-start.9 = (s32[1,64]{1,0:T(1,128)S(1)}, s32[1,64]{1,0:T(1,128)}, u32[]{:S(2)}) copy-start(s32[1,64]{1,0:T(1,128)} %param.11) | copy-start | bytes 772
  40.4 4.3 %collective-permute-start.2 = (f32[128,128]{1,0:T(8,128)S(1)}, f32[128,128]{1,0:T(8,128)S(1)}, u32[]{:S(2)}, u32[]{:S(2)}) collective-permute-start(f32[128,128]{1,0:T(8,128)S(1)} %shard_map.95), channel_id=1, source_target_pairs={{0,4},{4,0},{8,12},{12,8},{1,5},{5,1},{9,13},{13,9},{2,6},{6,2},{1... | collective-permute-start | bytes 196616 | tf_op jit(solution)/shard_map/ppermute | solution.py:225
  41.2 11.0 %copy-start.3 = (bf16[128,2048]{1,0:T(8,128)(2,1)S(1)}, bf16[128,2048]{1,0:T(8,128)(2,1)}, u32[]{:S(2)}) copy-start(bf16[128,2048]{1,0:T(8,128)(2,1)} %cot_ref.3) | copy-start | bytes 1572868
  41.2 11.0 %copy-start.8 = (s32[128]{0:T(128)S(1)}, s32[128]{0:T(128)}, u32[]{:S(2)}) copy-start(s32[128]{0:T(128)} %param.9) | copy-start | bytes 1540
  41.2 13.6 %collective-permute-start.8 = (bf16[6,128,128]{2,1,0:T(8,128)(2,1)}, bf16[6,128,128]{2,1,0:T(8,128)(2,1)}, u32[]{:S(2)}, u32[]{:S(2)}) collective-permute-start(bf16[6,128,128]{2,1,0:T(8,128)(2,1)} %dynamic-slice_bitcast_fusion.2), channel_id=1, source_target_pairs={{0,2},{1,3},{2,0},{3,1},{4,6},{5,7},{6,4},{7,5},{8,10},{9,11},{10,... | collective-permute-start | bytes 589832 | tf_op jit(solution)/shard_map/ppermute | solution.py:236
  44.7 7.4 %collective-permute-start.5 = (f32[128,128]{1,0:T(8,128)S(1)}, f32[128,128]{1,0:T(8,128)}, u32[]{:S(2)}, u32[]{:S(2)}) collective-permute-start(f32[128,128]{1,0:T(8,128)S(1)} %add.23.both_ref), channel_id=1, source_target_pairs={{0,8},{4,12},{8,0},{12,4},{1,9},{5,13},{9,1},{13,5},{2,10},{6,14},... | collective-permute-start | bytes 196616 | tf_op jit(solution)/shard_map/ppermute | solution.py:229
  46.3 13.4 %collective-permute-start.10 = (bf16[10,128,128]{2,1,0:T(8,128)(2,1)}, bf16[10,128,128]{2,1,0:T(8,128)(2,1)}, u32[]{:S(2)}, u32[]{:S(2)}) collective-permute-start(bf16[10,128,128]{2,1,0:T(8,128)(2,1)} %collective-permute-done.4.rest_1_), channel_id=1, source_target_pairs={{0,16},{16,0},{1,17},{17,1},{2,18},{18,2},{3,19},{19,3},{4,20},{20... | collective-permute-start | bytes 983048 | tf_op jit(solution)/shard_map/ppermute | solution.py:239
  53.2 10.4 %collective-permute-start.6 = (bf16[64,2176]{1,0:T(8,128)(2,1)S(1)}, bf16[64,2176]{1,0:T(8,128)(2,1)S(1)}, u32[]{:S(2)}, u32[]{:S(2)}) collective-permute-start(bf16[64,2176]{1,0:T(8,128)(2,1)S(1)} %get-tuple-element.30.pack_ref), channel_id=1, source_target_pairs={{0,1},{1,0},{2,3},{3,2},{4,5},{5,4},{6,7},{7,6},{8,9},{9,8},{10,11... | collective-permute-start | bytes 835592 | tf_op jit(solution)/shard_map/ppermute | solution.py:232
  54.8 10.5 %collective-permute-start.11 = (bf16[6,128,128]{2,1,0:T(8,128)(2,1)}, bf16[6,128,128]{2,1,0:T(8,128)(2,1)S(1)}, u32[]{:S(2)}, u32[]{:S(2)}) collective-permute-start(bf16[6,128,128]{2,1,0:T(8,128)(2,1)} %collective-permute-done.8.rest_2_), channel_id=1, source_target_pairs={{0,16},{16,0},{1,17},{17,1},{2,18},{18,2},{3,19},{19,3},{4,20},{20... | collective-permute-start | bytes 589832 | tf_op jit(solution)/shard_map/ppermute | solution.py:239
  55.3 4.4 %collective-permute-start.7 = (s32[64]{0:T(128)S(1)}, s32[64]{0:T(128)S(1)}, u32[]{:S(2)}, u32[]{:S(2)}) collective-permute-start(s32[64]{0:T(128)S(1)} %bitcast.29), channel_id=1, source_target_pairs={{0,2},{1,3},{2,0},{3,1},{4,6},{5,7},{6,4},{7,5},{8,10},{9,11},{10,... | collective-permute-start | bytes 776 | tf_op jit(solution)/shard_map/ppermute | solution.py:236
  66.3 2.7 %collective-permute-start.13 = (bf16[2,16,128,128]{3,2,1,0:T(8,128)(2,1)S(1)}, bf16[2,16,128,128]{3,2,1,0:T(8,128)(2,1)S(1)}, u32[]{:S(2)}, u32[]{:S(2)}) collective-permute-start(bf16[2,16,128,128]{3,2,1,0:T(8,128)(2,1)S(1)} %get-tuple-element.37), channel_id=1, source_target_pairs={{0,4},{4,0},{8,12},{12,8},{1,5},{5,1},{9,13},{13,9},{2,6},{6,2},{1... | collective-permute-start | bytes 3145736 | tf_op jit(solution)/shard_map/ppermute | solution.py:225
  66.4 20.2 %collective-permute-start.12 = (bf16[2,16,128,128]{3,2,1,0:T(8,128)(2,1)S(1)}, bf16[2,16,128,128]{3,2,1,0:T(8,128)(2,1)S(1)}, u32[]{:S(2)}, u32[]{:S(2)}) collective-permute-start(bf16[2,16,128,128]{3,2,1,0:T(8,128)(2,1)S(1)} %get-tuple-element.36), channel_id=1, source_target_pairs={{0,4},{4,0},{8,12},{12,8},{1,5},{5,1},{9,13},{13,9},{2,6},{6,2},{1... | collective-permute-start | bytes 3145736 | tf_op jit(solution)/shard_map/ppermute | solution.py:225
  69.6 9.2 %collective-permute-start.14 = (bf16[8,128,128]{2,1,0:T(8,128)(2,1)S(1)}, bf16[8,128,128]{2,1,0:T(8,128)(2,1)S(1)}, u32[]{:S(2)}, u32[]{:S(2)}) collective-permute-start(bf16[8,128,128]{2,1,0:T(8,128)(2,1)S(1)} %bitcast.23), channel_id=1, source_target_pairs={{0,8},{4,12},{8,0},{12,4},{1,9},{5,13},{9,1},{13,5},{2,10},{6,14},... | collective-permute-start | bytes 786440 | tf_op jit(solution)/shard_map/ppermute | solution.py:229
  71.8 11.9 %collective-permute-start.16 = (bf16[8,128,128]{2,1,0:T(8,128)(2,1)S(1)}, bf16[8,128,128]{2,1,0:T(8,128)(2,1)S(1)}, u32[]{:S(2)}, u32[]{:S(2)}) collective-permute-start(bf16[8,128,128]{2,1,0:T(8,128)(2,1)S(1)} %bitcast.22), channel_id=1, source_target_pairs={{0,8},{4,12},{8,0},{12,4},{1,9},{5,13},{9,1},{13,5},{2,10},{6,14},... | collective-permute-start | bytes 786440 | tf_op jit(solution)/shard_map/ppermute | solution.py:229
  72.4 17.9 %collective-permute-start.19 = (bf16[64,2688]{1,0:T(8,128)(2,1)S(1)}, bf16[64,2688]{1,0:T(8,128)(2,1)S(1)}, u32[]{:S(2)}, u32[]{:S(2)}) collective-permute-start(bf16[64,2688]{1,0:T(8,128)(2,1)S(1)} %get-tuple-element.31.half_ref), channel_id=1, source_target_pairs={{0,2},{1,3},{2,0},{3,1},{4,6},{5,7},{6,4},{7,5},{8,10},{9,11},{10,... | collective-permute-start | bytes 1032200 | tf_op jit(solution)/shard_map/ppermute | solution.py:236
  79.5 14.8 %collective-permute-start.15 = (bf16[8,128,128]{2,1,0:T(8,128)(2,1)S(1)}, bf16[8,128,128]{2,1,0:T(8,128)(2,1)S(1)}, u32[]{:S(2)}, u32[]{:S(2)}) collective-permute-start(bf16[8,128,128]{2,1,0:T(8,128)(2,1)S(1)} %shard_map.101), channel_id=1, source_target_pairs={{0,1},{1,0},{2,3},{3,2},{4,5},{5,4},{6,7},{7,6},{8,9},{9,8},{10,11... | collective-permute-start | bytes 786440 | tf_op jit(solution)/shard_map/ppermute | solution.py:232
  84.3 13.7 %copy-start.5 = (bf16[64,2048]{1,0:T(8,128)(2,1)S(1)}, bf16[64,2048]{1,0:T(8,128)(2,1)}, u32[]{:S(2)}) copy-start(bf16[64,2048]{1,0:T(8,128)(2,1)} %adapter_ref.3) | copy-start | bytes 786436
  84.3 13.7 %collective-permute-start.17 = (bf16[8,128,128]{2,1,0:T(8,128)(2,1)S(1)}, bf16[8,128,128]{2,1,0:T(8,128)(2,1)S(1)}, u32[]{:S(2)}, u32[]{:S(2)}) collective-permute-start(bf16[8,128,128]{2,1,0:T(8,128)(2,1)S(1)} %shard_map.103), channel_id=1, source_target_pairs={{0,1},{1,0},{2,3},{3,2},{4,5},{5,4},{6,7},{7,6},{8,9},{9,8},{10,11... | collective-permute-start | bytes 786440 | tf_op jit(solution)/shard_map/ppermute | solution.py:232
  87.3 12.9 %collective-permute-start.18 = (bf16[16,128,128]{2,1,0:T(8,128)(2,1)S(1)}, bf16[16,128,128]{2,1,0:T(8,128)(2,1)S(1)}, u32[]{:S(2)}, u32[]{:S(2)}) collective-permute-start(bf16[16,128,128]{2,1,0:T(8,128)(2,1)S(1)} %bitcast.20), channel_id=1, source_target_pairs={{0,8},{4,12},{8,0},{12,4},{1,9},{5,13},{9,1},{13,5},{2,10},{6,14},... | collective-permute-start | bytes 1572872 | tf_op jit(solution)/shard_map/ppermute | solution.py:229
  98.0 8.1 %collective-permute-start.20 = (bf16[64,2688]{1,0:T(8,128)(2,1)S(1)}, bf16[64,2688]{1,0:T(8,128)(2,1)S(1)}, u32[]{:S(2)}, u32[]{:S(2)}) collective-permute-start(bf16[64,2688]{1,0:T(8,128)(2,1)S(1)} %collective-permute-done.19.rest_0_), channel_id=1, source_target_pairs={{0,1},{1,0},{2,3},{3,2},{4,5},{5,4},{6,7},{7,6},{8,9},{9,8},{10,11... | collective-permute-start | bytes 1032200 | tf_op jit(solution)/shard_map/ppermute | solution.py:232

commit v7 on v6

--- a/solution.py
+++ b/solution.py
@@ -55,34 +55,51 @@
     add_arrivals(where_ref, ids_ref, tiles_ref, rest[:-1], rest[-1], **plan)
 
 
-def last_kernel(where_ref, ids_ref, tiles_ref, old_ref, *rest, **plan):
-    blocks, (total_ref, send_mate, send_own) = rest[:-3], rest[-3:]
+def last_kernel(where_ref, ids_ref, tiles_ref, old_ref, *rest, block_count, **plan):
+    blocks, total_ref, sends = rest[:block_count], rest[block_count], rest[block_count + 1:]
     add_arrivals(where_ref, ids_ref, tiles_ref, blocks, total_ref, **plan)
-    chips, share, tokens, _ = send_mate.shape
-    for chip in range(chips):
-        other = (2 * chip + 1 - where_ref[1]) * share
-        for q in range(share):
-            send_mate[chip, q] = total_ref[other + q, tokens:, :].astype(BF16)
-            send_own[chip, q] = total_ref[other + q, :tokens, :].astype(BF16)
-
-
-def chip_kernel(where_ref, total_ref, core_ref, leaving_ref, *, first, blocks):
-    chips, share, tokens, _ = core_ref.shape
+    far_mate, near_mate, far_own, near_own = sends[:4], sends[4:5], sends[5:7], sends[7:]
+    tokens, share = near_own[0].shape[1], near_own[0].shape[0]
+    chips = far_own[0].shape[0] + 1
+
+    def copy(pieces, token, d):
+        to_chip = lax.rem(where_ref[2] + d, chips)
+        block = (2 * to_chip + 1 - where_ref[1]) * share
+        for piece in pieces:
+            target = piece.at[d - 1] if d > 0 else piece
+            for k in range(target.shape[0]):
+                target[k] = total_ref[block + k, token:token + tokens, :].astype(BF16)
+            block = block + target.shape[0]
+
+    for d in range(1, chips):
+        copy(far_mate, tokens, d)
+    copy(near_mate, tokens, 0)
+    for d in range(1, chips):
+        copy(far_own, 0, d)
+    copy(near_own, 0, 0)
+
+
+def chip_kernel(where_ref, total_ref, *rest, token, block):
+    pieces, leaving_ref = rest[:-1], rest[-1]
+    others, _, tokens, _ = leaving_ref.shape
+    chips = others + 1
     for d in range(1, chips):
         to_chip = lax.rem(where_ref[2] + d, chips)
-        mine = (2 * to_chip + where_ref[1]) * share
-        for k, q in enumerate(blocks):
-            value = total_ref[mine + q, first:first + tokens, :] + core_ref[to_chip, q].astype(F32)
-            leaving_ref[d - 1, k] = value.astype(BF16)
-
-
-def mate_kernel(where_ref, total_ref, core_ref, *rest, blocks):
+        first = (2 * to_chip + where_ref[1]) * where_ref[5] + block
+        done = 0
+        for piece in pieces:
+            for k in range(piece.shape[1]):
+                value = total_ref[first + done, token:token + tokens, :] + piece[d - 1, k].astype(F32)
+                leaving_ref[d - 1, done] = value.astype(BF16)
+                done += 1
+
+
+def mate_kernel(where_ref, total_ref, core_ref, *rest, block):
     pieces, out_ref = rest[:-1], rest[-1]
-    _, share, tokens, _ = core_ref.shape
-    chip = where_ref[2]
-    mine = (2 * chip + where_ref[1]) * share
-    for k, q in enumerate(blocks):
-        value = total_ref[mine + q, tokens:, :] + core_ref[chip, q].astype(F32)
+    size, tokens, _ = out_ref.shape
+    first = (2 * where_ref[2] + where_ref[1]) * where_ref[5] + block
+    for k in range(size):
+        value = total_ref[first + k, tokens:, :] + core_ref[block + k].astype(F32)
         for piece in pieces:
             value += piece[k].astype(F32)
         out_ref[k] = value.astype(BF16)
@@ -172,15 +189,15 @@
 
 def near_kernel(where_ref, rounded_ref, adapter_ref, total_ref, core_ref, *rest):
     from_mate, near_ref = rest[:-1], rest[-1]
-    _, share, tokens, tile = core_ref.shape
+    share, tokens, tile = core_ref.shape
     rank = rounded_ref.shape[0] // 2
     low = rounded_ref[:rank, :].astype(F32).T.astype(BF16)
-    chip = where_ref[2]
-    mine = (2 * chip + where_ref[1]) * share
+    mine = (2 * where_ref[2] + where_ref[1]) * share
     size = from_mate[0].shape[0]
     for q in range(share):
-        value = total_ref[mine + q, :tokens, :] + core_ref[chip, q].astype(F32)
-        value += from_mate[q // size][q % size].astype(F32)
+        piece = from_mate[0][q] if q < size else from_mate[1][q - size]
+        value = total_ref[mine + q, :tokens, :] + core_ref[q].astype(F32)
+        value += piece.astype(F32)
         extra = jnp.dot(low, adapter_ref[:, q * tile:(q + 1) * tile], preferred_element_type=F32)
         near_ref[q] = value + adapter_scale * extra
 
@@ -249,9 +266,10 @@
         part = lax.axis_index("parts")
         row_index = lax.axis_index("row")
         dp_index = lax.axis_index("dp")
-        where = jnp.stack(
-            [part, lax.rem(row_index, 2), lax.div(row_index, 2), lax.rem(dp_index, 2), lax.div(dp_index, 2)]
-        ).astype(jnp.int32)
+        where = jnp.stack([
+            part, lax.rem(row_index, 2), lax.div(row_index, 2),
+            lax.rem(dp_index, 2), lax.div(dp_index, 2), jnp.int32(share),
+        ]).astype(jnp.int32)
         blocks = kept_blocks[0]
         ids = block_ids[0]
         labels = forget_labels[None, :]
@@ -261,103 +279,116 @@
         held = slots // n_parts
         sizes = [held * k // 32 for k in (16, 10, 6)]
         starts = [sum(sizes[:k]) for k in range(len(sizes))]
-
-        def leaving_chunk(k):
-            return lax.dynamic_slice_in_dim(blocks, part * held + starts[k], sizes[k], axis=0)
-
-        first_chunk = leaving_chunk(0)
-        soon = core_swap(after(ids, first_chunk))
-        leaving_chunks = [first_chunk] + [after(leaving_chunk(k), soon) for k in range(1, len(starts))]
+        leaving_chunks = [
+            after(lax.dynamic_slice_in_dim(blocks, part * held + start, size, axis=0), all_ids)
+            for start, size in zip(starts, sizes)
+        ]
         direct = [
             (group_shift(leaving_chunks[k], d), ((d - 1) * slots, 0, starts[k]))
             for d in range(1, group) for k in range(len(starts))
         ]
-        mate_activations = mate_swap(activations)
-
+        mate_activations = mate_swap(after(activations, all_ids))
+
+        soon = core_swap(after(ids + 1, all_ids, leaving_chunks[0]))
         (both,) = call(
             low_rank_kernel, (jax.ShapeDtypeStruct((2 * rank, tokens), F32),), (),
-            (activations, after(adapter_a, direct[0][0]).T, cotangent, output_adapter, labels),
+            (activations, after(adapter_a, soon).T, cotangent, after(output_adapter, soon), labels),
         )
         both = both + core_swap(both)
-        both_later = after(both, direct[1][0])
-        swapped = [
-            (part_shift(value, e), (offset, e, start))
-            for value, (offset, _, start) in direct for e in range(1, n_parts)
-        ]
-
-        def plan(items):
-            return dict(places=[item[1] for item in items], parts=n_parts, held=held, col_blocks=col_blocks)
-
-        def values(items):
-            return tuple(item[0] for item in items)
-
-        chunks, copies = len(direct), n_parts - 1
-        first = []
-        more = direct + swapped[:copies * (chunks - 1)]
-        last = swapped[copies * (chunks - 1):]
-        total_shape = pltpu.VMEM((col_blocks + 1, 2 * tokens, tile), F32)
-        total, tiles = call(
-            functools.partial(first_kernel, **plan(first)),
-            (total_shape, pltpu.VMEM((row_blocks, 2 * tokens, tile), BF16)),
-            (where, ids, ids), (activations, mate_activations, blocks) + values(first),
-        )
-
         rounded, pack = call(
             own_grad_kernel,
             (
                 jax.ShapeDtypeStruct((2 * rank, tokens), BF16),
                 jax.ShapeDtypeStruct((rank, feats + tokens), BF16),
             ),
-            (after(where, total),), (cotangent, labels, both) + tuple(chip_shift(both_later, d) for d in range(1, chips)),
+            (where,), (cotangent, labels, both) + tuple(chip_shift(both, d) for d in range(1, chips)),
         )
         mate_pack = mate_swap(pack)
 
+        def chunk(items, k):
+            return [item for item in items if item[1][2] == starts[k]]
+
+        def plan(items):
+            return dict(places=[item[1] for item in items], parts=n_parts, held=held, col_blocks=col_blocks)
+
+        def values(items):
+            return tuple(item[0] for item in items)
+
+        total_shape = pltpu.VMEM((col_blocks + 1, 2 * tokens, tile), F32)
+        total, tiles = call(
+            functools.partial(first_kernel, **plan([])),
+            (total_shape, pltpu.VMEM((row_blocks, 2 * tokens, tile), BF16)),
+            (after(where, rounded, leaving_chunks[-1]), ids, all_ids), (activations, mate_activations, blocks),
+        )
         half_shape = jax.ShapeDtypeStruct((rank, (shard_rows + feats) // 2), BF16)
         half_grads, other_grads = call(
             pair_grad_kernel, (half_shape, half_shape), (where,), (rounded, activations, mate_activations, pack, mate_pack),
         )
         far_grads = [group_shift(half_grads, d) for d in range(1, group)]
 
+        swapped = [
+            (part_shift(after(value, total) if start == 0 else after(value, half_grads) if start == starts[1] else value, e), (offset, e, start))
+            for value, (offset, _, start) in direct for e in range(1, n_parts)
+        ]
+        more = direct + chunk(swapped, 0) + chunk(swapped, 1)
+        last = chunk(swapped, 2)
+
         (total,) = call(
             functools.partial(more_kernel, **plan(more)), (total_shape,), (where, all_ids),
             (on_chip(tiles), on_chip(total)) + values(more), {3: 0},
         )
-        send = pltpu.VMEM((chips, share, tokens, tile), BF16)
-        total, send_mate, send_own = call(
-            functools.partial(last_kernel, **plan(last)), (total_shape, send, send),
+        small = share // 4
+        half = share // 2
+
+        def far_piece(size):
+            return pltpu.VMEM((chips - 1, size, tokens, tile), BF16)
+
+        def near_piece(size):
+            return pltpu.VMEM((size, tokens, tile), BF16)
+
+        total, *sends = call(
+            functools.partial(last_kernel, block_count=len(last), **plan(last)),
+            (total_shape,) + (far_piece(small),) * 4 + (near_piece(share),)
+            + (far_piece(half),) * 2 + (near_piece(share),),
             (after(where, half_grads), all_ids), (on_chip(tiles), on_chip(total)) + values(last), {3: 0},
         )
 
-        def for_chips(first, core_got, where, blocks):
+        cores = [core_swap(value) for value in sends[:5]]
+
+        def for_chips(pieces, token, block, *needed):
+            size = sum(piece.shape[1] for piece in pieces)
             (leaving,) = call(
-                functools.partial(chip_kernel, first=first, blocks=blocks),
-                (pltpu.VMEM((chips - 1, len(blocks), tokens, tile), BF16),),
-                (where,), (on_chip(total), core_got),
+                functools.partial(chip_kernel, token=token, block=block), (far_piece(size),),
+                (after(where, *needed) if needed else where,), (on_chip(total),) + tuple(pieces),
             )
-            return [chip_shift(leaving[d - 1], d) for d in range(1, chips)]
-
-        core_mate = core_swap(send_mate)
-        core_own = core_swap(send_own)
-        halves = [tuple(range(share // 2)), tuple(range(share // 2, share))]
-        mate_pieces = [for_chips(tokens, core_mate, where, part_blocks) for part_blocks in halves]
-        mate_totals = []
-        for part_blocks, got in zip(halves, mate_pieces):
-            mate_totals += call(
-                functools.partial(mate_kernel, blocks=part_blocks),
-                (pltpu.VMEM((len(part_blocks), tokens, tile), BF16),), (where,),
-                (on_chip(total), core_mate) + tuple(got),
+            return leaving, [chip_shift(leaving[d - 1], d) for d in range(1, chips)]
+
+        leaving_first, pieces_first = for_chips(cores[:1], tokens, 0)
+        leaving_second, pieces_second = for_chips(cores[1:4], tokens, small, leaving_first)
+        cores += [core_swap(after(value, leaving_second)) for value in sends[5:]]
+        leaving_own, own_pieces = for_chips(cores[5:7], 0, 0)
+        far_grads = [after(value, *pieces_first) for value in far_grads]
+        mate_grads = [mate_swap(value) for value in far_grads]
+
+        def for_mate(pieces, size, block, *needed):
+            (value,) = call(
+                functools.partial(mate_kernel, block=block), (near_piece(size),),
+                (after(where, *needed) if needed else where,), (on_chip(total), cores[4]) + tuple(pieces),
             )
-        from_mate = [mate_swap(value) for value in mate_totals]
-        own_pieces = for_chips(0, core_own, after(where, mate_totals[0]), tuple(range(share)))
-        from_mate_grads = [mate_swap(after(value, *from_mate)) for value in far_grads]
+            return mate_swap(value)
+
+        from_mate_first = for_mate(pieces_first, small, 0)
+        from_mate = [
+            from_mate_first, for_mate(pieces_second, share - small, small, from_mate_first, *mate_grads),
+        ]
         in_grad, out_grad = call(
             grad_sum_kernel,
             (jax.ShapeDtypeStruct((rank, shard_rows), F32), jax.ShapeDtypeStruct((rank, feats), F32)),
-            (where,), (half_grads, other_grads) + tuple(far_grads) + tuple(from_mate_grads),
+            (where,), (half_grads, other_grads) + tuple(far_grads) + tuple(mate_grads),
         )
         (near,) = call(
             near_kernel, (pltpu.VMEM((share, tokens, tile), F32),), (where,),
-            (rounded, output_adapter, on_chip(total), core_own) + tuple(from_mate),
+            (rounded, output_adapter, on_chip(total), cores[7]) + tuple(from_mate),
         )
         (projected,) = call(
             final_kernel, (jax.ShapeDtypeStruct((tokens, feats), BF16),), (), (on_chip(near),) + tuple(own_pieces),

time: 108 us -> 104 us (0.963)
  waiting for transfers between devices: 53.6 us -> 50.3 us
  starting transfers between devices: 26.7 us -> 24 us
  other arithmetic: 0.01 us -> 1.54 us
    ppermute x5, waiting for transfers between devices: 31.7 us -> 9.87 us  [group_shift(): return lax.ppermute(value, 'dp', pairs)]
    ppermute x5, waiting for transfers between devices: 12.6 us -> 31 us  [mate_swap(): return lax.ppermute(value, 'dp', [(i, i ^ 1) for i in range(n_dp)])]
    ppermute x4, waiting for transfers between devices: 7.19 us -> 2.87 us  [chip_shift(): return lax.ppermute(value, 'row', pairs)]
    ppermute x3, waiting for transfers between devices: 0.01 us -> 3.63 us  [part_shift(): lax.ppermute(value, 'parts', [(i, (i + d) % n_parts) for i in range(n_par...]
    ppermute x5, starting transfers between devices: 7.75 us -> 4.86 us  [mate_swap(): return lax.ppermute(value, 'dp', [(i, i ^ 1) for i in range(n_dp)])]
    ppermute x3, starting transfers between devices: 3.36 us -> 4.96 us  [part_shift(): lax.ppermute(value, 'parts', [(i, (i + d) % n_parts) for i in range(n_par...]
    unnamed x20 -> x24, local copies, waits for them, and re-layouts: 3.68 us -> 5.19 us
    ppermute x5, starting transfers between devices: 10.7 us -> 9.28 us  [group_shift(): return lax.ppermute(value, 'dp', pairs)]
  transfers between devices with their start and end apart: 21 -> 27, of which waited for: 11 -> 18; matrix products, arithmetic and copies ran while one was open for 3% -> 4% of each run, Pallas kernels for 15% -> 17%
where the time goes in v7:
time: 104 us
  waiting for transfers between devices  50.3 us (48%)
  starting transfers between devices  24 us (23%)
  Pallas kernels  18.9 us (18%)
  local copies, waits for them, and re-layouts  7.99 us (8%)
  other arithmetic  1.54 us (1%)
    ppermute x5, waiting for transfers between devices, mate_swap(): return lax.ppermute(value, 'dp', [(i, i ^ 1) for i in range(n_dp)])  31 us
    pallas_call x14, Pallas kernels, call(): pl.pallas_call(kernel, out_shape=outs, in_specs=[smem] * len(scalars) + [...  18.9 us
    ppermute x5, waiting for transfers between devices, group_shift(): return lax.ppermute(value, 'dp', pairs)  9.87 us
    ppermute x5, starting transfers between devices, group_shift(): return lax.ppermute(value, 'dp', pairs)  9.28 us
    unnamed x24, local copies, waits for them, and re-layouts  5.19 us
    ppermute x3, starting transfers between devices, part_shift(): lax.ppermute(value, 'parts', [(i, (i + d) % n_parts) for i in range(n_par...  4.96 us
    ppermute x5, starting transfers between devices, mate_swap(): return lax.ppermute(value, 'dp', [(i, i ^ 1) for i in range(n_dp)])  4.86 us
    ppermute x3, waiting for transfers between devices, part_shift(): lax.ppermute(value, 'parts', [(i, (i + d) % n_parts) for i in range(n_par...  3.63 us
  transfers between devices with their start and end apart: 27, of which 18 were waited for; matrix products, arithmetic and copies ran while one was open for 4% of the time, Pallas kernels for 17%

profile of v7, /device:TPU:0, one launch (start us, length us, event | category | flops | bytes accessed | tf_op | source)
XLA Modules:
  0.0 103.5 jit_solution(6719374461125758167)
XLA Ops:
  0.6 4.1 %collective-permute-start = (s32[64]{0:T(128)}, s32[64]{0:T(128)S(1)}, u32[]{:S(2)}, u32[]{:S(2)}) collective-permute-start(s32[64]{0:T(128)} %bitcast.27), channel_id=1, source_target_pairs={{0,2},{1,3},{2,0},{3,1},{4,6},{5,7},{6,4},{7,5},{8,10},{9,11},{10,... | collective-permute-start | bytes 776 | tf_op jit(solution)/shard_map/ppermute | solution.py:253
  4.7 1.7 %collective-permute-done.ids_ref = s32[64]{0:T(128)S(1)} collective-permute-done((s32[64]{0:T(128)}, s32[64]{0:T(128)S(1)}, u32[]{:S(2)}, u32[]{:S(2)}) %collective-permute-start) | collective-permute-done | bytes 288 | tf_op jit(solution)/shard_map/ppermute | solution.py:253
  6.4 1.9 %collective-permute-start.4 = (bf16[128,3328]{1,0:T(8,128)(2,1)}, bf16[128,3328]{1,0:T(8,128)(2,1)}, u32[]{:S(2)}, u32[]{:S(2)}) collective-permute-start(bf16[128,3328]{1,0:T(8,128)(2,1)} %own_ref.1), channel_id=1, source_target_pairs={{0,1},{1,0},{2,3},{3,2},{4,5},{5,4},{6,7},{7,6},{8,9},{9,8},{10,11... | collective-permute-start | bytes 2555912 | tf_op jit(solution)/shard_map/ppermute | solution.py:249
  8.3 2.0 %dynamic-slice_bitcast_fusion = bf16[16,128,128]{2,1,0:T(8,128)(2,1)} fusion(bf16[1,64,128,128]{3,2,1,0:T(8,128)(2,1)} %param.10, s32[]{:T(128)S(6)} %select_n.9), kind=kLoop, calls=%fused_computation | loop fusion | bytes 1048580 | tf_op jit(solution)/shard_map/dynamic_slice | solution.py:283
  10.3 2.6 %collective-permute-start.6 = (bf16[16,128,128]{2,1,0:T(8,128)(2,1)}, bf16[16,128,128]{2,1,0:T(8,128)(2,1)}, u32[]{:S(2)}, u32[]{:S(2)}) collective-permute-start(bf16[16,128,128]{2,1,0:T(8,128)(2,1)} %dynamic-slice_bitcast_fusion), channel_id=1, source_target_pairs={{0,2},{1,3},{2,0},{3,1},{4,6},{5,7},{6,4},{7,5},{8,10},{9,11},{10,... | collective-permute-start | bytes 1572872 | tf_op jit(solution)/shard_map/ppermute | solution.py:253
  13.5 1.1 %collective-permute-done.1 = s32[64]{0:T(128)S(1)} collective-permute-done((s32[64]{0:T(128)S(1)}, s32[64]{0:T(128)S(1)}, u32[]{:S(2)}, u32[]{:S(2)}) %collective-permute-start.1) | collective-permute-done | bytes 288 | tf_op jit(solution)/shard_map/ppermute | solution.py:242
  14.6 1.2 %copy-done = bf16[128,3328]{1,0:T(8,128)(2,1)S(1)} copy-done((bf16[128,3328]{1,0:T(8,128)(2,1)S(1)}, bf16[128,3328]{1,0:T(8,128)(2,1)}, u32[]{:S(2)}) %copy-start) | copy-done | bytes 851992
  15.8 1.0 %copy-done.3 = bf16[128,2048]{1,0:T(8,128)(2,1)S(1)} copy-done((bf16[128,2048]{1,0:T(8,128)(2,1)S(1)}, bf16[128,2048]{1,0:T(8,128)(2,1)}, u32[]{:S(2)}) %copy-start.3) | copy-done | bytes 524312
  22.4 1.6 %collective-permute-start.3 = (f32[128,128]{1,0:T(8,128)S(1)}, f32[128,128]{1,0:T(8,128)}, u32[]{:S(2)}, u32[]{:S(2)}) collective-permute-start(f32[128,128]{1,0:T(8,128)S(1)} %add.31.both_ref), channel_id=1, source_target_pairs={{0,8},{4,12},{8,0},{12,4},{1,9},{5,13},{9,1},{13,5},{2,10},{6,14},... | collective-permute-start | bytes 196616 | tf_op jit(solution)/shard_map/ppermute | solution.py:246
  25.1 1.7 %collective-permute-done.3.rest_0_ = f32[128,128]{1,0:T(8,128)} collective-permute-done((f32[128,128]{1,0:T(8,128)S(1)}, f32[128,128]{1,0:T(8,128)}, u32[]{:S(2)}, u32[]{:S(2)}) %collective-permute-start.3) | collective-permute-done | bytes 65568 | tf_op jit(solution)/shard_map/ppermute | solution.py:246
  26.8 1.1 %shard_map.95 = (bf16[128,128]{1,0:T(8,128)(2,1)S(1)}, bf16[64,2176]{1,0:T(8,128)(2,1)S(1)}) custom-call(s32[6]{0:T(128)S(1)} %stack.23.where_ref, bf16[128,2048]{1,0:T(8,128)(2,1)S(1)} %copy-done.4, s32[1,128]{1,0:T(1,128)S(1)} %bitcast.26, f32[128,128]{1,0:T(8,128)S(1)} %add.31.both_ref, f32[128,128]{1,0:T(8,128)} %collective-permute-done.3.rest_0_), custom_call_target="tpu_custom_call" | custom-call | tf_op jit(solution)/shard_map/pallas_call | solution.py:218
  28.4 12.7 %collective-permute-done.4.mate_acts_ref.mate_ref = bf16[128,3328]{1,0:T(8,128)(2,1)} collective-permute-done((bf16[128,3328]{1,0:T(8,128)(2,1)}, bf16[128,3328]{1,0:T(8,128)(2,1)}, u32[]{:S(2)}, u32[]{:S(2)}) %collective-permute-start.4) | collective-permute-done | bytes 852000 | tf_op jit(solution)/shard_map/ppermute | solution.py:249
  41.2 4.4 %shard_map.97 = (f32[65,256,128]{2,1,0:T(8,128)S(1)}, bf16[26,256,128]{2,1,0:T(8,128)(2,1)S(1)}) custom-call(s32[6]{0:T(128)S(1)} %stack.23.where_ref, s32[64]{0:T(128)S(1)} %bitcast.28, s32[64]{0:T(128)S(1)} %collective-permute-done.ids_ref, bf16[128,3328]{1,0:T(8,128)(2,1)S(1)} %copy-done.1, ...), custom_call_target="tpu_custom_call" | custom-call | tf_op jit(solution)/shard_map/pallas_call | solution.py:218
  45.6 1.9 %collective-permute-start.9 = (bf16[16,128,128]{2,1,0:T(8,128)(2,1)}, bf16[16,128,128]{2,1,0:T(8,128)(2,1)S(1)}, u32[]{:S(2)}, u32[]{:S(2)}) collective-permute-start(bf16[16,128,128]{2,1,0:T(8,128)(2,1)} %collective-permute-done.6.rest_0_), channel_id=1, source_target_pairs={{0,16},{16,0},{1,17},{17,1},{2,18},{18,2},{3,19},{19,3},{4,20},{20... | collective-permute-start | bytes 1572872 | tf_op jit(solution)/shard_map/ppermute | solution.py:256
  47.5 2.2 %collective-permute-start.8 = (bf16[6,128,128]{2,1,0:T(8,128)(2,1)S(1)}, bf16[6,128,128]{2,1,0:T(8,128)(2,1)S(1)}, u32[]{:S(2)}, u32[]{:S(2)}) collective-permute-start(bf16[6,128,128]{2,1,0:T(8,128)(2,1)S(1)} %dynamic-slice_bitcast_fusion.2), channel_id=1, source_target_pairs={{0,2},{1,3},{2,0},{3,1},{4,6},{5,7},{6,4},{7,5},{8,10},{9,11},{10,... | collective-permute-start | bytes 589832 | tf_op jit(solution)/shard_map/ppermute | solution.py:253
  49.7 2.2 %collective-permute-done.5.mate_pack_ref = bf16[64,2176]{1,0:T(8,128)(2,1)S(1)} collective-permute-done((bf16[64,2176]{1,0:T(8,128)(2,1)S(1)}, bf16[64,2176]{1,0:T(8,128)(2,1)S(1)}, u32[]{:S(2)}, u32[]{:S(2)}) %collective-permute-start.5) | collective-permute-done | bytes 278560 | tf_op jit(solution)/shard_map/ppermute | solution.py:249
  51.9 1.6 %shard_map.96 = (bf16[64,2688]{1,0:T(8,128)(2,1)S(1)}, bf16[64,2688]{1,0:T(8,128)(2,1)S(1)}) custom-call(s32[6]{0:T(128)S(1)} %stack.23.where_ref, bf16[128,128]{1,0:T(8,128)(2,1)S(1)} %get-tuple-element.41.rounded_ref, bf16[128,3328]{1,0:T(8,128)(2,1)S(1)} %copy-done.1, bf16[128,3328]{1,0:T(8,128)(2,1)} %collective-permute-done.4.mate_acts_ref.mate_ref, ...), custom_call_target="tpu_custom_call" | custom-call | tf_op jit(solution)/shard_map/pallas_call | solution.py:218
  53.6 3.8 %collective-permute-done.7.rest_1_ = bf16[10,128,128]{2,1,0:T(8,128)(2,1)} collective-permute-done((bf16[10,128,128]{2,1,0:T(8,128)(2,1)}, bf16[10,128,128]{2,1,0:T(8,128)(2,1)}, u32[]{:S(2)}, u32[]{:S(2)}) %collective-permute-start.7) | collective-permute-done | bytes 327712 | tf_op jit(solution)/shard_map/ppermute | solution.py:253
  57.4 1.5 %collective-permute-start.10 = (bf16[10,128,128]{2,1,0:T(8,128)(2,1)}, bf16[10,128,128]{2,1,0:T(8,128)(2,1)S(1)}, u32[]{:S(2)}, u32[]{:S(2)}) collective-permute-start(bf16[10,128,128]{2,1,0:T(8,128)(2,1)} %collective-permute-done.7.rest_1_), channel_id=1, source_target_pairs={{0,16},{16,0},{1,17},{17,1},{2,18},{18,2},{3,19},{19,3},{4,20},{20... | collective-permute-start | bytes 983048 | tf_op jit(solution)/shard_map/ppermute | solution.py:256
  58.9 2.1 %collective-permute-done.8.rest_2_ = bf16[6,128,128]{2,1,0:T(8,128)(2,1)S(1)} collective-permute-done((bf16[6,128,128]{2,1,0:T(8,128)(2,1)S(1)}, bf16[6,128,128]{2,1,0:T(8,128)(2,1)S(1)}, u32[]{:S(2)}, u32[]{:S(2)}) %collective-permute-start.8) | collective-permute-done | bytes 196640 | tf_op jit(solution)/shard_map/ppermute | solution.py:253
  61.0 1.5 %collective-permute-start.11 = (bf16[6,128,128]{2,1,0:T(8,128)(2,1)S(1)}, bf16[6,128,128]{2,1,0:T(8,128)(2,1)S(1)}, u32[]{:S(2)}, u32[]{:S(2)}) collective-permute-start(bf16[6,128,128]{2,1,0:T(8,128)(2,1)S(1)} %collective-permute-done.8.rest_2_), channel_id=1, source_target_pairs={{0,16},{16,0},{1,17},{17,1},{2,18},{18,2},{3,19},{19,3},{4,20},{20... | collective-permute-start | bytes 589832 | tf_op jit(solution)/shard_map/ppermute | solution.py:256
  62.5 3.6 %collective-permute-done.10.rest_4_ = bf16[10,128,128]{2,1,0:T(8,128)(2,1)S(1)} collective-permute-done((bf16[10,128,128]{2,1,0:T(8,128)(2,1)}, bf16[10,128,128]{2,1,0:T(8,128)(2,1)S(1)}, u32[]{:S(2)}, u32[]{:S(2)}) %collective-permute-start.10) | collective-permute-done | bytes 327712 | tf_op jit(solution)/shard_map/ppermute | solution.py:256
  66.1 3.6 %shard_map.98.old_ref = f32[65,256,128]{2,1,0:T(8,128)S(1)} custom-call(s32[6]{0:T(128)S(1)} %stack.23.where_ref, s32[64]{0:T(128)S(1)} %collective-permute-done.ids_ref, bf16[26,256,128]{2,1,0:T(8,128)(2,1)S(1)} %get-tuple-element.48.tiles_ref, f32[65,256,128]{2,1,0:T(8,128)S(1)} %get-tuple-element.49.old_ref, ...), custom_call_target="tpu_custom_call", output_to_operand_aliasing={{}: (3, {})} | custom-call | tf_op jit(solution)/shard_map/pallas_call | solution.py:218
  69.7 1.0 shard_map.99
  74.4 1.4 %collective-permute-start.22 = (bf16[12,128,128]{2,1,0:T(8,128)(2,1)S(1)}, bf16[12,128,128]{2,1,0:T(8,128)(2,1)S(1)}, u32[]{:S(2)}, u32[]{:S(2)}) collective-permute-start(bf16[12,128,128]{2,1,0:T(8,128)(2,1)S(1)} %bitcast.23), channel_id=1, source_target_pairs={{0,8},{4,12},{8,0},{12,4},{1,9},{5,13},{9,1},{13,5},{2,10},{6,14},... | collective-permute-start | bytes 1179656 | tf_op jit(solution)/shard_map/ppermute | solution.py:246
  75.8 2.4 %collective-permute-done.20.rest_0_ = bf16[64,2688]{1,0:T(8,128)(2,1)S(1)} collective-permute-done((bf16[64,2688]{1,0:T(8,128)(2,1)S(1)}, bf16[64,2688]{1,0:T(8,128)(2,1)S(1)}, u32[]{:S(2)}, u32[]{:S(2)}) %collective-permute-start.20) | collective-permute-done | bytes 344096 | tf_op jit(solution)/shard_map/ppermute | solution.py:253
  78.2 1.2 %collective-permute-done.18.rest_0_ = bf16[4,128,128]{2,1,0:T(8,128)(2,1)S(1)} collective-permute-done((bf16[4,128,128]{2,1,0:T(8,128)(2,1)S(1)}, bf16[4,128,128]{2,1,0:T(8,128)(2,1)S(1)}, u32[]{:S(2)}, u32[]{:S(2)}) %collective-permute-start.18) | collective-permute-done | bytes 131104 | tf_op jit(solution)/shard_map/ppermute | solution.py:246
  80.0 2.1 %collective-permute-start.19 = (bf16[4,128,128]{2,1,0:T(8,128)(2,1)S(1)}, bf16[4,128,128]{2,1,0:T(8,128)(2,1)S(1)}, u32[]{:S(2)}, u32[]{:S(2)}) collective-permute-start(bf16[4,128,128]{2,1,0:T(8,128)(2,1)S(1)} %shard_map.102), channel_id=1, source_target_pairs={{0,1},{1,0},{2,3},{3,2},{4,5},{5,4},{6,7},{7,6},{8,9},{9,8},{10,11... | collective-permute-start | bytes 393224 | tf_op jit(solution)/shard_map/ppermute | solution.py:249
  82.8 7.3 %collective-permute-done.21.rest_1_ = bf16[64,2688]{1,0:T(8,128)(2,1)S(1)} collective-permute-done((bf16[64,2688]{1,0:T(8,128)(2,1)S(1)}, bf16[64,2688]{1,0:T(8,128)(2,1)S(1)}, u32[]{:S(2)}, u32[]{:S(2)}) %collective-permute-start.21) | collective-permute-done | bytes 344096 | tf_op jit(solution)/shard_map/ppermute | solution.py:249
  90.1 1.4 %collective-permute-done.19.rest_0_ = bf16[4,128,128]{2,1,0:T(8,128)(2,1)S(1)} collective-permute-done((bf16[4,128,128]{2,1,0:T(8,128)(2,1)S(1)}, bf16[4,128,128]{2,1,0:T(8,128)(2,1)S(1)}, u32[]{:S(2)}, u32[]{:S(2)}) %collective-permute-start.19) | collective-permute-done | bytes 131104 | tf_op jit(solution)/shard_map/ppermute | solution.py:249
  92.5 1.8 %shard_map.107 = (f32[64,3328]{1,0:T(8,128)}, f32[64,2048]{1,0:T(8,128)}) custom-call(s32[6]{0:T(128)S(1)} %stack.23.where_ref, bf16[64,2688]{1,0:T(8,128)(2,1)S(1)} %get-tuple-element.44.half_ref, bf16[64,2688]{1,0:T(8,128)(2,1)S(1)} %get-tuple-element.68.other_ref, bf16[64,2688]{1,0:T(8,128)(2,1)S(1)} %collective-permute-done.20.rest_0_, ...), custom_call_target="tpu_custom_call" | custom-call | tf_op jit(solution)/shard_map/pallas_call | solution.py:218
  94.3 7.4 %collective-permute-done.23.rest_1_ = bf16[12,128,128]{2,1,0:T(8,128)(2,1)S(1)} collective-permute-done((bf16[12,128,128]{2,1,0:T(8,128)(2,1)S(1)}, bf16[12,128,128]{2,1,0:T(8,128)(2,1)S(1)}, u32[]{:S(2)}, u32[]{:S(2)}) %collective-permute-start.23) | collective-permute-done | bytes 393248 | tf_op jit(solution)/shard_map/ppermute | solution.py:249
  (66 shorter events, 15.8 us)
Async XLA Ops:
  0.6 26.2 %copy-start.10 = (s32[128]{0:T(128)S(1)}, s32[128]{0:T(128)}, u32[]{:S(2)}) copy-start(s32[128]{0:T(128)} %param.9) | copy-start | bytes 1540
  0.6 5.8 %collective-permute-start = (s32[64]{0:T(128)}, s32[64]{0:T(128)S(1)}, u32[]{:S(2)}, u32[]{:S(2)}) collective-permute-start(s32[64]{0:T(128)} %bitcast.27), channel_id=1, source_target_pairs={{0,2},{1,3},{2,0},{3,1},{4,6},{5,7},{6,4},{7,5},{8,10},{9,11},{10,... | collective-permute-start | bytes 776 | tf_op jit(solution)/shard_map/ppermute | solution.py:253
  6.4 34.8 %collective-permute-start.4 = (bf16[128,3328]{1,0:T(8,128)(2,1)}, bf16[128,3328]{1,0:T(8,128)(2,1)}, u32[]{:S(2)}, u32[]{:S(2)}) collective-permute-start(bf16[128,3328]{1,0:T(8,128)(2,1)} %own_ref.1), channel_id=1, source_target_pairs={{0,1},{1,0},{2,3},{3,2},{4,5},{5,4},{6,7},{7,6},{8,9},{9,8},{10,11... | collective-permute-start | bytes 2555912 | tf_op jit(solution)/shard_map/ppermute | solution.py:249
  8.3 32.9 %copy-start.1 = (bf16[128,3328]{1,0:T(8,128)(2,1)S(1)}, bf16[128,3328]{1,0:T(8,128)(2,1)}, u32[]{:S(2)}) copy-start(bf16[128,3328]{1,0:T(8,128)(2,1)} %own_ref.1) | copy-start | bytes 2555908
  10.3 30.9 %copy-start.11 = (s32[1,64]{1,0:T(1,128)S(1)}, s32[1,64]{1,0:T(1,128)}, u32[]{:S(2)}) copy-start(s32[1,64]{1,0:T(1,128)} %param.11) | copy-start | bytes 772
  10.3 35.3 %collective-permute-start.6 = (bf16[16,128,128]{2,1,0:T(8,128)(2,1)}, bf16[16,128,128]{2,1,0:T(8,128)(2,1)}, u32[]{:S(2)}, u32[]{:S(2)}) collective-permute-start(bf16[16,128,128]{2,1,0:T(8,128)(2,1)} %dynamic-slice_bitcast_fusion), channel_id=1, source_target_pairs={{0,2},{1,3},{2,0},{3,1},{4,6},{5,7},{6,4},{7,5},{8,10},{9,11},{10,... | collective-permute-start | bytes 1572872 | tf_op jit(solution)/shard_map/ppermute | solution.py:253
  13.5 1.1 %collective-permute-start.1 = (s32[64]{0:T(128)S(1)}, s32[64]{0:T(128)S(1)}, u32[]{:S(2)}, u32[]{:S(2)}) collective-permute-start(s32[64]{0:T(128)S(1)} %broadcast_add_fusion), channel_id=1, source_target_pairs={{0,4},{4,0},{8,12},{12,8},{1,5},{5,1},{9,13},{13,9},{2,6},{6,2},{1... | collective-permute-start | bytes 776 | tf_op jit(solution)/shard_map/ppermute | solution.py:242
  19.5 7.4 %copy-start.4 = (bf16[128,2048]{1,0:T(8,128)(2,1)S(1)}, bf16[128,2048]{1,0:T(8,128)(2,1)}, u32[]{:S(2)}) copy-start(bf16[128,2048]{1,0:T(8,128)(2,1)} %cot_ref.3) | copy-start | bytes 1572868
  20.1 1.5 %collective-permute-start.2 = (f32[128,128]{1,0:T(8,128)S(1)}, f32[128,128]{1,0:T(8,128)}, u32[]{:S(2)}, u32[]{:S(2)}) collective-permute-start(f32[128,128]{1,0:T(8,128)S(1)} %shard_map.94), channel_id=1, source_target_pairs={{0,4},{4,0},{8,12},{12,8},{1,5},{5,1},{9,13},{13,9},{2,6},{6,2},{1... | collective-permute-start | bytes 196616 | tf_op jit(solution)/shard_map/ppermute | solution.py:242
  22.4 4.4 %collective-permute-start.3 = (f32[128,128]{1,0:T(8,128)S(1)}, f32[128,128]{1,0:T(8,128)}, u32[]{:S(2)}, u32[]{:S(2)}) collective-permute-start(f32[128,128]{1,0:T(8,128)S(1)} %add.31.both_ref), channel_id=1, source_target_pairs={{0,8},{4,12},{8,0},{12,4},{1,9},{5,13},{9,1},{13,5},{2,10},{6,14},... | collective-permute-start | bytes 196616 | tf_op jit(solution)/shard_map/ppermute | solution.py:246
  24.7 32.7 %collective-permute-start.7 = (bf16[10,128,128]{2,1,0:T(8,128)(2,1)}, bf16[10,128,128]{2,1,0:T(8,128)(2,1)}, u32[]{:S(2)}, u32[]{:S(2)}) collective-permute-start(bf16[10,128,128]{2,1,0:T(8,128)(2,1)} %dynamic-slice_bitcast_fusion.1), channel_id=1, source_target_pairs={{0,2},{1,3},{2,0},{3,1},{4,6},{5,7},{6,4},{7,5},{8,10},{9,11},{10,... | collective-permute-start | bytes 983048 | tf_op jit(solution)/shard_map/ppermute | solution.py:253
  27.9 24.0 %collective-permute-start.5 = (bf16[64,2176]{1,0:T(8,128)(2,1)S(1)}, bf16[64,2176]{1,0:T(8,128)(2,1)S(1)}, u32[]{:S(2)}, u32[]{:S(2)}) collective-permute-start(bf16[64,2176]{1,0:T(8,128)(2,1)S(1)} %get-tuple-element.43.pack_ref), channel_id=1, source_target_pairs={{0,1},{1,0},{2,3},{3,2},{4,5},{5,4},{6,7},{7,6},{8,9},{9,8},{10,11... | collective-permute-start | bytes 835592 | tf_op jit(solution)/shard_map/ppermute | solution.py:249
  45.6 20.5 %collective-permute-start.9 = (bf16[16,128,128]{2,1,0:T(8,128)(2,1)}, bf16[16,128,128]{2,1,0:T(8,128)(2,1)S(1)}, u32[]{:S(2)}, u32[]{:S(2)}) collective-permute-start(bf16[16,128,128]{2,1,0:T(8,128)(2,1)} %collective-permute-done.6.rest_0_), channel_id=1, source_target_pairs={{0,16},{16,0},{1,17},{17,1},{2,18},{18,2},{3,19},{19,3},{4,20},{20... | collective-permute-start | bytes 1572872 | tf_op jit(solution)/shard_map/ppermute | solution.py:256
  47.5 13.5 %collective-permute-start.8 = (bf16[6,128,128]{2,1,0:T(8,128)(2,1)S(1)}, bf16[6,128,128]{2,1,0:T(8,128)(2,1)S(1)}, u32[]{:S(2)}, u32[]{:S(2)}) collective-permute-start(bf16[6,128,128]{2,1,0:T(8,128)(2,1)S(1)} %dynamic-slice_bitcast_fusion.2), channel_id=1, source_target_pairs={{0,2},{1,3},{2,0},{3,1},{4,6},{5,7},{6,4},{7,5},{8,10},{9,11},{10,... | collective-permute-start | bytes 589832 | tf_op jit(solution)/shard_map/ppermute | solution.py:253
  57.4 8.7 %collective-permute-start.10 = (bf16[10,128,128]{2,1,0:T(8,128)(2,1)}, bf16[10,128,128]{2,1,0:T(8,128)(2,1)S(1)}, u32[]{:S(2)}, u32[]{:S(2)}) collective-permute-start(bf16[10,128,128]{2,1,0:T(8,128)(2,1)} %collective-permute-done.7.rest_1_), channel_id=1, source_target_pairs={{0,16},{16,0},{1,17},{17,1},{2,18},{18,2},{3,19},{19,3},{4,20},{20... | collective-permute-start | bytes 983048 | tf_op jit(solution)/shard_map/ppermute | solution.py:256
  61.0 8.7 %collective-permute-start.11 = (bf16[6,128,128]{2,1,0:T(8,128)(2,1)S(1)}, bf16[6,128,128]{2,1,0:T(8,128)(2,1)S(1)}, u32[]{:S(2)}, u32[]{:S(2)}) collective-permute-start(bf16[6,128,128]{2,1,0:T(8,128)(2,1)S(1)} %collective-permute-done.8.rest_2_), channel_id=1, source_target_pairs={{0,16},{16,0},{1,17},{17,1},{2,18},{18,2},{3,19},{19,3},{4,20},{20... | collective-permute-start | bytes 589832 | tf_op jit(solution)/shard_map/ppermute | solution.py:256
  62.5 15.7 %collective-permute-start.20 = (bf16[64,2688]{1,0:T(8,128)(2,1)S(1)}, bf16[64,2688]{1,0:T(8,128)(2,1)S(1)}, u32[]{:S(2)}, u32[]{:S(2)}) collective-permute-start(bf16[64,2688]{1,0:T(8,128)(2,1)S(1)} %get-tuple-element.44.half_ref), channel_id=1, source_target_pairs={{0,2},{1,3},{2,0},{3,1},{4,6},{5,7},{6,4},{7,5},{8,10},{9,11},{10,... | collective-permute-start | bytes 1032200 | tf_op jit(solution)/shard_map/ppermute | solution.py:253
  70.7 1.4 %collective-permute-start.12 = (bf16[1,4,128,128]{3,2,1,0:T(8,128)(2,1)S(1)}, bf16[1,4,128,128]{3,2,1,0:T(8,128)(2,1)S(1)}, u32[]{:S(2)}, u32[]{:S(2)}) collective-permute-start(bf16[1,4,128,128]{3,2,1,0:T(8,128)(2,1)S(1)} %get-tuple-element.55), channel_id=1, source_target_pairs={{0,4},{4,0},{8,12},{12,8},{1,5},{5,1},{9,13},{13,9},{2,6},{6,2},{1... | collective-permute-start | bytes 393224 | tf_op jit(solution)/shard_map/ppermute | solution.py:242
  70.8 8.6 %collective-permute-start.17 = (bf16[16,128,128]{2,1,0:T(8,128)(2,1)S(1)}, bf16[16,128,128]{2,1,0:T(8,128)(2,1)S(1)}, u32[]{:S(2)}, u32[]{:S(2)}) collective-permute-start(bf16[16,128,128]{2,1,0:T(8,128)(2,1)S(1)} %get-tuple-element.61), channel_id=1, source_target_pairs={{0,4},{4,0},{8,12},{12,8},{1,5},{5,1},{9,13},{13,9},{2,6},{6,2},{1... | collective-permute-start | bytes 1572872 | tf_op jit(solution)/shard_map/ppermute | solution.py:242
  71.3 1.8 %collective-permute-start.13 = (bf16[1,4,128,128]{3,2,1,0:T(8,128)(2,1)S(1)}, bf16[1,4,128,128]{3,2,1,0:T(8,128)(2,1)S(1)}, u32[]{:S(2)}, u32[]{:S(2)}) collective-permute-start(bf16[1,4,128,128]{3,2,1,0:T(8,128)(2,1)S(1)} %get-tuple-element.57), channel_id=1, source_target_pairs={{0,4},{4,0},{8,12},{12,8},{1,5},{5,1},{9,13},{13,9},{2,6},{6,2},{1... | collective-permute-start | bytes 393224 | tf_op jit(solution)/shard_map/ppermute | solution.py:242
  71.4 1.9 %collective-permute-start.14 = (bf16[1,4,128,128]{3,2,1,0:T(8,128)(2,1)S(1)}, bf16[1,4,128,128]{3,2,1,0:T(8,128)(2,1)S(1)}, u32[]{:S(2)}, u32[]{:S(2)}) collective-permute-start(bf16[1,4,128,128]{3,2,1,0:T(8,128)(2,1)S(1)} %get-tuple-element.58), channel_id=1, source_target_pairs={{0,4},{4,0},{8,12},{12,8},{1,5},{5,1},{9,13},{13,9},{2,6},{6,2},{1... | collective-permute-start | bytes 393224 | tf_op jit(solution)/shard_map/ppermute | solution.py:242
  72.1 1.3 %collective-permute-start.15 = (bf16[1,4,128,128]{3,2,1,0:T(8,128)(2,1)S(1)}, bf16[1,4,128,128]{3,2,1,0:T(8,128)(2,1)S(1)}, u32[]{:S(2)}, u32[]{:S(2)}) collective-permute-start(bf16[1,4,128,128]{3,2,1,0:T(8,128)(2,1)S(1)} %get-tuple-element.59), channel_id=1, source_target_pairs={{0,4},{4,0},{8,12},{12,8},{1,5},{5,1},{9,13},{13,9},{2,6},{6,2},{1... | collective-permute-start | bytes 393224 | tf_op jit(solution)/shard_map/ppermute | solution.py:242
  73.0 6.3 %collective-permute-start.18 = (bf16[4,128,128]{2,1,0:T(8,128)(2,1)S(1)}, bf16[4,128,128]{2,1,0:T(8,128)(2,1)S(1)}, u32[]{:S(2)}, u32[]{:S(2)}) collective-permute-start(bf16[4,128,128]{2,1,0:T(8,128)(2,1)S(1)} %bitcast.24), channel_id=1, source_target_pairs={{0,8},{4,12},{8,0},{12,4},{1,9},{5,13},{9,1},{13,5},{2,10},{6,14},... | collective-permute-start | bytes 393224 | tf_op jit(solution)/shard_map/ppermute | solution.py:246
  74.1 8.0 %collective-permute-start.25 = (bf16[1,8,128,128]{3,2,1,0:T(8,128)(2,1)S(1)}, bf16[1,8,128,128]{3,2,1,0:T(8,128)(2,1)S(1)}, u32[]{:S(2)}, u32[]{:S(2)}) collective-permute-start(bf16[1,8,128,128]{3,2,1,0:T(8,128)(2,1)S(1)} %get-tuple-element.67), channel_id=1, source_target_pairs={{0,4},{4,0},{8,12},{12,8},{1,5},{5,1},{9,13},{13,9},{2,6},{6,2},{1... | collective-permute-start | bytes 786440 | tf_op jit(solution)/shard_map/ppermute | solution.py:242
  74.4 17.1 %collective-permute-start.22 = (bf16[12,128,128]{2,1,0:T(8,128)(2,1)S(1)}, bf16[12,128,128]{2,1,0:T(8,128)(2,1)S(1)}, u32[]{:S(2)}, u32[]{:S(2)}) collective-permute-start(bf16[12,128,128]{2,1,0:T(8,128)(2,1)S(1)} %bitcast.23), channel_id=1, source_target_pairs={{0,8},{4,12},{8,0},{12,4},{1,9},{5,13},{9,1},{13,5},{2,10},{6,14},... | collective-permute-start | bytes 1179656 | tf_op jit(solution)/shard_map/ppermute | solution.py:246
  78.2 3.9 %collective-permute-start.24 = (bf16[1,8,128,128]{3,2,1,0:T(8,128)(2,1)S(1)}, bf16[1,8,128,128]{3,2,1,0:T(8,128)(2,1)S(1)}, u32[]{:S(2)}, u32[]{:S(2)}) collective-permute-start(bf16[1,8,128,128]{3,2,1,0:T(8,128)(2,1)S(1)} %get-tuple-element.65), channel_id=1, source_target_pairs={{0,4},{4,0},{8,12},{12,8},{1,5},{5,1},{9,13},{13,9},{2,6},{6,2},{1... | collective-permute-start | bytes 786440 | tf_op jit(solution)/shard_map/ppermute | solution.py:242
  79.4 10.7 %collective-permute-start.21 = (bf16[64,2688]{1,0:T(8,128)(2,1)S(1)}, bf16[64,2688]{1,0:T(8,128)(2,1)S(1)}, u32[]{:S(2)}, u32[]{:S(2)}) collective-permute-start(bf16[64,2688]{1,0:T(8,128)(2,1)S(1)} %collective-permute-done.20.rest_0_), channel_id=1, source_target_pairs={{0,1},{1,0},{2,3},{3,2},{4,5},{5,4},{6,7},{7,6},{8,9},{9,8},{10,11... | collective-permute-start | bytes 1032200 | tf_op jit(solution)/shard_map/ppermute | solution.py:249
  80.0 11.5 %collective-permute-start.19 = (bf16[4,128,128]{2,1,0:T(8,128)(2,1)S(1)}, bf16[4,128,128]{2,1,0:T(8,128)(2,1)S(1)}, u32[]{:S(2)}, u32[]{:S(2)}) collective-permute-start(bf16[4,128,128]{2,1,0:T(8,128)(2,1)S(1)} %shard_map.102), channel_id=1, source_target_pairs={{0,1},{1,0},{2,3},{3,2},{4,5},{5,4},{6,7},{7,6},{8,9},{9,8},{10,11... | collective-permute-start | bytes 393224 | tf_op jit(solution)/shard_map/ppermute | solution.py:249
  82.1 12.2 %collective-permute-start.16 = (bf16[16,128,128]{2,1,0:T(8,128)(2,1)S(1)}, bf16[16,128,128]{2,1,0:T(8,128)(2,1)S(1)}, u32[]{:S(2)}, u32[]{:S(2)}) collective-permute-start(bf16[16,128,128]{2,1,0:T(8,128)(2,1)S(1)} %get-tuple-element.60), channel_id=1, source_target_pairs={{0,4},{4,0},{8,12},{12,8},{1,5},{5,1},{9,13},{13,9},{2,6},{6,2},{1... | collective-permute-start | bytes 1572872 | tf_op jit(solution)/shard_map/ppermute | solution.py:242
  82.7 19.0 %copy-start.6 = (bf16[64,2048]{1,0:T(8,128)(2,1)S(1)}, bf16[64,2048]{1,0:T(8,128)(2,1)}, u32[]{:S(2)}) copy-start(bf16[64,2048]{1,0:T(8,128)(2,1)} %adapter_ref.2) | copy-start | bytes 786436
  82.7 19.9 %collective-permute-start.26 = (bf16[16,128,128]{2,1,0:T(8,128)(2,1)S(1)}, bf16[16,128,128]{2,1,0:T(8,128)(2,1)S(1)}, u32[]{:S(2)}, u32[]{:S(2)}) collective-permute-start(bf16[16,128,128]{2,1,0:T(8,128)(2,1)S(1)} %bitcast.21), channel_id=1, source_target_pairs={{0,8},{4,12},{8,0},{12,4},{1,9},{5,13},{9,1},{13,5},{2,10},{6,14},... | collective-permute-start | bytes 1572872 | tf_op jit(solution)/shard_map/ppermute | solution.py:246
  92.2 9.5 %collective-permute-start.23 = (bf16[12,128,128]{2,1,0:T(8,128)(2,1)S(1)}, bf16[12,128,128]{2,1,0:T(8,128)(2,1)S(1)}, u32[]{:S(2)}, u32[]{:S(2)}) collective-permute-start(bf16[12,128,128]{2,1,0:T(8,128)(2,1)S(1)} %shard_map.103), channel_id=1, source_target_pairs={{0,1},{1,0},{2,3},{3,2},{4,5},{5,4},{6,7},{7,6},{8,9},{9,8},{10,11... | collective-permute-start | bytes 1179656 | tf_op jit(solution)/shard_map/ppermute | solution.py:249
  (7 other events, 10.0 us)

commit v8 on v7

--- a/solution.py
+++ b/solution.py
@@ -15,14 +15,13 @@
 BF16 = jnp.bfloat16
 
 
-def add_blocks(total_ref, tiles_ref, blocks_ref, ids_ref, base, col_blocks):
-    count = blocks_ref.shape[0]
+def add_blocks(total_ref, tiles_ref, blocks_ref, count, ident_at, col_blocks):
     unroll = max(u for u in range(1, 9) if count % u == 0)
 
     def one(step, carry):
         for u in range(unroll):
             k = step * unroll + u
-            ident = ids_ref[base + k]
+            ident = ident_at(k)
             known = jnp.maximum(ident, 0)
             row = lax.div(known, col_blocks)
             col = jnp.where(ident >= 0, lax.rem(known, col_blocks), col_blocks)
@@ -33,22 +32,30 @@
 
 
 def add_arrivals(where_ref, ids_ref, tiles_ref, blocks, total_ref, places, parts, held, col_blocks):
-    for blocks_ref, (offset, shift, start) in zip(blocks, places):
-        source = lax.rem(where_ref[0] + (parts - shift), parts)
-        base = offset + source * held + start
-        add_blocks(total_ref, tiles_ref, blocks_ref, ids_ref, base, col_blocks)
-
-
-def first_kernel(where_ref, own_ids_ref, ids_ref, own_ref, mate_ref, own_blocks_ref, *rest, **plan):
-    blocks, (total_ref, tiles_ref) = rest[:-2], rest[-2:]
+    for blocks_ref, (source, shift, start, size) in zip(blocks, places):
+        base = lax.rem(where_ref[0] + (parts - shift), parts) * held + start
+        add_blocks(
+            total_ref, tiles_ref, blocks_ref, size, lambda k: ids_ref[source, base + k], col_blocks
+        )
+
+
+def ids_kernel(*refs, col_blocks):
+    coded, ids_ref = refs[:-1], refs[-1]
+    for source, ref in enumerate(coded):
+        code = ref[ref.shape[0] - 1].astype(F32)
+        ids_ref[source:source + 1, :] = (code[0:1, :] * col_blocks + code[1:2, :]).astype(jnp.int32)
+
+
+def first_kernel(where_ref, ids_ref, own_ref, mate_ref, own_blocks_ref, total_ref, tiles_ref, *, col_blocks):
     row_blocks, _, tile = tiles_ref.shape
     tokens = own_ref.shape[0]
     total_ref[...] = jnp.zeros_like(total_ref)
     for i in range(row_blocks):
         tiles_ref[i, :tokens, :] = own_ref[:, i * tile:(i + 1) * tile]
         tiles_ref[i, tokens:, :] = mate_ref[:, i * tile:(i + 1) * tile]
-    add_blocks(total_ref, tiles_ref, own_blocks_ref, own_ids_ref, 0, plan["col_blocks"])
-    add_arrivals(where_ref, ids_ref, tiles_ref, blocks, total_ref, **plan)
+    add_blocks(
+        total_ref, tiles_ref, own_blocks_ref, own_blocks_ref.shape[0], lambda k: ids_ref[k], col_blocks
+    )
 
 
 def more_kernel(where_ref, ids_ref, tiles_ref, old_ref, *rest, **plan):
@@ -274,22 +281,28 @@
         ids = block_ids[0]
         labels = forget_labels[None, :]
 
-        far_ids = [group_shift(ids, d) for d in range(1, group)]
-        all_ids = far_ids[0] if group == 2 else jnp.concatenate(far_ids)
         held = slots // n_parts
-        sizes = [held * k // 32 for k in (16, 10, 6)]
+        sizes = [held * k // 32 for k in (14, 12, 6)]
         starts = [sum(sizes[:k]) for k in range(len(sizes))]
         leaving_chunks = [
-            after(lax.dynamic_slice_in_dim(blocks, part * held + start, size, axis=0), all_ids)
+            lax.dynamic_slice_in_dim(blocks, part * held + start, size, axis=0)
             for start, size in zip(starts, sizes)
         ]
+        known = jnp.maximum(ids, 0)
+        code = jnp.stack([
+            jnp.where(ids >= 0, lax.div(known, col_blocks), -1),
+            jnp.where(ids >= 0, lax.rem(known, col_blocks), 0),
+        ]).astype(BF16)
+        code = jnp.pad(code, ((0, tile - 2), (0, tile - slots)))[None]
+        soon = core_swap(after(ids + 1, leaving_chunks[0]))
+        leaving_chunks[1] = jnp.concatenate([leaving_chunks[1], code], axis=0)
+        leaving_chunks[1:] = [after(chunk, soon) for chunk in leaving_chunks[1:]]
         direct = [
-            (group_shift(leaving_chunks[k], d), ((d - 1) * slots, 0, starts[k]))
+            (group_shift(leaving_chunks[k], d), (d - 1, 0, starts[k], sizes[k]))
             for d in range(1, group) for k in range(len(starts))
         ]
-        mate_activations = mate_swap(after(activations, all_ids))
-
-        soon = core_swap(after(ids + 1, all_ids, leaving_chunks[0]))
+        mate_activations = mate_swap(activations)
+
         (both,) = call(
             low_rank_kernel, (jax.ShapeDtypeStruct((2 * rank, tokens), F32),), (),
             (activations, after(adapter_a, soon).T, cotangent, after(output_adapter, soon), labels),
@@ -316,9 +329,9 @@
 
         total_shape = pltpu.VMEM((col_blocks + 1, 2 * tokens, tile), F32)
         total, tiles = call(
-            functools.partial(first_kernel, **plan([])),
+            functools.partial(first_kernel, col_blocks=col_blocks),
             (total_shape, pltpu.VMEM((row_blocks, 2 * tokens, tile), BF16)),
-            (after(where, rounded, leaving_chunks[-1]), ids, all_ids), (activations, mate_activations, blocks),
+            (after(where, rounded, leaving_chunks[-1]), ids), (activations, mate_activations, blocks),
         )
         half_shape = jax.ShapeDtypeStruct((rank, (shard_rows + feats) // 2), BF16)
         half_grads, other_grads = call(
@@ -326,9 +339,15 @@
         )
         far_grads = [group_shift(half_grads, d) for d in range(1, group)]
 
+        (all_ids,) = call(
+            functools.partial(ids_kernel, col_blocks=col_blocks),
+            (jax.ShapeDtypeStruct((group - 1, tile), jnp.int32),), (),
+            tuple(value for value, place in direct if place[2] == starts[1]),
+        )
+        gates = {starts[0]: rounded, starts[1]: total, starts[2]: half_grads}
         swapped = [
-            (part_shift(after(value, total) if start == 0 else after(value, half_grads) if start == starts[1] else value, e), (offset, e, start))
-            for value, (offset, _, start) in direct for e in range(1, n_parts)
+            (part_shift(after(value, gates[start])[:size], e), (source, e, start, size))
+            for value, (source, _, start, size) in direct for e in range(1, n_parts)
         ]
         more = direct + chunk(swapped, 0) + chunk(swapped, 1)
         last = chunk(swapped, 2)

time: 104 us -> 105 us (level)
  waiting for transfers between devices: 50.3 us -> 54.9 us
  starting transfers between devices: 24 us -> 20.7 us
    ppermute x5 -> x4, waiting for transfers between devices: 9.87 us -> 5.13 us  [group_shift(): return lax.ppermute(value, 'dp', pairs)]
    ppermute x5 -> x4, starting transfers between devices: 9.28 us -> 4.92 us  [group_shift(): return lax.ppermute(value, 'dp', pairs)]
    ppermute x5, waiting for transfers between devices: 31 us -> 34.8 us  [mate_swap(): return lax.ppermute(value, 'dp', [(i, i ^ 1) for i in range(n_dp)])]
    ppermute x3, waiting for transfers between devices: 3.63 us -> 7.34 us  [part_shift(): lax.ppermute(value, 'parts', [(i, (i + d) % n_parts) for i in range(n_par...]
    ppermute x4, waiting for transfers between devices: 2.87 us -> 5.77 us  [chip_shift(): return lax.ppermute(value, 'row', pairs)]
    ppermute x4, starting transfers between devices: 3.04 us -> 5.26 us  [chip_shift(): return lax.ppermute(value, 'row', pairs)]
    unnamed x24 -> x18, local copies, waits for them, and re-layouts: 5.19 us -> 4.07 us
    ppermute x10, waiting for transfers between devices: 2.9 us -> 1.8 us  [core_swap(): return lax.ppermute(value, 'row', [(i, i ^ 1) for i in range(n_row)])]
  transfers between devices with their start and end apart: 27 -> 26, of which waited for: 18 -> 12; matrix products, arithmetic and copies ran while one was open for 4% -> 3% of each run, Pallas kernels for 17% -> 17%
where the time goes in v8:
time: 105 us; the launch traced here: 104 us
  waiting for transfers between devices  54.9 us (52%)
  starting transfers between devices  20.7 us (20%)
  Pallas kernels  18.6 us (18%)
  local copies, waits for them, and re-layouts  7.11 us (7%)
  other arithmetic  2.28 us (2%)
    ppermute x5, waiting for transfers between devices, mate_swap(): return lax.ppermute(value, 'dp', [(i, i ^ 1) for i in range(n_dp)])  34.8 us
    pallas_call x15, Pallas kernels, call(): pl.pallas_call(kernel, out_shape=outs, in_specs=[smem] * len(scalars) + [...  18.6 us
    ppermute x3, waiting for transfers between devices, part_shift(): lax.ppermute(value, 'parts', [(i, (i + d) % n_parts) for i in range(n_par...  7.34 us
    ppermute x4, waiting for transfers between devices, chip_shift(): return lax.ppermute(value, 'row', pairs)  5.77 us
    ppermute x4, starting transfers between devices, chip_shift(): return lax.ppermute(value, 'row', pairs)  5.26 us
    ppermute x4, waiting for transfers between devices, group_shift(): return lax.ppermute(value, 'dp', pairs)  5.13 us
    ppermute x4, starting transfers between devices, group_shift(): return lax.ppermute(value, 'dp', pairs)  4.92 us
    ppermute x3, starting transfers between devices, part_shift(): lax.ppermute(value, 'parts', [(i, (i + d) % n_parts) for i in range(n_par...  4.52 us
  transfers between devices with their start and end apart: 26, of which 12 were waited for; matrix products, arithmetic and copies ran while one was open for 3% of the time, Pallas kernels for 17%

profile of v8, /device:TPU:0, one launch (start us, length us, event | category | flops | bytes accessed | tf_op | source)
XLA Modules:
  0.0 104.4 jit_solution(16642357094782993234)
XLA Ops:
  0.7 1.9 %dynamic-slice_bitcast_fusion = bf16[14,128,128]{2,1,0:T(8,128)(2,1)} fusion(bf16[1,64,128,128]{3,2,1,0:T(8,128)(2,1)} %param.10, s32[]{:T(128)S(6)} %select_n.18), kind=kLoop, calls=%fused_computation | loop fusion | bytes 917508 | tf_op jit(solution)/shard_map/dynamic_slice | solution.py:288
  2.6 4.0 %collective-permute-start.6 = (bf16[14,128,128]{2,1,0:T(8,128)(2,1)}, bf16[14,128,128]{2,1,0:T(8,128)(2,1)}, u32[]{:S(2)}, u32[]{:S(2)}) collective-permute-start(bf16[14,128,128]{2,1,0:T(8,128)(2,1)} %dynamic-slice_bitcast_fusion), channel_id=1, source_target_pairs={{0,2},{1,3},{2,0},{3,1},{4,6},{5,7},{6,4},{7,5},{8,10},{9,11},{10,... | collective-permute-start | bytes 1376264 | tf_op jit(solution)/shard_map/ppermute | solution.py:260
  7.3 1.6 %collective-permute-start.3 = (bf16[128,3328]{1,0:T(8,128)(2,1)}, bf16[128,3328]{1,0:T(8,128)(2,1)}, u32[]{:S(2)}, u32[]{:S(2)}) collective-permute-start(bf16[128,3328]{1,0:T(8,128)(2,1)} %own_ref.1), channel_id=1, source_target_pairs={{0,1},{1,0},{2,3},{3,2},{4,5},{5,4},{6,7},{7,6},{8,9},{9,8},{10,11... | collective-permute-start | bytes 2555912 | tf_op jit(solution)/shard_map/ppermute | solution.py:256
  8.8 1.0 dynamic-slice_bitcast_fusion.1
  9.9 0.8 fusion.7
  11.8 1.0 copy-done.2
  12.9 0.9 copy-done.4
  13.8 1.0 copy-done.6
  15.5 1.2 %collective-permute-done.1 = f32[128,128]{1,0:T(8,128)S(1)} collective-permute-done((f32[128,128]{1,0:T(8,128)S(1)}, f32[128,128]{1,0:T(8,128)S(1)}, u32[]{:S(2)}, u32[]{:S(2)}) %collective-permute-start.1) | collective-permute-done | bytes 65568 | tf_op jit(solution)/shard_map/ppermute | solution.py:249
  16.8 1.6 %collective-permute-start.2 = (f32[128,128]{1,0:T(8,128)S(1)}, f32[128,128]{1,0:T(8,128)S(1)}, u32[]{:S(2)}, u32[]{:S(2)}) collective-permute-start(f32[128,128]{1,0:T(8,128)S(1)} %add.33.both_ref), channel_id=1, source_target_pairs={{0,8},{4,12},{8,0},{12,4},{1,9},{5,13},{9,1},{13,5},{2,10},{6,14},... | collective-permute-start | bytes 196616 | tf_op jit(solution)/shard_map/ppermute | solution.py:253
  18.4 2.7 %collective-permute-done.2.rest_0_ = f32[128,128]{1,0:T(8,128)S(1)} collective-permute-done((f32[128,128]{1,0:T(8,128)S(1)}, f32[128,128]{1,0:T(8,128)S(1)}, u32[]{:S(2)}, u32[]{:S(2)}) %collective-permute-start.2) | collective-permute-done | bytes 65568 | tf_op jit(solution)/shard_map/ppermute | solution.py:253
  21.1 1.0 copy-done.3
  23.1 5.1 %collective-permute-done.6.rest_0_ = bf16[14,128,128]{2,1,0:T(8,128)(2,1)} collective-permute-done((bf16[14,128,128]{2,1,0:T(8,128)(2,1)}, bf16[14,128,128]{2,1,0:T(8,128)(2,1)}, u32[]{:S(2)}, u32[]{:S(2)}) %collective-permute-start.6) | collective-permute-done | bytes 458784 | tf_op jit(solution)/shard_map/ppermute | solution.py:260
  28.2 1.9 %collective-permute-start.8 = (bf16[14,128,128]{2,1,0:T(8,128)(2,1)}, bf16[14,128,128]{2,1,0:T(8,128)(2,1)S(1)}, u32[]{:S(2)}, u32[]{:S(2)}) collective-permute-start(bf16[14,128,128]{2,1,0:T(8,128)(2,1)} %collective-permute-done.6.rest_0_), channel_id=1, source_target_pairs={{0,16},{16,0},{1,17},{17,1},{2,18},{18,2},{3,19},{19,3},{4,20},{20... | collective-permute-start | bytes 1376264 | tf_op jit(solution)/shard_map/ppermute | solution.py:263
  30.2 21.2 %collective-permute-done.3.mate_acts_ref.mate_ref = bf16[128,3328]{1,0:T(8,128)(2,1)} collective-permute-done((bf16[128,3328]{1,0:T(8,128)(2,1)}, bf16[128,3328]{1,0:T(8,128)(2,1)}, u32[]{:S(2)}, u32[]{:S(2)}) %collective-permute-start.3) | collective-permute-done | bytes 852000 | tf_op jit(solution)/shard_map/ppermute | solution.py:256
  51.3 4.4 %shard_map.98 = (f32[65,256,128]{2,1,0:T(8,128)S(1)}, bf16[26,256,128]{2,1,0:T(8,128)(2,1)S(1)}) custom-call(s32[6]{0:T(128)S(1)} %stack.29.where_ref, s32[64]{0:T(128)S(1)} %bitcast.29, bf16[128,3328]{1,0:T(8,128)(2,1)S(1)} %copy-done, bf16[128,3328]{1,0:T(8,128)(2,1)} %collective-permute-done.3.mate_acts_ref.mate_ref, bf16[64,128,128]{2,1,0:T(8,128)(2,1)S(1)} %bitcast.22), custom_call_target="tpu_custom_call" | custom-call | tf_op jit(solution)/shard_map/pallas_call | solution.py:225
  55.8 1.6 %collective-permute-start.9 = (bf16[12,128,128]{2,1,0:T(8,128)(2,1)S(1)}, bf16[12,128,128]{2,1,0:T(8,128)(2,1)S(1)}, u32[]{:S(2)}, u32[]{:S(2)}) collective-permute-start(bf16[12,128,128]{2,1,0:T(8,128)(2,1)S(1)} %slice.3), channel_id=1, source_target_pairs={{0,16},{16,0},{1,17},{17,1},{2,18},{18,2},{3,19},{19,3},{4,20},{20... | collective-permute-start | bytes 1179656 | tf_op jit(solution)/shard_map/ppermute | solution.py:263
  57.4 1.6 %shard_map.96 = (bf16[64,2688]{1,0:T(8,128)(2,1)S(1)}, bf16[64,2688]{1,0:T(8,128)(2,1)S(1)}) custom-call(s32[6]{0:T(128)S(1)} %stack.29.where_ref, bf16[128,128]{1,0:T(8,128)(2,1)S(1)} %get-tuple-element.39.rounded_ref, bf16[128,3328]{1,0:T(8,128)(2,1)S(1)} %copy-done, bf16[128,3328]{1,0:T(8,128)(2,1)} %collective-permute-done.3.mate_acts_ref.mate_ref, ...), custom_call_target="tpu_custom_call" | custom-call | tf_op jit(solution)/shard_map/pallas_call | solution.py:225
  59.0 1.0 collective-permute-start.10
  60.6 7.3 %collective-permute-done.9.rest_4_ = bf16[12,128,128]{2,1,0:T(8,128)(2,1)S(1)} collective-permute-done((bf16[12,128,128]{2,1,0:T(8,128)(2,1)S(1)}, bf16[12,128,128]{2,1,0:T(8,128)(2,1)S(1)}, u32[]{:S(2)}, u32[]{:S(2)}) %collective-permute-start.9) | collective-permute-done | bytes 393248 | tf_op jit(solution)/shard_map/ppermute | solution.py:263
  67.9 3.5 %shard_map.99.old_ref = f32[65,256,128]{2,1,0:T(8,128)S(1)} custom-call(s32[6]{0:T(128)S(1)} %stack.29.where_ref, s32[1,128]{1,0:T(1,128)S(1)} %shard_map.97.ids_ref, bf16[26,256,128]{2,1,0:T(8,128)(2,1)S(1)} %get-tuple-element.46.tiles_ref, f32[65,256,128]{2,1,0:T(8,128)S(1)} %get-tuple-element.47.old_ref, ...), custom_call_target="tpu_custom_call", output_to_operand_aliasing={{}: (3, {})} | custom-call | tf_op jit(solution)/shard_map/pallas_call | solution.py:225
  71.4 1.0 shard_map.100
  74.7 1.5 %collective-permute-start.17 = (bf16[4,128,128]{2,1,0:T(8,128)(2,1)S(1)}, bf16[4,128,128]{2,1,0:T(8,128)(2,1)S(1)}, u32[]{:S(2)}, u32[]{:S(2)}) collective-permute-start(bf16[4,128,128]{2,1,0:T(8,128)(2,1)S(1)} %bitcast.26), channel_id=1, source_target_pairs={{0,8},{4,12},{8,0},{12,4},{1,9},{5,13},{9,1},{13,5},{2,10},{6,14},... | collective-permute-start | bytes 393224 | tf_op jit(solution)/shard_map/ppermute | solution.py:253
  78.0 3.1 %collective-permute-done.17.rest_0_ = bf16[4,128,128]{2,1,0:T(8,128)(2,1)S(1)} collective-permute-done((bf16[4,128,128]{2,1,0:T(8,128)(2,1)S(1)}, bf16[4,128,128]{2,1,0:T(8,128)(2,1)S(1)}, u32[]{:S(2)}, u32[]{:S(2)}) %collective-permute-start.17) | collective-permute-done | bytes 131104 | tf_op jit(solution)/shard_map/ppermute | solution.py:253
  81.6 2.1 %collective-permute-start.18 = (bf16[4,128,128]{2,1,0:T(8,128)(2,1)S(1)}, bf16[4,128,128]{2,1,0:T(8,128)(2,1)S(1)}, u32[]{:S(2)}, u32[]{:S(2)}) collective-permute-start(bf16[4,128,128]{2,1,0:T(8,128)(2,1)S(1)} %shard_map.103), channel_id=1, source_target_pairs={{0,1},{1,0},{2,3},{3,2},{4,5},{5,4},{6,7},{7,6},{8,9},{9,8},{10,11... | collective-permute-start | bytes 393224 | tf_op jit(solution)/shard_map/ppermute | solution.py:256
  84.4 1.6 %collective-permute-start.25 = (bf16[16,128,128]{2,1,0:T(8,128)(2,1)S(1)}, bf16[16,128,128]{2,1,0:T(8,128)(2,1)S(1)}, u32[]{:S(2)}, u32[]{:S(2)}) collective-permute-start(bf16[16,128,128]{2,1,0:T(8,128)(2,1)S(1)} %bitcast.23), channel_id=1, source_target_pairs={{0,8},{4,12},{8,0},{12,4},{1,9},{5,13},{9,1},{13,5},{2,10},{6,14},... | collective-permute-start | bytes 1572872 | tf_op jit(solution)/shard_map/ppermute | solution.py:253
  86.0 5.3 %collective-permute-done.20.rest_1_ = bf16[64,2688]{1,0:T(8,128)(2,1)S(1)} collective-permute-done((bf16[64,2688]{1,0:T(8,128)(2,1)S(1)}, bf16[64,2688]{1,0:T(8,128)(2,1)S(1)}, u32[]{:S(2)}, u32[]{:S(2)}) %collective-permute-start.20) | collective-permute-done | bytes 344096 | tf_op jit(solution)/shard_map/ppermute | solution.py:256
  91.3 1.4 %collective-permute-done.18.rest_0_ = bf16[4,128,128]{2,1,0:T(8,128)(2,1)S(1)} collective-permute-done((bf16[4,128,128]{2,1,0:T(8,128)(2,1)S(1)}, bf16[4,128,128]{2,1,0:T(8,128)(2,1)S(1)}, u32[]{:S(2)}, u32[]{:S(2)}) %collective-permute-start.18) | collective-permute-done | bytes 131104 | tf_op jit(solution)/shard_map/ppermute | solution.py:256
  93.8 1.8 %shard_map.108 = (f32[64,3328]{1,0:T(8,128)}, f32[64,2048]{1,0:T(8,128)}) custom-call(s32[6]{0:T(128)S(1)} %stack.29.where_ref, bf16[64,2688]{1,0:T(8,128)(2,1)S(1)} %get-tuple-element.41.half_ref, bf16[64,2688]{1,0:T(8,128)(2,1)S(1)} %get-tuple-element.66.other_ref, bf16[64,2688]{1,0:T(8,128)(2,1)S(1)} %collective-permute-done.19.rest_0_, ...), custom_call_target="tpu_custom_call" | custom-call | tf_op jit(solution)/shard_map/pallas_call | solution.py:225
  95.5 7.0 %collective-permute-done.22.rest_1_ = bf16[12,128,128]{2,1,0:T(8,128)(2,1)S(1)} collective-permute-done((bf16[12,128,128]{2,1,0:T(8,128)(2,1)S(1)}, bf16[12,128,128]{2,1,0:T(8,128)(2,1)S(1)}, u32[]{:S(2)}, u32[]{:S(2)}) %collective-permute-start.22) | collective-permute-done | bytes 393248 | tf_op jit(solution)/shard_map/ppermute | solution.py:256
  102.5 1.0 shard_map.105.near_ref
  103.5 0.9 shard_map.107
  (63 shorter events, 10.5 us)
Async XLA Ops:
  0.6 11.2 %copy-start = (bf16[128,3328]{1,0:T(8,128)(2,1)S(1)}, bf16[128,3328]{1,0:T(8,128)(2,1)}, u32[]{:S(2)}) copy-start(bf16[128,3328]{1,0:T(8,128)(2,1)} %own_ref.1) | copy-start | bytes 2555908
  0.6 11.2 %copy-start.7 = (s32[128]{0:T(128)S(1)}, s32[128]{0:T(128)}, u32[]{:S(2)}) copy-start(s32[128]{0:T(128)} %param.9) | copy-start | bytes 1540
  2.6 25.6 %collective-permute-start.6 = (bf16[14,128,128]{2,1,0:T(8,128)(2,1)}, bf16[14,128,128]{2,1,0:T(8,128)(2,1)}, u32[]{:S(2)}, u32[]{:S(2)}) collective-permute-start(bf16[14,128,128]{2,1,0:T(8,128)(2,1)} %dynamic-slice_bitcast_fusion), channel_id=1, source_target_pairs={{0,2},{1,3},{2,0},{3,1},{4,6},{5,7},{6,4},{7,5},{8,10},{9,11},{10,... | collective-permute-start | bytes 1376264 | tf_op jit(solution)/shard_map/ppermute | solution.py:260
  7.3 4.2 %collective-permute-start = (s32[64]{0:T(128)S(1)}, s32[64]{0:T(128)S(1)}, u32[]{:S(2)}, u32[]{:S(2)}) collective-permute-start(s32[64]{0:T(128)S(1)} %broadcast_add_fusion), channel_id=1, source_target_pairs={{0,4},{4,0},{8,12},{12,8},{1,5},{5,1},{9,13},{13,9},{2,6},{6,2},{1... | collective-permute-start | bytes 776 | tf_op jit(solution)/shard_map/ppermute | solution.py:249
  7.3 44.1 %collective-permute-start.3 = (bf16[128,3328]{1,0:T(8,128)(2,1)}, bf16[128,3328]{1,0:T(8,128)(2,1)}, u32[]{:S(2)}, u32[]{:S(2)}) collective-permute-start(bf16[128,3328]{1,0:T(8,128)(2,1)} %own_ref.1), channel_id=1, source_target_pairs={{0,1},{1,0},{2,3},{3,2},{4,5},{5,4},{6,7},{7,6},{8,9},{9,8},{10,11... | collective-permute-start | bytes 2555912 | tf_op jit(solution)/shard_map/ppermute | solution.py:256
  9.9 20.2 %copy-start.1 = (bf16[1,64,128,128]{3,2,1,0:T(8,128)(2,1)S(1)}, bf16[1,64,128,128]{3,2,1,0:T(8,128)(2,1)}, u32[]{:S(2)}) copy-start(bf16[1,64,128,128]{3,2,1,0:T(8,128)(2,1)} %param.10) | copy-start | bytes 6291460
  11.5 44.2 %collective-permute-start.5 = (bf16[13,128,128]{2,1,0:T(8,128)(2,1)}, bf16[13,128,128]{2,1,0:T(8,128)(2,1)S(1)}, u32[]{:S(2)}, u32[]{:S(2)}) collective-permute-start(bf16[13,128,128]{2,1,0:T(8,128)(2,1)} %pad_maximum_fusion), channel_id=1, source_target_pairs={{0,2},{1,3},{2,0},{3,1},{4,6},{5,7},{6,4},{7,5},{8,10},{9,11},{10,... | collective-permute-start | bytes 1277960 | tf_op jit(solution)/shard_map/ppermute | solution.py:260
  11.8 1.0 copy-start.2
  14.8 36.5 %copy-start.8 = (s32[1,64]{1,0:T(1,128)S(1)}, s32[1,64]{1,0:T(1,128)}, u32[]{:S(2)}) copy-start(s32[1,64]{1,0:T(1,128)} %param.11) | copy-start | bytes 772
  15.4 1.3 %collective-permute-start.1 = (f32[128,128]{1,0:T(8,128)S(1)}, f32[128,128]{1,0:T(8,128)S(1)}, u32[]{:S(2)}, u32[]{:S(2)}) collective-permute-start(f32[128,128]{1,0:T(8,128)S(1)} %shard_map.94), channel_id=1, source_target_pairs={{0,4},{4,0},{8,12},{12,8},{1,5},{5,1},{9,13},{13,9},{2,6},{6,2},{1... | collective-permute-start | bytes 196616 | tf_op jit(solution)/shard_map/ppermute | solution.py:249
  16.8 4.3 %collective-permute-start.2 = (f32[128,128]{1,0:T(8,128)S(1)}, f32[128,128]{1,0:T(8,128)S(1)}, u32[]{:S(2)}, u32[]{:S(2)}) collective-permute-start(f32[128,128]{1,0:T(8,128)S(1)} %add.33.both_ref), channel_id=1, source_target_pairs={{0,8},{4,12},{8,0},{12,4},{1,9},{5,13},{9,1},{13,5},{2,10},{6,14},... | collective-permute-start | bytes 196616 | tf_op jit(solution)/shard_map/ppermute | solution.py:253
  22.9 34.5 %collective-permute-start.4 = (bf16[64,2176]{1,0:T(8,128)(2,1)S(1)}, bf16[64,2176]{1,0:T(8,128)(2,1)S(1)}, u32[]{:S(2)}, u32[]{:S(2)}) collective-permute-start(bf16[64,2176]{1,0:T(8,128)(2,1)S(1)} %get-tuple-element.40.pack_ref), channel_id=1, source_target_pairs={{0,1},{1,0},{2,3},{3,2},{4,5},{5,4},{6,7},{7,6},{8,9},{9,8},{10,11... | collective-permute-start | bytes 835592 | tf_op jit(solution)/shard_map/ppermute | solution.py:256
  28.2 32.4 %collective-permute-start.8 = (bf16[14,128,128]{2,1,0:T(8,128)(2,1)}, bf16[14,128,128]{2,1,0:T(8,128)(2,1)S(1)}, u32[]{:S(2)}, u32[]{:S(2)}) collective-permute-start(bf16[14,128,128]{2,1,0:T(8,128)(2,1)} %collective-permute-done.6.rest_0_), channel_id=1, source_target_pairs={{0,16},{16,0},{1,17},{17,1},{2,18},{18,2},{3,19},{19,3},{4,20},{20... | collective-permute-start | bytes 1376264 | tf_op jit(solution)/shard_map/ppermute | solution.py:263
  30.1 29.0 %collective-permute-start.7 = (bf16[6,128,128]{2,1,0:T(8,128)(2,1)S(1)}, bf16[6,128,128]{2,1,0:T(8,128)(2,1)S(1)}, u32[]{:S(2)}, u32[]{:S(2)}) collective-permute-start(bf16[6,128,128]{2,1,0:T(8,128)(2,1)S(1)} %dynamic-slice_bitcast_fusion.2), channel_id=1, source_target_pairs={{0,2},{1,3},{2,0},{3,1},{4,6},{5,7},{6,4},{7,5},{8,10},{9,11},{10,... | collective-permute-start | bytes 589832 | tf_op jit(solution)/shard_map/ppermute | solution.py:260
  55.8 12.1 %collective-permute-start.9 = (bf16[12,128,128]{2,1,0:T(8,128)(2,1)S(1)}, bf16[12,128,128]{2,1,0:T(8,128)(2,1)S(1)}, u32[]{:S(2)}, u32[]{:S(2)}) collective-permute-start(bf16[12,128,128]{2,1,0:T(8,128)(2,1)S(1)} %slice.3), channel_id=1, source_target_pairs={{0,16},{16,0},{1,17},{17,1},{2,18},{18,2},{3,19},{19,3},{4,20},{20... | collective-permute-start | bytes 1179656 | tf_op jit(solution)/shard_map/ppermute | solution.py:263
  59.0 12.3 %collective-permute-start.10 = (bf16[6,128,128]{2,1,0:T(8,128)(2,1)S(1)}, bf16[6,128,128]{2,1,0:T(8,128)(2,1)S(1)}, u32[]{:S(2)}, u32[]{:S(2)}) collective-permute-start(bf16[6,128,128]{2,1,0:T(8,128)(2,1)S(1)} %collective-permute-done.7.rest_2_), channel_id=1, source_target_pairs={{0,16},{16,0},{1,17},{17,1},{2,18},{18,2},{3,19},{19,3},{4,20},{20... | collective-permute-start | bytes 589832 | tf_op jit(solution)/shard_map/ppermute | solution.py:263
  60.1 17.5 %collective-permute-start.19 = (bf16[64,2688]{1,0:T(8,128)(2,1)S(1)}, bf16[64,2688]{1,0:T(8,128)(2,1)S(1)}, u32[]{:S(2)}, u32[]{:S(2)}) collective-permute-start(bf16[64,2688]{1,0:T(8,128)(2,1)S(1)} %get-tuple-element.41.half_ref), channel_id=1, source_target_pairs={{0,2},{1,3},{2,0},{3,1},{4,6},{5,7},{6,4},{7,5},{8,10},{9,11},{10,... | collective-permute-start | bytes 1032200 | tf_op jit(solution)/shard_map/ppermute | solution.py:260
  72.4 1.4 %collective-permute-start.11 = (bf16[1,4,128,128]{3,2,1,0:T(8,128)(2,1)S(1)}, bf16[1,4,128,128]{3,2,1,0:T(8,128)(2,1)S(1)}, u32[]{:S(2)}, u32[]{:S(2)}) collective-permute-start(bf16[1,4,128,128]{3,2,1,0:T(8,128)(2,1)S(1)} %get-tuple-element.53), channel_id=1, source_target_pairs={{0,4},{4,0},{8,12},{12,8},{1,5},{5,1},{9,13},{13,9},{2,6},{6,2},{1... | collective-permute-start | bytes 393224 | tf_op jit(solution)/shard_map/ppermute | solution.py:249
  72.5 8.6 %collective-permute-start.16 = (bf16[16,128,128]{2,1,0:T(8,128)(2,1)S(1)}, bf16[16,128,128]{2,1,0:T(8,128)(2,1)S(1)}, u32[]{:S(2)}, u32[]{:S(2)}) collective-permute-start(bf16[16,128,128]{2,1,0:T(8,128)(2,1)S(1)} %get-tuple-element.59), channel_id=1, source_target_pairs={{0,4},{4,0},{8,12},{12,8},{1,5},{5,1},{9,13},{13,9},{2,6},{6,2},{1... | collective-permute-start | bytes 1572872 | tf_op jit(solution)/shard_map/ppermute | solution.py:249
  72.9 1.8 %collective-permute-start.12 = (bf16[1,4,128,128]{3,2,1,0:T(8,128)(2,1)S(1)}, bf16[1,4,128,128]{3,2,1,0:T(8,128)(2,1)S(1)}, u32[]{:S(2)}, u32[]{:S(2)}) collective-permute-start(bf16[1,4,128,128]{3,2,1,0:T(8,128)(2,1)S(1)} %get-tuple-element.55), channel_id=1, source_target_pairs={{0,4},{4,0},{8,12},{12,8},{1,5},{5,1},{9,13},{13,9},{2,6},{6,2},{1... | collective-permute-start | bytes 393224 | tf_op jit(solution)/shard_map/ppermute | solution.py:249
  73.0 3.2 %collective-permute-start.13 = (bf16[1,4,128,128]{3,2,1,0:T(8,128)(2,1)S(1)}, bf16[1,4,128,128]{3,2,1,0:T(8,128)(2,1)S(1)}, u32[]{:S(2)}, u32[]{:S(2)}) collective-permute-start(bf16[1,4,128,128]{3,2,1,0:T(8,128)(2,1)S(1)} %get-tuple-element.56), channel_id=1, source_target_pairs={{0,4},{4,0},{8,12},{12,8},{1,5},{5,1},{9,13},{13,9},{2,6},{6,2},{1... | collective-permute-start | bytes 393224 | tf_op jit(solution)/shard_map/ppermute | solution.py:249
  73.8 2.5 %collective-permute-start.14 = (bf16[1,4,128,128]{3,2,1,0:T(8,128)(2,1)S(1)}, bf16[1,4,128,128]{3,2,1,0:T(8,128)(2,1)S(1)}, u32[]{:S(2)}, u32[]{:S(2)}) collective-permute-start(bf16[1,4,128,128]{3,2,1,0:T(8,128)(2,1)S(1)} %get-tuple-element.57), channel_id=1, source_target_pairs={{0,4},{4,0},{8,12},{12,8},{1,5},{5,1},{9,13},{13,9},{2,6},{6,2},{1... | collective-permute-start | bytes 393224 | tf_op jit(solution)/shard_map/ppermute | solution.py:249
  74.7 6.3 %collective-permute-start.17 = (bf16[4,128,128]{2,1,0:T(8,128)(2,1)S(1)}, bf16[4,128,128]{2,1,0:T(8,128)(2,1)S(1)}, u32[]{:S(2)}, u32[]{:S(2)}) collective-permute-start(bf16[4,128,128]{2,1,0:T(8,128)(2,1)S(1)} %bitcast.26), channel_id=1, source_target_pairs={{0,8},{4,12},{8,0},{12,4},{1,9},{5,13},{9,1},{13,5},{2,10},{6,14},... | collective-permute-start | bytes 393224 | tf_op jit(solution)/shard_map/ppermute | solution.py:253
  76.9 15.8 %collective-permute-start.21 = (bf16[12,128,128]{2,1,0:T(8,128)(2,1)S(1)}, bf16[12,128,128]{2,1,0:T(8,128)(2,1)S(1)}, u32[]{:S(2)}, u32[]{:S(2)}) collective-permute-start(bf16[12,128,128]{2,1,0:T(8,128)(2,1)S(1)} %bitcast.25), channel_id=1, source_target_pairs={{0,8},{4,12},{8,0},{12,4},{1,9},{5,13},{9,1},{13,5},{2,10},{6,14},... | collective-permute-start | bytes 1179656 | tf_op jit(solution)/shard_map/ppermute | solution.py:253
  77.5 6.3 %collective-permute-start.23 = (bf16[1,8,128,128]{3,2,1,0:T(8,128)(2,1)S(1)}, bf16[1,8,128,128]{3,2,1,0:T(8,128)(2,1)S(1)}, u32[]{:S(2)}, u32[]{:S(2)}) collective-permute-start(bf16[1,8,128,128]{3,2,1,0:T(8,128)(2,1)S(1)} %get-tuple-element.63), channel_id=1, source_target_pairs={{0,4},{4,0},{8,12},{12,8},{1,5},{5,1},{9,13},{13,9},{2,6},{6,2},{1... | collective-permute-start | bytes 786440 | tf_op jit(solution)/shard_map/ppermute | solution.py:249
  77.5 6.2 %collective-permute-start.24 = (bf16[1,8,128,128]{3,2,1,0:T(8,128)(2,1)S(1)}, bf16[1,8,128,128]{3,2,1,0:T(8,128)(2,1)S(1)}, u32[]{:S(2)}, u32[]{:S(2)}) collective-permute-start(bf16[1,8,128,128]{3,2,1,0:T(8,128)(2,1)S(1)} %get-tuple-element.65), channel_id=1, source_target_pairs={{0,4},{4,0},{8,12},{12,8},{1,5},{5,1},{9,13},{13,9},{2,6},{6,2},{1... | collective-permute-start | bytes 786440 | tf_op jit(solution)/shard_map/ppermute | solution.py:249
  81.0 10.3 %collective-permute-start.20 = (bf16[64,2688]{1,0:T(8,128)(2,1)S(1)}, bf16[64,2688]{1,0:T(8,128)(2,1)S(1)}, u32[]{:S(2)}, u32[]{:S(2)}) collective-permute-start(bf16[64,2688]{1,0:T(8,128)(2,1)S(1)} %collective-permute-done.19.rest_0_), channel_id=1, source_target_pairs={{0,1},{1,0},{2,3},{3,2},{4,5},{5,4},{6,7},{7,6},{8,9},{9,8},{10,11... | collective-permute-start | bytes 1032200 | tf_op jit(solution)/shard_map/ppermute | solution.py:256
  81.6 11.1 %collective-permute-start.18 = (bf16[4,128,128]{2,1,0:T(8,128)(2,1)S(1)}, bf16[4,128,128]{2,1,0:T(8,128)(2,1)S(1)}, u32[]{:S(2)}, u32[]{:S(2)}) collective-permute-start(bf16[4,128,128]{2,1,0:T(8,128)(2,1)S(1)} %shard_map.103), channel_id=1, source_target_pairs={{0,1},{1,0},{2,3},{3,2},{4,5},{5,4},{6,7},{7,6},{8,9},{9,8},{10,11... | collective-permute-start | bytes 393224 | tf_op jit(solution)/shard_map/ppermute | solution.py:256
  83.7 11.8 %collective-permute-start.15 = (bf16[16,128,128]{2,1,0:T(8,128)(2,1)S(1)}, bf16[16,128,128]{2,1,0:T(8,128)(2,1)S(1)}, u32[]{:S(2)}, u32[]{:S(2)}) collective-permute-start(bf16[16,128,128]{2,1,0:T(8,128)(2,1)S(1)} %get-tuple-element.58), channel_id=1, source_target_pairs={{0,4},{4,0},{8,12},{12,8},{1,5},{5,1},{9,13},{13,9},{2,6},{6,2},{1... | collective-permute-start | bytes 1572872 | tf_op jit(solution)/shard_map/ppermute | solution.py:249
  84.4 18.1 %copy-start.5 = (bf16[64,2048]{1,0:T(8,128)(2,1)S(1)}, bf16[64,2048]{1,0:T(8,128)(2,1)}, u32[]{:S(2)}) copy-start(bf16[64,2048]{1,0:T(8,128)(2,1)} %adapter_ref.2) | copy-start | bytes 786436
  84.4 19.0 %collective-permute-start.25 = (bf16[16,128,128]{2,1,0:T(8,128)(2,1)S(1)}, bf16[16,128,128]{2,1,0:T(8,128)(2,1)S(1)}, u32[]{:S(2)}, u32[]{:S(2)}) collective-permute-start(bf16[16,128,128]{2,1,0:T(8,128)(2,1)S(1)} %bitcast.23), channel_id=1, source_target_pairs={{0,8},{4,12},{8,0},{12,4},{1,9},{5,13},{9,1},{13,5},{2,10},{6,14},... | collective-permute-start | bytes 1572872 | tf_op jit(solution)/shard_map/ppermute | solution.py:253
  93.4 9.1 %collective-permute-start.22 = (bf16[12,128,128]{2,1,0:T(8,128)(2,1)S(1)}, bf16[12,128,128]{2,1,0:T(8,128)(2,1)S(1)}, u32[]{:S(2)}, u32[]{:S(2)}) collective-permute-start(bf16[12,128,128]{2,1,0:T(8,128)(2,1)S(1)} %shard_map.104), channel_id=1, source_target_pairs={{0,1},{1,0},{2,3},{3,2},{4,5},{5,4},{6,7},{7,6},{8,9},{9,8},{10,11... | collective-permute-start | bytes 1179656 | tf_op jit(solution)/shard_map/ppermute | solution.py:256
  (3 other events, 3.0 us)

commit v9 on v8

--- a/solution.py
+++ b/solution.py
@@ -282,7 +282,7 @@
         labels = forget_labels[None, :]
 
         held = slots // n_parts
-        sizes = [held * k // 32 for k in (14, 12, 6)]
+        sizes = [held * k // 32 for k in (16, 10, 6)]
         starts = [sum(sizes[:k]) for k in range(len(sizes))]
         leaving_chunks = [
             lax.dynamic_slice_in_dim(blocks, part * held + start, size, axis=0)
@@ -335,7 +335,7 @@
         )
         half_shape = jax.ShapeDtypeStruct((rank, (shard_rows + feats) // 2), BF16)
         half_grads, other_grads = call(
-            pair_grad_kernel, (half_shape, half_shape), (where,), (rounded, activations, mate_activations, pack, mate_pack),
+            pair_grad_kernel, (half_shape, half_shape), (after(where, total),), (rounded, activations, mate_activations, pack, mate_pack),
         )
         far_grads = [group_shift(half_grads, d) for d in range(1, group)]
 
@@ -344,9 +344,9 @@
             (jax.ShapeDtypeStruct((group - 1, tile), jnp.int32),), (),
             tuple(value for value, place in direct if place[2] == starts[1]),
         )
-        gates = {starts[0]: rounded, starts[1]: total, starts[2]: half_grads}
+        gates = {starts[0]: (rounded,), starts[1]: (mate_activations,), starts[2]: (half_grads, total)}
         swapped = [
-            (part_shift(after(value, gates[start])[:size], e), (source, e, start, size))
+            (part_shift((after(value, *gates[start]) if gates[start] else value)[:size], e), (source, e, start, size))
             for value, (source, _, start, size) in direct for e in range(1, n_parts)
         ]
         more = direct + chunk(swapped, 0) + chunk(swapped, 1)

time: 105 us -> 105 us (level)
  waiting for transfers between devices: 54.9 us -> 51.2 us
  starting transfers between devices: 20.7 us -> 23.4 us
    ppermute x4, waiting for transfers between devices: 5.13 us -> 23.2 us  [group_shift(): return lax.ppermute(value, 'dp', pairs)]
    ppermute x5, waiting for transfers between devices: 34.8 us -> 22.8 us  [mate_swap(): return lax.ppermute(value, 'dp', [(i, i ^ 1) for i in range(n_dp)])]
    ppermute x3, waiting for transfers between devices: 7.34 us -> 0.73 us  [part_shift(): lax.ppermute(value, 'parts', [(i, (i + d) % n_parts) for i in range(n_par...]
    ppermute x4, starting transfers between devices: 4.92 us -> 8.03 us  [group_shift(): return lax.ppermute(value, 'dp', pairs)]
    ppermute x4, waiting for transfers between devices: 5.77 us -> 2.7 us  [chip_shift(): return lax.ppermute(value, 'row', pairs)]
    unnamed x18 -> x22, local copies, waits for them, and re-layouts: 4.07 us -> 4.78 us
where the time goes in v9:
time: 105 us; the launch traced here: 104 us
  waiting for transfers between devices  51.2 us (49%)
  starting transfers between devices  23.4 us (22%)
  Pallas kernels  18.6 us (18%)
  local copies, waits for them, and re-layouts  8 us (8%)
  other arithmetic  2.11 us (2%)
    ppermute x4, waiting for transfers between devices, group_shift(): return lax.ppermute(value, 'dp', pairs)  23.2 us
    ppermute x5, waiting for transfers between devices, mate_swap(): return lax.ppermute(value, 'dp', [(i, i ^ 1) for i in range(n_dp)])  22.8 us
    pallas_call x15, Pallas kernels, call(): pl.pallas_call(kernel, out_shape=outs, in_specs=[smem] * len(scalars) + [...  18.6 us
    ppermute x4, starting transfers between devices, group_shift(): return lax.ppermute(value, 'dp', pairs)  8.03 us
    ppermute x4, starting transfers between devices, chip_shift(): return lax.ppermute(value, 'row', pairs)  5.3 us
    unnamed x22, local copies, waits for them, and re-layouts  4.78 us
    ppermute x3, starting transfers between devices, part_shift(): lax.ppermute(value, 'parts', [(i, (i + d) % n_parts) for i in range(n_par...  4.57 us
    ppermute x5, starting transfers between devices, mate_swap(): return lax.ppermute(value, 'dp', [(i, i ^ 1) for i in range(n_dp)])  4.01 us
  transfers between devices with their start and end apart: 26, of which 12 were waited for; matrix products, arithmetic and copies ran while one was open for 3% of the time, Pallas kernels for 17%

profile of v9, /device:TPU:0, one launch (start us, length us, event | category | flops | bytes accessed | tf_op | source)
XLA Modules:
  0.0 104.2 jit_solution(4258603491904701318)
XLA Ops:
  0.7 2.0 %dynamic-slice_bitcast_fusion = bf16[16,128,128]{2,1,0:T(8,128)(2,1)} fusion(bf16[1,64,128,128]{3,2,1,0:T(8,128)(2,1)} %param.10, s32[]{:T(128)S(6)} %select_n.18), kind=kLoop, calls=%fused_computation | loop fusion | bytes 1048580 | tf_op jit(solution)/shard_map/dynamic_slice | solution.py:288
  2.6 4.0 %collective-permute-start.6 = (bf16[16,128,128]{2,1,0:T(8,128)(2,1)}, bf16[16,128,128]{2,1,0:T(8,128)(2,1)}, u32[]{:S(2)}, u32[]{:S(2)}) collective-permute-start(bf16[16,128,128]{2,1,0:T(8,128)(2,1)} %dynamic-slice_bitcast_fusion), channel_id=1, source_target_pairs={{0,2},{1,3},{2,0},{3,1},{4,6},{5,7},{6,4},{7,5},{8,10},{9,11},{10,... | collective-permute-start | bytes 1572872 | tf_op jit(solution)/shard_map/ppermute | solution.py:260
  7.3 1.6 %collective-permute-start.3 = (bf16[128,3328]{1,0:T(8,128)(2,1)}, bf16[128,3328]{1,0:T(8,128)(2,1)}, u32[]{:S(2)}, u32[]{:S(2)}) collective-permute-start(bf16[128,3328]{1,0:T(8,128)(2,1)} %acts_ref.3), channel_id=1, source_target_pairs={{0,1},{1,0},{2,3},{3,2},{4,5},{5,4},{6,7},{7,6},{8,9},{9,8},{10,11... | collective-permute-start | bytes 2555912 | tf_op jit(solution)/shard_map/ppermute | solution.py:256
  9.6 1.1 %dynamic-slice_bitcast_fusion.1 = bf16[10,128,128]{2,1,0:T(8,128)(2,1)S(1)} fusion(bf16[1,64,128,128]{3,2,1,0:T(8,128)(2,1)} %param.10, s32[]{:T(128)S(6)} %select_n.20), kind=kLoop, calls=%fused_computation.2 | loop fusion | bytes 655364 | tf_op jit(solution)/shard_map/dynamic_slice | solution.py:288
  11.9 1.0 copy-done.2
  12.9 0.9 copy-done.4
  13.8 1.0 copy-done.6
  15.5 1.2 %collective-permute-done.1 = f32[128,128]{1,0:T(8,128)S(1)} collective-permute-done((f32[128,128]{1,0:T(8,128)S(1)}, f32[128,128]{1,0:T(8,128)S(1)}, u32[]{:S(2)}, u32[]{:S(2)}) %collective-permute-start.1) | collective-permute-done | bytes 65568 | tf_op jit(solution)/shard_map/ppermute | solution.py:249
  16.8 1.6 %collective-permute-start.2 = (f32[128,128]{1,0:T(8,128)S(1)}, f32[128,128]{1,0:T(8,128)S(1)}, u32[]{:S(2)}, u32[]{:S(2)}) collective-permute-start(f32[128,128]{1,0:T(8,128)S(1)} %add.33.both_ref), channel_id=1, source_target_pairs={{0,8},{4,12},{8,0},{12,4},{1,9},{5,13},{9,1},{13,5},{2,10},{6,14},... | collective-permute-start | bytes 196616 | tf_op jit(solution)/shard_map/ppermute | solution.py:253
  18.4 2.7 %collective-permute-done.2.rest_0_ = f32[128,128]{1,0:T(8,128)S(1)} collective-permute-done((f32[128,128]{1,0:T(8,128)S(1)}, f32[128,128]{1,0:T(8,128)S(1)}, u32[]{:S(2)}, u32[]{:S(2)}) %collective-permute-start.2) | collective-permute-done | bytes 65568 | tf_op jit(solution)/shard_map/ppermute | solution.py:253
  21.1 1.0 copy-done.3
  23.6 7.4 %collective-permute-done.6.rest_0_ = bf16[16,128,128]{2,1,0:T(8,128)(2,1)} collective-permute-done((bf16[16,128,128]{2,1,0:T(8,128)(2,1)}, bf16[16,128,128]{2,1,0:T(8,128)(2,1)}, u32[]{:S(2)}, u32[]{:S(2)}) %collective-permute-start.6) | collective-permute-done | bytes 524320 | tf_op jit(solution)/shard_map/ppermute | solution.py:260
  31.1 1.9 %collective-permute-start.8 = (bf16[16,128,128]{2,1,0:T(8,128)(2,1)}, bf16[16,128,128]{2,1,0:T(8,128)(2,1)}, u32[]{:S(2)}, u32[]{:S(2)}) collective-permute-start(bf16[16,128,128]{2,1,0:T(8,128)(2,1)} %collective-permute-done.6.rest_0_), channel_id=1, source_target_pairs={{0,16},{16,0},{1,17},{17,1},{2,18},{18,2},{3,19},{19,3},{4,20},{20... | collective-permute-start | bytes 1572872 | tf_op jit(solution)/shard_map/ppermute | solution.py:263
  33.0 3.1 %collective-permute-start.7 = (bf16[6,128,128]{2,1,0:T(8,128)(2,1)S(1)}, bf16[6,128,128]{2,1,0:T(8,128)(2,1)S(1)}, u32[]{:S(2)}, u32[]{:S(2)}) collective-permute-start(bf16[6,128,128]{2,1,0:T(8,128)(2,1)S(1)} %dynamic-slice_bitcast_fusion.2), channel_id=1, source_target_pairs={{0,2},{1,3},{2,0},{3,1},{4,6},{5,7},{6,4},{7,5},{8,10},{9,11},{10,... | collective-permute-start | bytes 589832 | tf_op jit(solution)/shard_map/ppermute | solution.py:260
  36.0 9.6 %collective-permute-done.5.refs_0_.rest_1_ = bf16[11,128,128]{2,1,0:T(8,128)(2,1)S(1)} collective-permute-done((bf16[11,128,128]{2,1,0:T(8,128)(2,1)}, bf16[11,128,128]{2,1,0:T(8,128)(2,1)S(1)}, u32[]{:S(2)}, u32[]{:S(2)}) %collective-permute-start.5) | collective-permute-done | bytes 360480 | tf_op jit(solution)/shard_map/ppermute | solution.py:260
  45.7 5.7 %collective-permute-done.3.mate_ref.mate_acts_ref = bf16[128,3328]{1,0:T(8,128)(2,1)} collective-permute-done((bf16[128,3328]{1,0:T(8,128)(2,1)}, bf16[128,3328]{1,0:T(8,128)(2,1)}, u32[]{:S(2)}, u32[]{:S(2)}) %collective-permute-start.3) | collective-permute-done | bytes 852000 | tf_op jit(solution)/shard_map/ppermute | solution.py:256
  51.4 1.6 %collective-permute-start.9 = (bf16[10,128,128]{2,1,0:T(8,128)(2,1)S(1)}, bf16[10,128,128]{2,1,0:T(8,128)(2,1)S(1)}, u32[]{:S(2)}, u32[]{:S(2)}) collective-permute-start(bf16[10,128,128]{2,1,0:T(8,128)(2,1)S(1)} %slice.3), channel_id=1, source_target_pairs={{0,16},{16,0},{1,17},{17,1},{2,18},{18,2},{3,19},{19,3},{4,20},{20... | collective-permute-start | bytes 983048 | tf_op jit(solution)/shard_map/ppermute | solution.py:263
  53.0 4.4 %shard_map.96 = (f32[65,256,128]{2,1,0:T(8,128)S(1)}, bf16[26,256,128]{2,1,0:T(8,128)(2,1)S(1)}) custom-call(s32[6]{0:T(128)S(1)} %stack.29.where_ref, s32[64]{0:T(128)S(1)} %bitcast.29, bf16[128,3328]{1,0:T(8,128)(2,1)S(1)} %copy-done, bf16[128,3328]{1,0:T(8,128)(2,1)} %collective-permute-done.3.mate_ref.mate_acts_ref, bf16[64,128,128]{2,1,0:T(8,128)(2,1)S(1)} %bitcast.22), custom_call_target="tpu_custom_call" | custom-call | tf_op jit(solution)/shard_map/pallas_call | solution.py:225
  57.4 1.6 %shard_map.97 = (bf16[64,2688]{1,0:T(8,128)(2,1)S(1)}, bf16[64,2688]{1,0:T(8,128)(2,1)S(1)}) custom-call(s32[6]{0:T(128)S(1)} %stack.29.where_ref, bf16[128,128]{1,0:T(8,128)(2,1)S(1)} %get-tuple-element.40.rounded_ref, bf16[128,3328]{1,0:T(8,128)(2,1)S(1)} %copy-done, bf16[128,3328]{1,0:T(8,128)(2,1)} %collective-permute-done.3.mate_ref.mate_acts_ref, ...), custom_call_target="tpu_custom_call" | custom-call | tf_op jit(solution)/shard_map/pallas_call | solution.py:225
  59.1 1.1 %collective-permute-start.10 = (bf16[6,128,128]{2,1,0:T(8,128)(2,1)S(1)}, bf16[6,128,128]{2,1,0:T(8,128)(2,1)S(1)}, u32[]{:S(2)}, u32[]{:S(2)}) collective-permute-start(bf16[6,128,128]{2,1,0:T(8,128)(2,1)S(1)} %collective-permute-done.7.rest_2_), channel_id=1, source_target_pairs={{0,16},{16,0},{1,17},{17,1},{2,18},{18,2},{3,19},{19,3},{4,20},{20... | collective-permute-start | bytes 589832 | tf_op jit(solution)/shard_map/ppermute | solution.py:263
  60.7 3.6 %shard_map.99.old_ref = f32[65,256,128]{2,1,0:T(8,128)S(1)} custom-call(s32[6]{0:T(128)S(1)} %stack.29.where_ref, s32[1,128]{1,0:T(1,128)S(1)} %shard_map.98.ids_ref, bf16[26,256,128]{2,1,0:T(8,128)(2,1)S(1)} %get-tuple-element.49.tiles_ref, f32[65,256,128]{2,1,0:T(8,128)S(1)} %get-tuple-element.43.old_ref, ...), custom_call_target="tpu_custom_call", output_to_operand_aliasing={{}: (3, {})} | custom-call | tf_op jit(solution)/shard_map/pallas_call | solution.py:225
  65.1 1.0 shard_map.100
  68.5 1.5 %collective-permute-start.17 = (bf16[4,128,128]{2,1,0:T(8,128)(2,1)S(1)}, bf16[4,128,128]{2,1,0:T(8,128)(2,1)S(1)}, u32[]{:S(2)}, u32[]{:S(2)}) collective-permute-start(bf16[4,128,128]{2,1,0:T(8,128)(2,1)S(1)} %bitcast.26), channel_id=1, source_target_pairs={{0,8},{4,12},{8,0},{12,4},{1,9},{5,13},{9,1},{13,5},{2,10},{6,14},... | collective-permute-start | bytes 393224 | tf_op jit(solution)/shard_map/ppermute | solution.py:253
  71.4 6.2 %collective-permute-done.19.rest_0_ = bf16[64,2688]{1,0:T(8,128)(2,1)S(1)} collective-permute-done((bf16[64,2688]{1,0:T(8,128)(2,1)S(1)}, bf16[64,2688]{1,0:T(8,128)(2,1)S(1)}, u32[]{:S(2)}, u32[]{:S(2)}) %collective-permute-start.19) | collective-permute-done | bytes 344096 | tf_op jit(solution)/shard_map/ppermute | solution.py:260
  78.2 2.1 %collective-permute-start.18 = (bf16[4,128,128]{2,1,0:T(8,128)(2,1)S(1)}, bf16[4,128,128]{2,1,0:T(8,128)(2,1)S(1)}, u32[]{:S(2)}, u32[]{:S(2)}) collective-permute-start(bf16[4,128,128]{2,1,0:T(8,128)(2,1)S(1)} %shard_map.103), channel_id=1, source_target_pairs={{0,1},{1,0},{2,3},{3,2},{4,5},{5,4},{6,7},{7,6},{8,9},{9,8},{10,11... | collective-permute-start | bytes 393224 | tf_op jit(solution)/shard_map/ppermute | solution.py:256
  81.0 1.6 %collective-permute-start.25 = (bf16[16,128,128]{2,1,0:T(8,128)(2,1)S(1)}, bf16[16,128,128]{2,1,0:T(8,128)(2,1)S(1)}, u32[]{:S(2)}, u32[]{:S(2)}) collective-permute-start(bf16[16,128,128]{2,1,0:T(8,128)(2,1)S(1)} %bitcast.23), channel_id=1, source_target_pairs={{0,8},{4,12},{8,0},{12,4},{1,9},{5,13},{9,1},{13,5},{2,10},{6,14},... | collective-permute-start | bytes 1572872 | tf_op jit(solution)/shard_map/ppermute | solution.py:253
  82.5 5.9 %collective-permute-done.20.rest_1_ = bf16[64,2688]{1,0:T(8,128)(2,1)S(1)} collective-permute-done((bf16[64,2688]{1,0:T(8,128)(2,1)S(1)}, bf16[64,2688]{1,0:T(8,128)(2,1)S(1)}, u32[]{:S(2)}, u32[]{:S(2)}) %collective-permute-start.20) | collective-permute-done | bytes 344096 | tf_op jit(solution)/shard_map/ppermute | solution.py:256
  88.5 2.4 %collective-permute-done.18.rest_0_ = bf16[4,128,128]{2,1,0:T(8,128)(2,1)S(1)} collective-permute-done((bf16[4,128,128]{2,1,0:T(8,128)(2,1)S(1)}, bf16[4,128,128]{2,1,0:T(8,128)(2,1)S(1)}, u32[]{:S(2)}, u32[]{:S(2)}) %collective-permute-start.18) | collective-permute-done | bytes 131104 | tf_op jit(solution)/shard_map/ppermute | solution.py:256
  91.9 1.8 %shard_map.108 = (f32[64,3328]{1,0:T(8,128)}, f32[64,2048]{1,0:T(8,128)}) custom-call(s32[6]{0:T(128)S(1)} %stack.29.where_ref, bf16[64,2688]{1,0:T(8,128)(2,1)S(1)} %get-tuple-element.46.half_ref, bf16[64,2688]{1,0:T(8,128)(2,1)S(1)} %get-tuple-element.68.other_ref, bf16[64,2688]{1,0:T(8,128)(2,1)S(1)} %collective-permute-done.19.rest_0_, ...), custom_call_target="tpu_custom_call" | custom-call | tf_op jit(solution)/shard_map/pallas_call | solution.py:225
  93.7 8.7 %collective-permute-done.22.rest_1_ = bf16[12,128,128]{2,1,0:T(8,128)(2,1)S(1)} collective-permute-done((bf16[12,128,128]{2,1,0:T(8,128)(2,1)S(1)}, bf16[12,128,128]{2,1,0:T(8,128)(2,1)S(1)}, u32[]{:S(2)}, u32[]{:S(2)}) %collective-permute-start.22) | collective-permute-done | bytes 393248 | tf_op jit(solution)/shard_map/ppermute | solution.py:256
  102.4 0.9 shard_map.105.near_ref
  103.3 0.9 shard_map.107
  (67 shorter events, 12.0 us)
Async XLA Ops:
  0.6 11.2 %copy-start = (bf16[128,3328]{1,0:T(8,128)(2,1)S(1)}, bf16[128,3328]{1,0:T(8,128)(2,1)}, u32[]{:S(2)}) copy-start(bf16[128,3328]{1,0:T(8,128)(2,1)} %acts_ref.3) | copy-start | bytes 2555908
  0.6 11.2 %copy-start.9 = (s32[128]{0:T(128)S(1)}, s32[128]{0:T(128)}, u32[]{:S(2)}) copy-start(s32[128]{0:T(128)} %param.9) | copy-start | bytes 1540
  2.6 28.4 %collective-permute-start.6 = (bf16[16,128,128]{2,1,0:T(8,128)(2,1)}, bf16[16,128,128]{2,1,0:T(8,128)(2,1)}, u32[]{:S(2)}, u32[]{:S(2)}) collective-permute-start(bf16[16,128,128]{2,1,0:T(8,128)(2,1)} %dynamic-slice_bitcast_fusion), channel_id=1, source_target_pairs={{0,2},{1,3},{2,0},{3,1},{4,6},{5,7},{6,4},{7,5},{8,10},{9,11},{10,... | collective-permute-start | bytes 1572872 | tf_op jit(solution)/shard_map/ppermute | solution.py:260
  7.3 4.2 %collective-permute-start = (s32[64]{0:T(128)S(1)}, s32[64]{0:T(128)S(1)}, u32[]{:S(2)}, u32[]{:S(2)}) collective-permute-start(s32[64]{0:T(128)S(1)} %broadcast_add_fusion), channel_id=1, source_target_pairs={{0,4},{4,0},{8,12},{12,8},{1,5},{5,1},{9,13},{13,9},{2,6},{6,2},{1... | collective-permute-start | bytes 776 | tf_op jit(solution)/shard_map/ppermute | solution.py:249
  7.3 44.1 %collective-permute-start.3 = (bf16[128,3328]{1,0:T(8,128)(2,1)}, bf16[128,3328]{1,0:T(8,128)(2,1)}, u32[]{:S(2)}, u32[]{:S(2)}) collective-permute-start(bf16[128,3328]{1,0:T(8,128)(2,1)} %acts_ref.3), channel_id=1, source_target_pairs={{0,1},{1,0},{2,3},{3,2},{4,5},{5,4},{6,7},{7,6},{8,9},{9,8},{10,11... | collective-permute-start | bytes 2555912 | tf_op jit(solution)/shard_map/ppermute | solution.py:256
  9.6 43.5 %copy-start.10 = (s32[1,64]{1,0:T(1,128)S(1)}, s32[1,64]{1,0:T(1,128)}, u32[]{:S(2)}) copy-start(s32[1,64]{1,0:T(1,128)} %param.11) | copy-start | bytes 772
  9.6 23.4 %copy-start.1 = (bf16[1,64,128,128]{3,2,1,0:T(8,128)(2,1)S(1)}, bf16[1,64,128,128]{3,2,1,0:T(8,128)(2,1)}, u32[]{:S(2)}) copy-start(bf16[1,64,128,128]{3,2,1,0:T(8,128)(2,1)} %param.10) | copy-start | bytes 6291460
  11.5 34.1 %collective-permute-start.5 = (bf16[11,128,128]{2,1,0:T(8,128)(2,1)}, bf16[11,128,128]{2,1,0:T(8,128)(2,1)S(1)}, u32[]{:S(2)}, u32[]{:S(2)}) collective-permute-start(bf16[11,128,128]{2,1,0:T(8,128)(2,1)} %pad_maximum_fusion), channel_id=1, source_target_pairs={{0,2},{1,3},{2,0},{3,1},{4,6},{5,7},{6,4},{7,5},{8,10},{9,11},{10,... | collective-permute-start | bytes 1081352 | tf_op jit(solution)/shard_map/ppermute | solution.py:260
  15.4 1.3 %collective-permute-start.1 = (f32[128,128]{1,0:T(8,128)S(1)}, f32[128,128]{1,0:T(8,128)S(1)}, u32[]{:S(2)}, u32[]{:S(2)}) collective-permute-start(f32[128,128]{1,0:T(8,128)S(1)} %shard_map.94), channel_id=1, source_target_pairs={{0,4},{4,0},{8,12},{12,8},{1,5},{5,1},{9,13},{13,9},{2,6},{6,2},{1... | collective-permute-start | bytes 196616 | tf_op jit(solution)/shard_map/ppermute | solution.py:249
  16.8 4.3 %collective-permute-start.2 = (f32[128,128]{1,0:T(8,128)S(1)}, f32[128,128]{1,0:T(8,128)S(1)}, u32[]{:S(2)}, u32[]{:S(2)}) collective-permute-start(f32[128,128]{1,0:T(8,128)S(1)} %add.33.both_ref), channel_id=1, source_target_pairs={{0,8},{4,12},{8,0},{12,4},{1,9},{5,13},{9,1},{13,5},{2,10},{6,14},... | collective-permute-start | bytes 196616 | tf_op jit(solution)/shard_map/ppermute | solution.py:253
  31.1 29.7 %collective-permute-start.8 = (bf16[16,128,128]{2,1,0:T(8,128)(2,1)}, bf16[16,128,128]{2,1,0:T(8,128)(2,1)}, u32[]{:S(2)}, u32[]{:S(2)}) collective-permute-start(bf16[16,128,128]{2,1,0:T(8,128)(2,1)} %collective-permute-done.6.rest_0_), channel_id=1, source_target_pairs={{0,16},{16,0},{1,17},{17,1},{2,18},{18,2},{3,19},{19,3},{4,20},{20... | collective-permute-start | bytes 1572872 | tf_op jit(solution)/shard_map/ppermute | solution.py:263
  32.9 24.5 %collective-permute-start.4 = (bf16[64,2176]{1,0:T(8,128)(2,1)}, bf16[64,2176]{1,0:T(8,128)(2,1)S(1)}, u32[]{:S(2)}, u32[]{:S(2)}) collective-permute-start(bf16[64,2176]{1,0:T(8,128)(2,1)} %copy-done.7), channel_id=1, source_target_pairs={{0,1},{1,0},{2,3},{3,2},{4,5},{5,4},{6,7},{7,6},{8,9},{9,8},{10,11... | collective-permute-start | bytes 835592 | tf_op jit(solution)/shard_map/ppermute | solution.py:256
  32.9 24.5 %copy-start.8 = (bf16[64,2176]{1,0:T(8,128)(2,1)S(1)}, bf16[64,2176]{1,0:T(8,128)(2,1)}, u32[]{:S(2)}) copy-start(bf16[64,2176]{1,0:T(8,128)(2,1)} %copy-done.7) | copy-start | bytes 835588
  33.0 26.1 %collective-permute-start.7 = (bf16[6,128,128]{2,1,0:T(8,128)(2,1)S(1)}, bf16[6,128,128]{2,1,0:T(8,128)(2,1)S(1)}, u32[]{:S(2)}, u32[]{:S(2)}) collective-permute-start(bf16[6,128,128]{2,1,0:T(8,128)(2,1)S(1)} %dynamic-slice_bitcast_fusion.2), channel_id=1, source_target_pairs={{0,2},{1,3},{2,0},{3,1},{4,6},{5,7},{6,4},{7,5},{8,10},{9,11},{10,... | collective-permute-start | bytes 589832 | tf_op jit(solution)/shard_map/ppermute | solution.py:260
  51.4 9.3 %collective-permute-start.9 = (bf16[10,128,128]{2,1,0:T(8,128)(2,1)S(1)}, bf16[10,128,128]{2,1,0:T(8,128)(2,1)S(1)}, u32[]{:S(2)}, u32[]{:S(2)}) collective-permute-start(bf16[10,128,128]{2,1,0:T(8,128)(2,1)S(1)} %slice.3), channel_id=1, source_target_pairs={{0,16},{16,0},{1,17},{17,1},{2,18},{18,2},{3,19},{19,3},{4,20},{20... | collective-permute-start | bytes 983048 | tf_op jit(solution)/shard_map/ppermute | solution.py:263
  59.1 6.0 %collective-permute-start.10 = (bf16[6,128,128]{2,1,0:T(8,128)(2,1)S(1)}, bf16[6,128,128]{2,1,0:T(8,128)(2,1)S(1)}, u32[]{:S(2)}, u32[]{:S(2)}) collective-permute-start(bf16[6,128,128]{2,1,0:T(8,128)(2,1)S(1)} %collective-permute-done.7.rest_2_), channel_id=1, source_target_pairs={{0,16},{16,0},{1,17},{17,1},{2,18},{18,2},{3,19},{19,3},{4,20},{20... | collective-permute-start | bytes 589832 | tf_op jit(solution)/shard_map/ppermute | solution.py:263
  60.1 17.5 %collective-permute-start.19 = (bf16[64,2688]{1,0:T(8,128)(2,1)S(1)}, bf16[64,2688]{1,0:T(8,128)(2,1)S(1)}, u32[]{:S(2)}, u32[]{:S(2)}) collective-permute-start(bf16[64,2688]{1,0:T(8,128)(2,1)S(1)} %get-tuple-element.46.half_ref), channel_id=1, source_target_pairs={{0,2},{1,3},{2,0},{3,1},{4,6},{5,7},{6,4},{7,5},{8,10},{9,11},{10,... | collective-permute-start | bytes 1032200 | tf_op jit(solution)/shard_map/ppermute | solution.py:260
  66.1 1.4 %collective-permute-start.11 = (bf16[1,4,128,128]{3,2,1,0:T(8,128)(2,1)S(1)}, bf16[1,4,128,128]{3,2,1,0:T(8,128)(2,1)S(1)}, u32[]{:S(2)}, u32[]{:S(2)}) collective-permute-start(bf16[1,4,128,128]{3,2,1,0:T(8,128)(2,1)S(1)} %get-tuple-element.55), channel_id=1, source_target_pairs={{0,4},{4,0},{8,12},{12,8},{1,5},{5,1},{9,13},{13,9},{2,6},{6,2},{1... | collective-permute-start | bytes 393224 | tf_op jit(solution)/shard_map/ppermute | solution.py:249
  66.2 11.4 %collective-permute-start.16 = (bf16[16,128,128]{2,1,0:T(8,128)(2,1)S(1)}, bf16[16,128,128]{2,1,0:T(8,128)(2,1)S(1)}, u32[]{:S(2)}, u32[]{:S(2)}) collective-permute-start(bf16[16,128,128]{2,1,0:T(8,128)(2,1)S(1)} %get-tuple-element.61), channel_id=1, source_target_pairs={{0,4},{4,0},{8,12},{12,8},{1,5},{5,1},{9,13},{13,9},{2,6},{6,2},{1... | collective-permute-start | bytes 1572872 | tf_op jit(solution)/shard_map/ppermute | solution.py:249
  66.7 1.8 %collective-permute-start.12 = (bf16[1,4,128,128]{3,2,1,0:T(8,128)(2,1)S(1)}, bf16[1,4,128,128]{3,2,1,0:T(8,128)(2,1)S(1)}, u32[]{:S(2)}, u32[]{:S(2)}) collective-permute-start(bf16[1,4,128,128]{3,2,1,0:T(8,128)(2,1)S(1)} %get-tuple-element.57), channel_id=1, source_target_pairs={{0,4},{4,0},{8,12},{12,8},{1,5},{5,1},{9,13},{13,9},{2,6},{6,2},{1... | collective-permute-start | bytes 393224 | tf_op jit(solution)/shard_map/ppermute | solution.py:249
  66.8 3.2 %collective-permute-start.13 = (bf16[1,4,128,128]{3,2,1,0:T(8,128)(2,1)S(1)}, bf16[1,4,128,128]{3,2,1,0:T(8,128)(2,1)S(1)}, u32[]{:S(2)}, u32[]{:S(2)}) collective-permute-start(bf16[1,4,128,128]{3,2,1,0:T(8,128)(2,1)S(1)} %get-tuple-element.58), channel_id=1, source_target_pairs={{0,4},{4,0},{8,12},{12,8},{1,5},{5,1},{9,13},{13,9},{2,6},{6,2},{1... | collective-permute-start | bytes 393224 | tf_op jit(solution)/shard_map/ppermute | solution.py:249
  67.5 2.5 %collective-permute-start.14 = (bf16[1,4,128,128]{3,2,1,0:T(8,128)(2,1)S(1)}, bf16[1,4,128,128]{3,2,1,0:T(8,128)(2,1)S(1)}, u32[]{:S(2)}, u32[]{:S(2)}) collective-permute-start(bf16[1,4,128,128]{3,2,1,0:T(8,128)(2,1)S(1)} %get-tuple-element.59), channel_id=1, source_target_pairs={{0,4},{4,0},{8,12},{12,8},{1,5},{5,1},{9,13},{13,9},{2,6},{6,2},{1... | collective-permute-start | bytes 393224 | tf_op jit(solution)/shard_map/ppermute | solution.py:249
  68.5 9.2 %collective-permute-start.17 = (bf16[4,128,128]{2,1,0:T(8,128)(2,1)S(1)}, bf16[4,128,128]{2,1,0:T(8,128)(2,1)S(1)}, u32[]{:S(2)}, u32[]{:S(2)}) collective-permute-start(bf16[4,128,128]{2,1,0:T(8,128)(2,1)S(1)} %bitcast.26), channel_id=1, source_target_pairs={{0,8},{4,12},{8,0},{12,4},{1,9},{5,13},{9,1},{13,5},{2,10},{6,14},... | collective-permute-start | bytes 393224 | tf_op jit(solution)/shard_map/ppermute | solution.py:253
  70.6 9.7 %collective-permute-start.24 = (bf16[1,8,128,128]{3,2,1,0:T(8,128)(2,1)S(1)}, bf16[1,8,128,128]{3,2,1,0:T(8,128)(2,1)S(1)}, u32[]{:S(2)}, u32[]{:S(2)}) collective-permute-start(bf16[1,8,128,128]{3,2,1,0:T(8,128)(2,1)S(1)} %get-tuple-element.67), channel_id=1, source_target_pairs={{0,4},{4,0},{8,12},{12,8},{1,5},{5,1},{9,13},{13,9},{2,6},{6,2},{1... | collective-permute-start | bytes 786440 | tf_op jit(solution)/shard_map/ppermute | solution.py:249
  70.7 20.1 %collective-permute-start.21 = (bf16[12,128,128]{2,1,0:T(8,128)(2,1)S(1)}, bf16[12,128,128]{2,1,0:T(8,128)(2,1)S(1)}, u32[]{:S(2)}, u32[]{:S(2)}) collective-permute-start(bf16[12,128,128]{2,1,0:T(8,128)(2,1)S(1)} %bitcast.25), channel_id=1, source_target_pairs={{0,8},{4,12},{8,0},{12,4},{1,9},{5,13},{9,1},{13,5},{2,10},{6,14},... | collective-permute-start | bytes 1179656 | tf_op jit(solution)/shard_map/ppermute | solution.py:253
  77.6 2.7 %collective-permute-start.23 = (bf16[1,8,128,128]{3,2,1,0:T(8,128)(2,1)S(1)}, bf16[1,8,128,128]{3,2,1,0:T(8,128)(2,1)S(1)}, u32[]{:S(2)}, u32[]{:S(2)}) collective-permute-start(bf16[1,8,128,128]{3,2,1,0:T(8,128)(2,1)S(1)} %get-tuple-element.65), channel_id=1, source_target_pairs={{0,4},{4,0},{8,12},{12,8},{1,5},{5,1},{9,13},{13,9},{2,6},{6,2},{1... | collective-permute-start | bytes 786440 | tf_op jit(solution)/shard_map/ppermute | solution.py:249
  77.6 10.9 %collective-permute-start.20 = (bf16[64,2688]{1,0:T(8,128)(2,1)S(1)}, bf16[64,2688]{1,0:T(8,128)(2,1)S(1)}, u32[]{:S(2)}, u32[]{:S(2)}) collective-permute-start(bf16[64,2688]{1,0:T(8,128)(2,1)S(1)} %collective-permute-done.19.rest_0_), channel_id=1, source_target_pairs={{0,1},{1,0},{2,3},{3,2},{4,5},{5,4},{6,7},{7,6},{8,9},{9,8},{10,11... | collective-permute-start | bytes 1032200 | tf_op jit(solution)/shard_map/ppermute | solution.py:256
  78.2 12.7 %collective-permute-start.18 = (bf16[4,128,128]{2,1,0:T(8,128)(2,1)S(1)}, bf16[4,128,128]{2,1,0:T(8,128)(2,1)S(1)}, u32[]{:S(2)}, u32[]{:S(2)}) collective-permute-start(bf16[4,128,128]{2,1,0:T(8,128)(2,1)S(1)} %shard_map.103), channel_id=1, source_target_pairs={{0,1},{1,0},{2,3},{3,2},{4,5},{5,4},{6,7},{7,6},{8,9},{9,8},{10,11... | collective-permute-start | bytes 393224 | tf_op jit(solution)/shard_map/ppermute | solution.py:256
  80.3 13.4 %collective-permute-start.15 = (bf16[16,128,128]{2,1,0:T(8,128)(2,1)S(1)}, bf16[16,128,128]{2,1,0:T(8,128)(2,1)S(1)}, u32[]{:S(2)}, u32[]{:S(2)}) collective-permute-start(bf16[16,128,128]{2,1,0:T(8,128)(2,1)S(1)} %get-tuple-element.60), channel_id=1, source_target_pairs={{0,4},{4,0},{8,12},{12,8},{1,5},{5,1},{9,13},{13,9},{2,6},{6,2},{1... | collective-permute-start | bytes 1572872 | tf_op jit(solution)/shard_map/ppermute | solution.py:249
  81.0 21.4 %copy-start.5 = (bf16[64,2048]{1,0:T(8,128)(2,1)S(1)}, bf16[64,2048]{1,0:T(8,128)(2,1)}, u32[]{:S(2)}) copy-start(bf16[64,2048]{1,0:T(8,128)(2,1)} %adapter_ref.2) | copy-start | bytes 786436
  81.0 22.3 %collective-permute-start.25 = (bf16[16,128,128]{2,1,0:T(8,128)(2,1)S(1)}, bf16[16,128,128]{2,1,0:T(8,128)(2,1)S(1)}, u32[]{:S(2)}, u32[]{:S(2)}) collective-permute-start(bf16[16,128,128]{2,1,0:T(8,128)(2,1)S(1)} %bitcast.23), channel_id=1, source_target_pairs={{0,8},{4,12},{8,0},{12,4},{1,9},{5,13},{9,1},{13,5},{2,10},{6,14},... | collective-permute-start | bytes 1572872 | tf_op jit(solution)/shard_map/ppermute | solution.py:253
  91.6 10.8 %collective-permute-start.22 = (bf16[12,128,128]{2,1,0:T(8,128)(2,1)S(1)}, bf16[12,128,128]{2,1,0:T(8,128)(2,1)S(1)}, u32[]{:S(2)}, u32[]{:S(2)}) collective-permute-start(bf16[12,128,128]{2,1,0:T(8,128)(2,1)S(1)} %shard_map.104), channel_id=1, source_target_pairs={{0,1},{1,0},{2,3},{3,2},{4,5},{5,4},{6,7},{7,6},{8,9},{9,8},{10,11... | collective-permute-start | bytes 1179656 | tf_op jit(solution)/shard_map/ppermute | solution.py:256
  (5 other events, 4.8 us)

commit v10 on v9

--- a/solution.py
+++ b/solution.py
@@ -294,7 +294,7 @@
             jnp.where(ids >= 0, lax.rem(known, col_blocks), 0),
         ]).astype(BF16)
         code = jnp.pad(code, ((0, tile - 2), (0, tile - slots)))[None]
-        soon = core_swap(after(ids + 1, leaving_chunks[0]))
+        soon = core_swap(after(ids, leaving_chunks[0]))
         leaving_chunks[1] = jnp.concatenate([leaving_chunks[1], code], axis=0)
         leaving_chunks[1:] = [after(chunk, soon) for chunk in leaving_chunks[1:]]
         direct = [
@@ -335,7 +335,7 @@
         )
         half_shape = jax.ShapeDtypeStruct((rank, (shard_rows + feats) // 2), BF16)
         half_grads, other_grads = call(
-            pair_grad_kernel, (half_shape, half_shape), (after(where, total),), (rounded, activations, mate_activations, pack, mate_pack),
+            pair_grad_kernel, (half_shape, half_shape), (where,), (rounded, activations, mate_activations, pack, mate_pack),
         )
         far_grads = [group_shift(half_grads, d) for d in range(1, group)]
 
@@ -344,9 +344,9 @@
             (jax.ShapeDtypeStruct((group - 1, tile), jnp.int32),), (),
             tuple(value for value, place in direct if place[2] == starts[1]),
         )
-        gates = {starts[0]: (rounded,), starts[1]: (mate_activations,), starts[2]: (half_grads, total)}
+        gates = {starts[0]: (rounded, mate_activations), starts[1]: (total,), starts[2]: (half_grads,)}
         swapped = [
-            (part_shift((after(value, *gates[start]) if gates[start] else value)[:size], e), (source, e, start, size))
+            (part_shift(after(value, *gates[start])[:size], e), (source, e, start, size))
             for value, (source, _, start, size) in direct for e in range(1, n_parts)
         ]
         more = direct + chunk(swapped, 0) + chunk(swapped, 1)

time: 105 us -> 98.5 us (0.938)
  waiting for transfers between devices: 51.2 us -> 44.7 us
    ppermute x4, waiting for transfers between devices: 23.2 us -> 13.7 us  [group_shift(): return lax.ppermute(value, 'dp', pairs)]
    ppermute x3, waiting for transfers between devices: 0.73 us -> 2.56 us  [part_shift(): lax.ppermute(value, 'parts', [(i, (i + d) % n_parts) for i in range(n_par...]
    ppermute x4, waiting for transfers between devices: 2.7 us -> 4.28 us  [chip_shift(): return lax.ppermute(value, 'row', pairs)]
    ppermute x5, starting transfers between devices: 4.01 us -> 5.53 us  [mate_swap(): return lax.ppermute(value, 'dp', [(i, i ^ 1) for i in range(n_dp)])]
  transfers between devices with their start and end apart: 26 -> 26, of which waited for: 12 -> 13; matrix products, arithmetic and copies ran while one was open for 3% -> 5% of each run, Pallas kernels for 17% -> 18%
where the time goes in v10:
time: 98.5 us; the launch traced here: 98.1 us
  waiting for transfers between devices  44.7 us (45%)
  starting transfers between devices  24.4 us (25%)
  Pallas kernels  18.8 us (19%)
  local copies, waits for them, and re-layouts  7.92 us (8%)
  other arithmetic  1.45 us (1%)
    ppermute x5, waiting for transfers between devices, mate_swap(): return lax.ppermute(value, 'dp', [(i, i ^ 1) for i in range(n_dp)])  22.5 us
    pallas_call x15, Pallas kernels, call(): pl.pallas_call(kernel, out_shape=outs, in_specs=[smem] * len(scalars) + [...  18.8 us
    ppermute x4, waiting for transfers between devices, group_shift(): return lax.ppermute(value, 'dp', pairs)  13.7 us
    ppermute x4, starting transfers between devices, group_shift(): return lax.ppermute(value, 'dp', pairs)  7.94 us
    ppermute x5, starting transfers between devices, mate_swap(): return lax.ppermute(value, 'dp', [(i, i ^ 1) for i in range(n_dp)])  5.53 us
    ppermute x4, starting transfers between devices, chip_shift(): return lax.ppermute(value, 'row', pairs)  5.41 us
    unnamed x22, local copies, waits for them, and re-layouts  4.77 us
    ppermute x4, waiting for transfers between devices, chip_shift(): return lax.ppermute(value, 'row', pairs)  4.28 us
  transfers between devices with their start and end apart: 26, of which 13 were waited for; matrix products, arithmetic and copies ran while one was open for 5% of the time, Pallas kernels for 18%

profile of v10, /device:TPU:0, one launch (start us, length us, event | category | flops | bytes accessed | tf_op | source)
XLA Modules:
  0.0 98.1 jit_solution(11457418678538221637)
XLA Ops:
  0.6 3.1 %collective-permute-start.3 = (bf16[128,3328]{1,0:T(8,128)(2,1)}, bf16[128,3328]{1,0:T(8,128)(2,1)}, u32[]{:S(2)}, u32[]{:S(2)}) collective-permute-start(bf16[128,3328]{1,0:T(8,128)(2,1)} %own_ref.1), channel_id=1, source_target_pairs={{0,1},{1,0},{2,3},{3,2},{4,5},{5,4},{6,7},{7,6},{8,9},{9,8},{10,11... | collective-permute-start | bytes 2555912 | tf_op jit(solution)/shard_map/ppermute | solution.py:256
  3.7 1.9 %dynamic-slice_bitcast_fusion = bf16[16,128,128]{2,1,0:T(8,128)(2,1)} fusion(bf16[1,64,128,128]{3,2,1,0:T(8,128)(2,1)} %param.10, s32[]{:T(128)S(6)} %select_n.18), kind=kLoop, calls=%fused_computation | loop fusion | bytes 1048580 | tf_op jit(solution)/shard_map/dynamic_slice | solution.py:288
  5.6 2.6 %collective-permute-start.6 = (bf16[16,128,128]{2,1,0:T(8,128)(2,1)}, bf16[16,128,128]{2,1,0:T(8,128)(2,1)}, u32[]{:S(2)}, u32[]{:S(2)}) collective-permute-start(bf16[16,128,128]{2,1,0:T(8,128)(2,1)} %dynamic-slice_bitcast_fusion), channel_id=1, source_target_pairs={{0,2},{1,3},{2,0},{3,1},{4,6},{5,7},{6,4},{7,5},{8,10},{9,11},{10,... | collective-permute-start | bytes 1572872 | tf_op jit(solution)/shard_map/ppermute | solution.py:260
  8.9 1.1 %dynamic-slice_bitcast_fusion.1 = bf16[10,128,128]{2,1,0:T(8,128)(2,1)S(1)} fusion(bf16[1,64,128,128]{3,2,1,0:T(8,128)(2,1)} %param.10, s32[]{:T(128)S(6)} %select_n.19), kind=kLoop, calls=%fused_computation.2 | loop fusion | bytes 655364 | tf_op jit(solution)/shard_map/dynamic_slice | solution.py:288
  11.2 1.0 %copy-done.2 = bf16[128,2048]{1,0:T(8,128)(2,1)S(1)} copy-done((bf16[128,2048]{1,0:T(8,128)(2,1)S(1)}, bf16[128,2048]{1,0:T(8,128)(2,1)}, u32[]{:S(2)}) %copy-start.2) | copy-done | bytes 524312
  12.2 0.9 copy-done.4
  13.2 1.0 %copy-done.6 = bf16[3328,64]{0,1:T(8,128)(2,1)S(1)} copy-done((bf16[3328,64]{0,1:T(8,128)(2,1)S(1)}, bf16[3328,64]{0,1:T(8,128)(2,1)}, u32[]{:S(2)}) %copy-start.6) | copy-done | bytes 426008
  15.1 1.0 %collective-permute-done.1 = f32[128,128]{1,0:T(8,128)S(1)} collective-permute-done((f32[128,128]{1,0:T(8,128)S(1)}, f32[128,128]{1,0:T(8,128)S(1)}, u32[]{:S(2)}, u32[]{:S(2)}) %collective-permute-start.1) | collective-permute-done | bytes 65568 | tf_op jit(solution)/shard_map/ppermute | solution.py:249
  16.1 1.6 %collective-permute-start.2 = (f32[128,128]{1,0:T(8,128)S(1)}, f32[128,128]{1,0:T(8,128)S(1)}, u32[]{:S(2)}, u32[]{:S(2)}) collective-permute-start(f32[128,128]{1,0:T(8,128)S(1)} %add.25.both_ref), channel_id=1, source_target_pairs={{0,8},{4,12},{8,0},{12,4},{1,9},{5,13},{9,1},{13,5},{2,10},{6,14},... | collective-permute-start | bytes 196616 | tf_op jit(solution)/shard_map/ppermute | solution.py:253
  17.7 2.7 %collective-permute-done.2.rest_0_ = f32[128,128]{1,0:T(8,128)S(1)} collective-permute-done((f32[128,128]{1,0:T(8,128)S(1)}, f32[128,128]{1,0:T(8,128)S(1)}, u32[]{:S(2)}, u32[]{:S(2)}) %collective-permute-start.2) | collective-permute-done | bytes 65568 | tf_op jit(solution)/shard_map/ppermute | solution.py:253
  20.4 1.0 %copy-done.3 = bf16[128,2048]{1,0:T(8,128)(2,1)S(1)} copy-done((bf16[128,2048]{1,0:T(8,128)(2,1)S(1)}, bf16[128,2048]{1,0:T(8,128)(2,1)}, u32[]{:S(2)}) %copy-start.3) | copy-done | bytes 524312
  23.0 11.7 %collective-permute-done.6.rest_0_ = bf16[16,128,128]{2,1,0:T(8,128)(2,1)} collective-permute-done((bf16[16,128,128]{2,1,0:T(8,128)(2,1)}, bf16[16,128,128]{2,1,0:T(8,128)(2,1)}, u32[]{:S(2)}, u32[]{:S(2)}) %collective-permute-start.6) | collective-permute-done | bytes 524320 | tf_op jit(solution)/shard_map/ppermute | solution.py:260
  34.7 4.6 %collective-permute-done.3.mate_acts_ref.mate_ref = bf16[128,3328]{1,0:T(8,128)(2,1)} collective-permute-done((bf16[128,3328]{1,0:T(8,128)(2,1)}, bf16[128,3328]{1,0:T(8,128)(2,1)}, u32[]{:S(2)}, u32[]{:S(2)}) %collective-permute-start.3) | collective-permute-done | bytes 852000 | tf_op jit(solution)/shard_map/ppermute | solution.py:256
  39.3 1.7 %collective-permute-start.8 = (bf16[16,128,128]{2,1,0:T(8,128)(2,1)}, bf16[16,128,128]{2,1,0:T(8,128)(2,1)}, u32[]{:S(2)}, u32[]{:S(2)}) collective-permute-start(bf16[16,128,128]{2,1,0:T(8,128)(2,1)} %collective-permute-done.6.rest_0_), channel_id=1, source_target_pairs={{0,16},{16,0},{1,17},{17,1},{2,18},{18,2},{3,19},{19,3},{4,20},{20... | collective-permute-start | bytes 1572872 | tf_op jit(solution)/shard_map/ppermute | solution.py:263
  41.0 3.1 %collective-permute-start.7 = (bf16[6,128,128]{2,1,0:T(8,128)(2,1)S(1)}, bf16[6,128,128]{2,1,0:T(8,128)(2,1)S(1)}, u32[]{:S(2)}, u32[]{:S(2)}) collective-permute-start(bf16[6,128,128]{2,1,0:T(8,128)(2,1)S(1)} %dynamic-slice_bitcast_fusion.2), channel_id=1, source_target_pairs={{0,2},{1,3},{2,0},{3,1},{4,6},{5,7},{6,4},{7,5},{8,10},{9,11},{10,... | collective-permute-start | bytes 589832 | tf_op jit(solution)/shard_map/ppermute | solution.py:260
  44.0 4.4 %shard_map.98 = (f32[65,256,128]{2,1,0:T(8,128)S(1)}, bf16[26,256,128]{2,1,0:T(8,128)(2,1)S(1)}) custom-call(s32[6]{0:T(128)S(1)} %stack.29.where_ref, s32[64]{0:T(128)S(1)} %bitcast.29, bf16[128,3328]{1,0:T(8,128)(2,1)S(1)} %copy-done, bf16[128,3328]{1,0:T(8,128)(2,1)} %collective-permute-done.3.mate_acts_ref.mate_ref, bf16[64,128,128]{2,1,0:T(8,128)(2,1)S(1)} %bitcast.21), custom_call_target="tpu_custom_call" | custom-call | tf_op jit(solution)/shard_map/pallas_call | solution.py:225
  48.5 1.5 %collective-permute-start.9 = (bf16[10,128,128]{2,1,0:T(8,128)(2,1)S(1)}, bf16[10,128,128]{2,1,0:T(8,128)(2,1)S(1)}, u32[]{:S(2)}, u32[]{:S(2)}) collective-permute-start(bf16[10,128,128]{2,1,0:T(8,128)(2,1)S(1)} %slice.3), channel_id=1, source_target_pairs={{0,16},{16,0},{1,17},{17,1},{2,18},{18,2},{3,19},{19,3},{4,20},{20... | collective-permute-start | bytes 983048 | tf_op jit(solution)/shard_map/ppermute | solution.py:263
  50.0 4.4 %collective-permute-done.4.mate_pack_ref = bf16[64,2176]{1,0:T(8,128)(2,1)S(1)} collective-permute-done((bf16[64,2176]{1,0:T(8,128)(2,1)}, bf16[64,2176]{1,0:T(8,128)(2,1)S(1)}, u32[]{:S(2)}, u32[]{:S(2)}) %collective-permute-start.4) | collective-permute-done | bytes 278560 | tf_op jit(solution)/shard_map/ppermute | solution.py:256
  54.4 1.6 %shard_map.96 = (bf16[64,2688]{1,0:T(8,128)(2,1)S(1)}, bf16[64,2688]{1,0:T(8,128)(2,1)S(1)}) custom-call(s32[6]{0:T(128)S(1)} %stack.29.where_ref, bf16[128,128]{1,0:T(8,128)(2,1)S(1)} %get-tuple-element.39.rounded_ref, bf16[128,3328]{1,0:T(8,128)(2,1)S(1)} %copy-done, bf16[128,3328]{1,0:T(8,128)(2,1)} %collective-permute-done.3.mate_acts_ref.mate_ref, ...), custom_call_target="tpu_custom_call" | custom-call | tf_op jit(solution)/shard_map/pallas_call | solution.py:225
  56.8 1.9 %collective-permute-start.19 = (bf16[64,2688]{1,0:T(8,128)(2,1)S(1)}, bf16[64,2688]{1,0:T(8,128)(2,1)S(1)}, u32[]{:S(2)}, u32[]{:S(2)}) collective-permute-start(bf16[64,2688]{1,0:T(8,128)(2,1)S(1)} %get-tuple-element.41.half_ref), channel_id=1, source_target_pairs={{0,2},{1,3},{2,0},{3,1},{4,6},{5,7},{6,4},{7,5},{8,10},{9,11},{10,... | collective-permute-start | bytes 1032200 | tf_op jit(solution)/shard_map/ppermute | solution.py:260
  58.8 2.6 %collective-permute-done.9.rest_4_ = bf16[10,128,128]{2,1,0:T(8,128)(2,1)S(1)} collective-permute-done((bf16[10,128,128]{2,1,0:T(8,128)(2,1)S(1)}, bf16[10,128,128]{2,1,0:T(8,128)(2,1)S(1)}, u32[]{:S(2)}, u32[]{:S(2)}) %collective-permute-start.9) | collective-permute-done | bytes 327712 | tf_op jit(solution)/shard_map/ppermute | solution.py:263
  61.4 3.6 %shard_map.99.old_ref = f32[65,256,128]{2,1,0:T(8,128)S(1)} custom-call(s32[6]{0:T(128)S(1)} %stack.29.where_ref, s32[1,128]{1,0:T(1,128)S(1)} %shard_map.97.ids_ref, bf16[26,256,128]{2,1,0:T(8,128)(2,1)S(1)} %get-tuple-element.46.tiles_ref, f32[65,256,128]{2,1,0:T(8,128)S(1)} %get-tuple-element.47.old_ref, ...), custom_call_target="tpu_custom_call", output_to_operand_aliasing={{}: (3, {})} | custom-call | tf_op jit(solution)/shard_map/pallas_call | solution.py:225
  65.0 1.0 %shard_map.100 = (f32[65,256,128]{2,1,0:T(8,128)S(1)}, bf16[1,4,128,128]{3,2,1,0:T(8,128)(2,1)S(1)}, bf16[1,4,128,128]{3,2,1,0:T(8,128)(2,1)S(1)}, bf16[1,4,128,...) custom-call(s32[6]{0:T(128)S(1)} %stack.29.where_ref, ...), custom_call_target="tpu_custom_call", output_to_operand_aliasing={{0}: (3, {})} | custom-call | tf_op jit(solution)/shard_map/pallas_call | solution.py:225
  68.4 1.7 %collective-permute-start.17 = (bf16[4,128,128]{2,1,0:T(8,128)(2,1)S(1)}, bf16[4,128,128]{2,1,0:T(8,128)(2,1)S(1)}, u32[]{:S(2)}, u32[]{:S(2)}) collective-permute-start(bf16[4,128,128]{2,1,0:T(8,128)(2,1)S(1)} %bitcast.25), channel_id=1, source_target_pairs={{0,8},{4,12},{8,0},{12,4},{1,9},{5,13},{9,1},{13,5},{2,10},{6,14},... | collective-permute-start | bytes 393224 | tf_op jit(solution)/shard_map/ppermute | solution.py:253
  71.2 2.0 %collective-permute-done.19.rest_0_ = bf16[64,2688]{1,0:T(8,128)(2,1)S(1)} collective-permute-done((bf16[64,2688]{1,0:T(8,128)(2,1)S(1)}, bf16[64,2688]{1,0:T(8,128)(2,1)S(1)}, u32[]{:S(2)}, u32[]{:S(2)}) %collective-permute-start.19) | collective-permute-done | bytes 344096 | tf_op jit(solution)/shard_map/ppermute | solution.py:260
  73.1 1.6 %collective-permute-done.17.rest_0_ = bf16[4,128,128]{2,1,0:T(8,128)(2,1)S(1)} collective-permute-done((bf16[4,128,128]{2,1,0:T(8,128)(2,1)S(1)}, bf16[4,128,128]{2,1,0:T(8,128)(2,1)S(1)}, u32[]{:S(2)}, u32[]{:S(2)}) %collective-permute-start.17) | collective-permute-done | bytes 131104 | tf_op jit(solution)/shard_map/ppermute | solution.py:253
  75.3 2.1 %collective-permute-start.18 = (bf16[4,128,128]{2,1,0:T(8,128)(2,1)S(1)}, bf16[4,128,128]{2,1,0:T(8,128)(2,1)S(1)}, u32[]{:S(2)}, u32[]{:S(2)}) collective-permute-start(bf16[4,128,128]{2,1,0:T(8,128)(2,1)S(1)} %shard_map.103), channel_id=1, source_target_pairs={{0,1},{1,0},{2,3},{3,2},{4,5},{5,4},{6,7},{7,6},{8,9},{9,8},{10,11... | collective-permute-start | bytes 393224 | tf_op jit(solution)/shard_map/ppermute | solution.py:256
  78.1 1.7 %collective-permute-start.25 = (bf16[16,128,128]{2,1,0:T(8,128)(2,1)S(1)}, bf16[16,128,128]{2,1,0:T(8,128)(2,1)S(1)}, u32[]{:S(2)}, u32[]{:S(2)}) collective-permute-start(bf16[16,128,128]{2,1,0:T(8,128)(2,1)S(1)} %bitcast.22), channel_id=1, source_target_pairs={{0,8},{4,12},{8,0},{12,4},{1,9},{5,13},{9,1},{13,5},{2,10},{6,14},... | collective-permute-start | bytes 1572872 | tf_op jit(solution)/shard_map/ppermute | solution.py:253
  79.8 5.2 %collective-permute-done.20.rest_1_ = bf16[64,2688]{1,0:T(8,128)(2,1)S(1)} collective-permute-done((bf16[64,2688]{1,0:T(8,128)(2,1)S(1)}, bf16[64,2688]{1,0:T(8,128)(2,1)S(1)}, u32[]{:S(2)}, u32[]{:S(2)}) %collective-permute-start.20) | collective-permute-done | bytes 344096 | tf_op jit(solution)/shard_map/ppermute | solution.py:256
  85.0 1.4 %collective-permute-done.18.rest_0_ = bf16[4,128,128]{2,1,0:T(8,128)(2,1)S(1)} collective-permute-done((bf16[4,128,128]{2,1,0:T(8,128)(2,1)S(1)}, bf16[4,128,128]{2,1,0:T(8,128)(2,1)S(1)}, u32[]{:S(2)}, u32[]{:S(2)}) %collective-permute-start.18) | collective-permute-done | bytes 131104 | tf_op jit(solution)/shard_map/ppermute | solution.py:256
  87.4 1.8 %shard_map.108 = (f32[64,3328]{1,0:T(8,128)}, f32[64,2048]{1,0:T(8,128)}) custom-call(s32[6]{0:T(128)S(1)} %stack.29.where_ref, bf16[64,2688]{1,0:T(8,128)(2,1)S(1)} %get-tuple-element.41.half_ref, bf16[64,2688]{1,0:T(8,128)(2,1)S(1)} %get-tuple-element.66.other_ref, bf16[64,2688]{1,0:T(8,128)(2,1)S(1)} %collective-permute-done.19.rest_0_, ...), custom_call_target="tpu_custom_call" | custom-call | tf_op jit(solution)/shard_map/pallas_call | solution.py:225
  89.2 7.0 %collective-permute-done.22.rest_1_ = bf16[12,128,128]{2,1,0:T(8,128)(2,1)S(1)} collective-permute-done((bf16[12,128,128]{2,1,0:T(8,128)(2,1)S(1)}, bf16[12,128,128]{2,1,0:T(8,128)(2,1)S(1)}, u32[]{:S(2)}, u32[]{:S(2)}) %collective-permute-start.22) | collective-permute-done | bytes 393248 | tf_op jit(solution)/shard_map/ppermute | solution.py:256
  (66 shorter events, 12.8 us)
Async XLA Ops:
  0.6 10.5 %copy-start = (bf16[128,3328]{1,0:T(8,128)(2,1)S(1)}, bf16[128,3328]{1,0:T(8,128)(2,1)}, u32[]{:S(2)}) copy-start(bf16[128,3328]{1,0:T(8,128)(2,1)} %own_ref.1) | copy-start | bytes 2555908
  0.6 10.5 %copy-start.9 = (s32[128]{0:T(128)S(1)}, s32[128]{0:T(128)}, u32[]{:S(2)}) copy-start(s32[128]{0:T(128)} %param.9) | copy-start | bytes 1540
  0.6 38.6 %collective-permute-start.3 = (bf16[128,3328]{1,0:T(8,128)(2,1)}, bf16[128,3328]{1,0:T(8,128)(2,1)}, u32[]{:S(2)}, u32[]{:S(2)}) collective-permute-start(bf16[128,3328]{1,0:T(8,128)(2,1)} %own_ref.1), channel_id=1, source_target_pairs={{0,1},{1,0},{2,3},{3,2},{4,5},{5,4},{6,7},{7,6},{8,9},{9,8},{10,11... | collective-permute-start | bytes 2555912 | tf_op jit(solution)/shard_map/ppermute | solution.py:256
  5.6 29.1 %collective-permute-start.6 = (bf16[16,128,128]{2,1,0:T(8,128)(2,1)}, bf16[16,128,128]{2,1,0:T(8,128)(2,1)}, u32[]{:S(2)}, u32[]{:S(2)}) collective-permute-start(bf16[16,128,128]{2,1,0:T(8,128)(2,1)} %dynamic-slice_bitcast_fusion), channel_id=1, source_target_pairs={{0,2},{1,3},{2,0},{3,1},{4,6},{5,7},{6,4},{7,5},{8,10},{9,11},{10,... | collective-permute-start | bytes 1572872 | tf_op jit(solution)/shard_map/ppermute | solution.py:260
  8.2 2.6 %collective-permute-start = (s32[64]{0:T(128)}, s32[64]{0:T(128)S(1)}, u32[]{:S(2)}, u32[]{:S(2)}) collective-permute-start(s32[64]{0:T(128)} %bitcast.28), channel_id=1, source_target_pairs={{0,4},{4,0},{8,12},{12,8},{1,5},{5,1},{9,13},{13,9},{2,6},{6,2},{1... | collective-permute-start | bytes 776 | tf_op jit(solution)/shard_map/ppermute | solution.py:249
  8.9 35.2 %copy-start.10 = (s32[1,64]{1,0:T(1,128)S(1)}, s32[1,64]{1,0:T(1,128)}, u32[]{:S(2)}) copy-start(s32[1,64]{1,0:T(1,128)} %param.11) | copy-start | bytes 772
  8.9 32.1 %copy-start.1 = (bf16[1,64,128,128]{3,2,1,0:T(8,128)(2,1)S(1)}, bf16[1,64,128,128]{3,2,1,0:T(8,128)(2,1)}, u32[]{:S(2)}) copy-start(bf16[1,64,128,128]{3,2,1,0:T(8,128)(2,1)} %param.10) | copy-start | bytes 6291460
  10.8 37.6 %collective-permute-start.5 = (bf16[11,128,128]{2,1,0:T(8,128)(2,1)}, bf16[11,128,128]{2,1,0:T(8,128)(2,1)S(1)}, u32[]{:S(2)}, u32[]{:S(2)}) collective-permute-start(bf16[11,128,128]{2,1,0:T(8,128)(2,1)} %pad_maximum_fusion), channel_id=1, source_target_pairs={{0,2},{1,3},{2,0},{3,1},{4,6},{5,7},{6,4},{7,5},{8,10},{9,11},{10,... | collective-permute-start | bytes 1081352 | tf_op jit(solution)/shard_map/ppermute | solution.py:260
  14.8 1.3 %collective-permute-start.1 = (f32[128,128]{1,0:T(8,128)S(1)}, f32[128,128]{1,0:T(8,128)S(1)}, u32[]{:S(2)}, u32[]{:S(2)}) collective-permute-start(f32[128,128]{1,0:T(8,128)S(1)} %shard_map.94), channel_id=1, source_target_pairs={{0,4},{4,0},{8,12},{12,8},{1,5},{5,1},{9,13},{13,9},{2,6},{6,2},{1... | collective-permute-start | bytes 196616 | tf_op jit(solution)/shard_map/ppermute | solution.py:249
  16.1 4.3 %collective-permute-start.2 = (f32[128,128]{1,0:T(8,128)S(1)}, f32[128,128]{1,0:T(8,128)S(1)}, u32[]{:S(2)}, u32[]{:S(2)}) collective-permute-start(f32[128,128]{1,0:T(8,128)S(1)} %add.25.both_ref), channel_id=1, source_target_pairs={{0,8},{4,12},{8,0},{12,4},{1,9},{5,13},{9,1},{13,5},{2,10},{6,14},... | collective-permute-start | bytes 196616 | tf_op jit(solution)/shard_map/ppermute | solution.py:253
  39.3 22.1 %collective-permute-start.8 = (bf16[16,128,128]{2,1,0:T(8,128)(2,1)}, bf16[16,128,128]{2,1,0:T(8,128)(2,1)}, u32[]{:S(2)}, u32[]{:S(2)}) collective-permute-start(bf16[16,128,128]{2,1,0:T(8,128)(2,1)} %collective-permute-done.6.rest_0_), channel_id=1, source_target_pairs={{0,16},{16,0},{1,17},{17,1},{2,18},{18,2},{3,19},{19,3},{4,20},{20... | collective-permute-start | bytes 1572872 | tf_op jit(solution)/shard_map/ppermute | solution.py:263
  40.9 13.4 %collective-permute-start.4 = (bf16[64,2176]{1,0:T(8,128)(2,1)}, bf16[64,2176]{1,0:T(8,128)(2,1)S(1)}, u32[]{:S(2)}, u32[]{:S(2)}) collective-permute-start(bf16[64,2176]{1,0:T(8,128)(2,1)} %copy-done.7), channel_id=1, source_target_pairs={{0,1},{1,0},{2,3},{3,2},{4,5},{5,4},{6,7},{7,6},{8,9},{9,8},{10,11... | collective-permute-start | bytes 835592 | tf_op jit(solution)/shard_map/ppermute | solution.py:256
  41.0 15.0 %collective-permute-start.7 = (bf16[6,128,128]{2,1,0:T(8,128)(2,1)S(1)}, bf16[6,128,128]{2,1,0:T(8,128)(2,1)S(1)}, u32[]{:S(2)}, u32[]{:S(2)}) collective-permute-start(bf16[6,128,128]{2,1,0:T(8,128)(2,1)S(1)} %dynamic-slice_bitcast_fusion.2), channel_id=1, source_target_pairs={{0,2},{1,3},{2,0},{3,1},{4,6},{5,7},{6,4},{7,5},{8,10},{9,11},{10,... | collective-permute-start | bytes 589832 | tf_op jit(solution)/shard_map/ppermute | solution.py:260
  44.0 10.3 %copy-start.8 = (bf16[64,2176]{1,0:T(8,128)(2,1)S(1)}, bf16[64,2176]{1,0:T(8,128)(2,1)}, u32[]{:S(2)}) copy-start(bf16[64,2176]{1,0:T(8,128)(2,1)} %copy-done.7) | copy-start | bytes 835588
  48.5 12.9 %collective-permute-start.9 = (bf16[10,128,128]{2,1,0:T(8,128)(2,1)S(1)}, bf16[10,128,128]{2,1,0:T(8,128)(2,1)S(1)}, u32[]{:S(2)}, u32[]{:S(2)}) collective-permute-start(bf16[10,128,128]{2,1,0:T(8,128)(2,1)S(1)} %slice.3), channel_id=1, source_target_pairs={{0,16},{16,0},{1,17},{17,1},{2,18},{18,2},{3,19},{19,3},{4,20},{20... | collective-permute-start | bytes 983048 | tf_op jit(solution)/shard_map/ppermute | solution.py:263
  56.0 9.0 %collective-permute-start.10 = (bf16[6,128,128]{2,1,0:T(8,128)(2,1)S(1)}, bf16[6,128,128]{2,1,0:T(8,128)(2,1)S(1)}, u32[]{:S(2)}, u32[]{:S(2)}) collective-permute-start(bf16[6,128,128]{2,1,0:T(8,128)(2,1)S(1)} %collective-permute-done.7.rest_2_), channel_id=1, source_target_pairs={{0,16},{16,0},{1,17},{17,1},{2,18},{18,2},{3,19},{19,3},{4,20},{20... | collective-permute-start | bytes 589832 | tf_op jit(solution)/shard_map/ppermute | solution.py:263
  56.8 16.3 %collective-permute-start.19 = (bf16[64,2688]{1,0:T(8,128)(2,1)S(1)}, bf16[64,2688]{1,0:T(8,128)(2,1)S(1)}, u32[]{:S(2)}, u32[]{:S(2)}) collective-permute-start(bf16[64,2688]{1,0:T(8,128)(2,1)S(1)} %get-tuple-element.41.half_ref), channel_id=1, source_target_pairs={{0,2},{1,3},{2,0},{3,1},{4,6},{5,7},{6,4},{7,5},{8,10},{9,11},{10,... | collective-permute-start | bytes 1032200 | tf_op jit(solution)/shard_map/ppermute | solution.py:260
  66.0 1.4 %collective-permute-start.11 = (bf16[1,4,128,128]{3,2,1,0:T(8,128)(2,1)S(1)}, bf16[1,4,128,128]{3,2,1,0:T(8,128)(2,1)S(1)}, u32[]{:S(2)}, u32[]{:S(2)}) collective-permute-start(bf16[1,4,128,128]{3,2,1,0:T(8,128)(2,1)S(1)} %get-tuple-element.53), channel_id=1, source_target_pairs={{0,4},{4,0},{8,12},{12,8},{1,5},{5,1},{9,13},{13,9},{2,6},{6,2},{1... | collective-permute-start | bytes 393224 | tf_op jit(solution)/shard_map/ppermute | solution.py:249
  66.1 8.6 %collective-permute-start.16 = (bf16[16,128,128]{2,1,0:T(8,128)(2,1)S(1)}, bf16[16,128,128]{2,1,0:T(8,128)(2,1)S(1)}, u32[]{:S(2)}, u32[]{:S(2)}) collective-permute-start(bf16[16,128,128]{2,1,0:T(8,128)(2,1)S(1)} %get-tuple-element.59), channel_id=1, source_target_pairs={{0,4},{4,0},{8,12},{12,8},{1,5},{5,1},{9,13},{13,9},{2,6},{6,2},{1... | collective-permute-start | bytes 1572872 | tf_op jit(solution)/shard_map/ppermute | solution.py:249
  66.6 1.8 %collective-permute-start.12 = (bf16[1,4,128,128]{3,2,1,0:T(8,128)(2,1)S(1)}, bf16[1,4,128,128]{3,2,1,0:T(8,128)(2,1)S(1)}, u32[]{:S(2)}, u32[]{:S(2)}) collective-permute-start(bf16[1,4,128,128]{3,2,1,0:T(8,128)(2,1)S(1)} %get-tuple-element.55), channel_id=1, source_target_pairs={{0,4},{4,0},{8,12},{12,8},{1,5},{5,1},{9,13},{13,9},{2,6},{6,2},{1... | collective-permute-start | bytes 393224 | tf_op jit(solution)/shard_map/ppermute | solution.py:249
  66.7 3.4 %collective-permute-start.13 = (bf16[1,4,128,128]{3,2,1,0:T(8,128)(2,1)S(1)}, bf16[1,4,128,128]{3,2,1,0:T(8,128)(2,1)S(1)}, u32[]{:S(2)}, u32[]{:S(2)}) collective-permute-start(bf16[1,4,128,128]{3,2,1,0:T(8,128)(2,1)S(1)} %get-tuple-element.56), channel_id=1, source_target_pairs={{0,4},{4,0},{8,12},{12,8},{1,5},{5,1},{9,13},{13,9},{2,6},{6,2},{1... | collective-permute-start | bytes 393224 | tf_op jit(solution)/shard_map/ppermute | solution.py:249
  67.4 2.6 %collective-permute-start.14 = (bf16[1,4,128,128]{3,2,1,0:T(8,128)(2,1)S(1)}, bf16[1,4,128,128]{3,2,1,0:T(8,128)(2,1)S(1)}, u32[]{:S(2)}, u32[]{:S(2)}) collective-permute-start(bf16[1,4,128,128]{3,2,1,0:T(8,128)(2,1)S(1)} %get-tuple-element.57), channel_id=1, source_target_pairs={{0,4},{4,0},{8,12},{12,8},{1,5},{5,1},{9,13},{13,9},{2,6},{6,2},{1... | collective-permute-start | bytes 393224 | tf_op jit(solution)/shard_map/ppermute | solution.py:249
  68.4 6.3 %collective-permute-start.17 = (bf16[4,128,128]{2,1,0:T(8,128)(2,1)S(1)}, bf16[4,128,128]{2,1,0:T(8,128)(2,1)S(1)}, u32[]{:S(2)}, u32[]{:S(2)}) collective-permute-start(bf16[4,128,128]{2,1,0:T(8,128)(2,1)S(1)} %bitcast.25), channel_id=1, source_target_pairs={{0,8},{4,12},{8,0},{12,4},{1,9},{5,13},{9,1},{13,5},{2,10},{6,14},... | collective-permute-start | bytes 393224 | tf_op jit(solution)/shard_map/ppermute | solution.py:253
  70.7 15.7 %collective-permute-start.21 = (bf16[12,128,128]{2,1,0:T(8,128)(2,1)S(1)}, bf16[12,128,128]{2,1,0:T(8,128)(2,1)S(1)}, u32[]{:S(2)}, u32[]{:S(2)}) collective-permute-start(bf16[12,128,128]{2,1,0:T(8,128)(2,1)S(1)} %bitcast.24), channel_id=1, source_target_pairs={{0,8},{4,12},{8,0},{12,4},{1,9},{5,13},{9,1},{13,5},{2,10},{6,14},... | collective-permute-start | bytes 1179656 | tf_op jit(solution)/shard_map/ppermute | solution.py:253
  71.1 6.2 %collective-permute-start.23 = (bf16[1,8,128,128]{3,2,1,0:T(8,128)(2,1)S(1)}, bf16[1,8,128,128]{3,2,1,0:T(8,128)(2,1)S(1)}, u32[]{:S(2)}, u32[]{:S(2)}) collective-permute-start(bf16[1,8,128,128]{3,2,1,0:T(8,128)(2,1)S(1)} %get-tuple-element.63), channel_id=1, source_target_pairs={{0,4},{4,0},{8,12},{12,8},{1,5},{5,1},{9,13},{13,9},{2,6},{6,2},{1... | collective-permute-start | bytes 786440 | tf_op jit(solution)/shard_map/ppermute | solution.py:249
  73.1 4.3 %collective-permute-start.24 = (bf16[1,8,128,128]{3,2,1,0:T(8,128)(2,1)S(1)}, bf16[1,8,128,128]{3,2,1,0:T(8,128)(2,1)S(1)}, u32[]{:S(2)}, u32[]{:S(2)}) collective-permute-start(bf16[1,8,128,128]{3,2,1,0:T(8,128)(2,1)S(1)} %get-tuple-element.65), channel_id=1, source_target_pairs={{0,4},{4,0},{8,12},{12,8},{1,5},{5,1},{9,13},{13,9},{2,6},{6,2},{1... | collective-permute-start | bytes 786440 | tf_op jit(solution)/shard_map/ppermute | solution.py:249
  74.7 10.3 %collective-permute-start.20 = (bf16[64,2688]{1,0:T(8,128)(2,1)S(1)}, bf16[64,2688]{1,0:T(8,128)(2,1)S(1)}, u32[]{:S(2)}, u32[]{:S(2)}) collective-permute-start(bf16[64,2688]{1,0:T(8,128)(2,1)S(1)} %collective-permute-done.19.rest_0_), channel_id=1, source_target_pairs={{0,1},{1,0},{2,3},{3,2},{4,5},{5,4},{6,7},{7,6},{8,9},{9,8},{10,11... | collective-permute-start | bytes 1032200 | tf_op jit(solution)/shard_map/ppermute | solution.py:256
  75.3 11.1 %collective-permute-start.18 = (bf16[4,128,128]{2,1,0:T(8,128)(2,1)S(1)}, bf16[4,128,128]{2,1,0:T(8,128)(2,1)S(1)}, u32[]{:S(2)}, u32[]{:S(2)}) collective-permute-start(bf16[4,128,128]{2,1,0:T(8,128)(2,1)S(1)} %shard_map.103), channel_id=1, source_target_pairs={{0,1},{1,0},{2,3},{3,2},{4,5},{5,4},{6,7},{7,6},{8,9},{9,8},{10,11... | collective-permute-start | bytes 393224 | tf_op jit(solution)/shard_map/ppermute | solution.py:256
  77.4 11.8 %collective-permute-start.15 = (bf16[16,128,128]{2,1,0:T(8,128)(2,1)S(1)}, bf16[16,128,128]{2,1,0:T(8,128)(2,1)S(1)}, u32[]{:S(2)}, u32[]{:S(2)}) collective-permute-start(bf16[16,128,128]{2,1,0:T(8,128)(2,1)S(1)} %get-tuple-element.58), channel_id=1, source_target_pairs={{0,4},{4,0},{8,12},{12,8},{1,5},{5,1},{9,13},{13,9},{2,6},{6,2},{1... | collective-permute-start | bytes 1572872 | tf_op jit(solution)/shard_map/ppermute | solution.py:249
  78.1 18.1 %copy-start.5 = (bf16[64,2048]{1,0:T(8,128)(2,1)S(1)}, bf16[64,2048]{1,0:T(8,128)(2,1)}, u32[]{:S(2)}) copy-start(bf16[64,2048]{1,0:T(8,128)(2,1)} %adapter_ref.2) | copy-start | bytes 786436
  78.1 19.1 %collective-permute-start.25 = (bf16[16,128,128]{2,1,0:T(8,128)(2,1)S(1)}, bf16[16,128,128]{2,1,0:T(8,128)(2,1)S(1)}, u32[]{:S(2)}, u32[]{:S(2)}) collective-permute-start(bf16[16,128,128]{2,1,0:T(8,128)(2,1)S(1)} %bitcast.22), channel_id=1, source_target_pairs={{0,8},{4,12},{8,0},{12,4},{1,9},{5,13},{9,1},{13,5},{2,10},{6,14},... | collective-permute-start | bytes 1572872 | tf_op jit(solution)/shard_map/ppermute | solution.py:253
  87.1 9.1 %collective-permute-start.22 = (bf16[12,128,128]{2,1,0:T(8,128)(2,1)S(1)}, bf16[12,128,128]{2,1,0:T(8,128)(2,1)S(1)}, u32[]{:S(2)}, u32[]{:S(2)}) collective-permute-start(bf16[12,128,128]{2,1,0:T(8,128)(2,1)S(1)} %shard_map.104), channel_id=1, source_target_pairs={{0,1},{1,0},{2,3},{3,2},{4,5},{5,4},{6,7},{7,6},{8,9},{9,8},{10,11... | collective-permute-start | bytes 1179656 | tf_op jit(solution)/shard_map/ppermute | solution.py:256
  (5 other events, 4.8 us)

commit v11 on v10

--- a/solution.py
+++ b/solution.py
@@ -294,9 +294,9 @@
             jnp.where(ids >= 0, lax.rem(known, col_blocks), 0),
         ]).astype(BF16)
         code = jnp.pad(code, ((0, tile - 2), (0, tile - slots)))[None]
-        soon = core_swap(after(ids, leaving_chunks[0]))
+        soon = core_swap(ids)
         leaving_chunks[1] = jnp.concatenate([leaving_chunks[1], code], axis=0)
-        leaving_chunks[1:] = [after(chunk, soon) for chunk in leaving_chunks[1:]]
+        leaving_chunks = [after(chunk, soon) for chunk in leaving_chunks]
         direct = [
             (group_shift(leaving_chunks[k], d), (d - 1, 0, starts[k], sizes[k]))
             for d in range(1, group) for k in range(len(starts))
@@ -344,7 +344,7 @@
             (jax.ShapeDtypeStruct((group - 1, tile), jnp.int32),), (),
             tuple(value for value, place in direct if place[2] == starts[1]),
         )
-        gates = {starts[0]: (rounded, mate_activations), starts[1]: (total,), starts[2]: (half_grads,)}
+        gates = {starts[0]: (rounded,), starts[1]: (total,), starts[2]: (half_grads,)}
         swapped = [
             (part_shift(after(value, *gates[start])[:size], e), (source, e, start, size))
             for value, (source, _, start, size) in direct for e in range(1, n_parts)

time: 98.5 us -> 102 us (1.036)
  waiting for transfers between devices: 44.7 us -> 49 us
  starting transfers between devices: 24.4 us -> 23.3 us
    ppermute x4, waiting for transfers between devices: 13.7 us -> 24.7 us  [group_shift(): return lax.ppermute(value, 'dp', pairs)]
    ppermute x4, starting transfers between devices: 7.94 us -> 3 us  [group_shift(): return lax.ppermute(value, 'dp', pairs)]
    ppermute x5, waiting for transfers between devices: 22.5 us -> 18.9 us  [mate_swap(): return lax.ppermute(value, 'dp', [(i, i ^ 1) for i in range(n_dp)])]
    ppermute x5, starting transfers between devices: 5.53 us -> 8.64 us  [mate_swap(): return lax.ppermute(value, 'dp', [(i, i ^ 1) for i in range(n_dp)])]
    ppermute x3, waiting for transfers between devices: 2.56 us -> 0.96 us  [part_shift(): lax.ppermute(value, 'parts', [(i, (i + d) % n_parts) for i in range(n_par...]
    ppermute x4, waiting for transfers between devices: 4.28 us -> 2.7 us  [chip_shift(): return lax.ppermute(value, 'row', pairs)]
  transfers between devices with their start and end apart: 26 -> 26, of which waited for: 13 -> 14; matrix products, arithmetic and copies ran while one was open for 5% -> 5% of each run, Pallas kernels for 18% -> 18%
where the time goes in v11:
time: 102 us; the launch traced here: 101 us
  waiting for transfers between devices  49 us (48%)
  starting transfers between devices  23.3 us (23%)
  Pallas kernels  18.8 us (18%)
  local copies, waits for them, and re-layouts  7.92 us (8%)
  other arithmetic  1.45 us (1%)
    ppermute x4, waiting for transfers between devices, group_shift(): return lax.ppermute(value, 'dp', pairs)  24.7 us
    ppermute x5, waiting for transfers between devices, mate_swap(): return lax.ppermute(value, 'dp', [(i, i ^ 1) for i in range(n_dp)])  18.9 us
    pallas_call x15, Pallas kernels, call(): pl.pallas_call(kernel, out_shape=outs, in_specs=[smem] * len(scalars) + [...  18.8 us
    ppermute x5, starting transfers between devices, mate_swap(): return lax.ppermute(value, 'dp', [(i, i ^ 1) for i in range(n_dp)])  8.64 us
    ppermute x4, starting transfers between devices, chip_shift(): return lax.ppermute(value, 'row', pairs)  5.21 us
    unnamed x22, local copies, waits for them, and re-layouts  4.77 us
    ppermute x3, starting transfers between devices, part_shift(): lax.ppermute(value, 'parts', [(i, (i + d) % n_parts) for i in range(n_par...  4.62 us
    dynamic_slice x3, local copies, waits for them, and re-layouts, body(): lax.dynamic_slice_in_dim(blocks, part * held + start, size, axis=0)  3.05 us
  transfers between devices with their start and end apart: 26, of which 14 were waited for; matrix products, arithmetic and copies ran while one was open for 5% of the time, Pallas kernels for 18%

profile of v11, /device:TPU:0, one launch (start us, length us, event | category | flops | bytes accessed | tf_op | source)
XLA Modules:
  0.0 101.3 jit_solution(992525028117826829)
XLA Ops:
  1.2 2.7 %collective-permute-start.3 = (bf16[128,3328]{1,0:T(8,128)(2,1)}, bf16[128,3328]{1,0:T(8,128)(2,1)}, u32[]{:S(2)}, u32[]{:S(2)}) collective-permute-start(bf16[128,3328]{1,0:T(8,128)(2,1)} %own_ref.1), channel_id=1, source_target_pairs={{0,1},{1,0},{2,3},{3,2},{4,5},{5,4},{6,7},{7,6},{8,9},{9,8},{10,11... | collective-permute-start | bytes 2555912 | tf_op jit(solution)/shard_map/ppermute | solution.py:256
  3.8 1.9 %dynamic-slice_bitcast_fusion = bf16[16,128,128]{2,1,0:T(8,128)(2,1)} fusion(bf16[1,64,128,128]{3,2,1,0:T(8,128)(2,1)} %param.10, s32[]{:T(128)S(6)} %select_n.22), kind=kLoop, calls=%fused_computation | loop fusion | bytes 1048580 | tf_op jit(solution)/shard_map/dynamic_slice | solution.py:288
  5.7 2.6 %collective-permute-start.6 = (bf16[16,128,128]{2,1,0:T(8,128)(2,1)}, bf16[16,128,128]{2,1,0:T(8,128)(2,1)}, u32[]{:S(2)}, u32[]{:S(2)}) collective-permute-start(bf16[16,128,128]{2,1,0:T(8,128)(2,1)} %dynamic-slice_bitcast_fusion), channel_id=1, source_target_pairs={{0,2},{1,3},{2,0},{3,1},{4,6},{5,7},{6,4},{7,5},{8,10},{9,11},{10,... | collective-permute-start | bytes 1572872 | tf_op jit(solution)/shard_map/ppermute | solution.py:260
  9.0 1.1 %dynamic-slice_bitcast_fusion.1 = bf16[10,128,128]{2,1,0:T(8,128)(2,1)S(1)} fusion(bf16[1,64,128,128]{3,2,1,0:T(8,128)(2,1)} %param.10, s32[]{:T(128)S(6)} %select_n.18), kind=kLoop, calls=%fused_computation.2 | loop fusion | bytes 655364 | tf_op jit(solution)/shard_map/dynamic_slice | solution.py:288
  11.3 1.0 %copy-done.2 = bf16[128,2048]{1,0:T(8,128)(2,1)S(1)} copy-done((bf16[128,2048]{1,0:T(8,128)(2,1)S(1)}, bf16[128,2048]{1,0:T(8,128)(2,1)}, u32[]{:S(2)}) %copy-start.2) | copy-done | bytes 524312
  12.3 0.9 copy-done.4
  13.2 1.0 copy-done.6
  14.9 1.2 %collective-permute-done.1 = f32[128,128]{1,0:T(8,128)S(1)} collective-permute-done((f32[128,128]{1,0:T(8,128)S(1)}, f32[128,128]{1,0:T(8,128)S(1)}, u32[]{:S(2)}, u32[]{:S(2)}) %collective-permute-start.1) | collective-permute-done | bytes 65568 | tf_op jit(solution)/shard_map/ppermute | solution.py:249
  16.2 1.6 %collective-permute-start.2 = (f32[128,128]{1,0:T(8,128)S(1)}, f32[128,128]{1,0:T(8,128)S(1)}, u32[]{:S(2)}, u32[]{:S(2)}) collective-permute-start(f32[128,128]{1,0:T(8,128)S(1)} %add.24.both_ref), channel_id=1, source_target_pairs={{0,8},{4,12},{8,0},{12,4},{1,9},{5,13},{9,1},{13,5},{2,10},{6,14},... | collective-permute-start | bytes 196616 | tf_op jit(solution)/shard_map/ppermute | solution.py:253
  17.8 2.7 %collective-permute-done.2.rest_0_ = f32[128,128]{1,0:T(8,128)S(1)} collective-permute-done((f32[128,128]{1,0:T(8,128)S(1)}, f32[128,128]{1,0:T(8,128)S(1)}, u32[]{:S(2)}, u32[]{:S(2)}) %collective-permute-start.2) | collective-permute-done | bytes 65568 | tf_op jit(solution)/shard_map/ppermute | solution.py:253
  20.5 1.0 %copy-done.3 = bf16[128,2048]{1,0:T(8,128)(2,1)S(1)} copy-done((bf16[128,2048]{1,0:T(8,128)(2,1)S(1)}, bf16[128,2048]{1,0:T(8,128)(2,1)}, u32[]{:S(2)}) %copy-start.3) | copy-done | bytes 524312
  23.0 11.6 %collective-permute-done.6.rest_0_ = bf16[16,128,128]{2,1,0:T(8,128)(2,1)} collective-permute-done((bf16[16,128,128]{2,1,0:T(8,128)(2,1)}, bf16[16,128,128]{2,1,0:T(8,128)(2,1)}, u32[]{:S(2)}, u32[]{:S(2)}) %collective-permute-start.6) | collective-permute-done | bytes 524320 | tf_op jit(solution)/shard_map/ppermute | solution.py:260
  34.7 1.5 %collective-permute-start.8 = (bf16[16,128,128]{2,1,0:T(8,128)(2,1)}, bf16[16,128,128]{2,1,0:T(8,128)(2,1)}, u32[]{:S(2)}, u32[]{:S(2)}) collective-permute-start(bf16[16,128,128]{2,1,0:T(8,128)(2,1)} %collective-permute-done.6.rest_0_), channel_id=1, source_target_pairs={{0,16},{16,0},{1,17},{17,1},{2,18},{18,2},{3,19},{19,3},{4,20},{20... | collective-permute-start | bytes 1572872 | tf_op jit(solution)/shard_map/ppermute | solution.py:263
  36.2 3.6 %collective-permute-start.4 = (bf16[64,2176]{1,0:T(8,128)(2,1)}, bf16[64,2176]{1,0:T(8,128)(2,1)S(1)}, u32[]{:S(2)}, u32[]{:S(2)}) collective-permute-start(bf16[64,2176]{1,0:T(8,128)(2,1)} %copy-done.7), channel_id=1, source_target_pairs={{0,1},{1,0},{2,3},{3,2},{4,5},{5,4},{6,7},{7,6},{8,9},{9,8},{10,11... | collective-permute-start | bytes 835592 | tf_op jit(solution)/shard_map/ppermute | solution.py:256
  40.0 4.4 %shard_map.98 = (f32[65,256,128]{2,1,0:T(8,128)S(1)}, bf16[26,256,128]{2,1,0:T(8,128)(2,1)S(1)}) custom-call(s32[6]{0:T(128)S(1)} %stack.29.where_ref, s32[64]{0:T(128)S(1)} %bitcast.29, bf16[128,3328]{1,0:T(8,128)(2,1)S(1)} %copy-done, bf16[128,3328]{1,0:T(8,128)(2,1)} %collective-permute-done.3.mate_acts_ref.mate_ref, bf16[64,128,128]{2,1,0:T(8,128)(2,1)S(1)} %bitcast.21), custom_call_target="tpu_custom_call" | custom-call | tf_op jit(solution)/shard_map/pallas_call | solution.py:225
  44.4 4.0 %collective-permute-done.5.refs_0_.rest_1_ = bf16[11,128,128]{2,1,0:T(8,128)(2,1)S(1)} collective-permute-done((bf16[11,128,128]{2,1,0:T(8,128)(2,1)}, bf16[11,128,128]{2,1,0:T(8,128)(2,1)S(1)}, u32[]{:S(2)}, u32[]{:S(2)}) %collective-permute-start.5) | collective-permute-done | bytes 360480 | tf_op jit(solution)/shard_map/ppermute | solution.py:260
  48.4 1.6 %collective-permute-start.9 = (bf16[10,128,128]{2,1,0:T(8,128)(2,1)S(1)}, bf16[10,128,128]{2,1,0:T(8,128)(2,1)S(1)}, u32[]{:S(2)}, u32[]{:S(2)}) collective-permute-start(bf16[10,128,128]{2,1,0:T(8,128)(2,1)S(1)} %slice.3), channel_id=1, source_target_pairs={{0,16},{16,0},{1,17},{17,1},{2,18},{18,2},{3,19},{19,3},{4,20},{20... | collective-permute-start | bytes 983048 | tf_op jit(solution)/shard_map/ppermute | solution.py:263
  50.0 1.7 %collective-permute-done.4.mate_pack_ref = bf16[64,2176]{1,0:T(8,128)(2,1)S(1)} collective-permute-done((bf16[64,2176]{1,0:T(8,128)(2,1)}, bf16[64,2176]{1,0:T(8,128)(2,1)S(1)}, u32[]{:S(2)}, u32[]{:S(2)}) %collective-permute-start.4) | collective-permute-done | bytes 278560 | tf_op jit(solution)/shard_map/ppermute | solution.py:256
  51.8 1.6 %shard_map.96 = (bf16[64,2688]{1,0:T(8,128)(2,1)S(1)}, bf16[64,2688]{1,0:T(8,128)(2,1)S(1)}) custom-call(s32[6]{0:T(128)S(1)} %stack.29.where_ref, bf16[128,128]{1,0:T(8,128)(2,1)S(1)} %get-tuple-element.38.rounded_ref, bf16[128,3328]{1,0:T(8,128)(2,1)S(1)} %copy-done, bf16[128,3328]{1,0:T(8,128)(2,1)} %collective-permute-done.3.mate_acts_ref.mate_ref, ...), custom_call_target="tpu_custom_call" | custom-call | tf_op jit(solution)/shard_map/pallas_call | solution.py:225
  53.4 2.6 %collective-permute-done.7.rest_2_ = bf16[6,128,128]{2,1,0:T(8,128)(2,1)S(1)} collective-permute-done((bf16[6,128,128]{2,1,0:T(8,128)(2,1)S(1)}, bf16[6,128,128]{2,1,0:T(8,128)(2,1)S(1)}, u32[]{:S(2)}, u32[]{:S(2)}) %collective-permute-start.7) | collective-permute-done | bytes 196640 | tf_op jit(solution)/shard_map/ppermute | solution.py:260
  56.0 1.5 %collective-permute-start.10 = (bf16[6,128,128]{2,1,0:T(8,128)(2,1)S(1)}, bf16[6,128,128]{2,1,0:T(8,128)(2,1)S(1)}, u32[]{:S(2)}, u32[]{:S(2)}) collective-permute-start(bf16[6,128,128]{2,1,0:T(8,128)(2,1)S(1)} %collective-permute-done.7.rest_2_), channel_id=1, source_target_pairs={{0,16},{16,0},{1,17},{17,1},{2,18},{18,2},{3,19},{19,3},{4,20},{20... | collective-permute-start | bytes 589832 | tf_op jit(solution)/shard_map/ppermute | solution.py:263
  57.6 3.6 %shard_map.99.old_ref = f32[65,256,128]{2,1,0:T(8,128)S(1)} custom-call(s32[6]{0:T(128)S(1)} %stack.29.where_ref, s32[1,128]{1,0:T(1,128)S(1)} %shard_map.97.ids_ref, bf16[26,256,128]{2,1,0:T(8,128)(2,1)S(1)} %get-tuple-element.45.tiles_ref, f32[65,256,128]{2,1,0:T(8,128)S(1)} %get-tuple-element.46.old_ref, ...), custom_call_target="tpu_custom_call", output_to_operand_aliasing={{}: (3, {})} | custom-call | tf_op jit(solution)/shard_map/pallas_call | solution.py:225
  61.2 1.0 collective-permute-done.10.rest_0_
  62.2 1.0 shard_map.100
  65.5 1.5 %collective-permute-start.17 = (bf16[4,128,128]{2,1,0:T(8,128)(2,1)S(1)}, bf16[4,128,128]{2,1,0:T(8,128)(2,1)S(1)}, u32[]{:S(2)}, u32[]{:S(2)}) collective-permute-start(bf16[4,128,128]{2,1,0:T(8,128)(2,1)S(1)} %bitcast.25), channel_id=1, source_target_pairs={{0,8},{4,12},{8,0},{12,4},{1,9},{5,13},{9,1},{13,5},{2,10},{6,14},... | collective-permute-start | bytes 393224 | tf_op jit(solution)/shard_map/ppermute | solution.py:253
  68.3 6.4 %collective-permute-done.19.rest_0_ = bf16[64,2688]{1,0:T(8,128)(2,1)S(1)} collective-permute-done((bf16[64,2688]{1,0:T(8,128)(2,1)S(1)}, bf16[64,2688]{1,0:T(8,128)(2,1)S(1)}, u32[]{:S(2)}, u32[]{:S(2)}) %collective-permute-start.19) | collective-permute-done | bytes 344096 | tf_op jit(solution)/shard_map/ppermute | solution.py:260
  75.3 2.1 %collective-permute-start.18 = (bf16[4,128,128]{2,1,0:T(8,128)(2,1)S(1)}, bf16[4,128,128]{2,1,0:T(8,128)(2,1)S(1)}, u32[]{:S(2)}, u32[]{:S(2)}) collective-permute-start(bf16[4,128,128]{2,1,0:T(8,128)(2,1)S(1)} %shard_map.103), channel_id=1, source_target_pairs={{0,1},{1,0},{2,3},{3,2},{4,5},{5,4},{6,7},{7,6},{8,9},{9,8},{10,11... | collective-permute-start | bytes 393224 | tf_op jit(solution)/shard_map/ppermute | solution.py:256
  78.1 1.6 %collective-permute-start.25 = (bf16[16,128,128]{2,1,0:T(8,128)(2,1)S(1)}, bf16[16,128,128]{2,1,0:T(8,128)(2,1)S(1)}, u32[]{:S(2)}, u32[]{:S(2)}) collective-permute-start(bf16[16,128,128]{2,1,0:T(8,128)(2,1)S(1)} %bitcast.22), channel_id=1, source_target_pairs={{0,8},{4,12},{8,0},{12,4},{1,9},{5,13},{9,1},{13,5},{2,10},{6,14},... | collective-permute-start | bytes 1572872 | tf_op jit(solution)/shard_map/ppermute | solution.py:253
  79.6 5.9 %collective-permute-done.20.rest_1_ = bf16[64,2688]{1,0:T(8,128)(2,1)S(1)} collective-permute-done((bf16[64,2688]{1,0:T(8,128)(2,1)S(1)}, bf16[64,2688]{1,0:T(8,128)(2,1)S(1)}, u32[]{:S(2)}, u32[]{:S(2)}) %collective-permute-start.20) | collective-permute-done | bytes 344096 | tf_op jit(solution)/shard_map/ppermute | solution.py:256
  85.5 2.4 %collective-permute-done.18.rest_0_ = bf16[4,128,128]{2,1,0:T(8,128)(2,1)S(1)} collective-permute-done((bf16[4,128,128]{2,1,0:T(8,128)(2,1)S(1)}, bf16[4,128,128]{2,1,0:T(8,128)(2,1)S(1)}, u32[]{:S(2)}, u32[]{:S(2)}) %collective-permute-start.18) | collective-permute-done | bytes 131104 | tf_op jit(solution)/shard_map/ppermute | solution.py:256
  89.0 1.8 %shard_map.108 = (f32[64,3328]{1,0:T(8,128)}, f32[64,2048]{1,0:T(8,128)}) custom-call(s32[6]{0:T(128)S(1)} %stack.29.where_ref, bf16[64,2688]{1,0:T(8,128)(2,1)S(1)} %get-tuple-element.40.half_ref, bf16[64,2688]{1,0:T(8,128)(2,1)S(1)} %get-tuple-element.66.other_ref, bf16[64,2688]{1,0:T(8,128)(2,1)S(1)} %collective-permute-done.19.rest_0_, ...), custom_call_target="tpu_custom_call" | custom-call | tf_op jit(solution)/shard_map/pallas_call | solution.py:225
  90.7 8.7 %collective-permute-done.22.rest_1_ = bf16[12,128,128]{2,1,0:T(8,128)(2,1)S(1)} collective-permute-done((bf16[12,128,128]{2,1,0:T(8,128)(2,1)S(1)}, bf16[12,128,128]{2,1,0:T(8,128)(2,1)S(1)}, u32[]{:S(2)}, u32[]{:S(2)}) %collective-permute-start.22) | collective-permute-done | bytes 393248 | tf_op jit(solution)/shard_map/ppermute | solution.py:256
  (66 shorter events, 12.6 us)
Async XLA Ops:
  0.6 10.6 %copy-start = (bf16[128,3328]{1,0:T(8,128)(2,1)S(1)}, bf16[128,3328]{1,0:T(8,128)(2,1)}, u32[]{:S(2)}) copy-start(bf16[128,3328]{1,0:T(8,128)(2,1)} %own_ref.1) | copy-start | bytes 2555908
  0.6 10.6 %copy-start.9 = (s32[128]{0:T(128)S(1)}, s32[128]{0:T(128)}, u32[]{:S(2)}) copy-start(s32[128]{0:T(128)} %param.9) | copy-start | bytes 1540
  0.6 5.1 %collective-permute-start = (s32[64]{0:T(128)}, s32[64]{0:T(128)S(1)}, u32[]{:S(2)}, u32[]{:S(2)}) collective-permute-start(s32[64]{0:T(128)} %bitcast.28), channel_id=1, source_target_pairs={{0,4},{4,0},{8,12},{12,8},{1,5},{5,1},{9,13},{13,9},{2,6},{6,2},{1... | collective-permute-start | bytes 776 | tf_op jit(solution)/shard_map/ppermute | solution.py:249
  1.2 38.8 %collective-permute-start.3 = (bf16[128,3328]{1,0:T(8,128)(2,1)}, bf16[128,3328]{1,0:T(8,128)(2,1)}, u32[]{:S(2)}, u32[]{:S(2)}) collective-permute-start(bf16[128,3328]{1,0:T(8,128)(2,1)} %own_ref.1), channel_id=1, source_target_pairs={{0,1},{1,0},{2,3},{3,2},{4,5},{5,4},{6,7},{7,6},{8,9},{9,8},{10,11... | collective-permute-start | bytes 2555912 | tf_op jit(solution)/shard_map/ppermute | solution.py:256
  5.7 29.0 %collective-permute-start.6 = (bf16[16,128,128]{2,1,0:T(8,128)(2,1)}, bf16[16,128,128]{2,1,0:T(8,128)(2,1)}, u32[]{:S(2)}, u32[]{:S(2)}) collective-permute-start(bf16[16,128,128]{2,1,0:T(8,128)(2,1)} %dynamic-slice_bitcast_fusion), channel_id=1, source_target_pairs={{0,2},{1,3},{2,0},{3,1},{4,6},{5,7},{6,4},{7,5},{8,10},{9,11},{10,... | collective-permute-start | bytes 1572872 | tf_op jit(solution)/shard_map/ppermute | solution.py:260
  9.0 31.0 %copy-start.10 = (s32[1,64]{1,0:T(1,128)S(1)}, s32[1,64]{1,0:T(1,128)}, u32[]{:S(2)}) copy-start(s32[1,64]{1,0:T(1,128)} %param.11) | copy-start | bytes 772
  9.0 30.8 %copy-start.1 = (bf16[1,64,128,128]{3,2,1,0:T(8,128)(2,1)S(1)}, bf16[1,64,128,128]{3,2,1,0:T(8,128)(2,1)}, u32[]{:S(2)}) copy-start(bf16[1,64,128,128]{3,2,1,0:T(8,128)(2,1)} %param.10) | copy-start | bytes 6291460
  10.9 37.5 %collective-permute-start.5 = (bf16[11,128,128]{2,1,0:T(8,128)(2,1)}, bf16[11,128,128]{2,1,0:T(8,128)(2,1)S(1)}, u32[]{:S(2)}, u32[]{:S(2)}) collective-permute-start(bf16[11,128,128]{2,1,0:T(8,128)(2,1)} %pad_maximum_fusion), channel_id=1, source_target_pairs={{0,2},{1,3},{2,0},{3,1},{4,6},{5,7},{6,4},{7,5},{8,10},{9,11},{10,... | collective-permute-start | bytes 1081352 | tf_op jit(solution)/shard_map/ppermute | solution.py:260
  14.8 1.3 %collective-permute-start.1 = (f32[128,128]{1,0:T(8,128)S(1)}, f32[128,128]{1,0:T(8,128)S(1)}, u32[]{:S(2)}, u32[]{:S(2)}) collective-permute-start(f32[128,128]{1,0:T(8,128)S(1)} %shard_map.94), channel_id=1, source_target_pairs={{0,4},{4,0},{8,12},{12,8},{1,5},{5,1},{9,13},{13,9},{2,6},{6,2},{1... | collective-permute-start | bytes 196616 | tf_op jit(solution)/shard_map/ppermute | solution.py:249
  16.2 4.3 %collective-permute-start.2 = (f32[128,128]{1,0:T(8,128)S(1)}, f32[128,128]{1,0:T(8,128)S(1)}, u32[]{:S(2)}, u32[]{:S(2)}) collective-permute-start(f32[128,128]{1,0:T(8,128)S(1)} %add.24.both_ref), channel_id=1, source_target_pairs={{0,8},{4,12},{8,0},{12,4},{1,9},{5,13},{9,1},{13,5},{2,10},{6,14},... | collective-permute-start | bytes 196616 | tf_op jit(solution)/shard_map/ppermute | solution.py:253
  34.7 22.9 %collective-permute-start.8 = (bf16[16,128,128]{2,1,0:T(8,128)(2,1)}, bf16[16,128,128]{2,1,0:T(8,128)(2,1)}, u32[]{:S(2)}, u32[]{:S(2)}) collective-permute-start(bf16[16,128,128]{2,1,0:T(8,128)(2,1)} %collective-permute-done.6.rest_0_), channel_id=1, source_target_pairs={{0,16},{16,0},{1,17},{17,1},{2,18},{18,2},{3,19},{19,3},{4,20},{20... | collective-permute-start | bytes 1572872 | tf_op jit(solution)/shard_map/ppermute | solution.py:263
  36.2 15.6 %collective-permute-start.4 = (bf16[64,2176]{1,0:T(8,128)(2,1)}, bf16[64,2176]{1,0:T(8,128)(2,1)S(1)}, u32[]{:S(2)}, u32[]{:S(2)}) collective-permute-start(bf16[64,2176]{1,0:T(8,128)(2,1)} %copy-done.7), channel_id=1, source_target_pairs={{0,1},{1,0},{2,3},{3,2},{4,5},{5,4},{6,7},{7,6},{8,9},{9,8},{10,11... | collective-permute-start | bytes 835592 | tf_op jit(solution)/shard_map/ppermute | solution.py:256
  39.8 16.2 %collective-permute-start.7 = (bf16[6,128,128]{2,1,0:T(8,128)(2,1)S(1)}, bf16[6,128,128]{2,1,0:T(8,128)(2,1)S(1)}, u32[]{:S(2)}, u32[]{:S(2)}) collective-permute-start(bf16[6,128,128]{2,1,0:T(8,128)(2,1)S(1)} %dynamic-slice_bitcast_fusion.2), channel_id=1, source_target_pairs={{0,2},{1,3},{2,0},{3,1},{4,6},{5,7},{6,4},{7,5},{8,10},{9,11},{10,... | collective-permute-start | bytes 589832 | tf_op jit(solution)/shard_map/ppermute | solution.py:260
  40.0 11.8 %copy-start.8 = (bf16[64,2176]{1,0:T(8,128)(2,1)S(1)}, bf16[64,2176]{1,0:T(8,128)(2,1)}, u32[]{:S(2)}) copy-start(bf16[64,2176]{1,0:T(8,128)(2,1)} %copy-done.7) | copy-start | bytes 835588
  48.4 9.1 %collective-permute-start.9 = (bf16[10,128,128]{2,1,0:T(8,128)(2,1)S(1)}, bf16[10,128,128]{2,1,0:T(8,128)(2,1)S(1)}, u32[]{:S(2)}, u32[]{:S(2)}) collective-permute-start(bf16[10,128,128]{2,1,0:T(8,128)(2,1)S(1)} %slice.3), channel_id=1, source_target_pairs={{0,16},{16,0},{1,17},{17,1},{2,18},{18,2},{3,19},{19,3},{4,20},{20... | collective-permute-start | bytes 983048 | tf_op jit(solution)/shard_map/ppermute | solution.py:263
  56.0 6.1 %collective-permute-start.10 = (bf16[6,128,128]{2,1,0:T(8,128)(2,1)S(1)}, bf16[6,128,128]{2,1,0:T(8,128)(2,1)S(1)}, u32[]{:S(2)}, u32[]{:S(2)}) collective-permute-start(bf16[6,128,128]{2,1,0:T(8,128)(2,1)S(1)} %collective-permute-done.7.rest_2_), channel_id=1, source_target_pairs={{0,16},{16,0},{1,17},{17,1},{2,18},{18,2},{3,19},{19,3},{4,20},{20... | collective-permute-start | bytes 589832 | tf_op jit(solution)/shard_map/ppermute | solution.py:263
  57.5 17.1 %collective-permute-start.19 = (bf16[64,2688]{1,0:T(8,128)(2,1)S(1)}, bf16[64,2688]{1,0:T(8,128)(2,1)S(1)}, u32[]{:S(2)}, u32[]{:S(2)}) collective-permute-start(bf16[64,2688]{1,0:T(8,128)(2,1)S(1)} %get-tuple-element.40.half_ref), channel_id=1, source_target_pairs={{0,2},{1,3},{2,0},{3,1},{4,6},{5,7},{6,4},{7,5},{8,10},{9,11},{10,... | collective-permute-start | bytes 1032200 | tf_op jit(solution)/shard_map/ppermute | solution.py:260
  63.2 1.4 %collective-permute-start.11 = (bf16[1,4,128,128]{3,2,1,0:T(8,128)(2,1)S(1)}, bf16[1,4,128,128]{3,2,1,0:T(8,128)(2,1)S(1)}, u32[]{:S(2)}, u32[]{:S(2)}) collective-permute-start(bf16[1,4,128,128]{3,2,1,0:T(8,128)(2,1)S(1)} %get-tuple-element.53), channel_id=1, source_target_pairs={{0,4},{4,0},{8,12},{12,8},{1,5},{5,1},{9,13},{13,9},{2,6},{6,2},{1... | collective-permute-start | bytes 393224 | tf_op jit(solution)/shard_map/ppermute | solution.py:249
  63.2 11.4 %collective-permute-start.16 = (bf16[16,128,128]{2,1,0:T(8,128)(2,1)S(1)}, bf16[16,128,128]{2,1,0:T(8,128)(2,1)S(1)}, u32[]{:S(2)}, u32[]{:S(2)}) collective-permute-start(bf16[16,128,128]{2,1,0:T(8,128)(2,1)S(1)} %get-tuple-element.59), channel_id=1, source_target_pairs={{0,4},{4,0},{8,12},{12,8},{1,5},{5,1},{9,13},{13,9},{2,6},{6,2},{1... | collective-permute-start | bytes 1572872 | tf_op jit(solution)/shard_map/ppermute | solution.py:249
  63.7 1.8 %collective-permute-start.12 = (bf16[1,4,128,128]{3,2,1,0:T(8,128)(2,1)S(1)}, bf16[1,4,128,128]{3,2,1,0:T(8,128)(2,1)S(1)}, u32[]{:S(2)}, u32[]{:S(2)}) collective-permute-start(bf16[1,4,128,128]{3,2,1,0:T(8,128)(2,1)S(1)} %get-tuple-element.55), channel_id=1, source_target_pairs={{0,4},{4,0},{8,12},{12,8},{1,5},{5,1},{9,13},{13,9},{2,6},{6,2},{1... | collective-permute-start | bytes 393224 | tf_op jit(solution)/shard_map/ppermute | solution.py:249
  63.8 3.2 %collective-permute-start.13 = (bf16[1,4,128,128]{3,2,1,0:T(8,128)(2,1)S(1)}, bf16[1,4,128,128]{3,2,1,0:T(8,128)(2,1)S(1)}, u32[]{:S(2)}, u32[]{:S(2)}) collective-permute-start(bf16[1,4,128,128]{3,2,1,0:T(8,128)(2,1)S(1)} %get-tuple-element.56), channel_id=1, source_target_pairs={{0,4},{4,0},{8,12},{12,8},{1,5},{5,1},{9,13},{13,9},{2,6},{6,2},{1... | collective-permute-start | bytes 393224 | tf_op jit(solution)/shard_map/ppermute | solution.py:249
  64.6 2.4 %collective-permute-start.14 = (bf16[1,4,128,128]{3,2,1,0:T(8,128)(2,1)S(1)}, bf16[1,4,128,128]{3,2,1,0:T(8,128)(2,1)S(1)}, u32[]{:S(2)}, u32[]{:S(2)}) collective-permute-start(bf16[1,4,128,128]{3,2,1,0:T(8,128)(2,1)S(1)} %get-tuple-element.57), channel_id=1, source_target_pairs={{0,4},{4,0},{8,12},{12,8},{1,5},{5,1},{9,13},{13,9},{2,6},{6,2},{1... | collective-permute-start | bytes 393224 | tf_op jit(solution)/shard_map/ppermute | solution.py:249
  65.5 9.2 %collective-permute-start.17 = (bf16[4,128,128]{2,1,0:T(8,128)(2,1)S(1)}, bf16[4,128,128]{2,1,0:T(8,128)(2,1)S(1)}, u32[]{:S(2)}, u32[]{:S(2)}) collective-permute-start(bf16[4,128,128]{2,1,0:T(8,128)(2,1)S(1)} %bitcast.25), channel_id=1, source_target_pairs={{0,8},{4,12},{8,0},{12,4},{1,9},{5,13},{9,1},{13,5},{2,10},{6,14},... | collective-permute-start | bytes 393224 | tf_op jit(solution)/shard_map/ppermute | solution.py:253
  67.7 20.3 %collective-permute-start.21 = (bf16[12,128,128]{2,1,0:T(8,128)(2,1)S(1)}, bf16[12,128,128]{2,1,0:T(8,128)(2,1)S(1)}, u32[]{:S(2)}, u32[]{:S(2)}) collective-permute-start(bf16[12,128,128]{2,1,0:T(8,128)(2,1)S(1)} %bitcast.24), channel_id=1, source_target_pairs={{0,8},{4,12},{8,0},{12,4},{1,9},{5,13},{9,1},{13,5},{2,10},{6,14},... | collective-permute-start | bytes 1179656 | tf_op jit(solution)/shard_map/ppermute | solution.py:253
  68.3 9.1 %collective-permute-start.23 = (bf16[1,8,128,128]{3,2,1,0:T(8,128)(2,1)S(1)}, bf16[1,8,128,128]{3,2,1,0:T(8,128)(2,1)S(1)}, u32[]{:S(2)}, u32[]{:S(2)}) collective-permute-start(bf16[1,8,128,128]{3,2,1,0:T(8,128)(2,1)S(1)} %get-tuple-element.63), channel_id=1, source_target_pairs={{0,4},{4,0},{8,12},{12,8},{1,5},{5,1},{9,13},{13,9},{2,6},{6,2},{1... | collective-permute-start | bytes 786440 | tf_op jit(solution)/shard_map/ppermute | solution.py:249
  74.7 2.7 %collective-permute-start.24 = (bf16[1,8,128,128]{3,2,1,0:T(8,128)(2,1)S(1)}, bf16[1,8,128,128]{3,2,1,0:T(8,128)(2,1)S(1)}, u32[]{:S(2)}, u32[]{:S(2)}) collective-permute-start(bf16[1,8,128,128]{3,2,1,0:T(8,128)(2,1)S(1)} %get-tuple-element.65), channel_id=1, source_target_pairs={{0,4},{4,0},{8,12},{12,8},{1,5},{5,1},{9,13},{13,9},{2,6},{6,2},{1... | collective-permute-start | bytes 786440 | tf_op jit(solution)/shard_map/ppermute | solution.py:249
  74.7 10.9 %collective-permute-start.20 = (bf16[64,2688]{1,0:T(8,128)(2,1)S(1)}, bf16[64,2688]{1,0:T(8,128)(2,1)S(1)}, u32[]{:S(2)}, u32[]{:S(2)}) collective-permute-start(bf16[64,2688]{1,0:T(8,128)(2,1)S(1)} %collective-permute-done.19.rest_0_), channel_id=1, source_target_pairs={{0,1},{1,0},{2,3},{3,2},{4,5},{5,4},{6,7},{7,6},{8,9},{9,8},{10,11... | collective-permute-start | bytes 1032200 | tf_op jit(solution)/shard_map/ppermute | solution.py:256
  75.3 12.7 %collective-permute-start.18 = (bf16[4,128,128]{2,1,0:T(8,128)(2,1)S(1)}, bf16[4,128,128]{2,1,0:T(8,128)(2,1)S(1)}, u32[]{:S(2)}, u32[]{:S(2)}) collective-permute-start(bf16[4,128,128]{2,1,0:T(8,128)(2,1)S(1)} %shard_map.103), channel_id=1, source_target_pairs={{0,1},{1,0},{2,3},{3,2},{4,5},{5,4},{6,7},{7,6},{8,9},{9,8},{10,11... | collective-permute-start | bytes 393224 | tf_op jit(solution)/shard_map/ppermute | solution.py:256
  77.4 13.4 %collective-permute-start.15 = (bf16[16,128,128]{2,1,0:T(8,128)(2,1)S(1)}, bf16[16,128,128]{2,1,0:T(8,128)(2,1)S(1)}, u32[]{:S(2)}, u32[]{:S(2)}) collective-permute-start(bf16[16,128,128]{2,1,0:T(8,128)(2,1)S(1)} %get-tuple-element.58), channel_id=1, source_target_pairs={{0,4},{4,0},{8,12},{12,8},{1,5},{5,1},{9,13},{13,9},{2,6},{6,2},{1... | collective-permute-start | bytes 1572872 | tf_op jit(solution)/shard_map/ppermute | solution.py:249
  78.0 21.4 %copy-start.5 = (bf16[64,2048]{1,0:T(8,128)(2,1)S(1)}, bf16[64,2048]{1,0:T(8,128)(2,1)}, u32[]{:S(2)}) copy-start(bf16[64,2048]{1,0:T(8,128)(2,1)} %adapter_ref.2) | copy-start | bytes 786436
  78.1 22.3 %collective-permute-start.25 = (bf16[16,128,128]{2,1,0:T(8,128)(2,1)S(1)}, bf16[16,128,128]{2,1,0:T(8,128)(2,1)S(1)}, u32[]{:S(2)}, u32[]{:S(2)}) collective-permute-start(bf16[16,128,128]{2,1,0:T(8,128)(2,1)S(1)} %bitcast.22), channel_id=1, source_target_pairs={{0,8},{4,12},{8,0},{12,4},{1,9},{5,13},{9,1},{13,5},{2,10},{6,14},... | collective-permute-start | bytes 1572872 | tf_op jit(solution)/shard_map/ppermute | solution.py:253
  88.6 10.8 %collective-permute-start.22 = (bf16[12,128,128]{2,1,0:T(8,128)(2,1)S(1)}, bf16[12,128,128]{2,1,0:T(8,128)(2,1)S(1)}, u32[]{:S(2)}, u32[]{:S(2)}) collective-permute-start(bf16[12,128,128]{2,1,0:T(8,128)(2,1)S(1)} %shard_map.104), channel_id=1, source_target_pairs={{0,1},{1,0},{2,3},{3,2},{4,5},{5,4},{6,7},{7,6},{8,9},{9,8},{10,11... | collective-permute-start | bytes 1179656 | tf_op jit(solution)/shard_map/ppermute | solution.py:256
  (5 other events, 4.8 us)

commit v12 on v11

--- a/solution.py
+++ b/solution.py
@@ -65,7 +65,7 @@
 def last_kernel(where_ref, ids_ref, tiles_ref, old_ref, *rest, block_count, **plan):
     blocks, total_ref, sends = rest[:block_count], rest[block_count], rest[block_count + 1:]
     add_arrivals(where_ref, ids_ref, tiles_ref, blocks, total_ref, **plan)
-    far_mate, near_mate, far_own, near_own = sends[:4], sends[4:5], sends[5:7], sends[7:]
+    far_mate, near_mate, far_own, near_own = sends[:4], sends[4:6], sends[6:8], sends[8:]
     tokens, share = near_own[0].shape[1], near_own[0].shape[0]
     chips = far_own[0].shape[0] + 1
 
@@ -106,7 +106,7 @@
     size, tokens, _ = out_ref.shape
     first = (2 * where_ref[2] + where_ref[1]) * where_ref[5] + block
     for k in range(size):
-        value = total_ref[first + k, tokens:, :] + core_ref[block + k].astype(F32)
+        value = total_ref[first + k, tokens:, :] + core_ref[k].astype(F32)
         for piece in pieces:
             value += piece[k].astype(F32)
         out_ref[k] = value.astype(BF16)
@@ -356,7 +356,9 @@
             functools.partial(more_kernel, **plan(more)), (total_shape,), (where, all_ids),
             (on_chip(tiles), on_chip(total)) + values(more), {3: 0},
         )
-        small = share // 4
+        small = max(1, 2 * share // 16)
+        rest = share - small
+        thirds = (rest - 2 * (rest // 3), rest // 3, rest // 3)
         half = share // 2
 
         def far_piece(size):
@@ -367,12 +369,13 @@
 
         total, *sends = call(
             functools.partial(last_kernel, block_count=len(last), **plan(last)),
-            (total_shape,) + (far_piece(small),) * 4 + (near_piece(share),)
+            (total_shape, far_piece(small)) + tuple(far_piece(size) for size in thirds)
+            + (near_piece(small), near_piece(rest))
             + (far_piece(half),) * 2 + (near_piece(share),),
             (after(where, half_grads), all_ids), (on_chip(tiles), on_chip(total)) + values(last), {3: 0},
         )
 
-        cores = [core_swap(value) for value in sends[:5]]
+        cores = [core_swap(value) for value in sends[:6]]
 
         def for_chips(pieces, token, block, *needed):
             size = sum(piece.shape[1] for piece in pieces)
@@ -384,21 +387,20 @@
 
         leaving_first, pieces_first = for_chips(cores[:1], tokens, 0)
         leaving_second, pieces_second = for_chips(cores[1:4], tokens, small, leaving_first)
-        cores += [core_swap(after(value, leaving_second)) for value in sends[5:]]
-        leaving_own, own_pieces = for_chips(cores[5:7], 0, 0)
-        far_grads = [after(value, *pieces_first) for value in far_grads]
-        mate_grads = [mate_swap(value) for value in far_grads]
-
-        def for_mate(pieces, size, block, *needed):
+        cores += [core_swap(after(value, leaving_second)) for value in sends[6:]]
+        leaving_own, own_pieces = for_chips(cores[6:8], 0, 0)
+        def for_mate(core_got, pieces, block, *needed):
             (value,) = call(
-                functools.partial(mate_kernel, block=block), (near_piece(size),),
-                (after(where, *needed) if needed else where,), (on_chip(total), cores[4]) + tuple(pieces),
+                functools.partial(mate_kernel, block=block), (near_piece(core_got.shape[0]),),
+                (after(where, *needed) if needed else where,), (on_chip(total), core_got) + tuple(pieces),
             )
             return mate_swap(value)
 
-        from_mate_first = for_mate(pieces_first, small, 0)
+        from_mate_first = for_mate(cores[4], pieces_first, 0)
+        far_grads = [after(value, from_mate_first) for value in far_grads]
+        mate_grads = [mate_swap(value) for value in far_grads]
         from_mate = [
-            from_mate_first, for_mate(pieces_second, share - small, small, from_mate_first, *mate_grads),
+            from_mate_first, for_mate(cores[5], pieces_second, small, *mate_grads),
         ]
         in_grad, out_grad = call(
             grad_sum_kernel,
@@ -407,7 +409,7 @@
         )
         (near,) = call(
             near_kernel, (pltpu.VMEM((share, tokens, tile), F32),), (where,),
-            (rounded, output_adapter, on_chip(total), cores[7]) + tuple(from_mate),
+            (rounded, output_adapter, on_chip(total), cores[8]) + tuple(from_mate),
         )
         (projected,) = call(
             final_kernel, (jax.ShapeDtypeStruct((tokens, feats), BF16),), (), (on_chip(near),) + tuple(own_pieces),

time: 102 us -> 101 us (level)
  waiting for transfers between devices: 49 us -> 45.7 us
  starting transfers between devices: 23.3 us -> 25.6 us
    ppermute x4, waiting for transfers between devices: 24.7 us -> 19.9 us  [group_shift(): return lax.ppermute(value, 'dp', pairs)]
    ppermute x5, waiting for transfers between devices: 18.9 us -> 17.2 us  [mate_swap(): return lax.ppermute(value, 'dp', [(i, i ^ 1) for i in range(n_dp)])]
    ppermute x10 -> x11, waiting for transfers between devices: 1.8 us -> 3.45 us  [core_swap(): return lax.ppermute(value, 'row', [(i, i ^ 1) for i in range(n_row)])]
    ppermute x4, waiting for transfers between devices: 2.7 us -> 4.2 us  [chip_shift(): return lax.ppermute(value, 'row', pairs)]
    ppermute x5, starting transfers between devices: 8.64 us -> 10 us  [mate_swap(): return lax.ppermute(value, 'dp', [(i, i ^ 1) for i in range(n_dp)])]
    ppermute x10 -> x11, starting transfers between devices: 1.84 us -> 2.64 us  [core_swap(): return lax.ppermute(value, 'row', [(i, i ^ 1) for i in range(n_row)])]
  transfers between devices with their start and end apart: 26 -> 27, of which waited for: 14 -> 16; matrix products, arithmetic and copies ran while one was open for 5% -> 5% of each run, Pallas kernels for 18% -> 18%
where the time goes in v12:
time: 101 us; the launch traced here: 100 us
  waiting for transfers between devices  45.7 us (45%)
  starting transfers between devices  25.6 us (25%)
  Pallas kernels  18.8 us (19%)
  local copies, waits for them, and re-layouts  7.92 us (8%)
  other arithmetic  1.45 us (1%)
    ppermute x4, waiting for transfers between devices, group_shift(): return lax.ppermute(value, 'dp', pairs)  19.9 us
    pallas_call x15, Pallas kernels, call(): pl.pallas_call(kernel, out_shape=outs, in_specs=[smem] * len(scalars) + [...  18.8 us
    ppermute x5, waiting for transfers between devices, mate_swap(): return lax.ppermute(value, 'dp', [(i, i ^ 1) for i in range(n_dp)])  17.2 us
    ppermute x5, starting transfers between devices, mate_swap(): return lax.ppermute(value, 'dp', [(i, i ^ 1) for i in range(n_dp)])  10 us
    ppermute x4, starting transfers between devices, chip_shift(): return lax.ppermute(value, 'row', pairs)  5.27 us
    unnamed x22, local copies, waits for them, and re-layouts  4.77 us
    ppermute x3, starting transfers between devices, part_shift(): lax.ppermute(value, 'parts', [(i, (i + d) % n_parts) for i in range(n_par...  4.62 us
    ppermute x4, waiting for transfers between devices, chip_shift(): return lax.ppermute(value, 'row', pairs)  4.2 us
  transfers between devices with their start and end apart: 27, of which 16 were waited for; matrix products, arithmetic and copies ran while one was open for 5% of the time, Pallas kernels for 18%

profile of v12, /device:TPU:0, one launch (start us, length us, event | category | flops | bytes accessed | tf_op | source)
XLA Modules:
  0.0 100.3 jit_solution(8436856618080760319)
XLA Ops:
  1.2 2.7 %collective-permute-start.3 = (bf16[128,3328]{1,0:T(8,128)(2,1)}, bf16[128,3328]{1,0:T(8,128)(2,1)}, u32[]{:S(2)}, u32[]{:S(2)}) collective-permute-start(bf16[128,3328]{1,0:T(8,128)(2,1)} %own_ref.1), channel_id=1, source_target_pairs={{0,1},{1,0},{2,3},{3,2},{4,5},{5,4},{6,7},{7,6},{8,9},{9,8},{10,11... | collective-permute-start | bytes 2555912 | tf_op jit(solution)/shard_map/ppermute | solution.py:256
  3.8 1.9 %dynamic-slice_bitcast_fusion = bf16[16,128,128]{2,1,0:T(8,128)(2,1)} fusion(bf16[1,64,128,128]{3,2,1,0:T(8,128)(2,1)} %param.10, s32[]{:T(128)S(6)} %select_n.22), kind=kLoop, calls=%fused_computation | loop fusion | bytes 1048580 | tf_op jit(solution)/shard_map/dynamic_slice | solution.py:288
  5.7 2.6 %collective-permute-start.6 = (bf16[16,128,128]{2,1,0:T(8,128)(2,1)}, bf16[16,128,128]{2,1,0:T(8,128)(2,1)}, u32[]{:S(2)}, u32[]{:S(2)}) collective-permute-start(bf16[16,128,128]{2,1,0:T(8,128)(2,1)} %dynamic-slice_bitcast_fusion), channel_id=1, source_target_pairs={{0,2},{1,3},{2,0},{3,1},{4,6},{5,7},{6,4},{7,5},{8,10},{9,11},{10,... | collective-permute-start | bytes 1572872 | tf_op jit(solution)/shard_map/ppermute | solution.py:260
  9.0 1.1 %dynamic-slice_bitcast_fusion.1 = bf16[10,128,128]{2,1,0:T(8,128)(2,1)S(1)} fusion(bf16[1,64,128,128]{3,2,1,0:T(8,128)(2,1)} %param.10, s32[]{:T(128)S(6)} %select_n.18), kind=kLoop, calls=%fused_computation.2 | loop fusion | bytes 655364 | tf_op jit(solution)/shard_map/dynamic_slice | solution.py:288
  11.3 1.0 %copy-done.2 = bf16[128,2048]{1,0:T(8,128)(2,1)S(1)} copy-done((bf16[128,2048]{1,0:T(8,128)(2,1)S(1)}, bf16[128,2048]{1,0:T(8,128)(2,1)}, u32[]{:S(2)}) %copy-start.2) | copy-done | bytes 524312
  13.2 1.0 %copy-done.6 = bf16[3328,64]{0,1:T(8,128)(2,1)S(1)} copy-done((bf16[3328,64]{0,1:T(8,128)(2,1)S(1)}, bf16[3328,64]{0,1:T(8,128)(2,1)}, u32[]{:S(2)}) %copy-start.6) | copy-done | bytes 426008
  14.9 1.2 %collective-permute-done.1 = f32[128,128]{1,0:T(8,128)S(1)} collective-permute-done((f32[128,128]{1,0:T(8,128)S(1)}, f32[128,128]{1,0:T(8,128)S(1)}, u32[]{:S(2)}, u32[]{:S(2)}) %collective-permute-start.1) | collective-permute-done | bytes 65568 | tf_op jit(solution)/shard_map/ppermute | solution.py:249
  16.2 1.6 %collective-permute-start.2 = (f32[128,128]{1,0:T(8,128)S(1)}, f32[128,128]{1,0:T(8,128)S(1)}, u32[]{:S(2)}, u32[]{:S(2)}) collective-permute-start(f32[128,128]{1,0:T(8,128)S(1)} %add.24.both_ref), channel_id=1, source_target_pairs={{0,8},{4,12},{8,0},{12,4},{1,9},{5,13},{9,1},{13,5},{2,10},{6,14},... | collective-permute-start | bytes 196616 | tf_op jit(solution)/shard_map/ppermute | solution.py:253
  17.8 2.7 %collective-permute-done.2.rest_0_ = f32[128,128]{1,0:T(8,128)S(1)} collective-permute-done((f32[128,128]{1,0:T(8,128)S(1)}, f32[128,128]{1,0:T(8,128)S(1)}, u32[]{:S(2)}, u32[]{:S(2)}) %collective-permute-start.2) | collective-permute-done | bytes 65568 | tf_op jit(solution)/shard_map/ppermute | solution.py:253
  20.5 1.0 %copy-done.3 = bf16[128,2048]{1,0:T(8,128)(2,1)S(1)} copy-done((bf16[128,2048]{1,0:T(8,128)(2,1)S(1)}, bf16[128,2048]{1,0:T(8,128)(2,1)}, u32[]{:S(2)}) %copy-start.3) | copy-done | bytes 524312
  23.0 11.6 %collective-permute-done.6.rest_0_ = bf16[16,128,128]{2,1,0:T(8,128)(2,1)} collective-permute-done((bf16[16,128,128]{2,1,0:T(8,128)(2,1)}, bf16[16,128,128]{2,1,0:T(8,128)(2,1)}, u32[]{:S(2)}, u32[]{:S(2)}) %collective-permute-start.6) | collective-permute-done | bytes 524320 | tf_op jit(solution)/shard_map/ppermute | solution.py:260
  34.7 1.5 %collective-permute-start.8 = (bf16[16,128,128]{2,1,0:T(8,128)(2,1)}, bf16[16,128,128]{2,1,0:T(8,128)(2,1)}, u32[]{:S(2)}, u32[]{:S(2)}) collective-permute-start(bf16[16,128,128]{2,1,0:T(8,128)(2,1)} %collective-permute-done.6.rest_0_), channel_id=1, source_target_pairs={{0,16},{16,0},{1,17},{17,1},{2,18},{18,2},{3,19},{19,3},{4,20},{20... | collective-permute-start | bytes 1572872 | tf_op jit(solution)/shard_map/ppermute | solution.py:263
  36.2 3.6 %collective-permute-start.4 = (bf16[64,2176]{1,0:T(8,128)(2,1)}, bf16[64,2176]{1,0:T(8,128)(2,1)S(1)}, u32[]{:S(2)}, u32[]{:S(2)}) collective-permute-start(bf16[64,2176]{1,0:T(8,128)(2,1)} %copy-done.7), channel_id=1, source_target_pairs={{0,1},{1,0},{2,3},{3,2},{4,5},{5,4},{6,7},{7,6},{8,9},{9,8},{10,11... | collective-permute-start | bytes 835592 | tf_op jit(solution)/shard_map/ppermute | solution.py:256
  40.0 4.4 %shard_map.98 = (f32[65,256,128]{2,1,0:T(8,128)S(1)}, bf16[26,256,128]{2,1,0:T(8,128)(2,1)S(1)}) custom-call(s32[6]{0:T(128)S(1)} %stack.29.where_ref, s32[64]{0:T(128)S(1)} %bitcast.29, bf16[128,3328]{1,0:T(8,128)(2,1)S(1)} %copy-done, bf16[128,3328]{1,0:T(8,128)(2,1)} %collective-permute-done.3.mate_acts_ref.mate_ref, bf16[64,128,128]{2,1,0:T(8,128)(2,1)S(1)} %bitcast.21), custom_call_target="tpu_custom_call" | custom-call | tf_op jit(solution)/shard_map/pallas_call | solution.py:225
  44.4 4.0 %collective-permute-done.5.refs_0_.rest_1_ = bf16[11,128,128]{2,1,0:T(8,128)(2,1)S(1)} collective-permute-done((bf16[11,128,128]{2,1,0:T(8,128)(2,1)}, bf16[11,128,128]{2,1,0:T(8,128)(2,1)S(1)}, u32[]{:S(2)}, u32[]{:S(2)}) %collective-permute-start.5) | collective-permute-done | bytes 360480 | tf_op jit(solution)/shard_map/ppermute | solution.py:260
  48.4 1.6 %collective-permute-start.9 = (bf16[10,128,128]{2,1,0:T(8,128)(2,1)S(1)}, bf16[10,128,128]{2,1,0:T(8,128)(2,1)S(1)}, u32[]{:S(2)}, u32[]{:S(2)}) collective-permute-start(bf16[10,128,128]{2,1,0:T(8,128)(2,1)S(1)} %slice.3), channel_id=1, source_target_pairs={{0,16},{16,0},{1,17},{17,1},{2,18},{18,2},{3,19},{19,3},{4,20},{20... | collective-permute-start | bytes 983048 | tf_op jit(solution)/shard_map/ppermute | solution.py:263
  50.0 1.7 %collective-permute-done.4.mate_pack_ref = bf16[64,2176]{1,0:T(8,128)(2,1)S(1)} collective-permute-done((bf16[64,2176]{1,0:T(8,128)(2,1)}, bf16[64,2176]{1,0:T(8,128)(2,1)S(1)}, u32[]{:S(2)}, u32[]{:S(2)}) %collective-permute-start.4) | collective-permute-done | bytes 278560 | tf_op jit(solution)/shard_map/ppermute | solution.py:256
  51.8 1.6 %shard_map.96 = (bf16[64,2688]{1,0:T(8,128)(2,1)S(1)}, bf16[64,2688]{1,0:T(8,128)(2,1)S(1)}) custom-call(s32[6]{0:T(128)S(1)} %stack.29.where_ref, bf16[128,128]{1,0:T(8,128)(2,1)S(1)} %get-tuple-element.39.rounded_ref, bf16[128,3328]{1,0:T(8,128)(2,1)S(1)} %copy-done, bf16[128,3328]{1,0:T(8,128)(2,1)} %collective-permute-done.3.mate_acts_ref.mate_ref, ...), custom_call_target="tpu_custom_call" | custom-call | tf_op jit(solution)/shard_map/pallas_call | solution.py:225
  53.4 2.6 %collective-permute-done.7.rest_2_ = bf16[6,128,128]{2,1,0:T(8,128)(2,1)S(1)} collective-permute-done((bf16[6,128,128]{2,1,0:T(8,128)(2,1)S(1)}, bf16[6,128,128]{2,1,0:T(8,128)(2,1)S(1)}, u32[]{:S(2)}, u32[]{:S(2)}) %collective-permute-start.7) | collective-permute-done | bytes 196640 | tf_op jit(solution)/shard_map/ppermute | solution.py:260
  56.0 1.5 %collective-permute-start.10 = (bf16[6,128,128]{2,1,0:T(8,128)(2,1)S(1)}, bf16[6,128,128]{2,1,0:T(8,128)(2,1)S(1)}, u32[]{:S(2)}, u32[]{:S(2)}) collective-permute-start(bf16[6,128,128]{2,1,0:T(8,128)(2,1)S(1)} %collective-permute-done.7.rest_2_), channel_id=1, source_target_pairs={{0,16},{16,0},{1,17},{17,1},{2,18},{18,2},{3,19},{19,3},{4,20},{20... | collective-permute-start | bytes 589832 | tf_op jit(solution)/shard_map/ppermute | solution.py:263
  57.6 3.6 %shard_map.99.old_ref = f32[65,256,128]{2,1,0:T(8,128)S(1)} custom-call(s32[6]{0:T(128)S(1)} %stack.29.where_ref, s32[1,128]{1,0:T(1,128)S(1)} %shard_map.97.ids_ref, bf16[26,256,128]{2,1,0:T(8,128)(2,1)S(1)} %get-tuple-element.46.tiles_ref, f32[65,256,128]{2,1,0:T(8,128)S(1)} %get-tuple-element.47.old_ref, ...), custom_call_target="tpu_custom_call", output_to_operand_aliasing={{}: (3, {})} | custom-call | tf_op jit(solution)/shard_map/pallas_call | solution.py:225
  66.1 1.6 %collective-permute-start.17 = (bf16[2,128,128]{2,1,0:T(8,128)(2,1)S(1)}, bf16[2,128,128]{2,1,0:T(8,128)(2,1)S(1)}, u32[]{:S(2)}, u32[]{:S(2)}) collective-permute-start(bf16[2,128,128]{2,1,0:T(8,128)(2,1)S(1)} %bitcast.25), channel_id=1, source_target_pairs={{0,8},{4,12},{8,0},{12,4},{1,9},{5,13},{9,1},{13,5},{2,10},{6,14},... | collective-permute-start | bytes 196616 | tf_op jit(solution)/shard_map/ppermute | solution.py:253
  68.9 1.5 %collective-permute-done.17.rest_0_ = bf16[2,128,128]{2,1,0:T(8,128)(2,1)S(1)} collective-permute-done((bf16[2,128,128]{2,1,0:T(8,128)(2,1)S(1)}, bf16[2,128,128]{2,1,0:T(8,128)(2,1)S(1)}, u32[]{:S(2)}, u32[]{:S(2)}) %collective-permute-start.17) | collective-permute-done | bytes 65568 | tf_op jit(solution)/shard_map/ppermute | solution.py:253
  71.0 2.1 %collective-permute-start.18 = (bf16[2,128,128]{2,1,0:T(8,128)(2,1)S(1)}, bf16[2,128,128]{2,1,0:T(8,128)(2,1)S(1)}, u32[]{:S(2)}, u32[]{:S(2)}) collective-permute-start(bf16[2,128,128]{2,1,0:T(8,128)(2,1)S(1)} %shard_map.103), channel_id=1, source_target_pairs={{0,1},{1,0},{2,3},{3,2},{4,5},{5,4},{6,7},{7,6},{8,9},{9,8},{10,11... | collective-permute-start | bytes 196616 | tf_op jit(solution)/shard_map/ppermute | solution.py:256
  73.1 1.6 %collective-permute-done.19.rest_0_ = bf16[64,2688]{1,0:T(8,128)(2,1)S(1)} collective-permute-done((bf16[64,2688]{1,0:T(8,128)(2,1)S(1)}, bf16[64,2688]{1,0:T(8,128)(2,1)S(1)}, u32[]{:S(2)}, u32[]{:S(2)}) %collective-permute-start.19) | collective-permute-done | bytes 344096 | tf_op jit(solution)/shard_map/ppermute | solution.py:260
  74.8 1.3 %collective-permute-done.18.rest_0_ = bf16[2,128,128]{2,1,0:T(8,128)(2,1)S(1)} collective-permute-done((bf16[2,128,128]{2,1,0:T(8,128)(2,1)S(1)}, bf16[2,128,128]{2,1,0:T(8,128)(2,1)S(1)}, u32[]{:S(2)}, u32[]{:S(2)}) %collective-permute-start.18) | collective-permute-done | bytes 65568 | tf_op jit(solution)/shard_map/ppermute | solution.py:256
  76.1 1.3 %collective-permute-start.20 = (bf16[64,2688]{1,0:T(8,128)(2,1)S(1)}, bf16[64,2688]{1,0:T(8,128)(2,1)S(1)}, u32[]{:S(2)}, u32[]{:S(2)}) collective-permute-start(bf16[64,2688]{1,0:T(8,128)(2,1)S(1)} %collective-permute-done.19.rest_0_), channel_id=1, source_target_pairs={{0,1},{1,0},{2,3},{3,2},{4,5},{5,4},{6,7},{7,6},{8,9},{9,8},{10,11... | collective-permute-start | bytes 1032200 | tf_op jit(solution)/shard_map/ppermute | solution.py:256
  77.9 1.0 %collective-permute-done.24.rest_0_ = bf16[1,8,128,128]{3,2,1,0:T(8,128)(2,1)S(1)} collective-permute-done((bf16[1,8,128,128]{3,2,1,0:T(8,128)(2,1)S(1)}, bf16[1,8,128,128]{3,2,1,0:T(8,128)(2,1)S(1)}, u32[]{:S(2)}, u32[]{:S(2)}) %collective-permute-start.24) | collective-permute-done | bytes 262176 | tf_op jit(solution)/shard_map/ppermute | solution.py:249
  80.0 1.6 %collective-permute-start.26 = (bf16[16,128,128]{2,1,0:T(8,128)(2,1)S(1)}, bf16[16,128,128]{2,1,0:T(8,128)(2,1)S(1)}, u32[]{:S(2)}, u32[]{:S(2)}) collective-permute-start(bf16[16,128,128]{2,1,0:T(8,128)(2,1)S(1)} %bitcast.22), channel_id=1, source_target_pairs={{0,8},{4,12},{8,0},{12,4},{1,9},{5,13},{9,1},{13,5},{2,10},{6,14},... | collective-permute-start | bytes 1572872 | tf_op jit(solution)/shard_map/ppermute | solution.py:253
  81.6 4.5 %collective-permute-done.20.rest_1_ = bf16[64,2688]{1,0:T(8,128)(2,1)S(1)} collective-permute-done((bf16[64,2688]{1,0:T(8,128)(2,1)S(1)}, bf16[64,2688]{1,0:T(8,128)(2,1)S(1)}, u32[]{:S(2)}, u32[]{:S(2)}) %collective-permute-start.20) | collective-permute-done | bytes 344096 | tf_op jit(solution)/shard_map/ppermute | solution.py:256
  87.1 1.8 %shard_map.108 = (f32[64,3328]{1,0:T(8,128)}, f32[64,2048]{1,0:T(8,128)}) custom-call(s32[6]{0:T(128)S(1)} %stack.29.where_ref, bf16[64,2688]{1,0:T(8,128)(2,1)S(1)} %get-tuple-element.41.half_ref, bf16[64,2688]{1,0:T(8,128)(2,1)S(1)} %get-tuple-element.68.other_ref, bf16[64,2688]{1,0:T(8,128)(2,1)S(1)} %collective-permute-done.19.rest_0_, ...), custom_call_target="tpu_custom_call" | custom-call | tf_op jit(solution)/shard_map/pallas_call | solution.py:225
  88.9 9.5 %collective-permute-done.23.rest_1_ = bf16[14,128,128]{2,1,0:T(8,128)(2,1)S(1)} collective-permute-done((bf16[14,128,128]{2,1,0:T(8,128)(2,1)S(1)}, bf16[14,128,128]{2,1,0:T(8,128)(2,1)S(1)}, u32[]{:S(2)}, u32[]{:S(2)}) %collective-permute-start.23) | collective-permute-done | bytes 458784 | tf_op jit(solution)/shard_map/ppermute | solution.py:256
  (68 shorter events, 16.9 us)
Async XLA Ops:
  0.6 10.6 %copy-start = (bf16[128,3328]{1,0:T(8,128)(2,1)S(1)}, bf16[128,3328]{1,0:T(8,128)(2,1)}, u32[]{:S(2)}) copy-start(bf16[128,3328]{1,0:T(8,128)(2,1)} %own_ref.1) | copy-start | bytes 2555908
  0.6 5.1 %collective-permute-start = (s32[64]{0:T(128)}, s32[64]{0:T(128)S(1)}, u32[]{:S(2)}, u32[]{:S(2)}) collective-permute-start(s32[64]{0:T(128)} %bitcast.28), channel_id=1, source_target_pairs={{0,4},{4,0},{8,12},{12,8},{1,5},{5,1},{9,13},{13,9},{2,6},{6,2},{1... | collective-permute-start | bytes 776 | tf_op jit(solution)/shard_map/ppermute | solution.py:249
  1.2 38.8 %collective-permute-start.3 = (bf16[128,3328]{1,0:T(8,128)(2,1)}, bf16[128,3328]{1,0:T(8,128)(2,1)}, u32[]{:S(2)}, u32[]{:S(2)}) collective-permute-start(bf16[128,3328]{1,0:T(8,128)(2,1)} %own_ref.1), channel_id=1, source_target_pairs={{0,1},{1,0},{2,3},{3,2},{4,5},{5,4},{6,7},{7,6},{8,9},{9,8},{10,11... | collective-permute-start | bytes 2555912 | tf_op jit(solution)/shard_map/ppermute | solution.py:256
  5.7 29.0 %collective-permute-start.6 = (bf16[16,128,128]{2,1,0:T(8,128)(2,1)}, bf16[16,128,128]{2,1,0:T(8,128)(2,1)}, u32[]{:S(2)}, u32[]{:S(2)}) collective-permute-start(bf16[16,128,128]{2,1,0:T(8,128)(2,1)} %dynamic-slice_bitcast_fusion), channel_id=1, source_target_pairs={{0,2},{1,3},{2,0},{3,1},{4,6},{5,7},{6,4},{7,5},{8,10},{9,11},{10,... | collective-permute-start | bytes 1572872 | tf_op jit(solution)/shard_map/ppermute | solution.py:260
  9.0 31.0 %copy-start.10 = (s32[1,64]{1,0:T(1,128)S(1)}, s32[1,64]{1,0:T(1,128)}, u32[]{:S(2)}) copy-start(s32[1,64]{1,0:T(1,128)} %param.11) | copy-start | bytes 772
  9.0 30.8 %copy-start.1 = (bf16[1,64,128,128]{3,2,1,0:T(8,128)(2,1)S(1)}, bf16[1,64,128,128]{3,2,1,0:T(8,128)(2,1)}, u32[]{:S(2)}) copy-start(bf16[1,64,128,128]{3,2,1,0:T(8,128)(2,1)} %param.10) | copy-start | bytes 6291460
  10.9 37.5 %collective-permute-start.5 = (bf16[11,128,128]{2,1,0:T(8,128)(2,1)}, bf16[11,128,128]{2,1,0:T(8,128)(2,1)S(1)}, u32[]{:S(2)}, u32[]{:S(2)}) collective-permute-start(bf16[11,128,128]{2,1,0:T(8,128)(2,1)} %pad_maximum_fusion), channel_id=1, source_target_pairs={{0,2},{1,3},{2,0},{3,1},{4,6},{5,7},{6,4},{7,5},{8,10},{9,11},{10,... | collective-permute-start | bytes 1081352 | tf_op jit(solution)/shard_map/ppermute | solution.py:260
  14.8 1.3 %collective-permute-start.1 = (f32[128,128]{1,0:T(8,128)S(1)}, f32[128,128]{1,0:T(8,128)S(1)}, u32[]{:S(2)}, u32[]{:S(2)}) collective-permute-start(f32[128,128]{1,0:T(8,128)S(1)} %shard_map.94), channel_id=1, source_target_pairs={{0,4},{4,0},{8,12},{12,8},{1,5},{5,1},{9,13},{13,9},{2,6},{6,2},{1... | collective-permute-start | bytes 196616 | tf_op jit(solution)/shard_map/ppermute | solution.py:249
  16.2 4.3 %collective-permute-start.2 = (f32[128,128]{1,0:T(8,128)S(1)}, f32[128,128]{1,0:T(8,128)S(1)}, u32[]{:S(2)}, u32[]{:S(2)}) collective-permute-start(f32[128,128]{1,0:T(8,128)S(1)} %add.24.both_ref), channel_id=1, source_target_pairs={{0,8},{4,12},{8,0},{12,4},{1,9},{5,13},{9,1},{13,5},{2,10},{6,14},... | collective-permute-start | bytes 196616 | tf_op jit(solution)/shard_map/ppermute | solution.py:253
  34.7 22.9 %collective-permute-start.8 = (bf16[16,128,128]{2,1,0:T(8,128)(2,1)}, bf16[16,128,128]{2,1,0:T(8,128)(2,1)}, u32[]{:S(2)}, u32[]{:S(2)}) collective-permute-start(bf16[16,128,128]{2,1,0:T(8,128)(2,1)} %collective-permute-done.6.rest_0_), channel_id=1, source_target_pairs={{0,16},{16,0},{1,17},{17,1},{2,18},{18,2},{3,19},{19,3},{4,20},{20... | collective-permute-start | bytes 1572872 | tf_op jit(solution)/shard_map/ppermute | solution.py:263
  36.2 15.6 %collective-permute-start.4 = (bf16[64,2176]{1,0:T(8,128)(2,1)}, bf16[64,2176]{1,0:T(8,128)(2,1)S(1)}, u32[]{:S(2)}, u32[]{:S(2)}) collective-permute-start(bf16[64,2176]{1,0:T(8,128)(2,1)} %copy-done.7), channel_id=1, source_target_pairs={{0,1},{1,0},{2,3},{3,2},{4,5},{5,4},{6,7},{7,6},{8,9},{9,8},{10,11... | collective-permute-start | bytes 835592 | tf_op jit(solution)/shard_map/ppermute | solution.py:256
  39.8 16.2 %collective-permute-start.7 = (bf16[6,128,128]{2,1,0:T(8,128)(2,1)S(1)}, bf16[6,128,128]{2,1,0:T(8,128)(2,1)S(1)}, u32[]{:S(2)}, u32[]{:S(2)}) collective-permute-start(bf16[6,128,128]{2,1,0:T(8,128)(2,1)S(1)} %dynamic-slice_bitcast_fusion.2), channel_id=1, source_target_pairs={{0,2},{1,3},{2,0},{3,1},{4,6},{5,7},{6,4},{7,5},{8,10},{9,11},{10,... | collective-permute-start | bytes 589832 | tf_op jit(solution)/shard_map/ppermute | solution.py:260
  40.0 11.8 %copy-start.8 = (bf16[64,2176]{1,0:T(8,128)(2,1)S(1)}, bf16[64,2176]{1,0:T(8,128)(2,1)}, u32[]{:S(2)}) copy-start(bf16[64,2176]{1,0:T(8,128)(2,1)} %copy-done.7) | copy-start | bytes 835588
  48.4 9.1 %collective-permute-start.9 = (bf16[10,128,128]{2,1,0:T(8,128)(2,1)S(1)}, bf16[10,128,128]{2,1,0:T(8,128)(2,1)S(1)}, u32[]{:S(2)}, u32[]{:S(2)}) collective-permute-start(bf16[10,128,128]{2,1,0:T(8,128)(2,1)S(1)} %slice.3), channel_id=1, source_target_pairs={{0,16},{16,0},{1,17},{17,1},{2,18},{18,2},{3,19},{19,3},{4,20},{20... | collective-permute-start | bytes 983048 | tf_op jit(solution)/shard_map/ppermute | solution.py:263
  56.0 6.1 %collective-permute-start.10 = (bf16[6,128,128]{2,1,0:T(8,128)(2,1)S(1)}, bf16[6,128,128]{2,1,0:T(8,128)(2,1)S(1)}, u32[]{:S(2)}, u32[]{:S(2)}) collective-permute-start(bf16[6,128,128]{2,1,0:T(8,128)(2,1)S(1)} %collective-permute-done.7.rest_2_), channel_id=1, source_target_pairs={{0,16},{16,0},{1,17},{17,1},{2,18},{18,2},{3,19},{19,3},{4,20},{20... | collective-permute-start | bytes 589832 | tf_op jit(solution)/shard_map/ppermute | solution.py:263
  57.5 17.2 %collective-permute-start.19 = (bf16[64,2688]{1,0:T(8,128)(2,1)S(1)}, bf16[64,2688]{1,0:T(8,128)(2,1)S(1)}, u32[]{:S(2)}, u32[]{:S(2)}) collective-permute-start(bf16[64,2688]{1,0:T(8,128)(2,1)S(1)} %get-tuple-element.41.half_ref), channel_id=1, source_target_pairs={{0,2},{1,3},{2,0},{3,1},{4,6},{5,7},{6,4},{7,5},{8,10},{9,11},{10,... | collective-permute-start | bytes 1032200 | tf_op jit(solution)/shard_map/ppermute | solution.py:260
  63.2 4.5 %collective-permute-start.12 = (bf16[1,6,128,128]{3,2,1,0:T(8,128)(2,1)S(1)}, bf16[1,6,128,128]{3,2,1,0:T(8,128)(2,1)S(1)}, u32[]{:S(2)}, u32[]{:S(2)}) collective-permute-start(bf16[1,6,128,128]{3,2,1,0:T(8,128)(2,1)S(1)} %get-tuple-element.56), channel_id=1, source_target_pairs={{0,4},{4,0},{8,12},{12,8},{1,5},{5,1},{9,13},{13,9},{2,6},{6,2},{1... | collective-permute-start | bytes 589832 | tf_op jit(solution)/shard_map/ppermute | solution.py:249
  63.2 2.8 %collective-permute-start.13 = (bf16[1,4,128,128]{3,2,1,0:T(8,128)(2,1)S(1)}, bf16[1,4,128,128]{3,2,1,0:T(8,128)(2,1)S(1)}, u32[]{:S(2)}, u32[]{:S(2)}) collective-permute-start(bf16[1,4,128,128]{3,2,1,0:T(8,128)(2,1)S(1)} %get-tuple-element.57), channel_id=1, source_target_pairs={{0,4},{4,0},{8,12},{12,8},{1,5},{5,1},{9,13},{13,9},{2,6},{6,2},{1... | collective-permute-start | bytes 393224 | tf_op jit(solution)/shard_map/ppermute | solution.py:249
  63.7 3.9 %collective-permute-start.14 = (bf16[1,4,128,128]{3,2,1,0:T(8,128)(2,1)S(1)}, bf16[1,4,128,128]{3,2,1,0:T(8,128)(2,1)S(1)}, u32[]{:S(2)}, u32[]{:S(2)}) collective-permute-start(bf16[1,4,128,128]{3,2,1,0:T(8,128)(2,1)S(1)} %get-tuple-element.58), channel_id=1, source_target_pairs={{0,4},{4,0},{8,12},{12,8},{1,5},{5,1},{9,13},{13,9},{2,6},{6,2},{1... | collective-permute-start | bytes 393224 | tf_op jit(solution)/shard_map/ppermute | solution.py:249
  63.8 1.4 %collective-permute-start.11 = (bf16[1,2,128,128]{3,2,1,0:T(8,128)(2,1)S(1)}, bf16[1,2,128,128]{3,2,1,0:T(8,128)(2,1)S(1)}, u32[]{:S(2)}, u32[]{:S(2)}) collective-permute-start(bf16[1,2,128,128]{3,2,1,0:T(8,128)(2,1)S(1)} %get-tuple-element.54), channel_id=1, source_target_pairs={{0,4},{4,0},{8,12},{12,8},{1,5},{5,1},{9,13},{13,9},{2,6},{6,2},{1... | collective-permute-start | bytes 196616 | tf_op jit(solution)/shard_map/ppermute | solution.py:249
  65.2 3.7 %collective-permute-start.16 = (bf16[2,128,128]{2,1,0:T(8,128)(2,1)S(1)}, bf16[2,128,128]{2,1,0:T(8,128)(2,1)S(1)}, u32[]{:S(2)}, u32[]{:S(2)}) collective-permute-start(bf16[2,128,128]{2,1,0:T(8,128)(2,1)S(1)} %get-tuple-element.60), channel_id=1, source_target_pairs={{0,4},{4,0},{8,12},{12,8},{1,5},{5,1},{9,13},{13,9},{2,6},{6,2},{1... | collective-permute-start | bytes 196616 | tf_op jit(solution)/shard_map/ppermute | solution.py:249
  66.1 4.3 %collective-permute-start.17 = (bf16[2,128,128]{2,1,0:T(8,128)(2,1)S(1)}, bf16[2,128,128]{2,1,0:T(8,128)(2,1)S(1)}, u32[]{:S(2)}, u32[]{:S(2)}) collective-permute-start(bf16[2,128,128]{2,1,0:T(8,128)(2,1)S(1)} %bitcast.25), channel_id=1, source_target_pairs={{0,8},{4,12},{8,0},{12,4},{1,9},{5,13},{9,1},{13,5},{2,10},{6,14},... | collective-permute-start | bytes 196616 | tf_op jit(solution)/shard_map/ppermute | solution.py:253
  67.6 18.4 %collective-permute-start.21 = (bf16[14,128,128]{2,1,0:T(8,128)(2,1)S(1)}, bf16[14,128,128]{2,1,0:T(8,128)(2,1)S(1)}, u32[]{:S(2)}, u32[]{:S(2)}) collective-permute-start(bf16[14,128,128]{2,1,0:T(8,128)(2,1)S(1)} %get-tuple-element.63), channel_id=1, source_target_pairs={{0,4},{4,0},{8,12},{12,8},{1,5},{5,1},{9,13},{13,9},{2,6},{6,2},{1... | collective-permute-start | bytes 1376264 | tf_op jit(solution)/shard_map/ppermute | solution.py:249
  68.3 17.7 %collective-permute-start.22 = (bf16[14,128,128]{2,1,0:T(8,128)(2,1)S(1)}, bf16[14,128,128]{2,1,0:T(8,128)(2,1)S(1)}, u32[]{:S(2)}, u32[]{:S(2)}) collective-permute-start(bf16[14,128,128]{2,1,0:T(8,128)(2,1)S(1)} %bitcast.23), channel_id=1, source_target_pairs={{0,8},{4,12},{8,0},{12,4},{1,9},{5,13},{9,1},{13,5},{2,10},{6,14},... | collective-permute-start | bytes 1376264 | tf_op jit(solution)/shard_map/ppermute | solution.py:253
  71.0 5.1 %collective-permute-start.18 = (bf16[2,128,128]{2,1,0:T(8,128)(2,1)S(1)}, bf16[2,128,128]{2,1,0:T(8,128)(2,1)S(1)}, u32[]{:S(2)}, u32[]{:S(2)}) collective-permute-start(bf16[2,128,128]{2,1,0:T(8,128)(2,1)S(1)} %shard_map.103), channel_id=1, source_target_pairs={{0,1},{1,0},{2,3},{3,2},{4,5},{5,4},{6,7},{7,6},{8,9},{9,8},{10,11... | collective-permute-start | bytes 196616 | tf_op jit(solution)/shard_map/ppermute | solution.py:256
  76.1 10.0 %collective-permute-start.20 = (bf16[64,2688]{1,0:T(8,128)(2,1)S(1)}, bf16[64,2688]{1,0:T(8,128)(2,1)S(1)}, u32[]{:S(2)}, u32[]{:S(2)}) collective-permute-start(bf16[64,2688]{1,0:T(8,128)(2,1)S(1)} %collective-permute-done.19.rest_0_), channel_id=1, source_target_pairs={{0,1},{1,0},{2,3},{3,2},{4,5},{5,4},{6,7},{7,6},{8,9},{9,8},{10,11... | collective-permute-start | bytes 1032200 | tf_op jit(solution)/shard_map/ppermute | solution.py:256
  77.4 1.5 %collective-permute-start.24 = (bf16[1,8,128,128]{3,2,1,0:T(8,128)(2,1)S(1)}, bf16[1,8,128,128]{3,2,1,0:T(8,128)(2,1)S(1)}, u32[]{:S(2)}, u32[]{:S(2)}) collective-permute-start(bf16[1,8,128,128]{3,2,1,0:T(8,128)(2,1)S(1)} %get-tuple-element.65), channel_id=1, source_target_pairs={{0,4},{4,0},{8,12},{12,8},{1,5},{5,1},{9,13},{13,9},{2,6},{6,2},{1... | collective-permute-start | bytes 786440 | tf_op jit(solution)/shard_map/ppermute | solution.py:249
  77.4 1.9 %collective-permute-start.25 = (bf16[1,8,128,128]{3,2,1,0:T(8,128)(2,1)S(1)}, bf16[1,8,128,128]{3,2,1,0:T(8,128)(2,1)S(1)}, u32[]{:S(2)}, u32[]{:S(2)}) collective-permute-start(bf16[1,8,128,128]{3,2,1,0:T(8,128)(2,1)S(1)} %get-tuple-element.67), channel_id=1, source_target_pairs={{0,4},{4,0},{8,12},{12,8},{1,5},{5,1},{9,13},{13,9},{2,6},{6,2},{1... | collective-permute-start | bytes 786440 | tf_op jit(solution)/shard_map/ppermute | solution.py:249
  78.9 9.9 %collective-permute-start.15 = (bf16[16,128,128]{2,1,0:T(8,128)(2,1)S(1)}, bf16[16,128,128]{2,1,0:T(8,128)(2,1)S(1)}, u32[]{:S(2)}, u32[]{:S(2)}) collective-permute-start(bf16[16,128,128]{2,1,0:T(8,128)(2,1)S(1)} %get-tuple-element.59), channel_id=1, source_target_pairs={{0,4},{4,0},{8,12},{12,8},{1,5},{5,1},{9,13},{13,9},{2,6},{6,2},{1... | collective-permute-start | bytes 1572872 | tf_op jit(solution)/shard_map/ppermute | solution.py:249
  80.0 18.4 %copy-start.5 = (bf16[64,2048]{1,0:T(8,128)(2,1)S(1)}, bf16[64,2048]{1,0:T(8,128)(2,1)}, u32[]{:S(2)}) copy-start(bf16[64,2048]{1,0:T(8,128)(2,1)} %adapter_ref.2) | copy-start | bytes 786436
  80.0 19.4 %collective-permute-start.26 = (bf16[16,128,128]{2,1,0:T(8,128)(2,1)S(1)}, bf16[16,128,128]{2,1,0:T(8,128)(2,1)S(1)}, u32[]{:S(2)}, u32[]{:S(2)}) collective-permute-start(bf16[16,128,128]{2,1,0:T(8,128)(2,1)S(1)} %bitcast.22), channel_id=1, source_target_pairs={{0,8},{4,12},{8,0},{12,4},{1,9},{5,13},{9,1},{13,5},{2,10},{6,14},... | collective-permute-start | bytes 1572872 | tf_op jit(solution)/shard_map/ppermute | solution.py:253
  86.7 11.7 %collective-permute-start.23 = (bf16[14,128,128]{2,1,0:T(8,128)(2,1)S(1)}, bf16[14,128,128]{2,1,0:T(8,128)(2,1)S(1)}, u32[]{:S(2)}, u32[]{:S(2)}) collective-permute-start(bf16[14,128,128]{2,1,0:T(8,128)(2,1)S(1)} %shard_map.104), channel_id=1, source_target_pairs={{0,1},{1,0},{2,3},{3,2},{4,5},{5,4},{6,7},{7,6},{8,9},{9,8},{10,11... | collective-permute-start | bytes 1376264 | tf_op jit(solution)/shard_map/ppermute | solution.py:256
  (6 other events, 15.4 us)

commit v13 on v10

--- a/solution.py
+++ b/solution.py
@@ -140,58 +140,74 @@
 
 
 def own_grad_kernel(where_ref, cot_ref, labels_ref, both_ref, *rest):
-    received, (rounded_ref, pack_ref) = rest[:-2], rest[-2:]
-    feats = cot_ref.shape[1]
+    received, (rounded_ref, kept_ref, pack_ref) = rest[:-3], rest[-3:]
+    half = kept_ref.shape[1]
     rounded = ordered_sum(both_ref[...], [ref[...] for ref in received], where_ref[2]).astype(BF16)
     rounded_ref[...] = rounded
     rank = rounded.shape[0] // 2
     signs = (1 - 2 * labels_ref[...]).astype(F32)
     signed_low = (rounded[:rank].astype(F32) * signs).astype(BF16)
-    grad = jnp.dot(signed_low, cot_ref[...], preferred_element_type=F32)
-    pack_ref[:, :feats] = (adapter_scale * grad).astype(BF16)
-    pack_ref[:, feats:] = rounded[rank:]
-
-
-def pair_grad_kernel(
-    where_ref, rounded_ref, acts_ref, mate_acts_ref, pack_ref, mate_pack_ref, half_ref, other_ref
-):
-    rank, shard_rows = rounded_ref.shape[0] // 2, acts_ref.shape[1]
-    feats = pack_ref.shape[1] - rounded_ref.shape[1]
-    in_half, out_half = shard_rows // 2, feats // 2
-    back, mate_back = rounded_ref[rank:, :], mate_pack_ref[:, feats:]
-
-    def fill(bit, out_ref):
-        cols = slice(bit * in_half, (bit + 1) * in_half)
-        grad = jnp.dot(back, acts_ref[:, cols], preferred_element_type=F32)
-        grad = grad + jnp.dot(mate_back, mate_acts_ref[:, cols], preferred_element_type=F32)
-        out_ref[:, :in_half] = (adapter_scale * grad).astype(BF16)
-        cols = slice(bit * out_half, (bit + 1) * out_half)
-        grad = pack_ref[:, cols].astype(F32) + mate_pack_ref[:, cols].astype(F32)
-        out_ref[:, in_half:] = grad.astype(BF16)
+
+    def grad(bit):
+        cols = cot_ref[:, bit * half:(bit + 1) * half]
+        return adapter_scale * jnp.dot(signed_low, cols, preferred_element_type=F32)
 
     for bit in range(2):
         @pl.when(where_ref[3] == bit)
         def _():
-            fill(bit, half_ref)
-            fill(1 - bit, other_ref)
+            kept_ref[...] = grad(bit)
+            pack_ref[:, :half] = grad(1 - bit).astype(BF16)
+    pack_ref[:, half:] = rounded[rank:]
+
+
+def pair_grad_kernel(
+    where_ref, rounded_ref, acts_ref, mate_acts_ref, kept_ref, mate_pack_ref, half_ref, other_ref
+):
+    rank, in_half, out_half = rounded_ref.shape[0] // 2, other_ref.shape[1], kept_ref.shape[1]
+    back, mate_back = rounded_ref[rank:, :], mate_pack_ref[:, out_half:]
+
+    def grad(bit):
+        cols = slice(bit * in_half, (bit + 1) * in_half)
+        own = jnp.dot(back, acts_ref[:, cols], preferred_element_type=F32)
+        mate = jnp.dot(mate_back, mate_acts_ref[:, cols], preferred_element_type=F32)
+        return (adapter_scale * (own + mate)).astype(BF16)
+
+    for bit in range(2):
+        @pl.when(where_ref[3] == bit)
+        def _():
+            half_ref[:, :in_half] = grad(bit)
+            other_ref[...] = grad(1 - bit)
+    half_ref[:, in_half:] = (kept_ref[...] + mate_pack_ref[:, :out_half].astype(F32)).astype(BF16)
+
+
+def forward_kernel(where_ref, half_ref, *rest, in_half):
+    count = len(rest) // 2
+    received, outs = rest[:count], rest[count:]
+    for ref, out_ref in zip(received, outs):
+        out_ref[:, :in_half] = ref[:, :in_half]
+    total = ordered_sum(
+        half_ref[:, in_half:].astype(F32), [ref[:, in_half:].astype(F32) for ref in received], where_ref[4]
+    )
+    outs[0][:, in_half:] = total.astype(BF16)
 
 
 def grad_sum_kernel(where_ref, half_ref, other_ref, *rest):
     received, (in_ref, out_ref) = rest[:-2], rest[-2:]
     in_half, out_half = in_ref.shape[1] // 2, out_ref.shape[1] // 2
-    count = len(received) // 2
-    place = where_ref[4]
-
-    def add(bit, own_ref, halves):
-        total = ordered_sum(own_ref[...].astype(F32), [ref[...].astype(F32) for ref in halves], place)
-        in_ref[:, bit * in_half:(bit + 1) * in_half] = total[:, :in_half]
-        out_ref[:, bit * out_half:(bit + 1) * out_half] = total[:, in_half:]
+    count = len(received) // 3
+    far, sent, passed = received[:count], received[count:2 * count], received[2 * count:]
+
+    def total(own, halves):
+        return ordered_sum(own.astype(F32), [ref[:, :in_half].astype(F32) for ref in halves], where_ref[4])
 
     for bit in range(2):
         @pl.when(where_ref[3] == bit)
         def _():
-            add(bit, half_ref, received[:count])
-            add(1 - bit, other_ref, received[count:])
+            mine, others = slice(bit * in_half, (bit + 1) * in_half), slice((1 - bit) * in_half, (2 - bit) * in_half)
+            in_ref[:, mine] = total(half_ref[:, :in_half], far)
+            in_ref[:, others] = total(other_ref[...], passed)
+            out_ref[:, bit * out_half:(bit + 1) * out_half] = sent[0][:, in_half:].astype(F32)
+            out_ref[:, (1 - bit) * out_half:(2 - bit) * out_half] = passed[0][:, in_half:].astype(F32)
 
 
 def near_kernel(where_ref, rounded_ref, adapter_ref, total_ref, core_ref, *rest):
@@ -308,11 +324,12 @@
             (activations, after(adapter_a, soon).T, cotangent, after(output_adapter, soon), labels),
         )
         both = both + core_swap(both)
-        rounded, pack = call(
+        rounded, kept, pack = call(
             own_grad_kernel,
             (
                 jax.ShapeDtypeStruct((2 * rank, tokens), BF16),
-                jax.ShapeDtypeStruct((rank, feats + tokens), BF16),
+                jax.ShapeDtypeStruct((rank, feats // 2), F32),
+                jax.ShapeDtypeStruct((rank, feats // 2 + tokens), BF16),
             ),
             (where,), (cotangent, labels, both) + tuple(chip_shift(both, d) for d in range(1, chips)),
         )
@@ -333,9 +350,11 @@
             (total_shape, pltpu.VMEM((row_blocks, 2 * tokens, tile), BF16)),
             (after(where, rounded, leaving_chunks[-1]), ids), (activations, mate_activations, blocks),
         )
-        half_shape = jax.ShapeDtypeStruct((rank, (shard_rows + feats) // 2), BF16)
+        in_half, both_halves = shard_rows // 2, (shard_rows + feats) // 2
         half_grads, other_grads = call(
-            pair_grad_kernel, (half_shape, half_shape), (where,), (rounded, activations, mate_activations, pack, mate_pack),
+            pair_grad_kernel,
+            (jax.ShapeDtypeStruct((rank, both_halves), BF16), jax.ShapeDtypeStruct((rank, in_half), BF16)),
+            (where,), (rounded, activations, mate_activations, kept, mate_pack),
         )
         far_grads = [group_shift(half_grads, d) for d in range(1, group)]
 
@@ -387,7 +406,12 @@
         cores += [core_swap(after(value, leaving_second)) for value in sends[5:]]
         leaving_own, own_pieces = for_chips(cores[5:7], 0, 0)
         far_grads = [after(value, *pieces_first) for value in far_grads]
-        mate_grads = [mate_swap(value) for value in far_grads]
+        passing = call(
+            functools.partial(forward_kernel, in_half=in_half),
+            tuple(jax.ShapeDtypeStruct((rank, in_half if d else both_halves), BF16) for d in range(group - 1)),
+            (where,), (half_grads,) + tuple(far_grads),
+        )
+        mate_grads = [mate_swap(value) for value in passing]
 
         def for_mate(pieces, size, block, *needed):
             (value,) = call(
@@ -403,7 +427,7 @@
         in_grad, out_grad = call(
             grad_sum_kernel,
             (jax.ShapeDtypeStruct((rank, shard_rows), F32), jax.ShapeDtypeStruct((rank, feats), F32)),
-            (where,), (half_grads, other_grads) + tuple(far_grads) + tuple(mate_grads),
+            (where,), (half_grads, other_grads) + tuple(far_grads) + tuple(passing) + tuple(mate_grads),
         )
         (near,) = call(
             near_kernel, (pltpu.VMEM((share, tokens, tile), F32),), (where,),

time: 98.5 us -> 99.6 us (1.011)
  starting transfers between devices: 24.4 us -> 22.7 us
  waiting for transfers between devices: 44.7 us -> 46.2 us
    ppermute x4, starting transfers between devices: 7.94 us -> 3.52 us  [group_shift(): return lax.ppermute(value, 'dp', pairs)]
    ppermute x5, waiting for transfers between devices: 22.5 us -> 18.3 us  [mate_swap(): return lax.ppermute(value, 'dp', [(i, i ^ 1) for i in range(n_dp)])]
    ppermute x4, waiting for transfers between devices: 13.7 us -> 16.9 us  [group_shift(): return lax.ppermute(value, 'dp', pairs)]
    ppermute x5, starting transfers between devices: 5.53 us -> 8.06 us  [mate_swap(): return lax.ppermute(value, 'dp', [(i, i ^ 1) for i in range(n_dp)])]
    ppermute x3, waiting for transfers between devices: 2.56 us -> 4.96 us  [part_shift(): lax.ppermute(value, 'parts', [(i, (i + d) % n_parts) for i in range(n_par...]
    unnamed x22 -> x24, local copies, waits for them, and re-layouts: 4.77 us -> 5.42 us
    pallas_call x15 -> x16, Pallas kernels: 18.8 us -> 19.4 us  [call(): pl.pallas_call(kernel, out_shape=outs, in_specs=[smem] * len(scalars) + [...]
  transfers between devices with their start and end apart: 26 -> 26, of which waited for: 13 -> 13; matrix products, arithmetic and copies ran while one was open for 5% -> 5% of each run, Pallas kernels for 18% -> 19%
where the time goes in v13:
time: 99.6 us; the launch traced here: 99.1 us
  waiting for transfers between devices  46.2 us (46%)
  starting transfers between devices  22.7 us (23%)
  Pallas kernels  19.4 us (19%)
  local copies, waits for them, and re-layouts  8.57 us (9%)
  other arithmetic  1.45 us (1%)
    pallas_call x16, Pallas kernels, call(): pl.pallas_call(kernel, out_shape=outs, in_specs=[smem] * len(scalars) + [...  19.4 us
    ppermute x5, waiting for transfers between devices, mate_swap(): return lax.ppermute(value, 'dp', [(i, i ^ 1) for i in range(n_dp)])  18.3 us
    ppermute x4, waiting for transfers between devices, group_shift(): return lax.ppermute(value, 'dp', pairs)  16.9 us
    ppermute x5, starting transfers between devices, mate_swap(): return lax.ppermute(value, 'dp', [(i, i ^ 1) for i in range(n_dp)])  8.06 us
    unnamed x24, local copies, waits for them, and re-layouts  5.42 us
    ppermute x4, starting transfers between devices, chip_shift(): return lax.ppermute(value, 'row', pairs)  5.2 us
    ppermute x3, waiting for transfers between devices, part_shift(): lax.ppermute(value, 'parts', [(i, (i + d) % n_parts) for i in range(n_par...  4.96 us
    ppermute x4, waiting for transfers between devices, chip_shift(): return lax.ppermute(value, 'row', pairs)  4.44 us
  transfers between devices with their start and end apart: 26, of which 13 were waited for; matrix products, arithmetic and copies ran while one was open for 5% of the time, Pallas kernels for 19%

profile of v13, /device:TPU:0, one launch (start us, length us, event | category | flops | bytes accessed | tf_op | source)
XLA Modules:
  0.0 99.1 jit_solution(11799034610004812532)
XLA Ops:
  0.6 3.1 %collective-permute-start.3 = (bf16[128,3328]{1,0:T(8,128)(2,1)}, bf16[128,3328]{1,0:T(8,128)(2,1)}, u32[]{:S(2)}, u32[]{:S(2)}) collective-permute-start(bf16[128,3328]{1,0:T(8,128)(2,1)} %own_ref.1), channel_id=1, source_target_pairs={{0,1},{1,0},{2,3},{3,2},{4,5},{5,4},{6,7},{7,6},{8,9},{9,8},{10,11... | collective-permute-start | bytes 2555912 | tf_op jit(solution)/shard_map/ppermute | solution.py:272
  3.7 1.9 %dynamic-slice_bitcast_fusion = bf16[16,128,128]{2,1,0:T(8,128)(2,1)} fusion(bf16[1,64,128,128]{3,2,1,0:T(8,128)(2,1)} %param.10, s32[]{:T(128)S(6)} %select_n.18), kind=kLoop, calls=%fused_computation | loop fusion | bytes 1048580 | tf_op jit(solution)/shard_map/dynamic_slice | solution.py:304
  5.6 2.6 %collective-permute-start.6 = (bf16[16,128,128]{2,1,0:T(8,128)(2,1)}, bf16[16,128,128]{2,1,0:T(8,128)(2,1)}, u32[]{:S(2)}, u32[]{:S(2)}) collective-permute-start(bf16[16,128,128]{2,1,0:T(8,128)(2,1)} %dynamic-slice_bitcast_fusion), channel_id=1, source_target_pairs={{0,2},{1,3},{2,0},{3,1},{4,6},{5,7},{6,4},{7,5},{8,10},{9,11},{10,... | collective-permute-start | bytes 1572872 | tf_op jit(solution)/shard_map/ppermute | solution.py:276
  8.9 1.1 %dynamic-slice_bitcast_fusion.1 = bf16[10,128,128]{2,1,0:T(8,128)(2,1)S(1)} fusion(bf16[1,64,128,128]{3,2,1,0:T(8,128)(2,1)} %param.10, s32[]{:T(128)S(6)} %select_n.19), kind=kLoop, calls=%fused_computation.2 | loop fusion | bytes 655364 | tf_op jit(solution)/shard_map/dynamic_slice | solution.py:304
  11.2 1.0 %copy-done.2 = bf16[128,2048]{1,0:T(8,128)(2,1)S(1)} copy-done((bf16[128,2048]{1,0:T(8,128)(2,1)S(1)}, bf16[128,2048]{1,0:T(8,128)(2,1)}, u32[]{:S(2)}) %copy-start.2) | copy-done | bytes 524312
  12.2 0.9 copy-done.4
  13.2 1.0 %copy-done.6 = bf16[3328,64]{0,1:T(8,128)(2,1)S(1)} copy-done((bf16[3328,64]{0,1:T(8,128)(2,1)S(1)}, bf16[3328,64]{0,1:T(8,128)(2,1)}, u32[]{:S(2)}) %copy-start.6) | copy-done | bytes 426008
  15.1 1.0 %collective-permute-done.1 = f32[128,128]{1,0:T(8,128)S(1)} collective-permute-done((f32[128,128]{1,0:T(8,128)S(1)}, f32[128,128]{1,0:T(8,128)S(1)}, u32[]{:S(2)}, u32[]{:S(2)}) %collective-permute-start.1) | collective-permute-done | bytes 65568 | tf_op jit(solution)/shard_map/ppermute | solution.py:265
  16.1 1.6 %collective-permute-start.2 = (f32[128,128]{1,0:T(8,128)S(1)}, f32[128,128]{1,0:T(8,128)S(1)}, u32[]{:S(2)}, u32[]{:S(2)}) collective-permute-start(f32[128,128]{1,0:T(8,128)S(1)} %add.25.both_ref), channel_id=1, source_target_pairs={{0,8},{4,12},{8,0},{12,4},{1,9},{5,13},{9,1},{13,5},{2,10},{6,14},... | collective-permute-start | bytes 196616 | tf_op jit(solution)/shard_map/ppermute | solution.py:269
  17.7 2.7 %collective-permute-done.2.rest_0_ = f32[128,128]{1,0:T(8,128)S(1)} collective-permute-done((f32[128,128]{1,0:T(8,128)S(1)}, f32[128,128]{1,0:T(8,128)S(1)}, u32[]{:S(2)}, u32[]{:S(2)}) %collective-permute-start.2) | collective-permute-done | bytes 65568 | tf_op jit(solution)/shard_map/ppermute | solution.py:269
  20.4 1.0 %copy-done.3 = bf16[128,2048]{1,0:T(8,128)(2,1)S(1)} copy-done((bf16[128,2048]{1,0:T(8,128)(2,1)S(1)}, bf16[128,2048]{1,0:T(8,128)(2,1)}, u32[]{:S(2)}) %copy-start.3) | copy-done | bytes 524312
  23.6 11.1 %collective-permute-done.6.rest_0_ = bf16[16,128,128]{2,1,0:T(8,128)(2,1)} collective-permute-done((bf16[16,128,128]{2,1,0:T(8,128)(2,1)}, bf16[16,128,128]{2,1,0:T(8,128)(2,1)}, u32[]{:S(2)}, u32[]{:S(2)}) %collective-permute-start.6) | collective-permute-done | bytes 524320 | tf_op jit(solution)/shard_map/ppermute | solution.py:276
  34.7 4.6 %collective-permute-done.3.mate_acts_ref.mate_ref = bf16[128,3328]{1,0:T(8,128)(2,1)} collective-permute-done((bf16[128,3328]{1,0:T(8,128)(2,1)}, bf16[128,3328]{1,0:T(8,128)(2,1)}, u32[]{:S(2)}, u32[]{:S(2)}) %collective-permute-start.3) | collective-permute-done | bytes 852000 | tf_op jit(solution)/shard_map/ppermute | solution.py:272
  39.3 1.7 %collective-permute-start.8 = (bf16[16,128,128]{2,1,0:T(8,128)(2,1)}, bf16[16,128,128]{2,1,0:T(8,128)(2,1)}, u32[]{:S(2)}, u32[]{:S(2)}) collective-permute-start(bf16[16,128,128]{2,1,0:T(8,128)(2,1)} %collective-permute-done.6.rest_0_), channel_id=1, source_target_pairs={{0,16},{16,0},{1,17},{17,1},{2,18},{18,2},{3,19},{19,3},{4,20},{20... | collective-permute-start | bytes 1572872 | tf_op jit(solution)/shard_map/ppermute | solution.py:279
  41.6 2.5 %collective-permute-start.4 = (bf16[64,1152]{1,0:T(8,128)(2,1)}, bf16[64,1152]{1,0:T(8,128)(2,1)S(1)}, u32[]{:S(2)}, u32[]{:S(2)}) collective-permute-start(bf16[64,1152]{1,0:T(8,128)(2,1)} %copy-done.11), channel_id=1, source_target_pairs={{0,1},{1,0},{2,3},{3,2},{4,5},{5,4},{6,7},{7,6},{8,9},{9,8},{10,11... | collective-permute-start | bytes 442376 | tf_op jit(solution)/shard_map/ppermute | solution.py:272
  44.0 4.4 %shard_map.98 = (f32[65,256,128]{2,1,0:T(8,128)S(1)}, bf16[26,256,128]{2,1,0:T(8,128)(2,1)S(1)}) custom-call(s32[6]{0:T(128)S(1)} %stack.29.where_ref, s32[64]{0:T(128)S(1)} %bitcast.29, bf16[128,3328]{1,0:T(8,128)(2,1)S(1)} %copy-done, bf16[128,3328]{1,0:T(8,128)(2,1)} %collective-permute-done.3.mate_acts_ref.mate_ref, bf16[64,128,128]{2,1,0:T(8,128)(2,1)S(1)} %bitcast.21), custom_call_target="tpu_custom_call" | custom-call | tf_op jit(solution)/shard_map/pallas_call | solution.py:241
  48.5 4.0 %collective-permute-done.5.refs_0_.rest_1_ = bf16[11,128,128]{2,1,0:T(8,128)(2,1)S(1)} collective-permute-done((bf16[11,128,128]{2,1,0:T(8,128)(2,1)}, bf16[11,128,128]{2,1,0:T(8,128)(2,1)S(1)}, u32[]{:S(2)}, u32[]{:S(2)}) %collective-permute-start.5) | collective-permute-done | bytes 360480 | tf_op jit(solution)/shard_map/ppermute | solution.py:276
  52.5 1.6 %collective-permute-start.9 = (bf16[10,128,128]{2,1,0:T(8,128)(2,1)S(1)}, bf16[10,128,128]{2,1,0:T(8,128)(2,1)S(1)}, u32[]{:S(2)}, u32[]{:S(2)}) collective-permute-start(bf16[10,128,128]{2,1,0:T(8,128)(2,1)S(1)} %slice.3), channel_id=1, source_target_pairs={{0,16},{16,0},{1,17},{17,1},{2,18},{18,2},{3,19},{19,3},{4,20},{20... | collective-permute-start | bytes 983048 | tf_op jit(solution)/shard_map/ppermute | solution.py:279
  54.1 1.6 %shard_map.96 = (bf16[64,2688]{1,0:T(8,128)(2,1)S(1)}, bf16[64,1664]{1,0:T(8,128)(2,1)S(1)}) custom-call(s32[6]{0:T(128)S(1)} %stack.29.where_ref, bf16[128,128]{1,0:T(8,128)(2,1)S(1)} %get-tuple-element.40.rounded_ref, bf16[128,3328]{1,0:T(8,128)(2,1)S(1)} %copy-done, bf16[128,3328]{1,0:T(8,128)(2,1)} %collective-permute-done.3.mate_acts_ref.mate_ref, ...), custom_call_target="tpu_custom_call" | custom-call | tf_op jit(solution)/shard_map/pallas_call | solution.py:241
  55.7 1.1 %collective-permute-start.10 = (bf16[6,128,128]{2,1,0:T(8,128)(2,1)S(1)}, bf16[6,128,128]{2,1,0:T(8,128)(2,1)S(1)}, u32[]{:S(2)}, u32[]{:S(2)}) collective-permute-start(bf16[6,128,128]{2,1,0:T(8,128)(2,1)S(1)} %collective-permute-done.7.rest_2_), channel_id=1, source_target_pairs={{0,16},{16,0},{1,17},{17,1},{2,18},{18,2},{3,19},{19,3},{4,20},{20... | collective-permute-start | bytes 589832 | tf_op jit(solution)/shard_map/ppermute | solution.py:279
  56.8 5.0 %collective-permute-done.9.rest_4_ = bf16[10,128,128]{2,1,0:T(8,128)(2,1)S(1)} collective-permute-done((bf16[10,128,128]{2,1,0:T(8,128)(2,1)S(1)}, bf16[10,128,128]{2,1,0:T(8,128)(2,1)S(1)}, u32[]{:S(2)}, u32[]{:S(2)}) %collective-permute-start.9) | collective-permute-done | bytes 327712 | tf_op jit(solution)/shard_map/ppermute | solution.py:279
  61.8 3.6 %shard_map.99.old_ref = f32[65,256,128]{2,1,0:T(8,128)S(1)} custom-call(s32[6]{0:T(128)S(1)} %stack.29.where_ref, s32[1,128]{1,0:T(1,128)S(1)} %shard_map.97.ids_ref, bf16[26,256,128]{2,1,0:T(8,128)(2,1)S(1)} %get-tuple-element.48.tiles_ref, f32[65,256,128]{2,1,0:T(8,128)S(1)} %get-tuple-element.49.old_ref, ...), custom_call_target="tpu_custom_call", output_to_operand_aliasing={{}: (3, {})} | custom-call | tf_op jit(solution)/shard_map/pallas_call | solution.py:241
  65.4 1.0 %shard_map.100 = (f32[65,256,128]{2,1,0:T(8,128)S(1)}, bf16[1,4,128,128]{3,2,1,0:T(8,128)(2,1)S(1)}, bf16[1,4,128,128]{3,2,1,0:T(8,128)(2,1)S(1)}, bf16[1,4,128,...) custom-call(s32[6]{0:T(128)S(1)} %stack.29.where_ref, ...), custom_call_target="tpu_custom_call", output_to_operand_aliasing={{0}: (3, {})} | custom-call | tf_op jit(solution)/shard_map/pallas_call | solution.py:241
  68.8 1.5 %collective-permute-start.17 = (bf16[4,128,128]{2,1,0:T(8,128)(2,1)S(1)}, bf16[4,128,128]{2,1,0:T(8,128)(2,1)S(1)}, u32[]{:S(2)}, u32[]{:S(2)}) collective-permute-start(bf16[4,128,128]{2,1,0:T(8,128)(2,1)S(1)} %bitcast.25), channel_id=1, source_target_pairs={{0,8},{4,12},{8,0},{12,4},{1,9},{5,13},{9,1},{13,5},{2,10},{6,14},... | collective-permute-start | bytes 393224 | tf_op jit(solution)/shard_map/ppermute | solution.py:269
  71.5 1.8 %collective-permute-done.19.rest_0_ = bf16[64,2688]{1,0:T(8,128)(2,1)S(1)} collective-permute-done((bf16[64,2688]{1,0:T(8,128)(2,1)S(1)}, bf16[64,2688]{1,0:T(8,128)(2,1)S(1)}, u32[]{:S(2)}, u32[]{:S(2)}) %collective-permute-start.19) | collective-permute-done | bytes 344096 | tf_op jit(solution)/shard_map/ppermute | solution.py:276
  73.4 1.7 %collective-permute-done.17.rest_0_ = bf16[4,128,128]{2,1,0:T(8,128)(2,1)S(1)} collective-permute-done((bf16[4,128,128]{2,1,0:T(8,128)(2,1)S(1)}, bf16[4,128,128]{2,1,0:T(8,128)(2,1)S(1)}, u32[]{:S(2)}, u32[]{:S(2)}) %collective-permute-start.17) | collective-permute-done | bytes 131104 | tf_op jit(solution)/shard_map/ppermute | solution.py:269
  76.4 2.1 %collective-permute-start.18 = (bf16[4,128,128]{2,1,0:T(8,128)(2,1)S(1)}, bf16[4,128,128]{2,1,0:T(8,128)(2,1)S(1)}, u32[]{:S(2)}, u32[]{:S(2)}) collective-permute-start(bf16[4,128,128]{2,1,0:T(8,128)(2,1)S(1)} %shard_map.103), channel_id=1, source_target_pairs={{0,1},{1,0},{2,3},{3,2},{4,5},{5,4},{6,7},{7,6},{8,9},{9,8},{10,11... | collective-permute-start | bytes 393224 | tf_op jit(solution)/shard_map/ppermute | solution.py:272
  79.1 1.6 %collective-permute-start.25 = (bf16[16,128,128]{2,1,0:T(8,128)(2,1)S(1)}, bf16[16,128,128]{2,1,0:T(8,128)(2,1)S(1)}, u32[]{:S(2)}, u32[]{:S(2)}) collective-permute-start(bf16[16,128,128]{2,1,0:T(8,128)(2,1)S(1)} %bitcast.22), channel_id=1, source_target_pairs={{0,8},{4,12},{8,0},{12,4},{1,9},{5,13},{9,1},{13,5},{2,10},{6,14},... | collective-permute-start | bytes 1572872 | tf_op jit(solution)/shard_map/ppermute | solution.py:269
  80.7 5.3 %collective-permute-done.20.rest_2_ = bf16[64,2688]{1,0:T(8,128)(2,1)S(1)} collective-permute-done((bf16[64,2688]{1,0:T(8,128)(2,1)S(1)}, bf16[64,2688]{1,0:T(8,128)(2,1)S(1)}, u32[]{:S(2)}, u32[]{:S(2)}) %collective-permute-start.20) | collective-permute-done | bytes 344096 | tf_op jit(solution)/shard_map/ppermute | solution.py:272
  86.0 1.4 %collective-permute-done.18.rest_0_ = bf16[4,128,128]{2,1,0:T(8,128)(2,1)S(1)} collective-permute-done((bf16[4,128,128]{2,1,0:T(8,128)(2,1)S(1)}, bf16[4,128,128]{2,1,0:T(8,128)(2,1)S(1)}, u32[]{:S(2)}, u32[]{:S(2)}) %collective-permute-start.18) | collective-permute-done | bytes 131104 | tf_op jit(solution)/shard_map/ppermute | solution.py:272
  88.5 1.7 %shard_map.109 = (f32[64,3328]{1,0:T(8,128)}, f32[64,2048]{1,0:T(8,128)}) custom-call(s32[6]{0:T(128)S(1)} %stack.29.where_ref, bf16[64,2688]{1,0:T(8,128)(2,1)S(1)} %get-tuple-element.43.half_ref, bf16[64,1664]{1,0:T(8,128)(2,1)S(1)} %get-tuple-element.68.other_ref, bf16[64,2688]{1,0:T(8,128)(2,1)S(1)} %collective-permute-done.19.rest_0_, ...), custom_call_target="tpu_custom_call" | custom-call | tf_op jit(solution)/shard_map/pallas_call | solution.py:241
  90.2 7.0 %collective-permute-done.22.rest_1_ = bf16[12,128,128]{2,1,0:T(8,128)(2,1)S(1)} collective-permute-done((bf16[12,128,128]{2,1,0:T(8,128)(2,1)S(1)}, bf16[12,128,128]{2,1,0:T(8,128)(2,1)S(1)}, u32[]{:S(2)}, u32[]{:S(2)}) %collective-permute-start.22) | collective-permute-done | bytes 393248 | tf_op jit(solution)/shard_map/ppermute | solution.py:272
  (69 shorter events, 14.0 us)
Async XLA Ops:
  0.6 10.5 %copy-start = (bf16[128,3328]{1,0:T(8,128)(2,1)S(1)}, bf16[128,3328]{1,0:T(8,128)(2,1)}, u32[]{:S(2)}) copy-start(bf16[128,3328]{1,0:T(8,128)(2,1)} %own_ref.1) | copy-start | bytes 2555908
  0.6 10.5 %copy-start.9 = (s32[128]{0:T(128)S(1)}, s32[128]{0:T(128)}, u32[]{:S(2)}) copy-start(s32[128]{0:T(128)} %param.9) | copy-start | bytes 1540
  0.6 38.6 %collective-permute-start.3 = (bf16[128,3328]{1,0:T(8,128)(2,1)}, bf16[128,3328]{1,0:T(8,128)(2,1)}, u32[]{:S(2)}, u32[]{:S(2)}) collective-permute-start(bf16[128,3328]{1,0:T(8,128)(2,1)} %own_ref.1), channel_id=1, source_target_pairs={{0,1},{1,0},{2,3},{3,2},{4,5},{5,4},{6,7},{7,6},{8,9},{9,8},{10,11... | collective-permute-start | bytes 2555912 | tf_op jit(solution)/shard_map/ppermute | solution.py:272
  5.6 29.1 %collective-permute-start.6 = (bf16[16,128,128]{2,1,0:T(8,128)(2,1)}, bf16[16,128,128]{2,1,0:T(8,128)(2,1)}, u32[]{:S(2)}, u32[]{:S(2)}) collective-permute-start(bf16[16,128,128]{2,1,0:T(8,128)(2,1)} %dynamic-slice_bitcast_fusion), channel_id=1, source_target_pairs={{0,2},{1,3},{2,0},{3,1},{4,6},{5,7},{6,4},{7,5},{8,10},{9,11},{10,... | collective-permute-start | bytes 1572872 | tf_op jit(solution)/shard_map/ppermute | solution.py:276
  8.2 2.6 %collective-permute-start = (s32[64]{0:T(128)}, s32[64]{0:T(128)S(1)}, u32[]{:S(2)}, u32[]{:S(2)}) collective-permute-start(s32[64]{0:T(128)} %bitcast.28), channel_id=1, source_target_pairs={{0,4},{4,0},{8,12},{12,8},{1,5},{5,1},{9,13},{13,9},{2,6},{6,2},{1... | collective-permute-start | bytes 776 | tf_op jit(solution)/shard_map/ppermute | solution.py:265
  8.9 35.2 %copy-start.10 = (s32[1,64]{1,0:T(1,128)S(1)}, s32[1,64]{1,0:T(1,128)}, u32[]{:S(2)}) copy-start(s32[1,64]{1,0:T(1,128)} %param.11) | copy-start | bytes 772
  8.9 32.1 %copy-start.1 = (bf16[1,64,128,128]{3,2,1,0:T(8,128)(2,1)S(1)}, bf16[1,64,128,128]{3,2,1,0:T(8,128)(2,1)}, u32[]{:S(2)}) copy-start(bf16[1,64,128,128]{3,2,1,0:T(8,128)(2,1)} %param.10) | copy-start | bytes 6291460
  10.8 41.7 %collective-permute-start.5 = (bf16[11,128,128]{2,1,0:T(8,128)(2,1)}, bf16[11,128,128]{2,1,0:T(8,128)(2,1)S(1)}, u32[]{:S(2)}, u32[]{:S(2)}) collective-permute-start(bf16[11,128,128]{2,1,0:T(8,128)(2,1)} %pad_maximum_fusion), channel_id=1, source_target_pairs={{0,2},{1,3},{2,0},{3,1},{4,6},{5,7},{6,4},{7,5},{8,10},{9,11},{10,... | collective-permute-start | bytes 1081352 | tf_op jit(solution)/shard_map/ppermute | solution.py:276
  14.8 1.3 %collective-permute-start.1 = (f32[128,128]{1,0:T(8,128)S(1)}, f32[128,128]{1,0:T(8,128)S(1)}, u32[]{:S(2)}, u32[]{:S(2)}) collective-permute-start(f32[128,128]{1,0:T(8,128)S(1)} %shard_map.94), channel_id=1, source_target_pairs={{0,4},{4,0},{8,12},{12,8},{1,5},{5,1},{9,13},{13,9},{2,6},{6,2},{1... | collective-permute-start | bytes 196616 | tf_op jit(solution)/shard_map/ppermute | solution.py:265
  16.1 4.3 %collective-permute-start.2 = (f32[128,128]{1,0:T(8,128)S(1)}, f32[128,128]{1,0:T(8,128)S(1)}, u32[]{:S(2)}, u32[]{:S(2)}) collective-permute-start(f32[128,128]{1,0:T(8,128)S(1)} %add.25.both_ref), channel_id=1, source_target_pairs={{0,8},{4,12},{8,0},{12,4},{1,9},{5,13},{9,1},{13,5},{2,10},{6,14},... | collective-permute-start | bytes 196616 | tf_op jit(solution)/shard_map/ppermute | solution.py:269
  39.3 22.5 %collective-permute-start.8 = (bf16[16,128,128]{2,1,0:T(8,128)(2,1)}, bf16[16,128,128]{2,1,0:T(8,128)(2,1)}, u32[]{:S(2)}, u32[]{:S(2)}) collective-permute-start(bf16[16,128,128]{2,1,0:T(8,128)(2,1)} %collective-permute-done.6.rest_0_), channel_id=1, source_target_pairs={{0,16},{16,0},{1,17},{17,1},{2,18},{18,2},{3,19},{19,3},{4,20},{20... | collective-permute-start | bytes 1572872 | tf_op jit(solution)/shard_map/ppermute | solution.py:279
  41.0 14.7 %collective-permute-start.7 = (bf16[6,128,128]{2,1,0:T(8,128)(2,1)S(1)}, bf16[6,128,128]{2,1,0:T(8,128)(2,1)S(1)}, u32[]{:S(2)}, u32[]{:S(2)}) collective-permute-start(bf16[6,128,128]{2,1,0:T(8,128)(2,1)S(1)} %dynamic-slice_bitcast_fusion.2), channel_id=1, source_target_pairs={{0,2},{1,3},{2,0},{3,1},{4,6},{5,7},{6,4},{7,5},{8,10},{9,11},{10,... | collective-permute-start | bytes 589832 | tf_op jit(solution)/shard_map/ppermute | solution.py:276
  41.6 12.5 %collective-permute-start.4 = (bf16[64,1152]{1,0:T(8,128)(2,1)}, bf16[64,1152]{1,0:T(8,128)(2,1)S(1)}, u32[]{:S(2)}, u32[]{:S(2)}) collective-permute-start(bf16[64,1152]{1,0:T(8,128)(2,1)} %copy-done.11), channel_id=1, source_target_pairs={{0,1},{1,0},{2,3},{3,2},{4,5},{5,4},{6,7},{7,6},{8,9},{9,8},{10,11... | collective-permute-start | bytes 442376 | tf_op jit(solution)/shard_map/ppermute | solution.py:272
  44.0 10.1 %copy-start.8 = (f32[64,1024]{1,0:T(8,128)S(1)}, f32[64,1024]{1,0:T(8,128)}, u32[]{:S(2)}) copy-start(f32[64,1024]{1,0:T(8,128)} %copy-done.7) | copy-start | bytes 786436
  52.5 9.2 %collective-permute-start.9 = (bf16[10,128,128]{2,1,0:T(8,128)(2,1)S(1)}, bf16[10,128,128]{2,1,0:T(8,128)(2,1)S(1)}, u32[]{:S(2)}, u32[]{:S(2)}) collective-permute-start(bf16[10,128,128]{2,1,0:T(8,128)(2,1)S(1)} %slice.3), channel_id=1, source_target_pairs={{0,16},{16,0},{1,17},{17,1},{2,18},{18,2},{3,19},{19,3},{4,20},{20... | collective-permute-start | bytes 983048 | tf_op jit(solution)/shard_map/ppermute | solution.py:279
  55.7 9.7 %collective-permute-start.10 = (bf16[6,128,128]{2,1,0:T(8,128)(2,1)S(1)}, bf16[6,128,128]{2,1,0:T(8,128)(2,1)S(1)}, u32[]{:S(2)}, u32[]{:S(2)}) collective-permute-start(bf16[6,128,128]{2,1,0:T(8,128)(2,1)S(1)} %collective-permute-done.7.rest_2_), channel_id=1, source_target_pairs={{0,16},{16,0},{1,17},{17,1},{2,18},{18,2},{3,19},{19,3},{4,20},{20... | collective-permute-start | bytes 589832 | tf_op jit(solution)/shard_map/ppermute | solution.py:279
  56.8 16.5 %collective-permute-start.19 = (bf16[64,2688]{1,0:T(8,128)(2,1)S(1)}, bf16[64,2688]{1,0:T(8,128)(2,1)S(1)}, u32[]{:S(2)}, u32[]{:S(2)}) collective-permute-start(bf16[64,2688]{1,0:T(8,128)(2,1)S(1)} %get-tuple-element.43.half_ref), channel_id=1, source_target_pairs={{0,2},{1,3},{2,0},{3,1},{4,6},{5,7},{6,4},{7,5},{8,10},{9,11},{10,... | collective-permute-start | bytes 1032200 | tf_op jit(solution)/shard_map/ppermute | solution.py:276
  66.4 1.4 %collective-permute-start.11 = (bf16[1,4,128,128]{3,2,1,0:T(8,128)(2,1)S(1)}, bf16[1,4,128,128]{3,2,1,0:T(8,128)(2,1)S(1)}, u32[]{:S(2)}, u32[]{:S(2)}) collective-permute-start(bf16[1,4,128,128]{3,2,1,0:T(8,128)(2,1)S(1)} %get-tuple-element.55), channel_id=1, source_target_pairs={{0,4},{4,0},{8,12},{12,8},{1,5},{5,1},{9,13},{13,9},{2,6},{6,2},{1... | collective-permute-start | bytes 393224 | tf_op jit(solution)/shard_map/ppermute | solution.py:265
  66.5 9.3 %collective-permute-start.16 = (bf16[16,128,128]{2,1,0:T(8,128)(2,1)S(1)}, bf16[16,128,128]{2,1,0:T(8,128)(2,1)S(1)}, u32[]{:S(2)}, u32[]{:S(2)}) collective-permute-start(bf16[16,128,128]{2,1,0:T(8,128)(2,1)S(1)} %get-tuple-element.61), channel_id=1, source_target_pairs={{0,4},{4,0},{8,12},{12,8},{1,5},{5,1},{9,13},{13,9},{2,6},{6,2},{1... | collective-permute-start | bytes 1572872 | tf_op jit(solution)/shard_map/ppermute | solution.py:265
  67.0 1.8 %collective-permute-start.12 = (bf16[1,4,128,128]{3,2,1,0:T(8,128)(2,1)S(1)}, bf16[1,4,128,128]{3,2,1,0:T(8,128)(2,1)S(1)}, u32[]{:S(2)}, u32[]{:S(2)}) collective-permute-start(bf16[1,4,128,128]{3,2,1,0:T(8,128)(2,1)S(1)} %get-tuple-element.57), channel_id=1, source_target_pairs={{0,4},{4,0},{8,12},{12,8},{1,5},{5,1},{9,13},{13,9},{2,6},{6,2},{1... | collective-permute-start | bytes 393224 | tf_op jit(solution)/shard_map/ppermute | solution.py:265
  67.1 3.2 %collective-permute-start.13 = (bf16[1,4,128,128]{3,2,1,0:T(8,128)(2,1)S(1)}, bf16[1,4,128,128]{3,2,1,0:T(8,128)(2,1)S(1)}, u32[]{:S(2)}, u32[]{:S(2)}) collective-permute-start(bf16[1,4,128,128]{3,2,1,0:T(8,128)(2,1)S(1)} %get-tuple-element.58), channel_id=1, source_target_pairs={{0,4},{4,0},{8,12},{12,8},{1,5},{5,1},{9,13},{13,9},{2,6},{6,2},{1... | collective-permute-start | bytes 393224 | tf_op jit(solution)/shard_map/ppermute | solution.py:265
  67.8 2.4 %collective-permute-start.14 = (bf16[1,4,128,128]{3,2,1,0:T(8,128)(2,1)S(1)}, bf16[1,4,128,128]{3,2,1,0:T(8,128)(2,1)S(1)}, u32[]{:S(2)}, u32[]{:S(2)}) collective-permute-start(bf16[1,4,128,128]{3,2,1,0:T(8,128)(2,1)S(1)} %get-tuple-element.59), channel_id=1, source_target_pairs={{0,4},{4,0},{8,12},{12,8},{1,5},{5,1},{9,13},{13,9},{2,6},{6,2},{1... | collective-permute-start | bytes 393224 | tf_op jit(solution)/shard_map/ppermute | solution.py:265
  68.8 6.3 %collective-permute-start.17 = (bf16[4,128,128]{2,1,0:T(8,128)(2,1)S(1)}, bf16[4,128,128]{2,1,0:T(8,128)(2,1)S(1)}, u32[]{:S(2)}, u32[]{:S(2)}) collective-permute-start(bf16[4,128,128]{2,1,0:T(8,128)(2,1)S(1)} %bitcast.25), channel_id=1, source_target_pairs={{0,8},{4,12},{8,0},{12,4},{1,9},{5,13},{9,1},{13,5},{2,10},{6,14},... | collective-permute-start | bytes 393224 | tf_op jit(solution)/shard_map/ppermute | solution.py:269
  70.9 16.5 %collective-permute-start.21 = (bf16[12,128,128]{2,1,0:T(8,128)(2,1)S(1)}, bf16[12,128,128]{2,1,0:T(8,128)(2,1)S(1)}, u32[]{:S(2)}, u32[]{:S(2)}) collective-permute-start(bf16[12,128,128]{2,1,0:T(8,128)(2,1)S(1)} %bitcast.24), channel_id=1, source_target_pairs={{0,8},{4,12},{8,0},{12,4},{1,9},{5,13},{9,1},{13,5},{2,10},{6,14},... | collective-permute-start | bytes 1179656 | tf_op jit(solution)/shard_map/ppermute | solution.py:269
  71.5 6.9 %collective-permute-start.23 = (bf16[1,8,128,128]{3,2,1,0:T(8,128)(2,1)S(1)}, bf16[1,8,128,128]{3,2,1,0:T(8,128)(2,1)S(1)}, u32[]{:S(2)}, u32[]{:S(2)}) collective-permute-start(bf16[1,8,128,128]{3,2,1,0:T(8,128)(2,1)S(1)} %get-tuple-element.65), channel_id=1, source_target_pairs={{0,4},{4,0},{8,12},{12,8},{1,5},{5,1},{9,13},{13,9},{2,6},{6,2},{1... | collective-permute-start | bytes 786440 | tf_op jit(solution)/shard_map/ppermute | solution.py:265
  73.3 5.1 %collective-permute-start.24 = (bf16[1,8,128,128]{3,2,1,0:T(8,128)(2,1)S(1)}, bf16[1,8,128,128]{3,2,1,0:T(8,128)(2,1)S(1)}, u32[]{:S(2)}, u32[]{:S(2)}) collective-permute-start(bf16[1,8,128,128]{3,2,1,0:T(8,128)(2,1)S(1)} %get-tuple-element.67), channel_id=1, source_target_pairs={{0,4},{4,0},{8,12},{12,8},{1,5},{5,1},{9,13},{13,9},{2,6},{6,2},{1... | collective-permute-start | bytes 786440 | tf_op jit(solution)/shard_map/ppermute | solution.py:265
  75.7 10.4 %collective-permute-start.20 = (bf16[64,2688]{1,0:T(8,128)(2,1)S(1)}, bf16[64,2688]{1,0:T(8,128)(2,1)S(1)}, u32[]{:S(2)}, u32[]{:S(2)}) collective-permute-start(bf16[64,2688]{1,0:T(8,128)(2,1)S(1)} %shard_map.104.rest_1_), channel_id=1, source_target_pairs={{0,1},{1,0},{2,3},{3,2},{4,5},{5,4},{6,7},{7,6},{8,9},{9,8},{10,11... | collective-permute-start | bytes 1032200 | tf_op jit(solution)/shard_map/ppermute | solution.py:272
  76.4 11.1 %collective-permute-start.18 = (bf16[4,128,128]{2,1,0:T(8,128)(2,1)S(1)}, bf16[4,128,128]{2,1,0:T(8,128)(2,1)S(1)}, u32[]{:S(2)}, u32[]{:S(2)}) collective-permute-start(bf16[4,128,128]{2,1,0:T(8,128)(2,1)S(1)} %shard_map.103), channel_id=1, source_target_pairs={{0,1},{1,0},{2,3},{3,2},{4,5},{5,4},{6,7},{7,6},{8,9},{9,8},{10,11... | collective-permute-start | bytes 393224 | tf_op jit(solution)/shard_map/ppermute | solution.py:272
  78.4 11.8 %collective-permute-start.15 = (bf16[16,128,128]{2,1,0:T(8,128)(2,1)S(1)}, bf16[16,128,128]{2,1,0:T(8,128)(2,1)S(1)}, u32[]{:S(2)}, u32[]{:S(2)}) collective-permute-start(bf16[16,128,128]{2,1,0:T(8,128)(2,1)S(1)} %get-tuple-element.60), channel_id=1, source_target_pairs={{0,4},{4,0},{8,12},{12,8},{1,5},{5,1},{9,13},{13,9},{2,6},{6,2},{1... | collective-permute-start | bytes 1572872 | tf_op jit(solution)/shard_map/ppermute | solution.py:265
  79.1 18.1 %copy-start.5 = (bf16[64,2048]{1,0:T(8,128)(2,1)S(1)}, bf16[64,2048]{1,0:T(8,128)(2,1)}, u32[]{:S(2)}) copy-start(bf16[64,2048]{1,0:T(8,128)(2,1)} %adapter_ref.2) | copy-start | bytes 786436
  79.1 19.0 %collective-permute-start.25 = (bf16[16,128,128]{2,1,0:T(8,128)(2,1)S(1)}, bf16[16,128,128]{2,1,0:T(8,128)(2,1)S(1)}, u32[]{:S(2)}, u32[]{:S(2)}) collective-permute-start(bf16[16,128,128]{2,1,0:T(8,128)(2,1)S(1)} %bitcast.22), channel_id=1, source_target_pairs={{0,8},{4,12},{8,0},{12,4},{1,9},{5,13},{9,1},{13,5},{2,10},{6,14},... | collective-permute-start | bytes 1572872 | tf_op jit(solution)/shard_map/ppermute | solution.py:269
  88.1 9.1 %collective-permute-start.22 = (bf16[12,128,128]{2,1,0:T(8,128)(2,1)S(1)}, bf16[12,128,128]{2,1,0:T(8,128)(2,1)S(1)}, u32[]{:S(2)}, u32[]{:S(2)}) collective-permute-start(bf16[12,128,128]{2,1,0:T(8,128)(2,1)S(1)} %shard_map.105), channel_id=1, source_target_pairs={{0,1},{1,0},{2,3},{3,2},{4,5},{5,4},{6,7},{7,6},{8,9},{9,8},{10,11... | collective-permute-start | bytes 1179656 | tf_op jit(solution)/shard_map/ppermute | solution.py:272
  (6 other events, 5.4 us)

commit v14 on v13

--- a/solution.py
+++ b/solution.py
@@ -65,7 +65,7 @@
 def last_kernel(where_ref, ids_ref, tiles_ref, old_ref, *rest, block_count, **plan):
     blocks, total_ref, sends = rest[:block_count], rest[block_count], rest[block_count + 1:]
     add_arrivals(where_ref, ids_ref, tiles_ref, blocks, total_ref, **plan)
-    far_mate, near_mate, far_own, near_own = sends[:4], sends[4:5], sends[5:7], sends[7:]
+    far_mate, near_mate, far_own, near_own = sends[:4], sends[4:6], sends[6:8], sends[8:]
     tokens, share = near_own[0].shape[1], near_own[0].shape[0]
     chips = far_own[0].shape[0] + 1
 
@@ -106,7 +106,7 @@
     size, tokens, _ = out_ref.shape
     first = (2 * where_ref[2] + where_ref[1]) * where_ref[5] + block
     for k in range(size):
-        value = total_ref[first + k, tokens:, :] + core_ref[block + k].astype(F32)
+        value = total_ref[first + k, tokens:, :] + core_ref[k].astype(F32)
         for piece in pieces:
             value += piece[k].astype(F32)
         out_ref[k] = value.astype(BF16)
@@ -310,9 +310,9 @@
             jnp.where(ids >= 0, lax.rem(known, col_blocks), 0),
         ]).astype(BF16)
         code = jnp.pad(code, ((0, tile - 2), (0, tile - slots)))[None]
-        soon = core_swap(after(ids, leaving_chunks[0]))
+        soon = core_swap(ids)
         leaving_chunks[1] = jnp.concatenate([leaving_chunks[1], code], axis=0)
-        leaving_chunks[1:] = [after(chunk, soon) for chunk in leaving_chunks[1:]]
+        leaving_chunks = [after(chunk, soon) for chunk in leaving_chunks]
         direct = [
             (group_shift(leaving_chunks[k], d), (d - 1, 0, starts[k], sizes[k]))
             for d in range(1, group) for k in range(len(starts))
@@ -363,7 +363,7 @@
             (jax.ShapeDtypeStruct((group - 1, tile), jnp.int32),), (),
             tuple(value for value, place in direct if place[2] == starts[1]),
         )
-        gates = {starts[0]: (rounded, mate_activations), starts[1]: (total,), starts[2]: (half_grads,)}
+        gates = {starts[0]: (rounded,), starts[1]: (total,), starts[2]: (half_grads,)}
         swapped = [
             (part_shift(after(value, *gates[start])[:size], e), (source, e, start, size))
             for value, (source, _, start, size) in direct for e in range(1, n_parts)
@@ -375,7 +375,9 @@
             functools.partial(more_kernel, **plan(more)), (total_shape,), (where, all_ids),
             (on_chip(tiles), on_chip(total)) + values(more), {3: 0},
         )
-        small = share // 4
+        small = max(1, 2 * share // 16)
+        rest = share - small
+        thirds = (rest - 2 * (rest // 3), rest // 3, rest // 3)
         half = share // 2
 
         def far_piece(size):
@@ -386,12 +388,13 @@
 
         total, *sends = call(
             functools.partial(last_kernel, block_count=len(last), **plan(last)),
-            (total_shape,) + (far_piece(small),) * 4 + (near_piece(share),)
+            (total_shape, far_piece(small)) + tuple(far_piece(size) for size in thirds)
+            + (near_piece(small), near_piece(rest))
             + (far_piece(half),) * 2 + (near_piece(share),),
             (after(where, half_grads), all_ids), (on_chip(tiles), on_chip(total)) + values(last), {3: 0},
         )
 
-        cores = [core_swap(value) for value in sends[:5]]
+        cores = [core_swap(value) for value in sends[:6]]
 
         def for_chips(pieces, token, block, *needed):
             size = sum(piece.shape[1] for piece in pieces)
@@ -403,26 +406,25 @@
 
         leaving_first, pieces_first = for_chips(cores[:1], tokens, 0)
         leaving_second, pieces_second = for_chips(cores[1:4], tokens, small, leaving_first)
-        cores += [core_swap(after(value, leaving_second)) for value in sends[5:]]
-        leaving_own, own_pieces = for_chips(cores[5:7], 0, 0)
-        far_grads = [after(value, *pieces_first) for value in far_grads]
+        cores += [core_swap(after(value, leaving_second)) for value in sends[6:]]
+        leaving_own, own_pieces = for_chips(cores[6:8], 0, 0)
+        def for_mate(core_got, pieces, block, *needed):
+            (value,) = call(
+                functools.partial(mate_kernel, block=block), (near_piece(core_got.shape[0]),),
+                (after(where, *needed) if needed else where,), (on_chip(total), core_got) + tuple(pieces),
+            )
+            return mate_swap(value)
+
+        from_mate_first = for_mate(cores[4], pieces_first, 0)
+        far_grads = [after(value, from_mate_first) for value in far_grads]
         passing = call(
             functools.partial(forward_kernel, in_half=in_half),
             tuple(jax.ShapeDtypeStruct((rank, in_half if d else both_halves), BF16) for d in range(group - 1)),
             (where,), (half_grads,) + tuple(far_grads),
         )
         mate_grads = [mate_swap(value) for value in passing]
-
-        def for_mate(pieces, size, block, *needed):
-            (value,) = call(
-                functools.partial(mate_kernel, block=block), (near_piece(size),),
-                (after(where, *needed) if needed else where,), (on_chip(total), cores[4]) + tuple(pieces),
-            )
-            return mate_swap(value)
-
-        from_mate_first = for_mate(pieces_first, small, 0)
         from_mate = [
-            from_mate_first, for_mate(pieces_second, share - small, small, from_mate_first, *mate_grads),
+            from_mate_first, for_mate(cores[5], pieces_second, small, *mate_grads),
         ]
         in_grad, out_grad = call(
             grad_sum_kernel,
@@ -431,7 +433,7 @@
         )
         (near,) = call(
             near_kernel, (pltpu.VMEM((share, tokens, tile), F32),), (where,),
-            (rounded, output_adapter, on_chip(total), cores[7]) + tuple(from_mate),
+            (rounded, output_adapter, on_chip(total), cores[8]) + tuple(from_mate),
         )
         (projected,) = call(
             final_kernel, (jax.ShapeDtypeStruct((tokens, feats), BF16),), (), (on_chip(near),) + tuple(own_pieces),

time: 99.6 us -> 102 us (1.024)
  waiting for transfers between devices: 46.2 us -> 48.8 us
    ppermute x5, starting transfers between devices: 8.06 us -> 3.34 us  [mate_swap(): return lax.ppermute(value, 'dp', [(i, i ^ 1) for i in range(n_dp)])]
    ppermute x4, starting transfers between devices: 3.52 us -> 6.43 us  [group_shift(): return lax.ppermute(value, 'dp', pairs)]
    ppermute x4, waiting for transfers between devices: 16.9 us -> 19.3 us  [group_shift(): return lax.ppermute(value, 'dp', pairs)]
    ppermute x5, waiting for transfers between devices: 18.3 us -> 16.4 us  [mate_swap(): return lax.ppermute(value, 'dp', [(i, i ^ 1) for i in range(n_dp)])]
    ppermute x10 -> x11, waiting for transfers between devices: 1.58 us -> 3.45 us  [core_swap(): return lax.ppermute(value, 'row', [(i, i ^ 1) for i in range(n_row)])]
    ppermute x10 -> x11, starting transfers between devices: 1.54 us -> 2.7 us  [core_swap(): return lax.ppermute(value, 'row', [(i, i ^ 1) for i in range(n_row)])]
  transfers between devices with their start and end apart: 26 -> 27, of which waited for: 13 -> 13; matrix products, arithmetic and copies ran while one was open for 5% -> 5% of each run, Pallas kernels for 19% -> 18%
where the time goes in v14:
time: 102 us; the launch traced here: 101 us
  waiting for transfers between devices  48.8 us (48%)
  starting transfers between devices  22.4 us (22%)
  Pallas kernels  19.4 us (19%)
  local copies, waits for them, and re-layouts  8.56 us (8%)
  other arithmetic  1.45 us (1%)
    pallas_call x16, Pallas kernels, call(): pl.pallas_call(kernel, out_shape=outs, in_specs=[smem] * len(scalars) + [...  19.4 us
    ppermute x4, waiting for transfers between devices, group_shift(): return lax.ppermute(value, 'dp', pairs)  19.3 us
    ppermute x5, waiting for transfers between devices, mate_swap(): return lax.ppermute(value, 'dp', [(i, i ^ 1) for i in range(n_dp)])  16.4 us
    ppermute x4, starting transfers between devices, group_shift(): return lax.ppermute(value, 'dp', pairs)  6.43 us
    unnamed x24, local copies, waits for them, and re-layouts  5.41 us
    ppermute x3, waiting for transfers between devices, part_shift(): lax.ppermute(value, 'parts', [(i, (i + d) % n_parts) for i in range(n_par...  5.41 us
    ppermute x4, starting transfers between devices, chip_shift(): return lax.ppermute(value, 'row', pairs)  5.27 us
    ppermute x3, starting transfers between devices, part_shift(): lax.ppermute(value, 'parts', [(i, (i + d) % n_parts) for i in range(n_par...  4.62 us
  transfers between devices with their start and end apart: 27, of which 13 were waited for; matrix products, arithmetic and copies ran while one was open for 5% of the time, Pallas kernels for 18%

profile of v14, /device:TPU:0, one launch (start us, length us, event | category | flops | bytes accessed | tf_op | source)
XLA Modules:
  0.0 101.5 jit_solution(1687633720344482782)
XLA Ops:
  1.2 2.7 %collective-permute-start.3 = (bf16[128,3328]{1,0:T(8,128)(2,1)}, bf16[128,3328]{1,0:T(8,128)(2,1)}, u32[]{:S(2)}, u32[]{:S(2)}) collective-permute-start(bf16[128,3328]{1,0:T(8,128)(2,1)} %own_ref.1), channel_id=1, source_target_pairs={{0,1},{1,0},{2,3},{3,2},{4,5},{5,4},{6,7},{7,6},{8,9},{9,8},{10,11... | collective-permute-start | bytes 2555912 | tf_op jit(solution)/shard_map/ppermute | solution.py:272
  3.8 1.9 %dynamic-slice_bitcast_fusion = bf16[16,128,128]{2,1,0:T(8,128)(2,1)} fusion(bf16[1,64,128,128]{3,2,1,0:T(8,128)(2,1)} %param.10, s32[]{:T(128)S(6)} %select_n.22), kind=kLoop, calls=%fused_computation | loop fusion | bytes 1048580 | tf_op jit(solution)/shard_map/dynamic_slice | solution.py:304
  5.7 2.6 %collective-permute-start.6 = (bf16[16,128,128]{2,1,0:T(8,128)(2,1)}, bf16[16,128,128]{2,1,0:T(8,128)(2,1)}, u32[]{:S(2)}, u32[]{:S(2)}) collective-permute-start(bf16[16,128,128]{2,1,0:T(8,128)(2,1)} %dynamic-slice_bitcast_fusion), channel_id=1, source_target_pairs={{0,2},{1,3},{2,0},{3,1},{4,6},{5,7},{6,4},{7,5},{8,10},{9,11},{10,... | collective-permute-start | bytes 1572872 | tf_op jit(solution)/shard_map/ppermute | solution.py:276
  9.0 1.1 %dynamic-slice_bitcast_fusion.1 = bf16[10,128,128]{2,1,0:T(8,128)(2,1)S(1)} fusion(bf16[1,64,128,128]{3,2,1,0:T(8,128)(2,1)} %param.10, s32[]{:T(128)S(6)} %select_n.18), kind=kLoop, calls=%fused_computation.2 | loop fusion | bytes 655364 | tf_op jit(solution)/shard_map/dynamic_slice | solution.py:304
  11.3 1.0 %copy-done.2 = bf16[128,2048]{1,0:T(8,128)(2,1)S(1)} copy-done((bf16[128,2048]{1,0:T(8,128)(2,1)S(1)}, bf16[128,2048]{1,0:T(8,128)(2,1)}, u32[]{:S(2)}) %copy-start.2) | copy-done | bytes 524312
  12.3 0.9 copy-done.4
  13.2 1.0 copy-done.6
  14.9 1.2 %collective-permute-done.1 = f32[128,128]{1,0:T(8,128)S(1)} collective-permute-done((f32[128,128]{1,0:T(8,128)S(1)}, f32[128,128]{1,0:T(8,128)S(1)}, u32[]{:S(2)}, u32[]{:S(2)}) %collective-permute-start.1) | collective-permute-done | bytes 65568 | tf_op jit(solution)/shard_map/ppermute | solution.py:265
  16.2 1.6 %collective-permute-start.2 = (f32[128,128]{1,0:T(8,128)S(1)}, f32[128,128]{1,0:T(8,128)S(1)}, u32[]{:S(2)}, u32[]{:S(2)}) collective-permute-start(f32[128,128]{1,0:T(8,128)S(1)} %add.24.both_ref), channel_id=1, source_target_pairs={{0,8},{4,12},{8,0},{12,4},{1,9},{5,13},{9,1},{13,5},{2,10},{6,14},... | collective-permute-start | bytes 196616 | tf_op jit(solution)/shard_map/ppermute | solution.py:269
  17.8 2.7 %collective-permute-done.2.rest_0_ = f32[128,128]{1,0:T(8,128)S(1)} collective-permute-done((f32[128,128]{1,0:T(8,128)S(1)}, f32[128,128]{1,0:T(8,128)S(1)}, u32[]{:S(2)}, u32[]{:S(2)}) %collective-permute-start.2) | collective-permute-done | bytes 65568 | tf_op jit(solution)/shard_map/ppermute | solution.py:269
  20.5 1.0 %copy-done.3 = bf16[128,2048]{1,0:T(8,128)(2,1)S(1)} copy-done((bf16[128,2048]{1,0:T(8,128)(2,1)S(1)}, bf16[128,2048]{1,0:T(8,128)(2,1)}, u32[]{:S(2)}) %copy-start.3) | copy-done | bytes 524312
  23.7 11.0 %collective-permute-done.6.rest_0_ = bf16[16,128,128]{2,1,0:T(8,128)(2,1)} collective-permute-done((bf16[16,128,128]{2,1,0:T(8,128)(2,1)}, bf16[16,128,128]{2,1,0:T(8,128)(2,1)}, u32[]{:S(2)}, u32[]{:S(2)}) %collective-permute-start.6) | collective-permute-done | bytes 524320 | tf_op jit(solution)/shard_map/ppermute | solution.py:276
  34.7 1.5 %collective-permute-start.8 = (bf16[16,128,128]{2,1,0:T(8,128)(2,1)}, bf16[16,128,128]{2,1,0:T(8,128)(2,1)}, u32[]{:S(2)}, u32[]{:S(2)}) collective-permute-start(bf16[16,128,128]{2,1,0:T(8,128)(2,1)} %collective-permute-done.6.rest_0_), channel_id=1, source_target_pairs={{0,16},{16,0},{1,17},{17,1},{2,18},{18,2},{3,19},{19,3},{4,20},{20... | collective-permute-start | bytes 1572872 | tf_op jit(solution)/shard_map/ppermute | solution.py:279
  36.2 3.5 %collective-permute-start.7 = (bf16[6,128,128]{2,1,0:T(8,128)(2,1)S(1)}, bf16[6,128,128]{2,1,0:T(8,128)(2,1)S(1)}, u32[]{:S(2)}, u32[]{:S(2)}) collective-permute-start(bf16[6,128,128]{2,1,0:T(8,128)(2,1)S(1)} %dynamic-slice_bitcast_fusion.2), channel_id=1, source_target_pairs={{0,2},{1,3},{2,0},{3,1},{4,6},{5,7},{6,4},{7,5},{8,10},{9,11},{10,... | collective-permute-start | bytes 589832 | tf_op jit(solution)/shard_map/ppermute | solution.py:276
  39.9 4.5 %shard_map.98 = (f32[65,256,128]{2,1,0:T(8,128)S(1)}, bf16[26,256,128]{2,1,0:T(8,128)(2,1)S(1)}) custom-call(s32[6]{0:T(128)S(1)} %stack.29.where_ref, s32[64]{0:T(128)S(1)} %bitcast.29, bf16[128,3328]{1,0:T(8,128)(2,1)S(1)} %copy-done, bf16[128,3328]{1,0:T(8,128)(2,1)} %collective-permute-done.3.mate_acts_ref.mate_ref, bf16[64,128,128]{2,1,0:T(8,128)(2,1)S(1)} %bitcast.21), custom_call_target="tpu_custom_call" | custom-call | tf_op jit(solution)/shard_map/pallas_call | solution.py:241
  44.4 8.1 %collective-permute-done.5.refs_0_.rest_1_ = bf16[11,128,128]{2,1,0:T(8,128)(2,1)S(1)} collective-permute-done((bf16[11,128,128]{2,1,0:T(8,128)(2,1)}, bf16[11,128,128]{2,1,0:T(8,128)(2,1)S(1)}, u32[]{:S(2)}, u32[]{:S(2)}) %collective-permute-start.5) | collective-permute-done | bytes 360480 | tf_op jit(solution)/shard_map/ppermute | solution.py:276
  52.6 1.6 %collective-permute-start.9 = (bf16[10,128,128]{2,1,0:T(8,128)(2,1)S(1)}, bf16[10,128,128]{2,1,0:T(8,128)(2,1)S(1)}, u32[]{:S(2)}, u32[]{:S(2)}) collective-permute-start(bf16[10,128,128]{2,1,0:T(8,128)(2,1)S(1)} %slice.3), channel_id=1, source_target_pairs={{0,16},{16,0},{1,17},{17,1},{2,18},{18,2},{3,19},{19,3},{4,20},{20... | collective-permute-start | bytes 983048 | tf_op jit(solution)/shard_map/ppermute | solution.py:279
  54.1 1.6 %shard_map.96 = (bf16[64,2688]{1,0:T(8,128)(2,1)S(1)}, bf16[64,1664]{1,0:T(8,128)(2,1)S(1)}) custom-call(s32[6]{0:T(128)S(1)} %stack.29.where_ref, bf16[128,128]{1,0:T(8,128)(2,1)S(1)} %get-tuple-element.40.rounded_ref, bf16[128,3328]{1,0:T(8,128)(2,1)S(1)} %copy-done, bf16[128,3328]{1,0:T(8,128)(2,1)} %collective-permute-done.3.mate_acts_ref.mate_ref, ...), custom_call_target="tpu_custom_call" | custom-call | tf_op jit(solution)/shard_map/pallas_call | solution.py:241
  56.0 1.5 %collective-permute-start.10 = (bf16[6,128,128]{2,1,0:T(8,128)(2,1)S(1)}, bf16[6,128,128]{2,1,0:T(8,128)(2,1)S(1)}, u32[]{:S(2)}, u32[]{:S(2)}) collective-permute-start(bf16[6,128,128]{2,1,0:T(8,128)(2,1)S(1)} %collective-permute-done.7.rest_2_), channel_id=1, source_target_pairs={{0,16},{16,0},{1,17},{17,1},{2,18},{18,2},{3,19},{19,3},{4,20},{20... | collective-permute-start | bytes 589832 | tf_op jit(solution)/shard_map/ppermute | solution.py:279
  57.5 5.4 %collective-permute-done.9.rest_4_ = bf16[10,128,128]{2,1,0:T(8,128)(2,1)S(1)} collective-permute-done((bf16[10,128,128]{2,1,0:T(8,128)(2,1)S(1)}, bf16[10,128,128]{2,1,0:T(8,128)(2,1)S(1)}, u32[]{:S(2)}, u32[]{:S(2)}) %collective-permute-start.9) | collective-permute-done | bytes 327712 | tf_op jit(solution)/shard_map/ppermute | solution.py:279
  62.9 3.6 %shard_map.99.old_ref = f32[65,256,128]{2,1,0:T(8,128)S(1)} custom-call(s32[6]{0:T(128)S(1)} %stack.29.where_ref, s32[1,128]{1,0:T(1,128)S(1)} %shard_map.97.ids_ref, bf16[26,256,128]{2,1,0:T(8,128)(2,1)S(1)} %get-tuple-element.48.tiles_ref, f32[65,256,128]{2,1,0:T(8,128)S(1)} %get-tuple-element.49.old_ref, ...), custom_call_target="tpu_custom_call", output_to_operand_aliasing={{}: (3, {})} | custom-call | tf_op jit(solution)/shard_map/pallas_call | solution.py:241
  66.6 1.0 shard_map.100
  68.7 0.9 collective-permute-done.11.rest_0_
  70.5 1.6 %collective-permute-start.17 = (bf16[2,128,128]{2,1,0:T(8,128)(2,1)S(1)}, bf16[2,128,128]{2,1,0:T(8,128)(2,1)S(1)}, u32[]{:S(2)}, u32[]{:S(2)}) collective-permute-start(bf16[2,128,128]{2,1,0:T(8,128)(2,1)S(1)} %bitcast.25), channel_id=1, source_target_pairs={{0,8},{4,12},{8,0},{12,4},{1,9},{5,13},{9,1},{13,5},{2,10},{6,14},... | collective-permute-start | bytes 196616 | tf_op jit(solution)/shard_map/ppermute | solution.py:269
  73.3 1.5 %collective-permute-done.17.rest_0_ = bf16[2,128,128]{2,1,0:T(8,128)(2,1)S(1)} collective-permute-done((bf16[2,128,128]{2,1,0:T(8,128)(2,1)S(1)}, bf16[2,128,128]{2,1,0:T(8,128)(2,1)S(1)}, u32[]{:S(2)}, u32[]{:S(2)}) %collective-permute-start.17) | collective-permute-done | bytes 65568 | tf_op jit(solution)/shard_map/ppermute | solution.py:269
  75.5 4.2 %collective-permute-done.18.rest_0_ = bf16[2,128,128]{2,1,0:T(8,128)(2,1)S(1)} collective-permute-done((bf16[2,128,128]{2,1,0:T(8,128)(2,1)S(1)}, bf16[2,128,128]{2,1,0:T(8,128)(2,1)S(1)}, u32[]{:S(2)}, u32[]{:S(2)}) %collective-permute-start.18) | collective-permute-done | bytes 65568 | tf_op jit(solution)/shard_map/ppermute | solution.py:272
  81.0 1.0 %collective-permute-done.24.rest_0_ = bf16[1,8,128,128]{3,2,1,0:T(8,128)(2,1)S(1)} collective-permute-done((bf16[1,8,128,128]{3,2,1,0:T(8,128)(2,1)S(1)}, bf16[1,8,128,128]{3,2,1,0:T(8,128)(2,1)S(1)}, u32[]{:S(2)}, u32[]{:S(2)}) %collective-permute-start.24) | collective-permute-done | bytes 262176 | tf_op jit(solution)/shard_map/ppermute | solution.py:265
  83.1 1.6 %collective-permute-start.26 = (bf16[16,128,128]{2,1,0:T(8,128)(2,1)S(1)}, bf16[16,128,128]{2,1,0:T(8,128)(2,1)S(1)}, u32[]{:S(2)}, u32[]{:S(2)}) collective-permute-start(bf16[16,128,128]{2,1,0:T(8,128)(2,1)S(1)} %bitcast.22), channel_id=1, source_target_pairs={{0,8},{4,12},{8,0},{12,4},{1,9},{5,13},{9,1},{13,5},{2,10},{6,14},... | collective-permute-start | bytes 1572872 | tf_op jit(solution)/shard_map/ppermute | solution.py:269
  84.6 4.2 %collective-permute-done.20.rest_2_ = bf16[64,2688]{1,0:T(8,128)(2,1)S(1)} collective-permute-done((bf16[64,2688]{1,0:T(8,128)(2,1)S(1)}, bf16[64,2688]{1,0:T(8,128)(2,1)S(1)}, u32[]{:S(2)}, u32[]{:S(2)}) %collective-permute-start.20) | collective-permute-done | bytes 344096 | tf_op jit(solution)/shard_map/ppermute | solution.py:272
  89.9 1.7 %shard_map.109 = (f32[64,3328]{1,0:T(8,128)}, f32[64,2048]{1,0:T(8,128)}) custom-call(s32[6]{0:T(128)S(1)} %stack.29.where_ref, bf16[64,2688]{1,0:T(8,128)(2,1)S(1)} %get-tuple-element.43.half_ref, bf16[64,1664]{1,0:T(8,128)(2,1)S(1)} %get-tuple-element.70.other_ref, bf16[64,2688]{1,0:T(8,128)(2,1)S(1)} %collective-permute-done.19.rest_0_, ...), custom_call_target="tpu_custom_call" | custom-call | tf_op jit(solution)/shard_map/pallas_call | solution.py:241
  91.6 7.9 %collective-permute-done.23.rest_1_ = bf16[14,128,128]{2,1,0:T(8,128)(2,1)S(1)} collective-permute-done((bf16[14,128,128]{2,1,0:T(8,128)(2,1)S(1)}, bf16[14,128,128]{2,1,0:T(8,128)(2,1)S(1)}, u32[]{:S(2)}, u32[]{:S(2)}) %collective-permute-start.23) | collective-permute-done | bytes 458784 | tf_op jit(solution)/shard_map/ppermute | solution.py:272
  99.6 1.0 shard_map.106.near_ref
  (71 shorter events, 13.8 us)
Async XLA Ops:
  0.6 10.6 %copy-start = (bf16[128,3328]{1,0:T(8,128)(2,1)S(1)}, bf16[128,3328]{1,0:T(8,128)(2,1)}, u32[]{:S(2)}) copy-start(bf16[128,3328]{1,0:T(8,128)(2,1)} %own_ref.1) | copy-start | bytes 2555908
  0.6 5.1 %collective-permute-start = (s32[64]{0:T(128)}, s32[64]{0:T(128)S(1)}, u32[]{:S(2)}, u32[]{:S(2)}) collective-permute-start(s32[64]{0:T(128)} %bitcast.28), channel_id=1, source_target_pairs={{0,4},{4,0},{8,12},{12,8},{1,5},{5,1},{9,13},{13,9},{2,6},{6,2},{1... | collective-permute-start | bytes 776 | tf_op jit(solution)/shard_map/ppermute | solution.py:265
  1.2 38.8 %collective-permute-start.3 = (bf16[128,3328]{1,0:T(8,128)(2,1)}, bf16[128,3328]{1,0:T(8,128)(2,1)}, u32[]{:S(2)}, u32[]{:S(2)}) collective-permute-start(bf16[128,3328]{1,0:T(8,128)(2,1)} %own_ref.1), channel_id=1, source_target_pairs={{0,1},{1,0},{2,3},{3,2},{4,5},{5,4},{6,7},{7,6},{8,9},{9,8},{10,11... | collective-permute-start | bytes 2555912 | tf_op jit(solution)/shard_map/ppermute | solution.py:272
  5.7 29.0 %collective-permute-start.6 = (bf16[16,128,128]{2,1,0:T(8,128)(2,1)}, bf16[16,128,128]{2,1,0:T(8,128)(2,1)}, u32[]{:S(2)}, u32[]{:S(2)}) collective-permute-start(bf16[16,128,128]{2,1,0:T(8,128)(2,1)} %dynamic-slice_bitcast_fusion), channel_id=1, source_target_pairs={{0,2},{1,3},{2,0},{3,1},{4,6},{5,7},{6,4},{7,5},{8,10},{9,11},{10,... | collective-permute-start | bytes 1572872 | tf_op jit(solution)/shard_map/ppermute | solution.py:276
  9.0 31.0 %copy-start.10 = (s32[1,64]{1,0:T(1,128)S(1)}, s32[1,64]{1,0:T(1,128)}, u32[]{:S(2)}) copy-start(s32[1,64]{1,0:T(1,128)} %param.11) | copy-start | bytes 772
  9.0 27.2 %copy-start.1 = (bf16[1,64,128,128]{3,2,1,0:T(8,128)(2,1)S(1)}, bf16[1,64,128,128]{3,2,1,0:T(8,128)(2,1)}, u32[]{:S(2)}) copy-start(bf16[1,64,128,128]{3,2,1,0:T(8,128)(2,1)} %param.10) | copy-start | bytes 6291460
  10.9 41.6 %collective-permute-start.5 = (bf16[11,128,128]{2,1,0:T(8,128)(2,1)}, bf16[11,128,128]{2,1,0:T(8,128)(2,1)S(1)}, u32[]{:S(2)}, u32[]{:S(2)}) collective-permute-start(bf16[11,128,128]{2,1,0:T(8,128)(2,1)} %pad_maximum_fusion), channel_id=1, source_target_pairs={{0,2},{1,3},{2,0},{3,1},{4,6},{5,7},{6,4},{7,5},{8,10},{9,11},{10,... | collective-permute-start | bytes 1081352 | tf_op jit(solution)/shard_map/ppermute | solution.py:276
  14.9 1.3 %collective-permute-start.1 = (f32[128,128]{1,0:T(8,128)S(1)}, f32[128,128]{1,0:T(8,128)S(1)}, u32[]{:S(2)}, u32[]{:S(2)}) collective-permute-start(f32[128,128]{1,0:T(8,128)S(1)} %shard_map.94), channel_id=1, source_target_pairs={{0,4},{4,0},{8,12},{12,8},{1,5},{5,1},{9,13},{13,9},{2,6},{6,2},{1... | collective-permute-start | bytes 196616 | tf_op jit(solution)/shard_map/ppermute | solution.py:265
  16.2 4.3 %collective-permute-start.2 = (f32[128,128]{1,0:T(8,128)S(1)}, f32[128,128]{1,0:T(8,128)S(1)}, u32[]{:S(2)}, u32[]{:S(2)}) collective-permute-start(f32[128,128]{1,0:T(8,128)S(1)} %add.24.both_ref), channel_id=1, source_target_pairs={{0,8},{4,12},{8,0},{12,4},{1,9},{5,13},{9,1},{13,5},{2,10},{6,14},... | collective-permute-start | bytes 196616 | tf_op jit(solution)/shard_map/ppermute | solution.py:269
  34.7 22.8 %collective-permute-start.8 = (bf16[16,128,128]{2,1,0:T(8,128)(2,1)}, bf16[16,128,128]{2,1,0:T(8,128)(2,1)}, u32[]{:S(2)}, u32[]{:S(2)}) collective-permute-start(bf16[16,128,128]{2,1,0:T(8,128)(2,1)} %collective-permute-done.6.rest_0_), channel_id=1, source_target_pairs={{0,16},{16,0},{1,17},{17,1},{2,18},{18,2},{3,19},{19,3},{4,20},{20... | collective-permute-start | bytes 1572872 | tf_op jit(solution)/shard_map/ppermute | solution.py:279
  36.2 19.7 %collective-permute-start.7 = (bf16[6,128,128]{2,1,0:T(8,128)(2,1)S(1)}, bf16[6,128,128]{2,1,0:T(8,128)(2,1)S(1)}, u32[]{:S(2)}, u32[]{:S(2)}) collective-permute-start(bf16[6,128,128]{2,1,0:T(8,128)(2,1)S(1)} %dynamic-slice_bitcast_fusion.2), channel_id=1, source_target_pairs={{0,2},{1,3},{2,0},{3,1},{4,6},{5,7},{6,4},{7,5},{8,10},{9,11},{10,... | collective-permute-start | bytes 589832 | tf_op jit(solution)/shard_map/ppermute | solution.py:276
  39.7 14.4 %collective-permute-start.4 = (bf16[64,1152]{1,0:T(8,128)(2,1)}, bf16[64,1152]{1,0:T(8,128)(2,1)S(1)}, u32[]{:S(2)}, u32[]{:S(2)}) collective-permute-start(bf16[64,1152]{1,0:T(8,128)(2,1)} %copy-done.11), channel_id=1, source_target_pairs={{0,1},{1,0},{2,3},{3,2},{4,5},{5,4},{6,7},{7,6},{8,9},{9,8},{10,11... | collective-permute-start | bytes 442376 | tf_op jit(solution)/shard_map/ppermute | solution.py:272
  39.9 14.2 %copy-start.8 = (f32[64,1024]{1,0:T(8,128)S(1)}, f32[64,1024]{1,0:T(8,128)}, u32[]{:S(2)}) copy-start(f32[64,1024]{1,0:T(8,128)} %copy-done.7) | copy-start | bytes 786436
  52.6 10.3 %collective-permute-start.9 = (bf16[10,128,128]{2,1,0:T(8,128)(2,1)S(1)}, bf16[10,128,128]{2,1,0:T(8,128)(2,1)S(1)}, u32[]{:S(2)}, u32[]{:S(2)}) collective-permute-start(bf16[10,128,128]{2,1,0:T(8,128)(2,1)S(1)} %slice.3), channel_id=1, source_target_pairs={{0,16},{16,0},{1,17},{17,1},{2,18},{18,2},{3,19},{19,3},{4,20},{20... | collective-permute-start | bytes 983048 | tf_op jit(solution)/shard_map/ppermute | solution.py:279
  56.0 10.6 %collective-permute-start.10 = (bf16[6,128,128]{2,1,0:T(8,128)(2,1)S(1)}, bf16[6,128,128]{2,1,0:T(8,128)(2,1)S(1)}, u32[]{:S(2)}, u32[]{:S(2)}) collective-permute-start(bf16[6,128,128]{2,1,0:T(8,128)(2,1)S(1)} %collective-permute-done.7.rest_2_), channel_id=1, source_target_pairs={{0,16},{16,0},{1,17},{17,1},{2,18},{18,2},{3,19},{19,3},{4,20},{20... | collective-permute-start | bytes 589832 | tf_op jit(solution)/shard_map/ppermute | solution.py:279
  57.5 18.0 %collective-permute-start.19 = (bf16[64,2688]{1,0:T(8,128)(2,1)S(1)}, bf16[64,2688]{1,0:T(8,128)(2,1)S(1)}, u32[]{:S(2)}, u32[]{:S(2)}) collective-permute-start(bf16[64,2688]{1,0:T(8,128)(2,1)S(1)} %get-tuple-element.43.half_ref), channel_id=1, source_target_pairs={{0,2},{1,3},{2,0},{3,1},{4,6},{5,7},{6,4},{7,5},{8,10},{9,11},{10,... | collective-permute-start | bytes 1032200 | tf_op jit(solution)/shard_map/ppermute | solution.py:276
  67.6 4.5 %collective-permute-start.12 = (bf16[1,6,128,128]{3,2,1,0:T(8,128)(2,1)S(1)}, bf16[1,6,128,128]{3,2,1,0:T(8,128)(2,1)S(1)}, u32[]{:S(2)}, u32[]{:S(2)}) collective-permute-start(bf16[1,6,128,128]{3,2,1,0:T(8,128)(2,1)S(1)} %get-tuple-element.58), channel_id=1, source_target_pairs={{0,4},{4,0},{8,12},{12,8},{1,5},{5,1},{9,13},{13,9},{2,6},{6,2},{1... | collective-permute-start | bytes 589832 | tf_op jit(solution)/shard_map/ppermute | solution.py:265
  67.6 2.8 %collective-permute-start.13 = (bf16[1,4,128,128]{3,2,1,0:T(8,128)(2,1)S(1)}, bf16[1,4,128,128]{3,2,1,0:T(8,128)(2,1)S(1)}, u32[]{:S(2)}, u32[]{:S(2)}) collective-permute-start(bf16[1,4,128,128]{3,2,1,0:T(8,128)(2,1)S(1)} %get-tuple-element.59), channel_id=1, source_target_pairs={{0,4},{4,0},{8,12},{12,8},{1,5},{5,1},{9,13},{13,9},{2,6},{6,2},{1... | collective-permute-start | bytes 393224 | tf_op jit(solution)/shard_map/ppermute | solution.py:265
  68.1 3.9 %collective-permute-start.14 = (bf16[1,4,128,128]{3,2,1,0:T(8,128)(2,1)S(1)}, bf16[1,4,128,128]{3,2,1,0:T(8,128)(2,1)S(1)}, u32[]{:S(2)}, u32[]{:S(2)}) collective-permute-start(bf16[1,4,128,128]{3,2,1,0:T(8,128)(2,1)S(1)} %get-tuple-element.60), channel_id=1, source_target_pairs={{0,4},{4,0},{8,12},{12,8},{1,5},{5,1},{9,13},{13,9},{2,6},{6,2},{1... | collective-permute-start | bytes 393224 | tf_op jit(solution)/shard_map/ppermute | solution.py:265
  68.2 1.4 %collective-permute-start.11 = (bf16[1,2,128,128]{3,2,1,0:T(8,128)(2,1)S(1)}, bf16[1,2,128,128]{3,2,1,0:T(8,128)(2,1)S(1)}, u32[]{:S(2)}, u32[]{:S(2)}) collective-permute-start(bf16[1,2,128,128]{3,2,1,0:T(8,128)(2,1)S(1)} %get-tuple-element.56), channel_id=1, source_target_pairs={{0,4},{4,0},{8,12},{12,8},{1,5},{5,1},{9,13},{13,9},{2,6},{6,2},{1... | collective-permute-start | bytes 196616 | tf_op jit(solution)/shard_map/ppermute | solution.py:265
  69.6 3.7 %collective-permute-start.16 = (bf16[2,128,128]{2,1,0:T(8,128)(2,1)S(1)}, bf16[2,128,128]{2,1,0:T(8,128)(2,1)S(1)}, u32[]{:S(2)}, u32[]{:S(2)}) collective-permute-start(bf16[2,128,128]{2,1,0:T(8,128)(2,1)S(1)} %get-tuple-element.62), channel_id=1, source_target_pairs={{0,4},{4,0},{8,12},{12,8},{1,5},{5,1},{9,13},{13,9},{2,6},{6,2},{1... | collective-permute-start | bytes 196616 | tf_op jit(solution)/shard_map/ppermute | solution.py:265
  70.5 4.3 %collective-permute-start.17 = (bf16[2,128,128]{2,1,0:T(8,128)(2,1)S(1)}, bf16[2,128,128]{2,1,0:T(8,128)(2,1)S(1)}, u32[]{:S(2)}, u32[]{:S(2)}) collective-permute-start(bf16[2,128,128]{2,1,0:T(8,128)(2,1)S(1)} %bitcast.25), channel_id=1, source_target_pairs={{0,8},{4,12},{8,0},{12,4},{1,9},{5,13},{9,1},{13,5},{2,10},{6,14},... | collective-permute-start | bytes 196616 | tf_op jit(solution)/shard_map/ppermute | solution.py:269
  72.0 16.8 %collective-permute-start.21 = (bf16[14,128,128]{2,1,0:T(8,128)(2,1)S(1)}, bf16[14,128,128]{2,1,0:T(8,128)(2,1)S(1)}, u32[]{:S(2)}, u32[]{:S(2)}) collective-permute-start(bf16[14,128,128]{2,1,0:T(8,128)(2,1)S(1)} %get-tuple-element.65), channel_id=1, source_target_pairs={{0,4},{4,0},{8,12},{12,8},{1,5},{5,1},{9,13},{13,9},{2,6},{6,2},{1... | collective-permute-start | bytes 1376264 | tf_op jit(solution)/shard_map/ppermute | solution.py:265
  72.7 16.1 %collective-permute-start.22 = (bf16[14,128,128]{2,1,0:T(8,128)(2,1)S(1)}, bf16[14,128,128]{2,1,0:T(8,128)(2,1)S(1)}, u32[]{:S(2)}, u32[]{:S(2)}) collective-permute-start(bf16[14,128,128]{2,1,0:T(8,128)(2,1)S(1)} %bitcast.23), channel_id=1, source_target_pairs={{0,8},{4,12},{8,0},{12,4},{1,9},{5,13},{9,1},{13,5},{2,10},{6,14},... | collective-permute-start | bytes 1376264 | tf_op jit(solution)/shard_map/ppermute | solution.py:269
  75.4 4.3 %collective-permute-start.18 = (bf16[2,128,128]{2,1,0:T(8,128)(2,1)S(1)}, bf16[2,128,128]{2,1,0:T(8,128)(2,1)S(1)}, u32[]{:S(2)}, u32[]{:S(2)}) collective-permute-start(bf16[2,128,128]{2,1,0:T(8,128)(2,1)S(1)} %shard_map.103), channel_id=1, source_target_pairs={{0,1},{1,0},{2,3},{3,2},{4,5},{5,4},{6,7},{7,6},{8,9},{9,8},{10,11... | collective-permute-start | bytes 196616 | tf_op jit(solution)/shard_map/ppermute | solution.py:272
  80.3 8.5 %collective-permute-start.20 = (bf16[64,2688]{1,0:T(8,128)(2,1)S(1)}, bf16[64,2688]{1,0:T(8,128)(2,1)S(1)}, u32[]{:S(2)}, u32[]{:S(2)}) collective-permute-start(bf16[64,2688]{1,0:T(8,128)(2,1)S(1)} %shard_map.104.rest_1_), channel_id=1, source_target_pairs={{0,1},{1,0},{2,3},{3,2},{4,5},{5,4},{6,7},{7,6},{8,9},{9,8},{10,11... | collective-permute-start | bytes 1032200 | tf_op jit(solution)/shard_map/ppermute | solution.py:272
  80.4 1.6 %collective-permute-start.24 = (bf16[1,8,128,128]{3,2,1,0:T(8,128)(2,1)S(1)}, bf16[1,8,128,128]{3,2,1,0:T(8,128)(2,1)S(1)}, u32[]{:S(2)}, u32[]{:S(2)}) collective-permute-start(bf16[1,8,128,128]{3,2,1,0:T(8,128)(2,1)S(1)} %get-tuple-element.67), channel_id=1, source_target_pairs={{0,4},{4,0},{8,12},{12,8},{1,5},{5,1},{9,13},{13,9},{2,6},{6,2},{1... | collective-permute-start | bytes 786440 | tf_op jit(solution)/shard_map/ppermute | solution.py:265
  80.5 1.9 %collective-permute-start.25 = (bf16[1,8,128,128]{3,2,1,0:T(8,128)(2,1)S(1)}, bf16[1,8,128,128]{3,2,1,0:T(8,128)(2,1)S(1)}, u32[]{:S(2)}, u32[]{:S(2)}) collective-permute-start(bf16[1,8,128,128]{3,2,1,0:T(8,128)(2,1)S(1)} %get-tuple-element.69), channel_id=1, source_target_pairs={{0,4},{4,0},{8,12},{12,8},{1,5},{5,1},{9,13},{13,9},{2,6},{6,2},{1... | collective-permute-start | bytes 786440 | tf_op jit(solution)/shard_map/ppermute | solution.py:265
  82.0 9.6 %collective-permute-start.15 = (bf16[16,128,128]{2,1,0:T(8,128)(2,1)S(1)}, bf16[16,128,128]{2,1,0:T(8,128)(2,1)S(1)}, u32[]{:S(2)}, u32[]{:S(2)}) collective-permute-start(bf16[16,128,128]{2,1,0:T(8,128)(2,1)S(1)} %get-tuple-element.61), channel_id=1, source_target_pairs={{0,4},{4,0},{8,12},{12,8},{1,5},{5,1},{9,13},{13,9},{2,6},{6,2},{1... | collective-permute-start | bytes 1572872 | tf_op jit(solution)/shard_map/ppermute | solution.py:265
  83.0 16.5 %copy-start.5 = (bf16[64,2048]{1,0:T(8,128)(2,1)S(1)}, bf16[64,2048]{1,0:T(8,128)(2,1)}, u32[]{:S(2)}) copy-start(bf16[64,2048]{1,0:T(8,128)(2,1)} %adapter_ref.2) | copy-start | bytes 786436
  83.1 17.5 %collective-permute-start.26 = (bf16[16,128,128]{2,1,0:T(8,128)(2,1)S(1)}, bf16[16,128,128]{2,1,0:T(8,128)(2,1)S(1)}, u32[]{:S(2)}, u32[]{:S(2)}) collective-permute-start(bf16[16,128,128]{2,1,0:T(8,128)(2,1)S(1)} %bitcast.22), channel_id=1, source_target_pairs={{0,8},{4,12},{8,0},{12,4},{1,9},{5,13},{9,1},{13,5},{2,10},{6,14},... | collective-permute-start | bytes 1572872 | tf_op jit(solution)/shard_map/ppermute | solution.py:269
  89.5 10.0 %collective-permute-start.23 = (bf16[14,128,128]{2,1,0:T(8,128)(2,1)S(1)}, bf16[14,128,128]{2,1,0:T(8,128)(2,1)S(1)}, u32[]{:S(2)}, u32[]{:S(2)}) collective-permute-start(bf16[14,128,128]{2,1,0:T(8,128)(2,1)S(1)} %shard_map.105), channel_id=1, source_target_pairs={{0,1},{1,0},{2,3},{3,2},{4,5},{5,4},{6,7},{7,6},{8,9},{9,8},{10,11... | collective-permute-start | bytes 1376264 | tf_op jit(solution)/shard_map/ppermute | solution.py:272
  (7 other events, 16.0 us)

commit v15 on v10

--- a/solution.py
+++ b/solution.py
@@ -349,8 +349,8 @@
             (part_shift(after(value, *gates[start])[:size], e), (source, e, start, size))
             for value, (source, _, start, size) in direct for e in range(1, n_parts)
         ]
-        more = direct + chunk(swapped, 0) + chunk(swapped, 1)
-        last = chunk(swapped, 2)
+        more = direct + chunk(swapped, 0)
+        last = chunk(swapped, 1) + chunk(swapped, 2)
 
         (total,) = call(
             functools.partial(more_kernel, **plan(more)), (total_shape,), (where, all_ids),

time: 98.5 us -> 99.4 us (level)
  waiting for transfers between devices: 44.7 us -> 45.7 us
    ppermute x5, waiting for transfers between devices: 22.5 us -> 24.4 us  [mate_swap(): return lax.ppermute(value, 'dp', [(i, i ^ 1) for i in range(n_dp)])]
where the time goes in v15:
time: 99.4 us; the launch traced here: 98.9 us
  waiting for transfers between devices  45.7 us (46%)
  starting transfers between devices  24.3 us (24%)
  Pallas kernels  18.8 us (19%)
  local copies, waits for them, and re-layouts  7.92 us (8%)
  other arithmetic  1.45 us (1%)
    ppermute x5, waiting for transfers between devices, mate_swap(): return lax.ppermute(value, 'dp', [(i, i ^ 1) for i in range(n_dp)])  24.4 us
    pallas_call x15, Pallas kernels, call(): pl.pallas_call(kernel, out_shape=outs, in_specs=[smem] * len(scalars) + [...  18.8 us
    ppermute x4, waiting for transfers between devices, group_shift(): return lax.ppermute(value, 'dp', pairs)  14.4 us
    ppermute x4, starting transfers between devices, group_shift(): return lax.ppermute(value, 'dp', pairs)  7.94 us
    ppermute x5, starting transfers between devices, mate_swap(): return lax.ppermute(value, 'dp', [(i, i ^ 1) for i in range(n_dp)])  5.53 us
    ppermute x4, starting transfers between devices, chip_shift(): return lax.ppermute(value, 'row', pairs)  5.14 us
    unnamed x22, local copies, waits for them, and re-layouts  4.77 us
    ppermute x3, starting transfers between devices, part_shift(): lax.ppermute(value, 'parts', [(i, (i + d) % n_parts) for i in range(n_par...  4.01 us
  transfers between devices with their start and end apart: 26, of which 13 were waited for; matrix products, arithmetic and copies ran while one was open for 5% of the time, Pallas kernels for 18%

profile of v15, /device:TPU:0, one launch (start us, length us, event | category | flops | bytes accessed | tf_op | source)
XLA Modules:
  0.0 98.9 jit_solution(837092931144204817)
XLA Ops:
  0.6 3.1 %collective-permute-start.3 = (bf16[128,3328]{1,0:T(8,128)(2,1)}, bf16[128,3328]{1,0:T(8,128)(2,1)}, u32[]{:S(2)}, u32[]{:S(2)}) collective-permute-start(bf16[128,3328]{1,0:T(8,128)(2,1)} %own_ref.1), channel_id=1, source_target_pairs={{0,1},{1,0},{2,3},{3,2},{4,5},{5,4},{6,7},{7,6},{8,9},{9,8},{10,11... | collective-permute-start | bytes 2555912 | tf_op jit(solution)/shard_map/ppermute | solution.py:256
  3.7 1.9 %dynamic-slice_bitcast_fusion = bf16[16,128,128]{2,1,0:T(8,128)(2,1)} fusion(bf16[1,64,128,128]{3,2,1,0:T(8,128)(2,1)} %param.10, s32[]{:T(128)S(6)} %select_n.18), kind=kLoop, calls=%fused_computation | loop fusion | bytes 1048580 | tf_op jit(solution)/shard_map/dynamic_slice | solution.py:288
  5.6 2.6 %collective-permute-start.6 = (bf16[16,128,128]{2,1,0:T(8,128)(2,1)}, bf16[16,128,128]{2,1,0:T(8,128)(2,1)}, u32[]{:S(2)}, u32[]{:S(2)}) collective-permute-start(bf16[16,128,128]{2,1,0:T(8,128)(2,1)} %dynamic-slice_bitcast_fusion), channel_id=1, source_target_pairs={{0,2},{1,3},{2,0},{3,1},{4,6},{5,7},{6,4},{7,5},{8,10},{9,11},{10,... | collective-permute-start | bytes 1572872 | tf_op jit(solution)/shard_map/ppermute | solution.py:260
  8.9 1.1 %dynamic-slice_bitcast_fusion.1 = bf16[10,128,128]{2,1,0:T(8,128)(2,1)S(1)} fusion(bf16[1,64,128,128]{3,2,1,0:T(8,128)(2,1)} %param.10, s32[]{:T(128)S(6)} %select_n.19), kind=kLoop, calls=%fused_computation.2 | loop fusion | bytes 655364 | tf_op jit(solution)/shard_map/dynamic_slice | solution.py:288
  11.2 1.0 %copy-done.2 = bf16[128,2048]{1,0:T(8,128)(2,1)S(1)} copy-done((bf16[128,2048]{1,0:T(8,128)(2,1)S(1)}, bf16[128,2048]{1,0:T(8,128)(2,1)}, u32[]{:S(2)}) %copy-start.2) | copy-done | bytes 524312
  12.2 0.9 copy-done.4
  13.2 1.0 %copy-done.6 = bf16[3328,64]{0,1:T(8,128)(2,1)S(1)} copy-done((bf16[3328,64]{0,1:T(8,128)(2,1)S(1)}, bf16[3328,64]{0,1:T(8,128)(2,1)}, u32[]{:S(2)}) %copy-start.6) | copy-done | bytes 426008
  15.1 1.0 %collective-permute-done.1 = f32[128,128]{1,0:T(8,128)S(1)} collective-permute-done((f32[128,128]{1,0:T(8,128)S(1)}, f32[128,128]{1,0:T(8,128)S(1)}, u32[]{:S(2)}, u32[]{:S(2)}) %collective-permute-start.1) | collective-permute-done | bytes 65568 | tf_op jit(solution)/shard_map/ppermute | solution.py:249
  16.1 1.6 %collective-permute-start.2 = (f32[128,128]{1,0:T(8,128)S(1)}, f32[128,128]{1,0:T(8,128)S(1)}, u32[]{:S(2)}, u32[]{:S(2)}) collective-permute-start(f32[128,128]{1,0:T(8,128)S(1)} %add.25.both_ref), channel_id=1, source_target_pairs={{0,8},{4,12},{8,0},{12,4},{1,9},{5,13},{9,1},{13,5},{2,10},{6,14},... | collective-permute-start | bytes 196616 | tf_op jit(solution)/shard_map/ppermute | solution.py:253
  17.7 2.7 %collective-permute-done.2.rest_0_ = f32[128,128]{1,0:T(8,128)S(1)} collective-permute-done((f32[128,128]{1,0:T(8,128)S(1)}, f32[128,128]{1,0:T(8,128)S(1)}, u32[]{:S(2)}, u32[]{:S(2)}) %collective-permute-start.2) | collective-permute-done | bytes 65568 | tf_op jit(solution)/shard_map/ppermute | solution.py:253
  20.4 1.0 %copy-done.3 = bf16[128,2048]{1,0:T(8,128)(2,1)S(1)} copy-done((bf16[128,2048]{1,0:T(8,128)(2,1)S(1)}, bf16[128,2048]{1,0:T(8,128)(2,1)}, u32[]{:S(2)}) %copy-start.3) | copy-done | bytes 524312
  23.0 11.7 %collective-permute-done.6.rest_0_ = bf16[16,128,128]{2,1,0:T(8,128)(2,1)} collective-permute-done((bf16[16,128,128]{2,1,0:T(8,128)(2,1)}, bf16[16,128,128]{2,1,0:T(8,128)(2,1)}, u32[]{:S(2)}, u32[]{:S(2)}) %collective-permute-start.6) | collective-permute-done | bytes 524320 | tf_op jit(solution)/shard_map/ppermute | solution.py:260
  34.7 4.6 %collective-permute-done.3.mate_acts_ref.mate_ref = bf16[128,3328]{1,0:T(8,128)(2,1)} collective-permute-done((bf16[128,3328]{1,0:T(8,128)(2,1)}, bf16[128,3328]{1,0:T(8,128)(2,1)}, u32[]{:S(2)}, u32[]{:S(2)}) %collective-permute-start.3) | collective-permute-done | bytes 852000 | tf_op jit(solution)/shard_map/ppermute | solution.py:256
  39.3 1.7 %collective-permute-start.8 = (bf16[16,128,128]{2,1,0:T(8,128)(2,1)}, bf16[16,128,128]{2,1,0:T(8,128)(2,1)}, u32[]{:S(2)}, u32[]{:S(2)}) collective-permute-start(bf16[16,128,128]{2,1,0:T(8,128)(2,1)} %collective-permute-done.6.rest_0_), channel_id=1, source_target_pairs={{0,16},{16,0},{1,17},{17,1},{2,18},{18,2},{3,19},{19,3},{4,20},{20... | collective-permute-start | bytes 1572872 | tf_op jit(solution)/shard_map/ppermute | solution.py:263
  41.0 3.1 %collective-permute-start.7 = (bf16[6,128,128]{2,1,0:T(8,128)(2,1)S(1)}, bf16[6,128,128]{2,1,0:T(8,128)(2,1)S(1)}, u32[]{:S(2)}, u32[]{:S(2)}) collective-permute-start(bf16[6,128,128]{2,1,0:T(8,128)(2,1)S(1)} %dynamic-slice_bitcast_fusion.2), channel_id=1, source_target_pairs={{0,2},{1,3},{2,0},{3,1},{4,6},{5,7},{6,4},{7,5},{8,10},{9,11},{10,... | collective-permute-start | bytes 589832 | tf_op jit(solution)/shard_map/ppermute | solution.py:260
  44.0 4.4 %shard_map.98 = (f32[65,256,128]{2,1,0:T(8,128)S(1)}, bf16[26,256,128]{2,1,0:T(8,128)(2,1)S(1)}) custom-call(s32[6]{0:T(128)S(1)} %stack.29.where_ref, s32[64]{0:T(128)S(1)} %bitcast.29, bf16[128,3328]{1,0:T(8,128)(2,1)S(1)} %copy-done, bf16[128,3328]{1,0:T(8,128)(2,1)} %collective-permute-done.3.mate_acts_ref.mate_ref, bf16[64,128,128]{2,1,0:T(8,128)(2,1)S(1)} %bitcast.21), custom_call_target="tpu_custom_call" | custom-call | tf_op jit(solution)/shard_map/pallas_call | solution.py:225
  48.5 1.5 %collective-permute-start.9 = (bf16[10,128,128]{2,1,0:T(8,128)(2,1)S(1)}, bf16[10,128,128]{2,1,0:T(8,128)(2,1)S(1)}, u32[]{:S(2)}, u32[]{:S(2)}) collective-permute-start(bf16[10,128,128]{2,1,0:T(8,128)(2,1)S(1)} %slice.3), channel_id=1, source_target_pairs={{0,16},{16,0},{1,17},{17,1},{2,18},{18,2},{3,19},{19,3},{4,20},{20... | collective-permute-start | bytes 983048 | tf_op jit(solution)/shard_map/ppermute | solution.py:263
  50.0 4.4 %collective-permute-done.4.mate_pack_ref = bf16[64,2176]{1,0:T(8,128)(2,1)S(1)} collective-permute-done((bf16[64,2176]{1,0:T(8,128)(2,1)}, bf16[64,2176]{1,0:T(8,128)(2,1)S(1)}, u32[]{:S(2)}, u32[]{:S(2)}) %collective-permute-start.4) | collective-permute-done | bytes 278560 | tf_op jit(solution)/shard_map/ppermute | solution.py:256
  54.4 1.6 %shard_map.96 = (bf16[64,2688]{1,0:T(8,128)(2,1)S(1)}, bf16[64,2688]{1,0:T(8,128)(2,1)S(1)}) custom-call(s32[6]{0:T(128)S(1)} %stack.29.where_ref, bf16[128,128]{1,0:T(8,128)(2,1)S(1)} %get-tuple-element.39.rounded_ref, bf16[128,3328]{1,0:T(8,128)(2,1)S(1)} %copy-done, bf16[128,3328]{1,0:T(8,128)(2,1)} %collective-permute-done.3.mate_acts_ref.mate_ref, ...), custom_call_target="tpu_custom_call" | custom-call | tf_op jit(solution)/shard_map/pallas_call | solution.py:225
  56.8 1.9 %collective-permute-start.19 = (bf16[64,2688]{1,0:T(8,128)(2,1)S(1)}, bf16[64,2688]{1,0:T(8,128)(2,1)S(1)}, u32[]{:S(2)}, u32[]{:S(2)}) collective-permute-start(bf16[64,2688]{1,0:T(8,128)(2,1)S(1)} %get-tuple-element.41.half_ref), channel_id=1, source_target_pairs={{0,2},{1,3},{2,0},{3,1},{4,6},{5,7},{6,4},{7,5},{8,10},{9,11},{10,... | collective-permute-start | bytes 1032200 | tf_op jit(solution)/shard_map/ppermute | solution.py:260
  58.8 3.1 %shard_map.99.old_ref = f32[65,256,128]{2,1,0:T(8,128)S(1)} custom-call(s32[6]{0:T(128)S(1)} %stack.29.where_ref, s32[1,128]{1,0:T(1,128)S(1)} %shard_map.97.ids_ref, bf16[26,256,128]{2,1,0:T(8,128)(2,1)S(1)} %get-tuple-element.46.tiles_ref, f32[65,256,128]{2,1,0:T(8,128)S(1)} %get-tuple-element.47.old_ref, ...), custom_call_target="tpu_custom_call", output_to_operand_aliasing={{}: (3, {})} | custom-call | tf_op jit(solution)/shard_map/pallas_call | solution.py:225
  61.9 1.9 %collective-permute-done.10.rest_1_ = bf16[6,128,128]{2,1,0:T(8,128)(2,1)S(1)} collective-permute-done((bf16[6,128,128]{2,1,0:T(8,128)(2,1)S(1)}, bf16[6,128,128]{2,1,0:T(8,128)(2,1)S(1)}, u32[]{:S(2)}, u32[]{:S(2)}) %collective-permute-start.10) | collective-permute-done | bytes 196640 | tf_op jit(solution)/shard_map/ppermute | solution.py:263
  63.8 1.5 %shard_map.100 = (f32[65,256,128]{2,1,0:T(8,128)S(1)}, bf16[1,4,128,128]{3,2,1,0:T(8,128)(2,1)S(1)}, bf16[1,4,128,128]{3,2,1,0:T(8,128)(2,1)S(1)}, bf16[1,4,128,...) custom-call(s32[6]{0:T(128)S(1)} %stack.29.where_ref, ...), custom_call_target="tpu_custom_call", output_to_operand_aliasing={{0}: (3, {})} | custom-call | tf_op jit(solution)/shard_map/pallas_call | solution.py:225
  67.7 1.3 %collective-permute-start.17 = (bf16[4,128,128]{2,1,0:T(8,128)(2,1)S(1)}, bf16[4,128,128]{2,1,0:T(8,128)(2,1)S(1)}, u32[]{:S(2)}, u32[]{:S(2)}) collective-permute-start(bf16[4,128,128]{2,1,0:T(8,128)(2,1)S(1)} %bitcast.25), channel_id=1, source_target_pairs={{0,8},{4,12},{8,0},{12,4},{1,9},{5,13},{9,1},{13,5},{2,10},{6,14},... | collective-permute-start | bytes 393224 | tf_op jit(solution)/shard_map/ppermute | solution.py:253
  70.5 2.6 %collective-permute-done.19.rest_0_ = bf16[64,2688]{1,0:T(8,128)(2,1)S(1)} collective-permute-done((bf16[64,2688]{1,0:T(8,128)(2,1)S(1)}, bf16[64,2688]{1,0:T(8,128)(2,1)S(1)}, u32[]{:S(2)}, u32[]{:S(2)}) %collective-permute-start.19) | collective-permute-done | bytes 344096 | tf_op jit(solution)/shard_map/ppermute | solution.py:260
  74.9 1.7 %collective-permute-start.18 = (bf16[4,128,128]{2,1,0:T(8,128)(2,1)S(1)}, bf16[4,128,128]{2,1,0:T(8,128)(2,1)S(1)}, u32[]{:S(2)}, u32[]{:S(2)}) collective-permute-start(bf16[4,128,128]{2,1,0:T(8,128)(2,1)S(1)} %shard_map.103), channel_id=1, source_target_pairs={{0,1},{1,0},{2,3},{3,2},{4,5},{5,4},{6,7},{7,6},{8,9},{9,8},{10,11... | collective-permute-start | bytes 393224 | tf_op jit(solution)/shard_map/ppermute | solution.py:256
  77.3 1.5 %collective-permute-start.25 = (bf16[16,128,128]{2,1,0:T(8,128)(2,1)S(1)}, bf16[16,128,128]{2,1,0:T(8,128)(2,1)S(1)}, u32[]{:S(2)}, u32[]{:S(2)}) collective-permute-start(bf16[16,128,128]{2,1,0:T(8,128)(2,1)S(1)} %bitcast.22), channel_id=1, source_target_pairs={{0,8},{4,12},{8,0},{12,4},{1,9},{5,13},{9,1},{13,5},{2,10},{6,14},... | collective-permute-start | bytes 1572872 | tf_op jit(solution)/shard_map/ppermute | solution.py:253
  78.8 6.1 %collective-permute-done.20.rest_1_ = bf16[64,2688]{1,0:T(8,128)(2,1)S(1)} collective-permute-done((bf16[64,2688]{1,0:T(8,128)(2,1)S(1)}, bf16[64,2688]{1,0:T(8,128)(2,1)S(1)}, u32[]{:S(2)}, u32[]{:S(2)}) %collective-permute-start.20) | collective-permute-done | bytes 344096 | tf_op jit(solution)/shard_map/ppermute | solution.py:256
  84.8 1.6 %collective-permute-done.18.rest_0_ = bf16[4,128,128]{2,1,0:T(8,128)(2,1)S(1)} collective-permute-done((bf16[4,128,128]{2,1,0:T(8,128)(2,1)S(1)}, bf16[4,128,128]{2,1,0:T(8,128)(2,1)S(1)}, u32[]{:S(2)}, u32[]{:S(2)}) %collective-permute-start.18) | collective-permute-done | bytes 131104 | tf_op jit(solution)/shard_map/ppermute | solution.py:256
  87.4 1.8 %shard_map.108 = (f32[64,3328]{1,0:T(8,128)}, f32[64,2048]{1,0:T(8,128)}) custom-call(s32[6]{0:T(128)S(1)} %stack.29.where_ref, bf16[64,2688]{1,0:T(8,128)(2,1)S(1)} %get-tuple-element.41.half_ref, bf16[64,2688]{1,0:T(8,128)(2,1)S(1)} %get-tuple-element.66.other_ref, bf16[64,2688]{1,0:T(8,128)(2,1)S(1)} %collective-permute-done.19.rest_0_, ...), custom_call_target="tpu_custom_call" | custom-call | tf_op jit(solution)/shard_map/pallas_call | solution.py:225
  89.2 7.8 %collective-permute-done.22.rest_1_ = bf16[12,128,128]{2,1,0:T(8,128)(2,1)S(1)} collective-permute-done((bf16[12,128,128]{2,1,0:T(8,128)(2,1)S(1)}, bf16[12,128,128]{2,1,0:T(8,128)(2,1)S(1)}, u32[]{:S(2)}, u32[]{:S(2)}) %collective-permute-start.22) | collective-permute-done | bytes 393248 | tf_op jit(solution)/shard_map/ppermute | solution.py:256
  97.0 0.9 shard_map.105.near_ref
  (66 shorter events, 13.3 us)
Async XLA Ops:
  0.6 10.5 %copy-start = (bf16[128,3328]{1,0:T(8,128)(2,1)S(1)}, bf16[128,3328]{1,0:T(8,128)(2,1)}, u32[]{:S(2)}) copy-start(bf16[128,3328]{1,0:T(8,128)(2,1)} %own_ref.1) | copy-start | bytes 2555908
  0.6 10.5 %copy-start.9 = (s32[128]{0:T(128)S(1)}, s32[128]{0:T(128)}, u32[]{:S(2)}) copy-start(s32[128]{0:T(128)} %param.9) | copy-start | bytes 1540
  0.6 38.6 %collective-permute-start.3 = (bf16[128,3328]{1,0:T(8,128)(2,1)}, bf16[128,3328]{1,0:T(8,128)(2,1)}, u32[]{:S(2)}, u32[]{:S(2)}) collective-permute-start(bf16[128,3328]{1,0:T(8,128)(2,1)} %own_ref.1), channel_id=1, source_target_pairs={{0,1},{1,0},{2,3},{3,2},{4,5},{5,4},{6,7},{7,6},{8,9},{9,8},{10,11... | collective-permute-start | bytes 2555912 | tf_op jit(solution)/shard_map/ppermute | solution.py:256
  5.6 29.1 %collective-permute-start.6 = (bf16[16,128,128]{2,1,0:T(8,128)(2,1)}, bf16[16,128,128]{2,1,0:T(8,128)(2,1)}, u32[]{:S(2)}, u32[]{:S(2)}) collective-permute-start(bf16[16,128,128]{2,1,0:T(8,128)(2,1)} %dynamic-slice_bitcast_fusion), channel_id=1, source_target_pairs={{0,2},{1,3},{2,0},{3,1},{4,6},{5,7},{6,4},{7,5},{8,10},{9,11},{10,... | collective-permute-start | bytes 1572872 | tf_op jit(solution)/shard_map/ppermute | solution.py:260
  8.2 2.6 %collective-permute-start = (s32[64]{0:T(128)}, s32[64]{0:T(128)S(1)}, u32[]{:S(2)}, u32[]{:S(2)}) collective-permute-start(s32[64]{0:T(128)} %bitcast.28), channel_id=1, source_target_pairs={{0,4},{4,0},{8,12},{12,8},{1,5},{5,1},{9,13},{13,9},{2,6},{6,2},{1... | collective-permute-start | bytes 776 | tf_op jit(solution)/shard_map/ppermute | solution.py:249
  8.9 35.2 %copy-start.10 = (s32[1,64]{1,0:T(1,128)S(1)}, s32[1,64]{1,0:T(1,128)}, u32[]{:S(2)}) copy-start(s32[1,64]{1,0:T(1,128)} %param.11) | copy-start | bytes 772
  8.9 32.1 %copy-start.1 = (bf16[1,64,128,128]{3,2,1,0:T(8,128)(2,1)S(1)}, bf16[1,64,128,128]{3,2,1,0:T(8,128)(2,1)}, u32[]{:S(2)}) copy-start(bf16[1,64,128,128]{3,2,1,0:T(8,128)(2,1)} %param.10) | copy-start | bytes 6291460
  10.8 37.6 %collective-permute-start.5 = (bf16[11,128,128]{2,1,0:T(8,128)(2,1)}, bf16[11,128,128]{2,1,0:T(8,128)(2,1)S(1)}, u32[]{:S(2)}, u32[]{:S(2)}) collective-permute-start(bf16[11,128,128]{2,1,0:T(8,128)(2,1)} %pad_maximum_fusion), channel_id=1, source_target_pairs={{0,2},{1,3},{2,0},{3,1},{4,6},{5,7},{6,4},{7,5},{8,10},{9,11},{10,... | collective-permute-start | bytes 1081352 | tf_op jit(solution)/shard_map/ppermute | solution.py:260
  14.8 1.3 %collective-permute-start.1 = (f32[128,128]{1,0:T(8,128)S(1)}, f32[128,128]{1,0:T(8,128)S(1)}, u32[]{:S(2)}, u32[]{:S(2)}) collective-permute-start(f32[128,128]{1,0:T(8,128)S(1)} %shard_map.94), channel_id=1, source_target_pairs={{0,4},{4,0},{8,12},{12,8},{1,5},{5,1},{9,13},{13,9},{2,6},{6,2},{1... | collective-permute-start | bytes 196616 | tf_op jit(solution)/shard_map/ppermute | solution.py:249
  16.1 4.3 %collective-permute-start.2 = (f32[128,128]{1,0:T(8,128)S(1)}, f32[128,128]{1,0:T(8,128)S(1)}, u32[]{:S(2)}, u32[]{:S(2)}) collective-permute-start(f32[128,128]{1,0:T(8,128)S(1)} %add.25.both_ref), channel_id=1, source_target_pairs={{0,8},{4,12},{8,0},{12,4},{1,9},{5,13},{9,1},{13,5},{2,10},{6,14},... | collective-permute-start | bytes 196616 | tf_op jit(solution)/shard_map/ppermute | solution.py:253
  39.3 19.5 %collective-permute-start.8 = (bf16[16,128,128]{2,1,0:T(8,128)(2,1)}, bf16[16,128,128]{2,1,0:T(8,128)(2,1)}, u32[]{:S(2)}, u32[]{:S(2)}) collective-permute-start(bf16[16,128,128]{2,1,0:T(8,128)(2,1)} %collective-permute-done.6.rest_0_), channel_id=1, source_target_pairs={{0,16},{16,0},{1,17},{17,1},{2,18},{18,2},{3,19},{19,3},{4,20},{20... | collective-permute-start | bytes 1572872 | tf_op jit(solution)/shard_map/ppermute | solution.py:263
  40.9 13.4 %collective-permute-start.4 = (bf16[64,2176]{1,0:T(8,128)(2,1)}, bf16[64,2176]{1,0:T(8,128)(2,1)S(1)}, u32[]{:S(2)}, u32[]{:S(2)}) collective-permute-start(bf16[64,2176]{1,0:T(8,128)(2,1)} %copy-done.7), channel_id=1, source_target_pairs={{0,1},{1,0},{2,3},{3,2},{4,5},{5,4},{6,7},{7,6},{8,9},{9,8},{10,11... | collective-permute-start | bytes 835592 | tf_op jit(solution)/shard_map/ppermute | solution.py:256
  41.0 15.0 %collective-permute-start.7 = (bf16[6,128,128]{2,1,0:T(8,128)(2,1)S(1)}, bf16[6,128,128]{2,1,0:T(8,128)(2,1)S(1)}, u32[]{:S(2)}, u32[]{:S(2)}) collective-permute-start(bf16[6,128,128]{2,1,0:T(8,128)(2,1)S(1)} %dynamic-slice_bitcast_fusion.2), channel_id=1, source_target_pairs={{0,2},{1,3},{2,0},{3,1},{4,6},{5,7},{6,4},{7,5},{8,10},{9,11},{10,... | collective-permute-start | bytes 589832 | tf_op jit(solution)/shard_map/ppermute | solution.py:260
  44.0 10.3 %copy-start.8 = (bf16[64,2176]{1,0:T(8,128)(2,1)S(1)}, bf16[64,2176]{1,0:T(8,128)(2,1)}, u32[]{:S(2)}) copy-start(bf16[64,2176]{1,0:T(8,128)(2,1)} %copy-done.7) | copy-start | bytes 835588
  48.5 15.3 %collective-permute-start.9 = (bf16[10,128,128]{2,1,0:T(8,128)(2,1)S(1)}, bf16[10,128,128]{2,1,0:T(8,128)(2,1)S(1)}, u32[]{:S(2)}, u32[]{:S(2)}) collective-permute-start(bf16[10,128,128]{2,1,0:T(8,128)(2,1)S(1)} %slice.3), channel_id=1, source_target_pairs={{0,16},{16,0},{1,17},{17,1},{2,18},{18,2},{3,19},{19,3},{4,20},{20... | collective-permute-start | bytes 983048 | tf_op jit(solution)/shard_map/ppermute | solution.py:263
  56.0 7.8 %collective-permute-start.10 = (bf16[6,128,128]{2,1,0:T(8,128)(2,1)S(1)}, bf16[6,128,128]{2,1,0:T(8,128)(2,1)S(1)}, u32[]{:S(2)}, u32[]{:S(2)}) collective-permute-start(bf16[6,128,128]{2,1,0:T(8,128)(2,1)S(1)} %collective-permute-done.7.rest_2_), channel_id=1, source_target_pairs={{0,16},{16,0},{1,17},{17,1},{2,18},{18,2},{3,19},{19,3},{4,20},{20... | collective-permute-start | bytes 589832 | tf_op jit(solution)/shard_map/ppermute | solution.py:263
  56.8 16.3 %collective-permute-start.19 = (bf16[64,2688]{1,0:T(8,128)(2,1)S(1)}, bf16[64,2688]{1,0:T(8,128)(2,1)S(1)}, u32[]{:S(2)}, u32[]{:S(2)}) collective-permute-start(bf16[64,2688]{1,0:T(8,128)(2,1)S(1)} %get-tuple-element.41.half_ref), channel_id=1, source_target_pairs={{0,2},{1,3},{2,0},{3,1},{4,6},{5,7},{6,4},{7,5},{8,10},{9,11},{10,... | collective-permute-start | bytes 1032200 | tf_op jit(solution)/shard_map/ppermute | solution.py:260
  65.3 1.4 %collective-permute-start.11 = (bf16[1,4,128,128]{3,2,1,0:T(8,128)(2,1)S(1)}, bf16[1,4,128,128]{3,2,1,0:T(8,128)(2,1)S(1)}, u32[]{:S(2)}, u32[]{:S(2)}) collective-permute-start(bf16[1,4,128,128]{3,2,1,0:T(8,128)(2,1)S(1)} %get-tuple-element.53), channel_id=1, source_target_pairs={{0,4},{4,0},{8,12},{12,8},{1,5},{5,1},{9,13},{13,9},{2,6},{6,2},{1... | collective-permute-start | bytes 393224 | tf_op jit(solution)/shard_map/ppermute | solution.py:249
  65.4 8.9 %collective-permute-start.16 = (bf16[16,128,128]{2,1,0:T(8,128)(2,1)S(1)}, bf16[16,128,128]{2,1,0:T(8,128)(2,1)S(1)}, u32[]{:S(2)}, u32[]{:S(2)}) collective-permute-start(bf16[16,128,128]{2,1,0:T(8,128)(2,1)S(1)} %get-tuple-element.59), channel_id=1, source_target_pairs={{0,4},{4,0},{8,12},{12,8},{1,5},{5,1},{9,13},{13,9},{2,6},{6,2},{1... | collective-permute-start | bytes 1572872 | tf_op jit(solution)/shard_map/ppermute | solution.py:249
  65.9 1.8 %collective-permute-start.12 = (bf16[1,4,128,128]{3,2,1,0:T(8,128)(2,1)S(1)}, bf16[1,4,128,128]{3,2,1,0:T(8,128)(2,1)S(1)}, u32[]{:S(2)}, u32[]{:S(2)}) collective-permute-start(bf16[1,4,128,128]{3,2,1,0:T(8,128)(2,1)S(1)} %get-tuple-element.55), channel_id=1, source_target_pairs={{0,4},{4,0},{8,12},{12,8},{1,5},{5,1},{9,13},{13,9},{2,6},{6,2},{1... | collective-permute-start | bytes 393224 | tf_op jit(solution)/shard_map/ppermute | solution.py:249
  66.0 3.0 %collective-permute-start.13 = (bf16[1,4,128,128]{3,2,1,0:T(8,128)(2,1)S(1)}, bf16[1,4,128,128]{3,2,1,0:T(8,128)(2,1)S(1)}, u32[]{:S(2)}, u32[]{:S(2)}) collective-permute-start(bf16[1,4,128,128]{3,2,1,0:T(8,128)(2,1)S(1)} %get-tuple-element.56), channel_id=1, source_target_pairs={{0,4},{4,0},{8,12},{12,8},{1,5},{5,1},{9,13},{13,9},{2,6},{6,2},{1... | collective-permute-start | bytes 393224 | tf_op jit(solution)/shard_map/ppermute | solution.py:249
  66.7 2.3 %collective-permute-start.14 = (bf16[1,4,128,128]{3,2,1,0:T(8,128)(2,1)S(1)}, bf16[1,4,128,128]{3,2,1,0:T(8,128)(2,1)S(1)}, u32[]{:S(2)}, u32[]{:S(2)}) collective-permute-start(bf16[1,4,128,128]{3,2,1,0:T(8,128)(2,1)S(1)} %get-tuple-element.57), channel_id=1, source_target_pairs={{0,4},{4,0},{8,12},{12,8},{1,5},{5,1},{9,13},{13,9},{2,6},{6,2},{1... | collective-permute-start | bytes 393224 | tf_op jit(solution)/shard_map/ppermute | solution.py:249
  67.7 6.2 %collective-permute-start.17 = (bf16[4,128,128]{2,1,0:T(8,128)(2,1)S(1)}, bf16[4,128,128]{2,1,0:T(8,128)(2,1)S(1)}, u32[]{:S(2)}, u32[]{:S(2)}) collective-permute-start(bf16[4,128,128]{2,1,0:T(8,128)(2,1)S(1)} %bitcast.25), channel_id=1, source_target_pairs={{0,8},{4,12},{8,0},{12,4},{1,9},{5,13},{9,1},{13,5},{2,10},{6,14},... | collective-permute-start | bytes 393224 | tf_op jit(solution)/shard_map/ppermute | solution.py:253
  69.7 6.9 %collective-permute-start.24 = (bf16[1,8,128,128]{3,2,1,0:T(8,128)(2,1)S(1)}, bf16[1,8,128,128]{3,2,1,0:T(8,128)(2,1)S(1)}, u32[]{:S(2)}, u32[]{:S(2)}) collective-permute-start(bf16[1,8,128,128]{3,2,1,0:T(8,128)(2,1)S(1)} %get-tuple-element.65), channel_id=1, source_target_pairs={{0,4},{4,0},{8,12},{12,8},{1,5},{5,1},{9,13},{13,9},{2,6},{6,2},{1... | collective-permute-start | bytes 786440 | tf_op jit(solution)/shard_map/ppermute | solution.py:249
  69.8 16.6 %collective-permute-start.21 = (bf16[12,128,128]{2,1,0:T(8,128)(2,1)S(1)}, bf16[12,128,128]{2,1,0:T(8,128)(2,1)S(1)}, u32[]{:S(2)}, u32[]{:S(2)}) collective-permute-start(bf16[12,128,128]{2,1,0:T(8,128)(2,1)S(1)} %bitcast.24), channel_id=1, source_target_pairs={{0,8},{4,12},{8,0},{12,4},{1,9},{5,13},{9,1},{13,5},{2,10},{6,14},... | collective-permute-start | bytes 1179656 | tf_op jit(solution)/shard_map/ppermute | solution.py:253
  73.1 3.5 %collective-permute-start.23 = (bf16[1,8,128,128]{3,2,1,0:T(8,128)(2,1)S(1)}, bf16[1,8,128,128]{3,2,1,0:T(8,128)(2,1)S(1)}, u32[]{:S(2)}, u32[]{:S(2)}) collective-permute-start(bf16[1,8,128,128]{3,2,1,0:T(8,128)(2,1)S(1)} %get-tuple-element.63), channel_id=1, source_target_pairs={{0,4},{4,0},{8,12},{12,8},{1,5},{5,1},{9,13},{13,9},{2,6},{6,2},{1... | collective-permute-start | bytes 786440 | tf_op jit(solution)/shard_map/ppermute | solution.py:249
  73.9 11.0 %collective-permute-start.20 = (bf16[64,2688]{1,0:T(8,128)(2,1)S(1)}, bf16[64,2688]{1,0:T(8,128)(2,1)S(1)}, u32[]{:S(2)}, u32[]{:S(2)}) collective-permute-start(bf16[64,2688]{1,0:T(8,128)(2,1)S(1)} %collective-permute-done.19.rest_0_), channel_id=1, source_target_pairs={{0,1},{1,0},{2,3},{3,2},{4,5},{5,4},{6,7},{7,6},{8,9},{9,8},{10,11... | collective-permute-start | bytes 1032200 | tf_op jit(solution)/shard_map/ppermute | solution.py:256
  74.9 11.5 %collective-permute-start.18 = (bf16[4,128,128]{2,1,0:T(8,128)(2,1)S(1)}, bf16[4,128,128]{2,1,0:T(8,128)(2,1)S(1)}, u32[]{:S(2)}, u32[]{:S(2)}) collective-permute-start(bf16[4,128,128]{2,1,0:T(8,128)(2,1)S(1)} %shard_map.103), channel_id=1, source_target_pairs={{0,1},{1,0},{2,3},{3,2},{4,5},{5,4},{6,7},{7,6},{8,9},{9,8},{10,11... | collective-permute-start | bytes 393224 | tf_op jit(solution)/shard_map/ppermute | solution.py:256
  76.6 12.6 %collective-permute-start.15 = (bf16[16,128,128]{2,1,0:T(8,128)(2,1)S(1)}, bf16[16,128,128]{2,1,0:T(8,128)(2,1)S(1)}, u32[]{:S(2)}, u32[]{:S(2)}) collective-permute-start(bf16[16,128,128]{2,1,0:T(8,128)(2,1)S(1)} %get-tuple-element.58), channel_id=1, source_target_pairs={{0,4},{4,0},{8,12},{12,8},{1,5},{5,1},{9,13},{13,9},{2,6},{6,2},{1... | collective-permute-start | bytes 1572872 | tf_op jit(solution)/shard_map/ppermute | solution.py:249
  77.3 19.8 %copy-start.5 = (bf16[64,2048]{1,0:T(8,128)(2,1)S(1)}, bf16[64,2048]{1,0:T(8,128)(2,1)}, u32[]{:S(2)}) copy-start(bf16[64,2048]{1,0:T(8,128)(2,1)} %adapter_ref.2) | copy-start | bytes 786436
  77.3 20.7 %collective-permute-start.25 = (bf16[16,128,128]{2,1,0:T(8,128)(2,1)S(1)}, bf16[16,128,128]{2,1,0:T(8,128)(2,1)S(1)}, u32[]{:S(2)}, u32[]{:S(2)}) collective-permute-start(bf16[16,128,128]{2,1,0:T(8,128)(2,1)S(1)} %bitcast.22), channel_id=1, source_target_pairs={{0,8},{4,12},{8,0},{12,4},{1,9},{5,13},{9,1},{13,5},{2,10},{6,14},... | collective-permute-start | bytes 1572872 | tf_op jit(solution)/shard_map/ppermute | solution.py:253
  87.1 9.9 %collective-permute-start.22 = (bf16[12,128,128]{2,1,0:T(8,128)(2,1)S(1)}, bf16[12,128,128]{2,1,0:T(8,128)(2,1)S(1)}, u32[]{:S(2)}, u32[]{:S(2)}) collective-permute-start(bf16[12,128,128]{2,1,0:T(8,128)(2,1)S(1)} %shard_map.104), channel_id=1, source_target_pairs={{0,1},{1,0},{2,3},{3,2},{4,5},{5,4},{6,7},{7,6},{8,9},{9,8},{10,11... | collective-permute-start | bytes 1179656 | tf_op jit(solution)/shard_map/ppermute | solution.py:256
  (5 other events, 4.8 us)

commit v16 on v15

--- a/solution.py
+++ b/solution.py
@@ -398,7 +398,7 @@
 
         from_mate_first = for_mate(pieces_first, small, 0)
         from_mate = [
-            from_mate_first, for_mate(pieces_second, share - small, small, from_mate_first, *mate_grads),
+            from_mate_first, for_mate(pieces_second, share - small, small, *mate_grads),
         ]
         in_grad, out_grad = call(
             grad_sum_kernel,

time: 99.4 us -> 99.4 us (level)
  transfers between devices with their start and end apart: 26 -> 26, of which waited for: 13 -> 12; matrix products, arithmetic and copies ran while one was open for 5% -> 5% of each run, Pallas kernels for 18% -> 18%
where the time goes in v16:
time: 99.4 us; the launch traced here: 99 us
  waiting for transfers between devices  45.7 us (46%)
  starting transfers between devices  24.3 us (24%)
  Pallas kernels  18.8 us (19%)
  local copies, waits for them, and re-layouts  7.92 us (8%)
  other arithmetic  1.45 us (1%)
    ppermute x5, waiting for transfers between devices, mate_swap(): return lax.ppermute(value, 'dp', [(i, i ^ 1) for i in range(n_dp)])  24.1 us
    pallas_call x15, Pallas kernels, call(): pl.pallas_call(kernel, out_shape=outs, in_specs=[smem] * len(scalars) + [...  18.8 us
    ppermute x4, waiting for transfers between devices, group_shift(): return lax.ppermute(value, 'dp', pairs)  14.5 us
    ppermute x4, starting transfers between devices, group_shift(): return lax.ppermute(value, 'dp', pairs)  7.94 us
    ppermute x5, starting transfers between devices, mate_swap(): return lax.ppermute(value, 'dp', [(i, i ^ 1) for i in range(n_dp)])  5.58 us
    ppermute x4, starting transfers between devices, chip_shift(): return lax.ppermute(value, 'row', pairs)  5.07 us
    unnamed x22, local copies, waits for them, and re-layouts  4.77 us
    ppermute x3, starting transfers between devices, part_shift(): lax.ppermute(value, 'parts', [(i, (i + d) % n_parts) for i in range(n_par...  4.01 us
  transfers between devices with their start and end apart: 26, of which 12 were waited for; matrix products, arithmetic and copies ran while one was open for 5% of the time, Pallas kernels for 18%

profile of v16, /device:TPU:0, one launch (start us, length us, event | category | flops | bytes accessed | tf_op | source)
XLA Modules:
  0.0 99.0 jit_solution(16850957594836216165)
XLA Ops:
  0.6 3.1 %collective-permute-start.3 = (bf16[128,3328]{1,0:T(8,128)(2,1)}, bf16[128,3328]{1,0:T(8,128)(2,1)}, u32[]{:S(2)}, u32[]{:S(2)}) collective-permute-start(bf16[128,3328]{1,0:T(8,128)(2,1)} %own_ref.1), channel_id=1, source_target_pairs={{0,1},{1,0},{2,3},{3,2},{4,5},{5,4},{6,7},{7,6},{8,9},{9,8},{10,11... | collective-permute-start | bytes 2555912 | tf_op jit(solution)/shard_map/ppermute | solution.py:256
  3.7 1.9 %dynamic-slice_bitcast_fusion = bf16[16,128,128]{2,1,0:T(8,128)(2,1)} fusion(bf16[1,64,128,128]{3,2,1,0:T(8,128)(2,1)} %param.10, s32[]{:T(128)S(6)} %select_n.18), kind=kLoop, calls=%fused_computation | loop fusion | bytes 1048580 | tf_op jit(solution)/shard_map/dynamic_slice | solution.py:288
  5.6 2.6 %collective-permute-start.6 = (bf16[16,128,128]{2,1,0:T(8,128)(2,1)}, bf16[16,128,128]{2,1,0:T(8,128)(2,1)}, u32[]{:S(2)}, u32[]{:S(2)}) collective-permute-start(bf16[16,128,128]{2,1,0:T(8,128)(2,1)} %dynamic-slice_bitcast_fusion), channel_id=1, source_target_pairs={{0,2},{1,3},{2,0},{3,1},{4,6},{5,7},{6,4},{7,5},{8,10},{9,11},{10,... | collective-permute-start | bytes 1572872 | tf_op jit(solution)/shard_map/ppermute | solution.py:260
  8.9 1.1 %dynamic-slice_bitcast_fusion.1 = bf16[10,128,128]{2,1,0:T(8,128)(2,1)S(1)} fusion(bf16[1,64,128,128]{3,2,1,0:T(8,128)(2,1)} %param.10, s32[]{:T(128)S(6)} %select_n.19), kind=kLoop, calls=%fused_computation.2 | loop fusion | bytes 655364 | tf_op jit(solution)/shard_map/dynamic_slice | solution.py:288
  11.2 1.0 %copy-done.2 = bf16[128,2048]{1,0:T(8,128)(2,1)S(1)} copy-done((bf16[128,2048]{1,0:T(8,128)(2,1)S(1)}, bf16[128,2048]{1,0:T(8,128)(2,1)}, u32[]{:S(2)}) %copy-start.2) | copy-done | bytes 524312
  12.2 0.9 copy-done.4
  13.2 1.0 %copy-done.6 = bf16[3328,64]{0,1:T(8,128)(2,1)S(1)} copy-done((bf16[3328,64]{0,1:T(8,128)(2,1)S(1)}, bf16[3328,64]{0,1:T(8,128)(2,1)}, u32[]{:S(2)}) %copy-start.6) | copy-done | bytes 426008
  15.1 1.0 %collective-permute-done.1 = f32[128,128]{1,0:T(8,128)S(1)} collective-permute-done((f32[128,128]{1,0:T(8,128)S(1)}, f32[128,128]{1,0:T(8,128)S(1)}, u32[]{:S(2)}, u32[]{:S(2)}) %collective-permute-start.1) | collective-permute-done | bytes 65568 | tf_op jit(solution)/shard_map/ppermute | solution.py:249
  16.1 1.6 %collective-permute-start.2 = (f32[128,128]{1,0:T(8,128)S(1)}, f32[128,128]{1,0:T(8,128)S(1)}, u32[]{:S(2)}, u32[]{:S(2)}) collective-permute-start(f32[128,128]{1,0:T(8,128)S(1)} %add.25.both_ref), channel_id=1, source_target_pairs={{0,8},{4,12},{8,0},{12,4},{1,9},{5,13},{9,1},{13,5},{2,10},{6,14},... | collective-permute-start | bytes 196616 | tf_op jit(solution)/shard_map/ppermute | solution.py:253
  17.7 2.7 %collective-permute-done.2.rest_0_ = f32[128,128]{1,0:T(8,128)S(1)} collective-permute-done((f32[128,128]{1,0:T(8,128)S(1)}, f32[128,128]{1,0:T(8,128)S(1)}, u32[]{:S(2)}, u32[]{:S(2)}) %collective-permute-start.2) | collective-permute-done | bytes 65568 | tf_op jit(solution)/shard_map/ppermute | solution.py:253
  20.4 1.0 %copy-done.3 = bf16[128,2048]{1,0:T(8,128)(2,1)S(1)} copy-done((bf16[128,2048]{1,0:T(8,128)(2,1)S(1)}, bf16[128,2048]{1,0:T(8,128)(2,1)}, u32[]{:S(2)}) %copy-start.3) | copy-done | bytes 524312
  23.0 11.7 %collective-permute-done.6.rest_0_ = bf16[16,128,128]{2,1,0:T(8,128)(2,1)} collective-permute-done((bf16[16,128,128]{2,1,0:T(8,128)(2,1)}, bf16[16,128,128]{2,1,0:T(8,128)(2,1)}, u32[]{:S(2)}, u32[]{:S(2)}) %collective-permute-start.6) | collective-permute-done | bytes 524320 | tf_op jit(solution)/shard_map/ppermute | solution.py:260
  34.7 4.6 %collective-permute-done.3.mate_acts_ref.mate_ref = bf16[128,3328]{1,0:T(8,128)(2,1)} collective-permute-done((bf16[128,3328]{1,0:T(8,128)(2,1)}, bf16[128,3328]{1,0:T(8,128)(2,1)}, u32[]{:S(2)}, u32[]{:S(2)}) %collective-permute-start.3) | collective-permute-done | bytes 852000 | tf_op jit(solution)/shard_map/ppermute | solution.py:256
  39.3 1.7 %collective-permute-start.8 = (bf16[16,128,128]{2,1,0:T(8,128)(2,1)}, bf16[16,128,128]{2,1,0:T(8,128)(2,1)}, u32[]{:S(2)}, u32[]{:S(2)}) collective-permute-start(bf16[16,128,128]{2,1,0:T(8,128)(2,1)} %collective-permute-done.6.rest_0_), channel_id=1, source_target_pairs={{0,16},{16,0},{1,17},{17,1},{2,18},{18,2},{3,19},{19,3},{4,20},{20... | collective-permute-start | bytes 1572872 | tf_op jit(solution)/shard_map/ppermute | solution.py:263
  41.0 3.1 %collective-permute-start.7 = (bf16[6,128,128]{2,1,0:T(8,128)(2,1)S(1)}, bf16[6,128,128]{2,1,0:T(8,128)(2,1)S(1)}, u32[]{:S(2)}, u32[]{:S(2)}) collective-permute-start(bf16[6,128,128]{2,1,0:T(8,128)(2,1)S(1)} %dynamic-slice_bitcast_fusion.2), channel_id=1, source_target_pairs={{0,2},{1,3},{2,0},{3,1},{4,6},{5,7},{6,4},{7,5},{8,10},{9,11},{10,... | collective-permute-start | bytes 589832 | tf_op jit(solution)/shard_map/ppermute | solution.py:260
  44.0 4.4 %shard_map.98 = (f32[65,256,128]{2,1,0:T(8,128)S(1)}, bf16[26,256,128]{2,1,0:T(8,128)(2,1)S(1)}) custom-call(s32[6]{0:T(128)S(1)} %stack.29.where_ref, s32[64]{0:T(128)S(1)} %bitcast.29, bf16[128,3328]{1,0:T(8,128)(2,1)S(1)} %copy-done, bf16[128,3328]{1,0:T(8,128)(2,1)} %collective-permute-done.3.mate_acts_ref.mate_ref, bf16[64,128,128]{2,1,0:T(8,128)(2,1)S(1)} %bitcast.21), custom_call_target="tpu_custom_call" | custom-call | tf_op jit(solution)/shard_map/pallas_call | solution.py:225
  48.5 1.5 %collective-permute-start.9 = (bf16[10,128,128]{2,1,0:T(8,128)(2,1)S(1)}, bf16[10,128,128]{2,1,0:T(8,128)(2,1)S(1)}, u32[]{:S(2)}, u32[]{:S(2)}) collective-permute-start(bf16[10,128,128]{2,1,0:T(8,128)(2,1)S(1)} %slice.3), channel_id=1, source_target_pairs={{0,16},{16,0},{1,17},{17,1},{2,18},{18,2},{3,19},{19,3},{4,20},{20... | collective-permute-start | bytes 983048 | tf_op jit(solution)/shard_map/ppermute | solution.py:263
  50.0 4.4 %collective-permute-done.4.mate_pack_ref = bf16[64,2176]{1,0:T(8,128)(2,1)S(1)} collective-permute-done((bf16[64,2176]{1,0:T(8,128)(2,1)}, bf16[64,2176]{1,0:T(8,128)(2,1)S(1)}, u32[]{:S(2)}, u32[]{:S(2)}) %collective-permute-start.4) | collective-permute-done | bytes 278560 | tf_op jit(solution)/shard_map/ppermute | solution.py:256
  54.4 1.6 %shard_map.96 = (bf16[64,2688]{1,0:T(8,128)(2,1)S(1)}, bf16[64,2688]{1,0:T(8,128)(2,1)S(1)}) custom-call(s32[6]{0:T(128)S(1)} %stack.29.where_ref, bf16[128,128]{1,0:T(8,128)(2,1)S(1)} %get-tuple-element.39.rounded_ref, bf16[128,3328]{1,0:T(8,128)(2,1)S(1)} %copy-done, bf16[128,3328]{1,0:T(8,128)(2,1)} %collective-permute-done.3.mate_acts_ref.mate_ref, ...), custom_call_target="tpu_custom_call" | custom-call | tf_op jit(solution)/shard_map/pallas_call | solution.py:225
  56.8 1.9 %collective-permute-start.19 = (bf16[64,2688]{1,0:T(8,128)(2,1)S(1)}, bf16[64,2688]{1,0:T(8,128)(2,1)S(1)}, u32[]{:S(2)}, u32[]{:S(2)}) collective-permute-start(bf16[64,2688]{1,0:T(8,128)(2,1)S(1)} %get-tuple-element.41.half_ref), channel_id=1, source_target_pairs={{0,2},{1,3},{2,0},{3,1},{4,6},{5,7},{6,4},{7,5},{8,10},{9,11},{10,... | collective-permute-start | bytes 1032200 | tf_op jit(solution)/shard_map/ppermute | solution.py:260
  58.8 3.1 %shard_map.99.old_ref = f32[65,256,128]{2,1,0:T(8,128)S(1)} custom-call(s32[6]{0:T(128)S(1)} %stack.29.where_ref, s32[1,128]{1,0:T(1,128)S(1)} %shard_map.97.ids_ref, bf16[26,256,128]{2,1,0:T(8,128)(2,1)S(1)} %get-tuple-element.46.tiles_ref, f32[65,256,128]{2,1,0:T(8,128)S(1)} %get-tuple-element.47.old_ref, ...), custom_call_target="tpu_custom_call", output_to_operand_aliasing={{}: (3, {})} | custom-call | tf_op jit(solution)/shard_map/pallas_call | solution.py:225
  61.9 1.9 %collective-permute-done.10.rest_1_ = bf16[6,128,128]{2,1,0:T(8,128)(2,1)S(1)} collective-permute-done((bf16[6,128,128]{2,1,0:T(8,128)(2,1)S(1)}, bf16[6,128,128]{2,1,0:T(8,128)(2,1)S(1)}, u32[]{:S(2)}, u32[]{:S(2)}) %collective-permute-start.10) | collective-permute-done | bytes 196640 | tf_op jit(solution)/shard_map/ppermute | solution.py:263
  63.8 1.5 %shard_map.100 = (f32[65,256,128]{2,1,0:T(8,128)S(1)}, bf16[1,4,128,128]{3,2,1,0:T(8,128)(2,1)S(1)}, bf16[1,4,128,128]{3,2,1,0:T(8,128)(2,1)S(1)}, bf16[1,4,128,...) custom-call(s32[6]{0:T(128)S(1)} %stack.29.where_ref, ...), custom_call_target="tpu_custom_call", output_to_operand_aliasing={{0}: (3, {})} | custom-call | tf_op jit(solution)/shard_map/pallas_call | solution.py:225
  67.5 1.4 %collective-permute-start.17 = (bf16[4,128,128]{2,1,0:T(8,128)(2,1)S(1)}, bf16[4,128,128]{2,1,0:T(8,128)(2,1)S(1)}, u32[]{:S(2)}, u32[]{:S(2)}) collective-permute-start(bf16[4,128,128]{2,1,0:T(8,128)(2,1)S(1)} %bitcast.25), channel_id=1, source_target_pairs={{0,8},{4,12},{8,0},{12,4},{1,9},{5,13},{9,1},{13,5},{2,10},{6,14},... | collective-permute-start | bytes 393224 | tf_op jit(solution)/shard_map/ppermute | solution.py:253
  70.4 2.7 %collective-permute-done.19.rest_0_ = bf16[64,2688]{1,0:T(8,128)(2,1)S(1)} collective-permute-done((bf16[64,2688]{1,0:T(8,128)(2,1)S(1)}, bf16[64,2688]{1,0:T(8,128)(2,1)S(1)}, u32[]{:S(2)}, u32[]{:S(2)}) %collective-permute-start.19) | collective-permute-done | bytes 344096 | tf_op jit(solution)/shard_map/ppermute | solution.py:260
  75.3 1.4 %collective-permute-start.25 = (bf16[16,128,128]{2,1,0:T(8,128)(2,1)S(1)}, bf16[16,128,128]{2,1,0:T(8,128)(2,1)S(1)}, u32[]{:S(2)}, u32[]{:S(2)}) collective-permute-start(bf16[16,128,128]{2,1,0:T(8,128)(2,1)S(1)} %bitcast.22), channel_id=1, source_target_pairs={{0,8},{4,12},{8,0},{12,4},{1,9},{5,13},{9,1},{13,5},{2,10},{6,14},... | collective-permute-start | bytes 1572872 | tf_op jit(solution)/shard_map/ppermute | solution.py:253
  76.7 6.9 %collective-permute-done.20.rest_1_ = bf16[64,2688]{1,0:T(8,128)(2,1)S(1)} collective-permute-done((bf16[64,2688]{1,0:T(8,128)(2,1)S(1)}, bf16[64,2688]{1,0:T(8,128)(2,1)S(1)}, u32[]{:S(2)}, u32[]{:S(2)}) %collective-permute-start.20) | collective-permute-done | bytes 344096 | tf_op jit(solution)/shard_map/ppermute | solution.py:256
  85.2 1.8 %collective-permute-start.18 = (bf16[4,128,128]{2,1,0:T(8,128)(2,1)S(1)}, bf16[4,128,128]{2,1,0:T(8,128)(2,1)S(1)}, u32[]{:S(2)}, u32[]{:S(2)}) collective-permute-start(bf16[4,128,128]{2,1,0:T(8,128)(2,1)S(1)} %shard_map.103), channel_id=1, source_target_pairs={{0,1},{1,0},{2,3},{3,2},{4,5},{5,4},{6,7},{7,6},{8,9},{9,8},{10,11... | collective-permute-start | bytes 393224 | tf_op jit(solution)/shard_map/ppermute | solution.py:256
  87.0 1.8 %shard_map.108 = (f32[64,3328]{1,0:T(8,128)}, f32[64,2048]{1,0:T(8,128)}) custom-call(s32[6]{0:T(128)S(1)} %stack.29.where_ref, bf16[64,2688]{1,0:T(8,128)(2,1)S(1)} %get-tuple-element.41.half_ref, bf16[64,2688]{1,0:T(8,128)(2,1)S(1)} %get-tuple-element.66.other_ref, bf16[64,2688]{1,0:T(8,128)(2,1)S(1)} %collective-permute-done.19.rest_0_, ...), custom_call_target="tpu_custom_call" | custom-call | tf_op jit(solution)/shard_map/pallas_call | solution.py:225
  88.8 8.3 %collective-permute-done.18.rest_0_ = bf16[4,128,128]{2,1,0:T(8,128)(2,1)S(1)} collective-permute-done((bf16[4,128,128]{2,1,0:T(8,128)(2,1)S(1)}, bf16[4,128,128]{2,1,0:T(8,128)(2,1)S(1)}, u32[]{:S(2)}, u32[]{:S(2)}) %collective-permute-start.18) | collective-permute-done | bytes 131104 | tf_op jit(solution)/shard_map/ppermute | solution.py:256
  97.1 0.9 shard_map.105.near_ref
  98.0 0.9 shard_map.107
  (66 shorter events, 12.6 us)
Async XLA Ops:
  0.6 10.5 %copy-start = (bf16[128,3328]{1,0:T(8,128)(2,1)S(1)}, bf16[128,3328]{1,0:T(8,128)(2,1)}, u32[]{:S(2)}) copy-start(bf16[128,3328]{1,0:T(8,128)(2,1)} %own_ref.1) | copy-start | bytes 2555908
  0.6 10.5 %copy-start.9 = (s32[128]{0:T(128)S(1)}, s32[128]{0:T(128)}, u32[]{:S(2)}) copy-start(s32[128]{0:T(128)} %param.9) | copy-start | bytes 1540
  0.6 38.6 %collective-permute-start.3 = (bf16[128,3328]{1,0:T(8,128)(2,1)}, bf16[128,3328]{1,0:T(8,128)(2,1)}, u32[]{:S(2)}, u32[]{:S(2)}) collective-permute-start(bf16[128,3328]{1,0:T(8,128)(2,1)} %own_ref.1), channel_id=1, source_target_pairs={{0,1},{1,0},{2,3},{3,2},{4,5},{5,4},{6,7},{7,6},{8,9},{9,8},{10,11... | collective-permute-start | bytes 2555912 | tf_op jit(solution)/shard_map/ppermute | solution.py:256
  5.6 29.1 %collective-permute-start.6 = (bf16[16,128,128]{2,1,0:T(8,128)(2,1)}, bf16[16,128,128]{2,1,0:T(8,128)(2,1)}, u32[]{:S(2)}, u32[]{:S(2)}) collective-permute-start(bf16[16,128,128]{2,1,0:T(8,128)(2,1)} %dynamic-slice_bitcast_fusion), channel_id=1, source_target_pairs={{0,2},{1,3},{2,0},{3,1},{4,6},{5,7},{6,4},{7,5},{8,10},{9,11},{10,... | collective-permute-start | bytes 1572872 | tf_op jit(solution)/shard_map/ppermute | solution.py:260
  8.2 2.6 %collective-permute-start = (s32[64]{0:T(128)}, s32[64]{0:T(128)S(1)}, u32[]{:S(2)}, u32[]{:S(2)}) collective-permute-start(s32[64]{0:T(128)} %bitcast.28), channel_id=1, source_target_pairs={{0,4},{4,0},{8,12},{12,8},{1,5},{5,1},{9,13},{13,9},{2,6},{6,2},{1... | collective-permute-start | bytes 776 | tf_op jit(solution)/shard_map/ppermute | solution.py:249
  8.9 35.2 %copy-start.10 = (s32[1,64]{1,0:T(1,128)S(1)}, s32[1,64]{1,0:T(1,128)}, u32[]{:S(2)}) copy-start(s32[1,64]{1,0:T(1,128)} %param.11) | copy-start | bytes 772
  8.9 32.1 %copy-start.1 = (bf16[1,64,128,128]{3,2,1,0:T(8,128)(2,1)S(1)}, bf16[1,64,128,128]{3,2,1,0:T(8,128)(2,1)}, u32[]{:S(2)}) copy-start(bf16[1,64,128,128]{3,2,1,0:T(8,128)(2,1)} %param.10) | copy-start | bytes 6291460
  10.8 37.6 %collective-permute-start.5 = (bf16[11,128,128]{2,1,0:T(8,128)(2,1)}, bf16[11,128,128]{2,1,0:T(8,128)(2,1)S(1)}, u32[]{:S(2)}, u32[]{:S(2)}) collective-permute-start(bf16[11,128,128]{2,1,0:T(8,128)(2,1)} %pad_maximum_fusion), channel_id=1, source_target_pairs={{0,2},{1,3},{2,0},{3,1},{4,6},{5,7},{6,4},{7,5},{8,10},{9,11},{10,... | collective-permute-start | bytes 1081352 | tf_op jit(solution)/shard_map/ppermute | solution.py:260
  14.8 1.3 %collective-permute-start.1 = (f32[128,128]{1,0:T(8,128)S(1)}, f32[128,128]{1,0:T(8,128)S(1)}, u32[]{:S(2)}, u32[]{:S(2)}) collective-permute-start(f32[128,128]{1,0:T(8,128)S(1)} %shard_map.94), channel_id=1, source_target_pairs={{0,4},{4,0},{8,12},{12,8},{1,5},{5,1},{9,13},{13,9},{2,6},{6,2},{1... | collective-permute-start | bytes 196616 | tf_op jit(solution)/shard_map/ppermute | solution.py:249
  16.1 4.3 %collective-permute-start.2 = (f32[128,128]{1,0:T(8,128)S(1)}, f32[128,128]{1,0:T(8,128)S(1)}, u32[]{:S(2)}, u32[]{:S(2)}) collective-permute-start(f32[128,128]{1,0:T(8,128)S(1)} %add.25.both_ref), channel_id=1, source_target_pairs={{0,8},{4,12},{8,0},{12,4},{1,9},{5,13},{9,1},{13,5},{2,10},{6,14},... | collective-permute-start | bytes 196616 | tf_op jit(solution)/shard_map/ppermute | solution.py:253
  39.3 19.5 %collective-permute-start.8 = (bf16[16,128,128]{2,1,0:T(8,128)(2,1)}, bf16[16,128,128]{2,1,0:T(8,128)(2,1)}, u32[]{:S(2)}, u32[]{:S(2)}) collective-permute-start(bf16[16,128,128]{2,1,0:T(8,128)(2,1)} %collective-permute-done.6.rest_0_), channel_id=1, source_target_pairs={{0,16},{16,0},{1,17},{17,1},{2,18},{18,2},{3,19},{19,3},{4,20},{20... | collective-permute-start | bytes 1572872 | tf_op jit(solution)/shard_map/ppermute | solution.py:263
  40.9 13.4 %collective-permute-start.4 = (bf16[64,2176]{1,0:T(8,128)(2,1)}, bf16[64,2176]{1,0:T(8,128)(2,1)S(1)}, u32[]{:S(2)}, u32[]{:S(2)}) collective-permute-start(bf16[64,2176]{1,0:T(8,128)(2,1)} %copy-done.7), channel_id=1, source_target_pairs={{0,1},{1,0},{2,3},{3,2},{4,5},{5,4},{6,7},{7,6},{8,9},{9,8},{10,11... | collective-permute-start | bytes 835592 | tf_op jit(solution)/shard_map/ppermute | solution.py:256
  41.0 15.0 %collective-permute-start.7 = (bf16[6,128,128]{2,1,0:T(8,128)(2,1)S(1)}, bf16[6,128,128]{2,1,0:T(8,128)(2,1)S(1)}, u32[]{:S(2)}, u32[]{:S(2)}) collective-permute-start(bf16[6,128,128]{2,1,0:T(8,128)(2,1)S(1)} %dynamic-slice_bitcast_fusion.2), channel_id=1, source_target_pairs={{0,2},{1,3},{2,0},{3,1},{4,6},{5,7},{6,4},{7,5},{8,10},{9,11},{10,... | collective-permute-start | bytes 589832 | tf_op jit(solution)/shard_map/ppermute | solution.py:260
  44.0 10.3 %copy-start.8 = (bf16[64,2176]{1,0:T(8,128)(2,1)S(1)}, bf16[64,2176]{1,0:T(8,128)(2,1)}, u32[]{:S(2)}) copy-start(bf16[64,2176]{1,0:T(8,128)(2,1)} %copy-done.7) | copy-start | bytes 835588
  48.5 15.3 %collective-permute-start.9 = (bf16[10,128,128]{2,1,0:T(8,128)(2,1)S(1)}, bf16[10,128,128]{2,1,0:T(8,128)(2,1)S(1)}, u32[]{:S(2)}, u32[]{:S(2)}) collective-permute-start(bf16[10,128,128]{2,1,0:T(8,128)(2,1)S(1)} %slice.3), channel_id=1, source_target_pairs={{0,16},{16,0},{1,17},{17,1},{2,18},{18,2},{3,19},{19,3},{4,20},{20... | collective-permute-start | bytes 983048 | tf_op jit(solution)/shard_map/ppermute | solution.py:263
  56.0 7.8 %collective-permute-start.10 = (bf16[6,128,128]{2,1,0:T(8,128)(2,1)S(1)}, bf16[6,128,128]{2,1,0:T(8,128)(2,1)S(1)}, u32[]{:S(2)}, u32[]{:S(2)}) collective-permute-start(bf16[6,128,128]{2,1,0:T(8,128)(2,1)S(1)} %collective-permute-done.7.rest_2_), channel_id=1, source_target_pairs={{0,16},{16,0},{1,17},{17,1},{2,18},{18,2},{3,19},{19,3},{4,20},{20... | collective-permute-start | bytes 589832 | tf_op jit(solution)/shard_map/ppermute | solution.py:263
  56.8 16.3 %collective-permute-start.19 = (bf16[64,2688]{1,0:T(8,128)(2,1)S(1)}, bf16[64,2688]{1,0:T(8,128)(2,1)S(1)}, u32[]{:S(2)}, u32[]{:S(2)}) collective-permute-start(bf16[64,2688]{1,0:T(8,128)(2,1)S(1)} %get-tuple-element.41.half_ref), channel_id=1, source_target_pairs={{0,2},{1,3},{2,0},{3,1},{4,6},{5,7},{6,4},{7,5},{8,10},{9,11},{10,... | collective-permute-start | bytes 1032200 | tf_op jit(solution)/shard_map/ppermute | solution.py:260
  65.3 1.4 %collective-permute-start.11 = (bf16[1,4,128,128]{3,2,1,0:T(8,128)(2,1)S(1)}, bf16[1,4,128,128]{3,2,1,0:T(8,128)(2,1)S(1)}, u32[]{:S(2)}, u32[]{:S(2)}) collective-permute-start(bf16[1,4,128,128]{3,2,1,0:T(8,128)(2,1)S(1)} %get-tuple-element.53), channel_id=1, source_target_pairs={{0,4},{4,0},{8,12},{12,8},{1,5},{5,1},{9,13},{13,9},{2,6},{6,2},{1... | collective-permute-start | bytes 393224 | tf_op jit(solution)/shard_map/ppermute | solution.py:249
  65.4 2.1 %collective-permute-start.12 = (bf16[1,4,128,128]{3,2,1,0:T(8,128)(2,1)S(1)}, bf16[1,4,128,128]{3,2,1,0:T(8,128)(2,1)S(1)}, u32[]{:S(2)}, u32[]{:S(2)}) collective-permute-start(bf16[1,4,128,128]{3,2,1,0:T(8,128)(2,1)S(1)} %get-tuple-element.55), channel_id=1, source_target_pairs={{0,4},{4,0},{8,12},{12,8},{1,5},{5,1},{9,13},{13,9},{2,6},{6,2},{1... | collective-permute-start | bytes 393224 | tf_op jit(solution)/shard_map/ppermute | solution.py:249
  65.9 3.0 %collective-permute-start.13 = (bf16[1,4,128,128]{3,2,1,0:T(8,128)(2,1)S(1)}, bf16[1,4,128,128]{3,2,1,0:T(8,128)(2,1)S(1)}, u32[]{:S(2)}, u32[]{:S(2)}) collective-permute-start(bf16[1,4,128,128]{3,2,1,0:T(8,128)(2,1)S(1)} %get-tuple-element.56), channel_id=1, source_target_pairs={{0,4},{4,0},{8,12},{12,8},{1,5},{5,1},{9,13},{13,9},{2,6},{6,2},{1... | collective-permute-start | bytes 393224 | tf_op jit(solution)/shard_map/ppermute | solution.py:249
  66.0 2.9 %collective-permute-start.14 = (bf16[1,4,128,128]{3,2,1,0:T(8,128)(2,1)S(1)}, bf16[1,4,128,128]{3,2,1,0:T(8,128)(2,1)S(1)}, u32[]{:S(2)}, u32[]{:S(2)}) collective-permute-start(bf16[1,4,128,128]{3,2,1,0:T(8,128)(2,1)S(1)} %get-tuple-element.57), channel_id=1, source_target_pairs={{0,4},{4,0},{8,12},{12,8},{1,5},{5,1},{9,13},{13,9},{2,6},{6,2},{1... | collective-permute-start | bytes 393224 | tf_op jit(solution)/shard_map/ppermute | solution.py:249
  66.7 16.9 %collective-permute-start.16 = (bf16[16,128,128]{2,1,0:T(8,128)(2,1)S(1)}, bf16[16,128,128]{2,1,0:T(8,128)(2,1)S(1)}, u32[]{:S(2)}, u32[]{:S(2)}) collective-permute-start(bf16[16,128,128]{2,1,0:T(8,128)(2,1)S(1)} %get-tuple-element.59), channel_id=1, source_target_pairs={{0,4},{4,0},{8,12},{12,8},{1,5},{5,1},{9,13},{13,9},{2,6},{6,2},{1... | collective-permute-start | bytes 1572872 | tf_op jit(solution)/shard_map/ppermute | solution.py:249
  67.5 6.4 %collective-permute-start.17 = (bf16[4,128,128]{2,1,0:T(8,128)(2,1)S(1)}, bf16[4,128,128]{2,1,0:T(8,128)(2,1)S(1)}, u32[]{:S(2)}, u32[]{:S(2)}) collective-permute-start(bf16[4,128,128]{2,1,0:T(8,128)(2,1)S(1)} %bitcast.25), channel_id=1, source_target_pairs={{0,8},{4,12},{8,0},{12,4},{1,9},{5,13},{9,1},{13,5},{2,10},{6,14},... | collective-permute-start | bytes 393224 | tf_op jit(solution)/shard_map/ppermute | solution.py:253
  69.5 4.7 %collective-permute-start.24 = (bf16[1,8,128,128]{3,2,1,0:T(8,128)(2,1)S(1)}, bf16[1,8,128,128]{3,2,1,0:T(8,128)(2,1)S(1)}, u32[]{:S(2)}, u32[]{:S(2)}) collective-permute-start(bf16[1,8,128,128]{3,2,1,0:T(8,128)(2,1)S(1)} %get-tuple-element.65), channel_id=1, source_target_pairs={{0,4},{4,0},{8,12},{12,8},{1,5},{5,1},{9,13},{13,9},{2,6},{6,2},{1... | collective-permute-start | bytes 786440 | tf_op jit(solution)/shard_map/ppermute | solution.py:249
  69.7 13.9 %collective-permute-start.21 = (bf16[12,128,128]{2,1,0:T(8,128)(2,1)S(1)}, bf16[12,128,128]{2,1,0:T(8,128)(2,1)S(1)}, u32[]{:S(2)}, u32[]{:S(2)}) collective-permute-start(bf16[12,128,128]{2,1,0:T(8,128)(2,1)S(1)} %bitcast.24), channel_id=1, source_target_pairs={{0,8},{4,12},{8,0},{12,4},{1,9},{5,13},{9,1},{13,5},{2,10},{6,14},... | collective-permute-start | bytes 1179656 | tf_op jit(solution)/shard_map/ppermute | solution.py:253
  73.1 1.5 %collective-permute-start.23 = (bf16[1,8,128,128]{3,2,1,0:T(8,128)(2,1)S(1)}, bf16[1,8,128,128]{3,2,1,0:T(8,128)(2,1)S(1)}, u32[]{:S(2)}, u32[]{:S(2)}) collective-permute-start(bf16[1,8,128,128]{3,2,1,0:T(8,128)(2,1)S(1)} %get-tuple-element.63), channel_id=1, source_target_pairs={{0,4},{4,0},{8,12},{12,8},{1,5},{5,1},{9,13},{13,9},{2,6},{6,2},{1... | collective-permute-start | bytes 786440 | tf_op jit(solution)/shard_map/ppermute | solution.py:249
  73.9 9.7 %collective-permute-start.20 = (bf16[64,2688]{1,0:T(8,128)(2,1)S(1)}, bf16[64,2688]{1,0:T(8,128)(2,1)S(1)}, u32[]{:S(2)}, u32[]{:S(2)}) collective-permute-start(bf16[64,2688]{1,0:T(8,128)(2,1)S(1)} %collective-permute-done.19.rest_0_), channel_id=1, source_target_pairs={{0,1},{1,0},{2,3},{3,2},{4,5},{5,4},{6,7},{7,6},{8,9},{9,8},{10,11... | collective-permute-start | bytes 1032200 | tf_op jit(solution)/shard_map/ppermute | solution.py:256
  74.2 14.6 %collective-permute-start.15 = (bf16[16,128,128]{2,1,0:T(8,128)(2,1)S(1)}, bf16[16,128,128]{2,1,0:T(8,128)(2,1)S(1)}, u32[]{:S(2)}, u32[]{:S(2)}) collective-permute-start(bf16[16,128,128]{2,1,0:T(8,128)(2,1)S(1)} %get-tuple-element.58), channel_id=1, source_target_pairs={{0,4},{4,0},{8,12},{12,8},{1,5},{5,1},{9,13},{13,9},{2,6},{6,2},{1... | collective-permute-start | bytes 1572872 | tf_op jit(solution)/shard_map/ppermute | solution.py:249
  75.3 22.7 %collective-permute-start.25 = (bf16[16,128,128]{2,1,0:T(8,128)(2,1)S(1)}, bf16[16,128,128]{2,1,0:T(8,128)(2,1)S(1)}, u32[]{:S(2)}, u32[]{:S(2)}) collective-permute-start(bf16[16,128,128]{2,1,0:T(8,128)(2,1)S(1)} %bitcast.22), channel_id=1, source_target_pairs={{0,8},{4,12},{8,0},{12,4},{1,9},{5,13},{9,1},{13,5},{2,10},{6,14},... | collective-permute-start | bytes 1572872 | tf_op jit(solution)/shard_map/ppermute | solution.py:253
  84.3 12.8 %copy-start.5 = (bf16[64,2048]{1,0:T(8,128)(2,1)S(1)}, bf16[64,2048]{1,0:T(8,128)(2,1)}, u32[]{:S(2)}) copy-start(bf16[64,2048]{1,0:T(8,128)(2,1)} %adapter_ref.2) | copy-start | bytes 786436
  84.3 12.8 %collective-permute-start.22 = (bf16[12,128,128]{2,1,0:T(8,128)(2,1)S(1)}, bf16[12,128,128]{2,1,0:T(8,128)(2,1)S(1)}, u32[]{:S(2)}, u32[]{:S(2)}) collective-permute-start(bf16[12,128,128]{2,1,0:T(8,128)(2,1)S(1)} %shard_map.104), channel_id=1, source_target_pairs={{0,1},{1,0},{2,3},{3,2},{4,5},{5,4},{6,7},{7,6},{8,9},{9,8},{10,11... | collective-permute-start | bytes 1179656 | tf_op jit(solution)/shard_map/ppermute | solution.py:256
  85.2 11.8 %collective-permute-start.18 = (bf16[4,128,128]{2,1,0:T(8,128)(2,1)S(1)}, bf16[4,128,128]{2,1,0:T(8,128)(2,1)S(1)}, u32[]{:S(2)}, u32[]{:S(2)}) collective-permute-start(bf16[4,128,128]{2,1,0:T(8,128)(2,1)S(1)} %shard_map.103), channel_id=1, source_target_pairs={{0,1},{1,0},{2,3},{3,2},{4,5},{5,4},{6,7},{7,6},{8,9},{9,8},{10,11... | collective-permute-start | bytes 393224 | tf_op jit(solution)/shard_map/ppermute | solution.py:256
  (5 other events, 4.8 us)
